TPU v7x, 32 devices: a whole 2x2x4 slice. The times are simulated.
32 devices in a mesh: dp: 8 (over y, x, core), fsdp: 4 (over z).
Axes of the slice: x: 2, y: 2, z: 4, core: 2. Of those that a mesh axis runs over, the one named last changes fastest.
Arguments:
- tokens: bfloat16 [32, 256, 1152], P(('dp', 'fsdp')), may hold values from -6 to 6
- condition: bfloat16 [32, 1152], P(('dp', 'fsdp')), may hold values from -6 to 6
- grid_sizes: int32 [32, 2], P(('dp', 'fsdp')), may hold values from 12 to 20, as said below
- w_ada: bfloat16 [1152, 6912], P('fsdp'), may hold values from -0.1875 to 0.1875
- w_qkv: bfloat16 [1152, 3456], P('fsdp'), may hold values from -0.1875 to 0.1875
- w_out: bfloat16 [1152, 1152], P('fsdp'), may hold values from -1 to 1
- w_up: bfloat16 [1152, 4608], P('fsdp'), may hold values from -0.1875 to 0.1875
- w_down: bfloat16 [4608, 1152], P('fsdp'), may hold values from -0.09375 to 0.09375
- b_ada: bfloat16 [6912], P('fsdp'), may hold values from -3 to 3
- b_qv: bfloat16 [2304], P('fsdp'), may hold values from -3 to 3
- b_out: bfloat16 [1152], P('fsdp'), may hold values from -3 to 3
- b_up: bfloat16 [4608], P('fsdp'), may hold values from -3 to 3
- b_down: bfloat16 [1152], P('fsdp'), may hold values from -3 to 3
- cotangent: bfloat16 [32, 256, 1152], P(('dp', 'fsdp')), may hold values from -6 to 6
Outputs:
- output: bfloat16 [32, 256, 1152], P(('dp', 'fsdp'))
- grad_tokens: bfloat16 [32, 256, 1152], P(('dp', 'fsdp'))
- grad_condition: float32 [32, 1152], P(('dp', 'fsdp'))
- grad_w_ada: float32 [1152, 6912], P('fsdp', 'dp')
- grad_w_qkv: float32 [1152, 3456], P('fsdp', 'dp')
- grad_w_out: float32 [1152, 1152], P('fsdp', 'dp')
- grad_w_up: float32 [1152, 4608], P('fsdp', 'dp')
- grad_w_down: float32 [4608, 1152], P('fsdp', 'dp')
- grad_b_ada: float32 [6912], P('fsdp')
- grad_b_qv: float32 [2304], P('fsdp')
- grad_b_out: float32 [1152], P('fsdp')
- grad_b_up: float32 [4608], P('fsdp')
- grad_b_down: float32 [1152], P('fsdp')
Inputs may be any that keep to these rules, and one draw needn't show every extreme that they name: `grid_sizes`: each image grid has 12 to 20 rows and columns and at most 256 tokens; image 0 has 12 rows and 20 columns, and image 1 has 20 rows and 12 columns.
All inputs are finite; a program needn't handle non-finite values.
Results may differ from a plain program's by a relative error of at most 0.015.
The roundings to bfloat16 on the way count: a program that leaves them out, or rounds other values in their place, can miss the bound.
Values may be sent and summed in bfloat16 or wider, within the bound.
No kernel may reach another device: no remote copies, remote signals or barrier semaphores. Data moves between devices by JAX's collectives and lax.ppermute only.
A program may use at most 256 MiB of HBM per device.

v0:
```python
import math

import jax
import jax.numpy as jnp
from jax import lax
from jax.sharding import PartitionSpec as P

HEAD_DIM = 72


epsilon = 1e-06
masked_value = -1e30
gelu_root = math.sqrt(2.0 / math.pi)


def layer_norm(values_in):
    centred = values_in - jnp.mean(values_in, axis=-1, keepdims=True)
    spread = jnp.mean(centred * centred, axis=-1, keepdims=True)
    return centred * lax.rsqrt(spread + epsilon)


def gelu_tanh(pre_act):
    return (
        0.5
        * pre_act
        * (1.0 + jnp.tanh(gelu_root * (pre_act + 0.044715 * pre_act * pre_act * pre_act)))
    )


def apply_rows(left, right):
    return jnp.einsum("isd,de->ise", left, right, preferred_element_type=jnp.float32)


def forward_pass(weights_full, tokens_wide, cond_act, live_keys, kept_lse):
    w_ada, w_qkv, w_out, w_up, w_down, b_ada, b_qv, b_out, b_up, b_down = weights_full
    width = w_out.shape[0]
    images = tokens_wide.shape[0]
    slots = tokens_wide.shape[1]
    heads = width // HEAD_DIM
    modulation = jnp.dot(cond_act, w_ada, preferred_element_type=jnp.float32) + b_ada.astype(
        jnp.float32
    )
    portions = jnp.split(modulation, 6, axis=1)
    modulated = tuple((portion[:, None, :] for portion in portions))
    shift_one, scale_one, gate_one, shift_two, scale_two, gate_two = modulated
    norm_one = layer_norm(tokens_wide)
    normed = (norm_one * (1.0 + scale_one) + shift_one).astype(jnp.bfloat16)
    projected = apply_rows(normed, w_qkv)
    bias_qv = b_qv.astype(jnp.float32)
    queries = (
        (projected[..., :width] + bias_qv[:width])
        .astype(jnp.bfloat16)
        .reshape(images, slots, heads, HEAD_DIM)
    )
    key_part = (
        projected[..., width : 2 * width]
        .astype(jnp.bfloat16)
        .reshape(images, slots, heads, HEAD_DIM)
    )
    values = (
        (projected[..., 2 * width :] + bias_qv[width:])
        .astype(jnp.bfloat16)
        .reshape(images, slots, heads, HEAD_DIM)
    )
    raw = jnp.einsum(
        "iqhe,ikhe->ihqk", queries, key_part, preferred_element_type=jnp.float32
    ) * HEAD_DIM ** (-0.5)
    scores = jnp.where(live_keys[:, None, None, :], raw, masked_value)
    if kept_lse is None:
        highest = jnp.max(scores, axis=-1, keepdims=True)
        lse = highest + jnp.log(jnp.sum(jnp.exp(scores - highest), axis=-1, keepdims=True))
    else:
        lse = kept_lse
    probs = jnp.exp(scores - lse)
    probs_low = probs.astype(jnp.bfloat16)
    attended = jnp.einsum("ihqk,ikhe->iqhe", probs_low, values, preferred_element_type=jnp.float32)
    attended = attended.reshape(images, slots, width).astype(jnp.bfloat16)
    attn_out = apply_rows(attended, w_out) + b_out.astype(jnp.float32)
    middle = tokens_wide + gate_one * attn_out
    norm_two = layer_norm(middle)
    normed_two = (norm_two * (1.0 + scale_two) + shift_two).astype(jnp.bfloat16)
    pre_act = apply_rows(normed_two, w_up) + b_up.astype(jnp.float32)
    activated = gelu_tanh(pre_act).astype(jnp.bfloat16)
    mlp_out = apply_rows(activated, w_down) + b_down.astype(jnp.float32)
    return (
        modulated,
        norm_one,
        normed,
        queries,
        key_part,
        values,
        lse,
        probs,
        probs_low,
        attended,
        attn_out,
        middle,
        norm_two,
        normed_two,
        pre_act,
        activated,
        mlp_out,
    )


def body(
    tokens,
    condition,
    grid_sizes,
    w_ada,
    w_qkv,
    w_out,
    w_up,
    w_down,
    b_ada,
    b_qv,
    b_out,
    b_up,
    b_down,
    cotangent,
):
    weights_full = (
        lax.all_gather(w_ada, "fsdp", axis=0, tiled=True),
        lax.all_gather(w_qkv, "fsdp", axis=0, tiled=True),
        lax.all_gather(w_out, "fsdp", axis=0, tiled=True),
        lax.all_gather(w_up, "fsdp", axis=0, tiled=True),
        lax.all_gather(w_down, "fsdp", axis=0, tiled=True),
        lax.all_gather(b_ada, "fsdp", axis=0, tiled=True),
        lax.all_gather(b_qv, "fsdp", axis=0, tiled=True),
        lax.all_gather(b_out, "fsdp", axis=0, tiled=True),
        lax.all_gather(b_up, "fsdp", axis=0, tiled=True),
        lax.all_gather(b_down, "fsdp", axis=0, tiled=True),
    )
    images = tokens.shape[0]
    slots = tokens.shape[1]
    width = tokens.shape[2]
    heads = width // HEAD_DIM
    live_counts = grid_sizes[:, 0] * grid_sizes[:, 1]
    live_keys = lax.broadcasted_iota(jnp.int32, (images, slots), 1) < live_counts[:, None]
    live_rows = live_keys.astype(jnp.float32)[:, :, None]
    tokens_wide = tokens.astype(jnp.float32)
    cond_wide = condition.astype(jnp.float32)
    cond_act = (cond_wide * jax.nn.sigmoid(cond_wide)).astype(jnp.bfloat16)
    saved = forward_pass(weights_full, tokens_wide, cond_act, live_keys, None)
    middle_first = saved[11]
    gate_first = saved[0][5]
    mlp_first = saved[16]
    output = (live_rows * (middle_first + gate_first * mlp_first)).astype(jnp.bfloat16)
    weights_back = (
        lax.all_gather(w_ada, "fsdp", axis=0, tiled=True),
        lax.all_gather(w_qkv, "fsdp", axis=0, tiled=True),
        lax.all_gather(w_out, "fsdp", axis=0, tiled=True),
        lax.all_gather(w_up, "fsdp", axis=0, tiled=True),
        lax.all_gather(w_down, "fsdp", axis=0, tiled=True),
        lax.all_gather(b_ada, "fsdp", axis=0, tiled=True),
        lax.all_gather(b_qv, "fsdp", axis=0, tiled=True),
        lax.all_gather(b_out, "fsdp", axis=0, tiled=True),
        lax.all_gather(b_up, "fsdp", axis=0, tiled=True),
        lax.all_gather(b_down, "fsdp", axis=0, tiled=True),
    )
    saved = forward_pass(weights_back, tokens_wide, cond_act, live_keys, saved[6])
    (
        modulated,
        norm_one,
        normed,
        queries,
        key_part,
        values,
        lse,
        probs,
        probs_low,
        attended,
        attn_out,
        middle,
        norm_two,
        normed_two,
        pre_act,
        activated,
        mlp_out,
    ) = saved
    shift_one, scale_one, gate_one, shift_two, scale_two, gate_two = modulated
    ada_full, qkv_full, out_full, up_full, down_full = (
        weights_back[0],
        weights_back[1],
        weights_back[2],
        weights_back[3],
        weights_back[4],
    )
    upstream = live_rows * cotangent.astype(jnp.float32)
    d_gate_two = jnp.sum(upstream * mlp_out, axis=1)
    d_mlp = (gate_two * upstream).astype(jnp.bfloat16)
    grad_w_down = jnp.einsum("isf,isd->fd", activated, d_mlp, preferred_element_type=jnp.float32)
    grad_b_down = jnp.sum(d_mlp.astype(jnp.float32), axis=(0, 1))
    d_act = jnp.einsum("isd,fd->isf", d_mlp, down_full, preferred_element_type=jnp.float32)
    unused_gelu, gelu_pull = jax.vjp(gelu_tanh, pre_act)
    d_pre = gelu_pull(d_act)[0].astype(jnp.bfloat16)
    grad_w_up = jnp.einsum("isd,isf->df", normed_two, d_pre, preferred_element_type=jnp.float32)
    grad_b_up = jnp.sum(d_pre.astype(jnp.float32), axis=(0, 1))
    d_normed_two = jnp.einsum("isf,df->isd", d_pre, up_full, preferred_element_type=jnp.float32)
    d_shift_two = jnp.sum(d_normed_two, axis=1)
    d_scale_two = jnp.sum(d_normed_two * norm_two, axis=1)
    unused_norm, second_pull = jax.vjp(layer_norm, middle)
    d_middle = upstream + second_pull(d_normed_two * (1.0 + scale_two))[0]
    d_gate_one = jnp.sum(d_middle * attn_out, axis=1)
    d_attn = (gate_one * d_middle).astype(jnp.bfloat16)
    grad_w_out = jnp.einsum("isd,ise->de", attended, d_attn, preferred_element_type=jnp.float32)
    grad_b_out = jnp.sum(d_attn.astype(jnp.float32), axis=(0, 1))
    d_attended = jnp.einsum("ise,de->isd", d_attn, out_full, preferred_element_type=jnp.float32)
    d_attended = d_attended.astype(jnp.bfloat16).reshape(images, slots, heads, HEAD_DIM)
    d_probs = jnp.einsum("iqhe,ikhe->ihqk", d_attended, values, preferred_element_type=jnp.float32)
    d_values = jnp.einsum(
        "ihqk,iqhe->ikhe", probs_low, d_attended, preferred_element_type=jnp.float32
    ).astype(jnp.bfloat16)
    row_inner = jnp.sum(probs * d_probs, axis=-1, keepdims=True)
    d_scores = (probs * (d_probs - row_inner)).astype(jnp.bfloat16)
    d_queries = (
        jnp.einsum("ihqk,ikhe->iqhe", d_scores, key_part, preferred_element_type=jnp.float32)
        * HEAD_DIM ** (-0.5)
    ).astype(jnp.bfloat16)
    d_keys = (
        jnp.einsum("ihqk,iqhe->ikhe", d_scores, queries, preferred_element_type=jnp.float32)
        * HEAD_DIM ** (-0.5)
    ).astype(jnp.bfloat16)
    d_projected = jnp.concatenate(
        [
            d_queries.reshape(images, slots, width),
            d_keys.reshape(images, slots, width),
            d_values.reshape(images, slots, width),
        ],
        axis=2,
    )
    grad_w_qkv = jnp.einsum("isd,ise->de", normed, d_projected, preferred_element_type=jnp.float32)
    grad_b_qv = jnp.concatenate(
        [
            jnp.sum(d_queries.astype(jnp.float32), axis=(0, 1)).reshape(width),
            jnp.sum(d_values.astype(jnp.float32), axis=(0, 1)).reshape(width),
        ]
    )
    d_normed = jnp.einsum("ise,de->isd", d_projected, qkv_full, preferred_element_type=jnp.float32)
    d_shift_one = jnp.sum(d_normed, axis=1)
    d_scale_one = jnp.sum(d_normed * norm_one, axis=1)
    unused_first, first_pull = jax.vjp(layer_norm, tokens_wide)
    grad_tokens = (d_middle + first_pull(d_normed * (1.0 + scale_one))[0]).astype(jnp.bfloat16)
    d_modulation = jnp.concatenate(
        [d_shift_one, d_scale_one, d_gate_one, d_shift_two, d_scale_two, d_gate_two], axis=1
    ).astype(jnp.bfloat16)
    grad_w_ada = jnp.einsum("id,ie->de", cond_act, d_modulation, preferred_element_type=jnp.float32)
    grad_b_ada = jnp.sum(d_modulation.astype(jnp.float32), axis=0)
    d_cond_act = jnp.einsum("ie,de->id", d_modulation, ada_full, preferred_element_type=jnp.float32)
    unused_silu, silu_pull = jax.vjp(lambda inner: inner * jax.nn.sigmoid(inner), cond_wide)
    grad_condition = silu_pull(d_cond_act)[0]
    narrow = (
        lax.psum_scatter(
            grad_w_ada.astype(jnp.bfloat16), "fsdp", scatter_dimension=0, tiled=True
        ).astype(jnp.float32),
        lax.psum_scatter(
            grad_w_qkv.astype(jnp.bfloat16), "fsdp", scatter_dimension=0, tiled=True
        ).astype(jnp.float32),
        lax.psum_scatter(
            grad_w_out.astype(jnp.bfloat16), "fsdp", scatter_dimension=0, tiled=True
        ).astype(jnp.float32),
        lax.psum_scatter(
            grad_w_up.astype(jnp.bfloat16), "fsdp", scatter_dimension=0, tiled=True
        ).astype(jnp.float32),
        lax.psum_scatter(
            grad_w_down.astype(jnp.bfloat16), "fsdp", scatter_dimension=0, tiled=True
        ).astype(jnp.float32),
        lax.psum_scatter(
            grad_b_ada.astype(jnp.bfloat16), "fsdp", scatter_dimension=0, tiled=True
        ).astype(jnp.float32),
        lax.psum_scatter(
            grad_b_qv.astype(jnp.bfloat16), "fsdp", scatter_dimension=0, tiled=True
        ).astype(jnp.float32),
        lax.psum_scatter(
            grad_b_out.astype(jnp.bfloat16), "fsdp", scatter_dimension=0, tiled=True
        ).astype(jnp.float32),
        lax.psum_scatter(
            grad_b_up.astype(jnp.bfloat16), "fsdp", scatter_dimension=0, tiled=True
        ).astype(jnp.float32),
        lax.psum_scatter(
            grad_b_down.astype(jnp.bfloat16), "fsdp", scatter_dimension=0, tiled=True
        ).astype(jnp.float32),
    )
    summed_weights = (
        lax.psum_scatter(narrow[0], "dp", scatter_dimension=1, tiled=True),
        lax.psum_scatter(narrow[1], "dp", scatter_dimension=1, tiled=True),
        lax.psum_scatter(narrow[2], "dp", scatter_dimension=1, tiled=True),
        lax.psum_scatter(narrow[3], "dp", scatter_dimension=1, tiled=True),
        lax.psum_scatter(narrow[4], "dp", scatter_dimension=1, tiled=True),
    )
    summed_biases = lax.psum((narrow[5], narrow[6], narrow[7], narrow[8], narrow[9]), "dp")
    return (
        output,
        grad_tokens,
        grad_condition,
        summed_weights[0],
        summed_weights[1],
        summed_weights[2],
        summed_weights[3],
        summed_weights[4],
        summed_biases[0],
        summed_biases[1],
        summed_biases[2],
        summed_biases[3],
        summed_biases[4],
    )


def solution(mesh):
    return jax.shard_map(
        body,
        mesh=mesh,
        in_specs=(
            P(("dp", "fsdp"), None, None),
            P(("dp", "fsdp"), None),
            P(("dp", "fsdp"), None),
            P("fsdp", None),
            P("fsdp", None),
            P("fsdp", None),
            P("fsdp", None),
            P("fsdp", None),
            P("fsdp"),
            P("fsdp"),
            P("fsdp"),
            P("fsdp"),
            P("fsdp"),
            P(("dp", "fsdp"), None, None),
        ),
        out_specs=(
            P(("dp", "fsdp"), None, None),
            P(("dp", "fsdp"), None, None),
            P(("dp", "fsdp"), None),
            P("fsdp", "dp"),
            P("fsdp", "dp"),
            P("fsdp", "dp"),
            P("fsdp", "dp"),
            P("fsdp", "dp"),
            P("fsdp"),
            P("fsdp"),
            P("fsdp"),
            P("fsdp"),
            P("fsdp"),
        ),
        check_vma=False,
    )
```

profile of v0, /device:TPU:25, one launch (start us, length us, event | category | flops | bytes accessed | tf_op | source)
XLA Modules:
  0.0 2051.7 jit_solution(9514321274415671537)
XLA Ops:
  14.3 12.2 all-reduce.11
  27.2 19.1 all-gather
  50.6 230.8 %all-gather.7.cloned.1.call-done = bf16[1152,6912]{1,0:T(8,128)(2,1)} async-done(((bf16[288,6912]{1,0:T(8,128)(2,1)}), bf16[1152,6912]{1,0:T(8,128)(2,1)}) %all-gather.7.cloned.1.call-update) | async-done | bytes 15925264 | tf_op jit(solution)/shard_map/all_gather | solution.py:123
  281.3 7.7 convolution_reduce_fusion
  289.8 133.9 %all-gather.9.cloned.1.call-done = bf16[1152,3456]{1,0:T(8,128)(2,1)} async-done(((bf16[288,3456]{1,0:T(8,128)(2,1)}), bf16[1152,3456]{1,0:T(8,128)(2,1)}) %all-gather.9.cloned.1.call-update) | async-done | bytes 7962640 | tf_op jit(solution)/shard_map/all_gather | solution.py:124
  423.7 6.0 convolution_bitcast_fusion
  429.7 0.9 slice.46
  431.3 1.3 copy.53
  432.6 1.1 fusion.6
  433.7 1.0 exponential_reduce_fusion
  434.7 0.9 copy-done
  435.7 1.7 convolution_convert_fusion.6
  437.4 42.1 %all-gather.11.cloned.1.call-done = bf16[1152,1152]{1,0:T(8,128)(2,1)} async-done(((bf16[288,1152]{1,0:T(8,128)(2,1)}), bf16[1152,1152]{1,0:T(8,128)(2,1)}) %all-gather.11.cloned.1.call-update) | async-done | bytes 2654224 | tf_op jit(solution)/shard_map/all_gather | solution.py:125
  479.4 3.9 fusion.60
  485.3 179.9 %all-gather.13.cloned.1.call-done = bf16[1152,4608]{1,0:T(8,128)(2,1)} async-done(((bf16[288,4608]{1,0:T(8,128)(2,1)}), bf16[1152,4608]{1,0:T(8,128)(2,1)}) %all-gather.13.cloned.1.call-update) | async-done | bytes 10616848 | tf_op jit(solution)/shard_map/all_gather | solution.py:126
  665.2 21.5 %convolution_add_fusion = f32[256,4608]{1,0:T(8,128)} fusion(bf16[1152,4608]{1,0:T(8,128)(2,1)} %all-gather.13.cloned.1.call-done, f32[4608]{0:T(1024)} %reshape.504, f32[1,256,1152]{2,1,0:T(8,128)S(1)} %get-tuple-element.85, f32[1152]{0:T(1024)} %get-tuple-element.59, f32[1152]{0:T(1024)} %get-tuple-element.60, f32[256]{0:T(256)} %fusion.46, f32[256]{0:T(256)} %copy-done.29), kind=kOutput, calls=%fused_computation.9 | convolution fusion | flops 2720563200 | bytes 16544768 | tf_op jit(solution)/shard_map/isd,de->ise/dot_general | solution.py:31
  686.7 164.2 %all-gather.15.cloned.1.call-done = bf16[4608,1152]{1,0:T(8,128)(2,1)} async-done(((bf16[1152,1152]{1,0:T(8,128)(2,1)}), bf16[4608,1152]{1,0:T(8,128)(2,1)}) %all-gather.15.cloned.1.call-update) | async-done | bytes 10616848 | tf_op jit(solution)/shard_map/all_gather | solution.py:127
  850.9 10.1 fusion.64
  861.0 8.8 fusion.24
  870.3 1.0 copy-done.15
  871.3 1.0 fusion.58
  873.1 1.9 convolution_convert_fusion.4
  875.0 2.1 copy.55
  877.1 4.3 bitcast_reduce_fusion
  881.5 1.5 multiply_reduce_fusion
  882.9 1.4 multiply_convert_fusion.2
  885.1 1.2 bitcast_reduce_fusion.1
  887.2 5.8 convolution_convert_fusion.2
  893.7 9.0 convolution_convert_fusion.1
  902.8 1.4 convert_element_type.228
  904.2 1.3 convert.45
  906.2 7.0 fusion.20
  913.9 0.9 dynamic-update-slice.4
  915.4 1.9 fusion.18
  917.4 0.9 dynamic-update-slice.5
  918.9 11.8 fusion.23
  930.7 0.9 dynamic-update-slice.6
  931.5 0.9 dynamic-update-slice.7
  932.4 0.9 dynamic-update-slice.8
  934.1 6.6 multiply_convert_fusion
  941.8 2.4 convolution_convert_fusion.3
  944.3 1.0 copy-done.16
  945.3 10.6 convolution_convert_fusion
  956.0 75.8 %reduce-scatter.23.cloned.1.call-done = bf16[288,3456]{1,0:T(8,128)(2,1)} async-done(((bf16[1152,3456]{1,0:T(8,128)(2,1)}), bf16[288,3456]{1,0:T(8,128)(2,1)}) %reduce-scatter.23.cloned.1.call-update) | async-done | bytes 1990672 | tf_op jit(solution)/shard_map/reduce_scatter | solution.py:256
  1031.8 4.5 copy.67
  1036.4 179.1 %reduce-scatter.27.cloned.1.call-done = bf16[288,4608]{1,0:T(8,128)(2,1)} async-done(((bf16[1152,4608]{1,0:T(8,128)(2,1)}), bf16[288,4608]{1,0:T(8,128)(2,1)}) %reduce-scatter.27.cloned.1.call-update) | async-done | bytes 2654224 | tf_op jit(solution)/shard_map/reduce_scatter | solution.py:262
  1215.5 5.5 copy.71
  1221.1 264.9 %reduce-scatter.21.cloned.1.call-done = bf16[288,6912]{1,0:T(8,128)(2,1)} async-done(((bf16[1152,6912]{1,0:T(8,128)(2,1)}), bf16[288,6912]{1,0:T(8,128)(2,1)}) %reduce-scatter.21.cloned.1.call-update) | async-done | bytes 3981328 | tf_op jit(solution)/shard_map/reduce_scatter | solution.py:253
  1485.9 7.7 copy.65
  1493.7 47.0 %reduce-scatter.25.cloned.1.call-done = bf16[288,1152]{1,0:T(8,128)(2,1)} async-done(((bf16[1152,1152]{1,0:T(8,128)(2,1)}), bf16[288,1152]{1,0:T(8,128)(2,1)}) %reduce-scatter.25.cloned.1.call-update) | async-done | bytes 663568 | tf_op jit(solution)/shard_map/reduce_scatter | solution.py:259
  1540.7 2.6 copy.69
  1543.4 180.8 %reduce-scatter.29.cloned.1.call-done = bf16[1152,1152]{1,0:T(8,128)(2,1)} async-done(((bf16[4608,1152]{1,0:T(8,128)(2,1)}), bf16[1152,1152]{1,0:T(8,128)(2,1)}) %reduce-scatter.29.cloned.1.call-update) | async-done | bytes 2654224 | tf_op jit(solution)/shard_map/reduce_scatter | solution.py:265
  1724.2 5.4 copy.73
  1732.5 12.4 all-reduce.10
  1745.2 24.5 %all-reduce.9 = (f32[1728]{0:T(1024)}, f32[576]{0:T(1024)}, f32[288]{0:T(512)}, f32[1152]{0:T(1024)}, f32[288]{0:T(512)}) all-reduce(f32[1728]{0:T(1024)S(1)} %dynamic-slice_convert_fusion.1, f32[576]{0:T(1024)S(1)} %dynamic-slice_convert_fusion.2, f32[288]{0:T(512)S(1)} %get-tuple-element.112, ...), channel_id=1, replica_groups=mesh['dp'=8,'fsdp'=4] {'dp'}, use_global_device_ids=true, to_apply=%region_28.29 | all-reduce | flops 4032 | bytes 32256 | tf_op jit(solution)/shard_map/psum | solution.py:291
  1769.7 10.4 fusion.40
  1780.1 5.9 reduce-scatter.33.cloned.1.call-done
  1786.0 2.1 copy.68
  1788.1 67.2 %reduce-scatter.37.cloned.1.call-done = f32[576,288]{1,0:T(8,128)} async-done(((f32[4608,288]{1,0:T(8,128)}), f32[576,288]{1,0:T(8,128)}) %reduce-scatter.37.cloned.1.call-update) | async-done | bytes 663568
  1855.3 2.3 copy.72
  1857.6 83.4 %reduce-scatter.31.cloned.1.call-done = f32[864,288]{1,0:T(8,128)} async-done(((f32[6912,288]{1,0:T(8,128)}), f32[864,288]{1,0:T(8,128)}) %reduce-scatter.31.cloned.1.call-update) | async-done | bytes 995344
  1941.0 2.7 copy.66
  1943.7 40.5 %reduce-scatter.35.cloned.1.call-done = f32[144,288]{1,0:T(8,128)} async-done(((f32[1152,288]{1,0:T(8,128)}), f32[144,288]{1,0:T(8,128)}) %reduce-scatter.35.cloned.1.call-update) | async-done | bytes 165904
  1984.2 60.8 %reduce-scatter.39.cloned.1.call-done = f32[144,1152]{1,0:T(8,128)} async-done(((f32[1152,1152]{1,0:T(8,128)}), f32[144,1152]{1,0:T(8,128)}) %reduce-scatter.39.cloned.1.call-update) | async-done | bytes 663568
  (202 shorter events, 21.2 us)
Async XLA Ops:
  7.2 274.1 %all-gather.7.cloned.1.call-start = ((), (), s32[]{:S(2)}) async-start(), calls=%async_computation.10 | async-start | bytes 19906560 | tf_op jit(solution)/shard_map/all_gather | solution.py:123
  7.9 415.8 %all-gather.9.cloned.1.call-start = ((), (), s32[]{:S(2)}) async-start(), calls=%async_computation.11 | async-start | bytes 9953280 | tf_op jit(solution)/shard_map/all_gather | solution.py:124
  8.7 470.8 %all-gather.11.cloned.1.call-start = ((), (), s32[]{:S(2)}) async-start(), calls=%async_computation.12 | async-start | bytes 3317760 | tf_op jit(solution)/shard_map/all_gather | solution.py:125
  9.4 1.3 copy-start.54
  9.4 3.9 copy-start.59
  9.4 4.1 copy-start.60
  9.4 4.4 copy-start.55
  9.4 4.6 copy-start.51
  9.5 17.7 copy-start.52
  9.5 37.5 %copy-start.56 = (s32[1,2]{1,0:T(1,128)S(1)}, s32[1,2]{1,0:T(1,128)}, u32[]{:S(2)}) copy-start(s32[1,2]{1,0:T(1,128)} %param.16) | copy-start | bytes 28
  9.5 39.9 %copy-start.2 = (bf16[1,256,1152]{2,1,0:T(8,128)(2,1)S(1)}, bf16[1,256,1152]{2,1,0:T(8,128)(2,1)}, u32[]{:S(2)}) copy-start(bf16[1,256,1152]{2,1,0:T(8,128)(2,1)} %param.14) | copy-start | bytes 1769476
  9.5 655.7 %all-gather.13.cloned.1.call-start = ((), (), s32[]{:S(2)}) async-start(), calls=%async_computation.13 | async-start | bytes 13271040 | tf_op jit(solution)/shard_map/all_gather | solution.py:126
  10.1 39.8 %copy-start.21 = (bf16[1,1152]{1,0:T(2,128)(2,1)S(1)}, bf16[1,1152]{1,0:T(2,128)(2,1)}, u32[]{:S(2)}) copy-start(bf16[1,1152]{1,0:T(2,128)(2,1)} %param.15) | copy-start | bytes 6916
  10.1 840.8 %all-gather.15.cloned.1.call-start = ((), (), s32[]{:S(2)}) async-start(), calls=%async_computation.14 | async-start | bytes 13271040 | tf_op jit(solution)/shard_map/all_gather | solution.py:127
  10.7 1021.2 %reduce-scatter.23.cloned.1.call-start = ((), (), s32[]{:S(2)}) async-start(), calls=%async_computation.16 | async-start | bytes 9953280 | tf_op jit(solution)/shard_map/reduce_scatter | solution.py:256
  48.8 384.9 %copy-start.47 = (pred[256]{0:T(512)(128)(4,1)}, pred[256]{0:T(512)(128)(4,1)S(1)}, u32[]{:S(2)}) copy-start(pred[256]{0:T(512)(128)(4,1)S(1)} %iota_compare_fusion) | copy-start | bytes 772
  49.6 374.1 %copy-start.38 = (f32[256]{0:T(256)}, f32[256]{0:T(256)S(1)}, u32[]{:S(2)}) copy-start(f32[256]{0:T(256)S(1)} %broadcast_multiply_fusion.1) | copy-start | bytes 3076
  49.9 239.2 %copy-start.42 = (f32[256]{0:T(256)}, f32[256]{0:T(256)S(1)}, u32[]{:S(2)}) copy-start(f32[256]{0:T(256)S(1)} %fusion.19) | copy-start | bytes 3076
  49.9 373.8 %copy-start.40 = (f32[256]{0:T(256)}, f32[256]{0:T(256)S(1)}, u32[]{:S(2)}) copy-start(f32[256]{0:T(256)S(1)} %fusion.45) | copy-start | bytes 3076
  50.6 238.5 %copy-start.23 = (f32[1,1152]{1,0:T(1,128)}, f32[1,1152]{1,0:T(1,128)S(1)}, u32[]{:S(2)}) copy-start(f32[1,1152]{1,0:T(1,128)S(1)} %get-tuple-element.81) | copy-start | bytes 13828
  289.8 139.9 %copy-start.27 = (f32[1152]{0:T(1024)}, f32[1152]{0:T(1024)S(1)}, u32[]{:S(2)}) copy-start(f32[1152]{0:T(1024)S(1)} %get-tuple-element.62) | copy-start | bytes 13828
  289.8 139.9 %copy-start.45 = (f32[1152]{0:T(1024)}, f32[1152]{0:T(1024)S(1)}, u32[]{:S(2)}) copy-start(f32[1152]{0:T(1024)S(1)} %get-tuple-element.61) | copy-start | bytes 13828
  431.0 3.7 copy-start.7
  433.7 2.0 copy-start
  850.9 10.1 copy-start.17
  850.9 10.1 copy-start.30
  850.9 10.1 copy-start.35
  860.9 8.9 copy-start.12
  861.0 8.9 copy-start.44
  869.8 2.5 copy-start.3
  869.8 1.5 copy-start.15
  869.8 1.5 copy-start.19
  869.8 1.5 copy-start.25
  869.8 1.5 copy-start.57
  869.9 3.3 copy-start.6
  870.3 2.1 copy-start.5
  870.3 2.0 copy-start.50
  877.1 4.3 copy-start.1
  877.1 4.3 copy-start.8
  877.1 4.3 copy-start.9
  877.1 4.3 copy-start.48
  881.4 4.9 copy-start.61
  885.1 2.1 copy-start.28
  885.1 2.1 copy-start.39
  885.1 2.1 copy-start.41
  885.1 2.1 copy-start.46
  893.0 322.5 %reduce-scatter.27.cloned.1.call-start = ((), (), s32[]{:S(2)}) async-start(), calls=%async_computation.18 | async-start | bytes 13271040 | tf_op jit(solution)/shard_map/reduce_scatter | solution.py:262
  902.7 2.7 copy-start.4
  902.8 583.2 %reduce-scatter.21.cloned.1.call-start = ((), (), s32[]{:S(2)}) async-start(), calls=%async_computation.15 | async-start | bytes 19906560 | tf_op jit(solution)/shard_map/reduce_scatter | solution.py:253
  915.4 1.9 copy-start.49
  940.8 599.9 %reduce-scatter.25.cloned.1.call-start = ((), (), s32[]{:S(2)}) async-start(), calls=%async_computation.17 | async-start | bytes 3317760 | tf_op jit(solution)/shard_map/reduce_scatter | solution.py:259
  944.2 780.0 %reduce-scatter.29.cloned.1.call-start = ((), (), s32[]{:S(2)}) async-start(), calls=%async_computation.19 | async-start | bytes 13271040 | tf_op jit(solution)/shard_map/reduce_scatter | solution.py:265
  955.9 830.1 %reduce-scatter.33.cloned.1.call-start = ((), (), s32[]{:S(2)}) async-start(), calls=%async_computation.21 | async-start | bytes 5971968
  1036.3 819.0 %reduce-scatter.37.cloned.1.call-start = ((), (), s32[]{:S(2)}) async-start(), calls=%async_computation.23 | async-start | bytes 7962624
  1221.0 720.0 %reduce-scatter.31.cloned.1.call-start = ((), (), s32[]{:S(2)}) async-start(), calls=%async_computation.20 | async-start | bytes 11943936
  1493.6 490.6 %reduce-scatter.35.cloned.1.call-start = ((), (), s32[]{:S(2)}) async-start(), calls=%async_computation.22 | async-start | bytes 1990656
  1543.3 501.7 %reduce-scatter.39.cloned.1.call-start = ((), (), s32[]{:S(2)}) async-start(), calls=%async_computation.24 | async-start | bytes 5971968
  1729.6 2.6 copy-start.53
  1729.6 2.7 copy-start.34
  1729.6 2.8 copy-start.32
  1729.6 2.9 copy-start.33
  1729.6 2.9 copy-start.37
  1729.6 40.1 %copy-start.22 = (bf16[1,1152]{1,0:T(2,128)(2,1)S(1)}, bf16[1,1152]{1,0:T(2,128)(2,1)}, u32[]{:S(2)}) copy-start(bf16[1,1152]{1,0:T(2,128)(2,1)} %param.15) | copy-start | bytes 6916
  1729.6 40.1 %copy-start.24 = (f32[1,1152]{1,0:T(1,128)S(1)}, f32[1,1152]{1,0:T(1,128)}, u32[]{:S(2)}) copy-start(f32[1,1152]{1,0:T(1,128)} %copy-done.23) | copy-start | bytes 13828
  (13 other events, 11.2 us)
Sparse Core Ops, SparseCore 0:
  9.6 271.6 all-gather.6
  282.9 140.7 all-gather.8
  425.3 54.0 all-gather.10
  480.9 184.2 all-gather.12
  666.6 184.2 all-gather.14
  893.1 138.6 reduce-scatter.22
  1034.3 181.1 reduce-scatter.26
  1217.9 268.0 reduce-scatter.20
  1488.4 52.2 reduce-scatter.24
  1543.0 181.1 reduce-scatter.28
  1727.6 58.3 reduce-scatter.32
  1789.8 65.4 reduce-scatter.36
  1858.8 82.1 reduce-scatter.30
  1944.8 39.4 reduce-scatter.34
  1988.1 56.9 reduce-scatter.38
where the time goes:
time: 2060 us; the launch traced here: 2050 us
  waiting for transfers between devices  1760 us (85%)
  matrix products  127 us (6%)
  blocking collectives  68.2 us (3%)
  local copies, waits for them, and re-layouts  52.8 us (3%)
  other arithmetic  22.1 us (1%)
    reduce_scatter x1, waiting for transfers between devices, body(): lax.psum_scatter(grad_w_ada.astype(jnp.bfloat16), 'fsdp', scatter_dimensi...  265 us
    unnamed x20, waiting for transfers between devices  261 us
    all_gather x1, waiting for transfers between devices, body(): lax.all_gather(w_ada, 'fsdp', axis=0, tiled=True)  231 us
    reduce_scatter x1, waiting for transfers between devices, body(): lax.psum_scatter(grad_w_down.astype(jnp.bfloat16), 'fsdp', scatter_dimens...  181 us
    all_gather x1, waiting for transfers between devices, body(): lax.all_gather(w_up, 'fsdp', axis=0, tiled=True)  180 us
    reduce_scatter x1, waiting for transfers between devices, body(): lax.psum_scatter(grad_w_up.astype(jnp.bfloat16), 'fsdp', scatter_dimensio...  179 us
    all_gather x1, waiting for transfers between devices, body(): lax.all_gather(w_down, 'fsdp', axis=0, tiled=True)  164 us
    all_gather x1, waiting for transfers between devices, body(): lax.all_gather(w_qkv, 'fsdp', axis=0, tiled=True)  134 us
  transfers between devices with their start and end apart: 15, of which 15 were waited for; matrix products, arithmetic and copies ran while one was open for 8% of the time, Pallas kernels for 0%

commit v1 on v0

v1 whole, which is shorter than its diff:
```python
import math

import jax
import jax.numpy as jnp
from jax import lax
from jax.experimental import pallas as pl
from jax.experimental.pallas import tpu as pltpu
from jax.sharding import PartitionSpec as P

HEAD_DIM = 72
BOX = 8

epsilon = 1e-06
masked_value = -1e30
gelu_root = math.sqrt(2.0 / math.pi)
f32 = jnp.float32
bf16 = jnp.bfloat16


def norm_parts(values_in):
    centred = values_in - jnp.mean(values_in, axis=-1, keepdims=True)
    spread = jnp.mean(centred * centred, axis=-1, keepdims=True)
    rate = lax.rsqrt(spread + epsilon)
    return centred * rate, rate


def norm_back(normal, rate, grad):
    mean_grad = jnp.mean(grad, axis=-1, keepdims=True)
    mean_both = jnp.mean(grad * normal, axis=-1, keepdims=True)
    return rate * (grad - mean_grad - normal * mean_both)


def gelu_tanh(pre_act):
    return (
        0.5
        * pre_act
        * (1.0 + jnp.tanh(gelu_root * (pre_act + 0.044715 * pre_act * pre_act * pre_act)))
    )


def after(value, other):
    return lax.optimization_barrier((value, other))[0]


def pick(array, index, axis=0):
    return lax.dynamic_index_in_dim(array, index, axis, keepdims=False)


def make_body(dp, fs):
    groups = dp // BOX

    def box_send(x, bits):
        return lax.ppermute(x, "dp", [(i, i ^ bits) for i in range(dp)])

    def ring_send(x, hops):
        return lax.ppermute(x, "fsdp", [(i, (i + hops) % fs) for i in range(fs)])

    def group_send(x, hops):
        return lax.ppermute(x, "dp", [(i, (i + hops * BOX) % dp) for i in range(dp)])

    def ring_gather(x):
        return [x] + [ring_send(x, k) for k in range(1, fs)]

    def ring_sorted(blocks, z):
        back = jnp.stack(blocks[::-1] + blocks[::-1])
        return lax.dynamic_slice_in_dim(back, fs - 1 - z, fs, 0)

    def box_gather_rows(x):
        half = x.shape[0] // 2
        along_x = box_send(x, 2)
        along_y = box_send(x, 4)
        far_top = box_send(along_x[:half], 4)
        far_low = box_send(along_y[half:], 2)
        mine = jnp.concatenate([x, along_x, along_y, far_top, far_low], axis=0)
        return jnp.concatenate([mine, box_send(mine, 1)], axis=0)

    def box_exchange(blocks, place):
        pairs = blocks.reshape((BOX // 2, 2) + blocks.shape[1:])
        core = lax.rem(place, 2)
        chip = lax.div(place, 2)
        kept = pick(pairs, core, 1)
        got = box_send(pick(pairs, 1 - core, 1), 1)
        first, second = [pick(kept, chip)], [pick(got, chip)]
        for k in range(1, BOX // 2):
            both = jnp.stack([pick(kept, chip ^ k), pick(got, chip ^ k)])
            both = box_send(both, 2 * k)
            first.append(both[0])
            second.append(both[1])
        return jnp.concatenate(first + second, axis=-1)

    def gather_small(x):
        for bits in (1, 2, 4):
            x = jnp.concatenate([x, box_send(x, bits)], axis=0)
        if groups > 1:
            x = jnp.concatenate([x] + [group_send(x, k) for k in range(1, groups)], axis=0)
        return x

    def sum_small(x, z):
        total = pick(x, z)
        for k in range(1, fs):
            total = total + ring_send(pick(x, lax.rem(z + k, fs)), k)
        for bits in (1, 2, 4):
            total = total + box_send(total, bits)
        part = total
        for k in range(1, groups):
            total = total + group_send(part, k)
        return total

    def ring_sum(x, z):
        total = pick(x, z)
        for k in range(1, fs):
            sent = pick(x, lax.rem(z + k, fs)).astype(bf16)
            total = total + ring_send(sent, k).astype(f32)
        return total

    def group_sum(x, group):
        total = pick(x, group)
        for k in range(1, groups):
            total = total + group_send(pick(x, lax.rem(group + k, groups)), k)
        return total

    def spread_shard(quarter):
        pieces = []
        held = quarter
        for k in range(1, fs):
            held = ring_send(held, 1)
            other = box_send(held, 2 if k % 2 else 4)
            pieces.append((k, 0, held))
            pieces.append((k, 1, other))
            pieces.append((k, 2, box_send(held, 1)))
            pieces.append((k, 3, box_send(other, 1)))
        return pieces

    def assemble(where, owns, pieces):
        n_own = len(owns)
        widths = [own.shape[-1] for own in owns]
        starts = [sum(widths[:i]) for i in range(n_own)]
        lead, width = pieces[0][2].shape[0], sum(widths)
        n_copies = n_own * (1 + len(pieces))

        def kernel(where_ref, *refs):
            own_refs = refs[:n_own]
            piece_refs = refs[n_own : n_own + len(pieces)]
            out_refs = refs[n_own + len(pieces) : -1]
            sems = refs[-1]
            copies = []
            for i in range(n_own):
                target = out_refs[i].at[where_ref[0]]
                copies.append((own_refs[i], target))
                for (k, kind, unused), piece in zip(pieces, piece_refs):
                    source = piece.at[:, :, pl.ds(starts[i], widths[i])]
                    target = out_refs[i].at[where_ref[k], where_ref[fs + kind]]
                    copies.append((source, target))
            started = [
                pltpu.make_async_copy(source, target, sems.at[j])
                for j, (source, target) in enumerate(copies)
            ]
            for copy in started:
                copy.start()
            for copy in started:
                copy.wait()

        any_spec = pl.BlockSpec(memory_space=pl.ANY)
        outs = pl.pallas_call(
            kernel,
            out_shape=[
                jax.ShapeDtypeStruct((fs, 4, lead, 8, each), bf16) for each in widths
            ],
            in_specs=[pl.BlockSpec(memory_space=pltpu.SMEM)]
            + [any_spec] * (n_own + len(pieces)),
            out_specs=[any_spec] * n_own,
            scratch_shapes=[pltpu.SemaphoreType.DMA((n_copies,))],
            cost_estimate=pl.CostEstimate(
                flops=0, transcendentals=0, bytes_accessed=fs * 4 * lead * 8 * width * 4
            ),
        )(
            where,
            *[own.reshape(4, lead, 8, own.shape[-1]) for own in owns],
            *[piece for unused, unused_kind, piece in pieces],
        )
        return [out.reshape(fs * 4 * lead * 8, out.shape[-1]) for out in outs]

    def body(
        tokens,
        condition,
        grid_sizes,
        w_ada,
        w_qkv,
        w_out,
        w_up,
        w_down,
        b_ada,
        b_qv,
        b_out,
        b_up,
        b_down,
        cotangent,
    ):
        slots, width = tokens.shape[1:]
        heads = width // HEAD_DIM
        hidden = w_up.shape[1]
        rank = lax.axis_index("dp")
        z = lax.axis_index("fsdp")
        place = lax.rem(rank, BOX)
        group = lax.div(rank, BOX)
        core = place & 1
        side = ((place >> 1) ^ (place >> 2)) & 1
        near = 2 * side + core
        far = 2 * (1 - side) + core
        where = jnp.stack(
            [lax.rem(z - k + fs, fs) for k in range(fs)] + [near, far, near ^ 1, far ^ 1]
        ).astype(jnp.int32)

        def quarter_of(shard):
            rows, cols = shard.shape
            return pick(shard.reshape(4, rows // 32, 8, cols), near)

        first_quarter = jnp.concatenate([quarter_of(w_qkv), quarter_of(w_out)], axis=-1)
        first_pieces = spread_shard(first_quarter)
        up_pieces = spread_shard(after(quarter_of(w_up), first_pieces[-4][2]))
        down_pieces = spread_shard(after(quarter_of(w_down), up_pieces[-4][2]))

        cond_wide = condition[0].astype(f32)
        gate = jax.nn.sigmoid(cond_wide)
        cond_act = (cond_wide * gate).astype(bf16)
        small = jnp.concatenate([cond_act, b_ada, b_qv, b_out, b_up, b_down])
        small_all = ring_gather(small)
        rows_z = width // fs
        conds = jnp.stack(
            [lax.dynamic_slice_in_dim(each, z * rows_z, rows_z, 0) for each in small_all]
        )
        biases = ring_sorted(small_all, z).astype(f32)
        ends = [width]
        for bias in (b_ada, b_qv, b_out, b_up, b_down):
            ends.append(ends[-1] + bias.shape[0])
        bias_ada, bias_qv, bias_out, bias_up, bias_down = [
            biases[:, ends[i] : ends[i + 1]].reshape(-1) for i in range(5)
        ]
        partial = jnp.dot(conds, w_ada, preferred_element_type=f32)
        modulation = partial[0] + bias_ada
        for k in range(1, fs):
            modulation = modulation + ring_send(partial[k], fs - k)
        shift_one, scale_one, gate_one, shift_two, scale_two, gate_two = [
            modulation[i * width : (i + 1) * width][None, :] for i in range(6)
        ]
        conds_all = gather_small(conds)

        live = grid_sizes[0, 0] * grid_sizes[0, 1]
        live_rows = (lax.broadcasted_iota(jnp.int32, (slots, 1), 0) < live).astype(f32)
        live_keys = lax.broadcasted_iota(jnp.int32, (1, 1, slots), 2) < live
        tokens_wide = tokens[0].astype(f32)
        norm_one, rate_one = norm_parts(tokens_wide)
        normed = (norm_one * (1.0 + scale_one) + shift_one).astype(bf16)
        upstream = live_rows * cotangent[0].astype(f32)
        d_mlp = (gate_two * upstream).astype(bf16)
        normed_box = box_gather_rows(normed)
        d_mlp_box = box_gather_rows(d_mlp)

        qkv_full, out_full = assemble(where, [w_qkv, w_out], first_pieces)
        projected = jnp.dot(normed, qkv_full, preferred_element_type=f32)
        queries = (projected[:, :width] + bias_qv[:width]).astype(bf16)
        key_part = projected[:, width : 2 * width].astype(bf16)
        values = (projected[:, 2 * width :] + bias_qv[width:]).astype(bf16)
        queries = queries.reshape(slots, heads, HEAD_DIM)
        key_part = key_part.reshape(slots, heads, HEAD_DIM)
        values = values.reshape(slots, heads, HEAD_DIM)
        raw = jnp.einsum("qhe,khe->hqk", queries, key_part, preferred_element_type=f32)
        scores = jnp.where(live_keys, raw * HEAD_DIM ** (-0.5), masked_value)
        highest = jnp.max(scores, axis=-1, keepdims=True)
        lse = highest + jnp.log(jnp.sum(jnp.exp(scores - highest), axis=-1, keepdims=True))
        probs = jnp.exp(scores - lse)
        probs_low = probs.astype(bf16)
        attended = jnp.einsum("hqk,khe->qhe", probs_low, values, preferred_element_type=f32)
        attended = attended.reshape(slots, width).astype(bf16)
        attn_out = jnp.dot(attended, out_full, preferred_element_type=f32) + bias_out
        middle = tokens_wide + gate_one * attn_out
        norm_two, rate_two = norm_parts(middle)
        normed_two = (norm_two * (1.0 + scale_two) + shift_two).astype(bf16)
        attended_box = box_gather_rows(attended)
        normed_two_box = box_gather_rows(normed_two)

        (up_full,) = assemble(where, [w_up], up_pieces)
        pre_act = jnp.dot(normed_two, up_full, preferred_element_type=f32) + bias_up
        activated = gelu_tanh(pre_act).astype(bf16)
        act_blocks = activated.T.reshape(fs, BOX, hidden // fs // BOX, slots)
        act_blocks = act_blocks.transpose(1, 0, 2, 3).reshape(BOX, hidden // BOX, slots)
        act_box = box_exchange(act_blocks, place)
        (down_full,) = assemble(where, [w_down], down_pieces)
        mlp_out = jnp.dot(activated, down_full, preferred_element_type=f32) + bias_down
        output = (live_rows * (middle + gate_two * mlp_out)).astype(bf16)

        def column_blocks(grad_t):
            n = grad_t.shape[0] // dp
            blocks = grad_t.reshape(groups, BOX, n, slots).transpose(1, 0, 2, 3)
            return blocks.reshape(BOX, groups * n, slots)

        def weight_grad(left_box, right_box):
            grad = lax.dot_general(
                left_box, right_box, (((0,), (1,)), ((), ())), preferred_element_type=f32
            )
            rows, cols = grad.shape
            grad = ring_sum(grad.reshape(fs, rows // fs, cols), z)
            grad = grad.reshape(rows // fs, groups, cols // groups)
            return group_sum(grad.transpose(1, 0, 2), group)

        d_gate_two = jnp.sum(upstream * mlp_out, axis=0)
        grad_down = jnp.dot(act_box, d_mlp_box, preferred_element_type=f32)
        grad_down = ring_sum(grad_down.reshape(fs, hidden // fs // BOX, width), z)
        grad_down = grad_down.reshape(hidden // fs // BOX, groups, width // groups)
        grad_down = group_sum(grad_down.transpose(1, 0, 2), group)
        down_rows = hidden // fs // BOX
        down_blocks = grad_down.reshape(down_rows, BOX, width // dp).transpose(1, 0, 2)
        down_parts = [pick(down_blocks, place)] + [
            box_send(pick(down_blocks, place ^ k), k) for k in range(1, BOX)
        ]
        down_order = jnp.stack([place ^ k for k in range(BOX)])
        grad_w_down = jnp.stack(down_parts)[down_order].reshape(BOX * down_rows, width // dp)

        d_act = lax.dot_general(
            d_mlp, down_full, (((1,), (1,)), ((), ())), preferred_element_type=f32
        )
        unused_gelu, gelu_pull = jax.vjp(gelu_tanh, pre_act)
        d_pre = gelu_pull(d_act)[0].astype(bf16)
        d_pre_box = box_exchange(column_blocks(d_pre.T), place)
        grad_w_up = weight_grad(normed_two_box, d_pre_box)
        d_normed_two = lax.dot_general(
            d_pre, up_full, (((1,), (1,)), ((), ())), preferred_element_type=f32
        )
        d_shift_two = jnp.sum(d_normed_two, axis=0)
        d_scale_two = jnp.sum(d_normed_two * norm_two, axis=0)
        d_middle = upstream + norm_back(norm_two, rate_two, d_normed_two * (1.0 + scale_two))
        d_gate_one = jnp.sum(d_middle * attn_out, axis=0)
        d_attn = (gate_one * d_middle).astype(bf16)
        d_attn_box = box_exchange(column_blocks(d_attn.T), place)
        grad_w_out = weight_grad(attended_box, d_attn_box)

        d_mod_early = jnp.concatenate([d_gate_one, d_shift_two, d_scale_two, d_gate_two])
        d_mod_early = jnp.stack(ring_gather(d_mod_early.astype(bf16)))
        d_mod_early_all = gather_small(d_mod_early)

        def shards(vector):
            return vector.reshape(fs, -1)

        bias_early = jnp.concatenate(
            [
                shards(jnp.sum(d_attn.astype(f32), axis=0)),
                shards(jnp.sum(d_pre.astype(f32), axis=0)),
                shards(jnp.sum(d_mlp.astype(f32), axis=0)),
            ],
            axis=1,
        )
        bias_early = sum_small(bias_early, z)
        grad_b_out = bias_early[: width // fs]
        grad_b_up = bias_early[width // fs : (width + hidden) // fs]
        grad_b_down = bias_early[(width + hidden) // fs :]

        d_attended = lax.dot_general(
            d_attn, out_full, (((1,), (1,)), ((), ())), preferred_element_type=f32
        )
        d_attended = d_attended.astype(bf16).reshape(slots, heads, HEAD_DIM)
        d_probs = jnp.einsum("qhe,khe->hqk", d_attended, values, preferred_element_type=f32)
        d_values = jnp.einsum(
            "hqk,qhe->khe", probs_low, d_attended, preferred_element_type=f32
        ).astype(bf16)
        row_inner = jnp.sum(probs * d_probs, axis=-1, keepdims=True)
        d_scores = (probs * (d_probs - row_inner)).astype(bf16)
        d_queries = (
            jnp.einsum("hqk,khe->qhe", d_scores, key_part, preferred_element_type=f32)
            * HEAD_DIM ** (-0.5)
        ).astype(bf16)
        d_keys = (
            jnp.einsum("hqk,qhe->khe", d_scores, queries, preferred_element_type=f32)
            * HEAD_DIM ** (-0.5)
        ).astype(bf16)
        d_projected = jnp.concatenate(
            [
                d_queries.reshape(slots, width),
                d_keys.reshape(slots, width),
                d_values.reshape(slots, width),
            ],
            axis=1,
        )
        d_projected_box = box_exchange(column_blocks(d_projected.T), place)
        grad_w_qkv = weight_grad(normed_box, d_projected_box)
        sums = jnp.sum(d_projected.astype(f32), axis=0)
        grad_b_qv = sum_small(
            shards(jnp.concatenate([sums[:width], sums[2 * width :]])), z
        )
        d_normed = lax.dot_general(
            d_projected, qkv_full, (((1,), (1,)), ((), ())), preferred_element_type=f32
        )
        d_shift_one = jnp.sum(d_normed, axis=0)
        d_scale_one = jnp.sum(d_normed * norm_one, axis=0)
        grad_tokens = d_middle + norm_back(norm_one, rate_one, d_normed * (1.0 + scale_one))

        d_mod_late = jnp.concatenate([d_shift_one, d_scale_one]).astype(bf16)
        d_mod_late = jnp.stack(ring_gather(d_mod_late))
        d_mod_all = jnp.concatenate([gather_small(d_mod_late), d_mod_early_all], axis=1)
        d_mod_near = jnp.concatenate([d_mod_late, d_mod_early], axis=1)
        ada_cols = w_ada.shape[1] // dp
        d_mod_cols = pick(d_mod_all.reshape(-1, dp, ada_cols), rank, 1)
        grad_w_ada = lax.dot_general(
            conds_all, d_mod_cols, (((0,), (0,)), ((), ())), preferred_element_type=f32
        )
        sums_ada = jnp.sum(d_mod_all.astype(f32), axis=0)
        grad_b_ada = pick(shards(sums_ada), z)
        d_conds = lax.dot_general(
            d_mod_near, w_ada, (((1,), (1,)), ((), ())), preferred_element_type=f32
        )
        cond_parts = [d_conds[0]] + [ring_send(d_conds[k], fs - k) for k in range(1, fs)]
        twice = jnp.stack(cond_parts + cond_parts)
        d_cond_act = lax.dynamic_slice_in_dim(twice, lax.rem(fs - z, fs), fs, 0).reshape(-1)
        grad_condition = d_cond_act * gate * (1.0 + cond_wide * (1.0 - gate))
        return (
            output[None],
            grad_tokens.astype(bf16)[None],
            grad_condition[None],
            grad_w_ada,
            grad_w_qkv,
            grad_w_out,
            grad_w_up,
            grad_w_down,
            grad_b_ada,
            grad_b_qv,
            grad_b_out,
            grad_b_up,
            grad_b_down,
        )

    return body


def solution(mesh):
    return jax.shard_map(
        make_body(mesh.shape["dp"], mesh.shape["fsdp"]),
        mesh=mesh,
        in_specs=(
            P(("dp", "fsdp"), None, None),
            P(("dp", "fsdp"), None),
            P(("dp", "fsdp"), None),
            P("fsdp", None),
            P("fsdp", None),
            P("fsdp", None),
            P("fsdp", None),
            P("fsdp", None),
            P("fsdp"),
            P("fsdp"),
            P("fsdp"),
            P("fsdp"),
            P("fsdp"),
            P(("dp", "fsdp"), None, None),
        ),
        out_specs=(
            P(("dp", "fsdp"), None, None),
            P(("dp", "fsdp"), None, None),
            P(("dp", "fsdp"), None),
            P("fsdp", "dp"),
            P("fsdp", "dp"),
            P("fsdp", "dp"),
            P("fsdp", "dp"),
            P("fsdp", "dp"),
            P("fsdp"),
            P("fsdp"),
            P("fsdp"),
            P("fsdp"),
            P("fsdp"),
        ),
        check_vma=False,
    )
```

time: 2060 us -> 1610 us (0.78)
  waiting for transfers between devices: 1760 us -> 252 us
  Pallas kernels: 0 us -> 971 us
  starting transfers between devices: 1.18 us -> 157 us
  blocking collectives: 68.2 us -> 0 us
  local copies, waits for them, and re-layouts: 52.8 us -> 104 us
  matrix products: 127 us -> 90.7 us
    pallas_call x0 -> x3, Pallas kernels: none -> 971 us  [assemble(): pl.pallas_call(kernel, out_shape=[jax.ShapeDtypeStruct((fs, 4, lead, 8, e...]
    all_gather x5 -> x0, waiting for transfers between devices: 751 us -> none  [the longest x1 231 us: body(): lax.all_gather(w_ada, 'fsdp', axis=0, tiled=True)]
    reduce_scatter x5 -> x0, waiting for transfers between devices: 748 us -> none  [the longest x1 265 us: body(): lax.psum_scatter(grad_w_ada.astype(jnp.bfloat16), 'fsdp', scatter_dimensi...]
    unnamed x20 -> x0, waiting for transfers between devices: 261 us -> none
    ppermute x0 -> x127, waiting for transfers between devices: none -> 252 us  [the longest x85 148 us: box_send(): return lax.ppermute(x, 'dp', [(i, i ^ bits) for i in range(dp)])]
    ppermute x0 -> x127, starting transfers between devices: none -> 157 us  [the longest x85 96.4 us: box_send(): return lax.ppermute(x, 'dp', [(i, i ^ bits) for i in range(dp)])]
    dot_general x20 -> x21, matrix products: 127 us -> 90.7 us  [the longest x3 13.9 us: weight_grad(): lax.dot_general(left_box, right_box, (((0,), (1,)), ((), ())), preferred_...]
    concatenate x2 -> x27, local copies, waits for them, and re-layouts: 0.87 us -> 25.8 us  [the longest x4 9.27 us: box_gather_rows(): return jnp.concatenate([mine, box_send(mine, 1)], axis=0)]
  transfers between devices with their start and end apart: 15 -> 127, of which waited for: 15 -> 36; matrix products, arithmetic and copies ran while one was open for 8% -> 8% of each run, Pallas kernels for 0% -> 40%
where the time goes in v1:
time: 1610 us
  Pallas kernels  971 us (60%)
  waiting for transfers between devices  252 us (16%)
  starting transfers between devices  157 us (10%)
  local copies, waits for them, and re-layouts  104 us (6%)
  matrix products  90.7 us (6%)
  other arithmetic  26 us (2%)
    pallas_call x3, Pallas kernels, assemble(): pl.pallas_call(kernel, out_shape=[jax.ShapeDtypeStruct((fs, 4, lead, 8, e...  971 us
    ppermute x85, waiting for transfers between devices, box_send(): return lax.ppermute(x, 'dp', [(i, i ^ bits) for i in range(dp)])  148 us
    ppermute x42, waiting for transfers between devices, ring_send(): return lax.ppermute(x, 'fsdp', [(i, (i + hops) % fs) for i in range(fs)])  105 us
    ppermute x85, starting transfers between devices, box_send(): return lax.ppermute(x, 'dp', [(i, i ^ bits) for i in range(dp)])  96.4 us
    ppermute x42, starting transfers between devices, ring_send(): return lax.ppermute(x, 'fsdp', [(i, (i + hops) % fs) for i in range(fs)])  60.8 us
  transfers between devices with their start and end apart: 127, of which 36 were waited for; matrix products, arithmetic and copies ran while one was open for 8% of the time, Pallas kernels for 40%

profile of v1, /device:TPU:25, one launch (start us, length us, event | category | flops | bytes accessed | tf_op | source)
XLA Modules:
  0.0 1606.0 jit_solution(17074609598813481573)
XLA Ops:
  1.4 3.5 concatenate.161
  8.6 3.1 collective-permute-start.6
  12.7 2.8 fusion.165
  16.5 2.6 collective-permute-start.5
  19.5 6.4 collective-permute-done.3
  26.4 6.6 collective-permute-start.10
  39.6 7.1 collective-permute-done.10.refs_6_
  46.7 4.1 collective-permute-start.14
  61.6 4.9 collective-permute-start.12
  71.0 5.2 collective-permute-done.7.refs_3_
  76.2 4.5 collective-permute-start.9
  81.3 9.1 collective-permute-done.15.refs_11_
  100.3 323.6 %shard_map.237 = (bf16[4,4,9,8,3456]{4,3,2,1,0:T(8,128)(2,1)}, bf16[4,4,9,8,1152]{4,3,2,1,0:T(8,128)(2,1)}) custom-call(s32[8]{0:T(128)} %stack.232.where_ref, bf16[4,9,8,3456]{3,2,1,0:T(8,128)(2,1)} %bitcast.472, bf16[4,9,8,1152]{3,2,1,0:T(8,128)(2,1)} %bitcast.493, bf16[9,8,4608]{2,1,0:T(8,128)(2,1)} %copy-done.41, ...), custom_call_target="tpu_custom_call" | custom-call | bytes 21233664 | tf_op jit(solution)/shard_map/pallas_call | solution.py:164
  423.9 6.0 fusion.61
  435.0 3.5 convolution_convert_fusion.2
  449.1 7.9 collective-permute-done.84
  462.9 10.8 collective-permute-done.53
  482.6 6.2 collective-permute-done.19.refs_2_
  489.0 6.1 collective-permute-done.87
  495.1 4.4 collective-permute-start.21
  503.5 2.8 collective-permute-start.88
  506.8 9.7 collective-permute-done.30.refs_1_
  520.3 13.6 collective-permute-done.34.refs_5_
  533.9 4.6 collective-permute-start.38
  540.1 12.1 collective-permute-done.38.refs_9_
  555.5 3.2 constant_dynamic-update-slice_fusion.11
  558.8 323.6 %shard_map.238 = bf16[4,4,9,8,4608]{4,3,2,1,0:T(8,128)(2,1)} custom-call(s32[8]{0:T(128)} %stack.232.where_ref, bf16[4,9,8,4608]{3,2,1,0:T(8,128)(2,1)} %bitcast.468, bf16[9,8,4608]{2,1,0:T(8,128)(2,1)} %collective-permute-done.18.refs_1_, bf16[9,8,4608]{2,1,0:T(8,128)(2,1)} %copy-done.28, bf16[9,8,4608]{2,1,0:T(8,128)(2,1)} %copy-done.29, ...), custom_call_target="tpu_custom_call" | custom-call | bytes 21233664 | tf_op jit(solution)/shard_map/pallas_call | solution.py:164
  885.5 9.0 convolution_add_fusion
  896.6 3.6 constant_dynamic-update-slice_fusion.22
  903.9 323.6 %shard_map.239 = bf16[4,4,36,8,1152]{4,3,2,1,0:T(8,128)(2,1)} custom-call(s32[8]{0:T(128)} %stack.232.where_ref, bf16[4,36,8,1152]{3,2,1,0:T(8,128)(2,1)} %bitcast.470, bf16[36,8,1152]{2,1,0:T(8,128)(2,1)} %copy-done.30, bf16[36,8,1152]{2,1,0:T(8,128)(2,1)} %collective-permute-done.31.refs_2_, bf16[36,8,1152]{2,1,0:T(8,128)(2,1)} %collective-permute-done.32.refs_3_, ...), custom_call_target="tpu_custom_call" | custom-call | bytes 21233664 | tf_op jit(solution)/shard_map/pallas_call | solution.py:164
  1227.7 11.5 convert_reduce_fusion
  1239.3 4.0 multiply_reduce_fusion.1
  1243.3 11.6 fusion.45
  1257.0 3.9 multiply_reduce_fusion
  1267.1 5.4 multiply_convert_fusion
  1272.5 4.3 copy.91
  1276.8 3.3 copy.92
  1294.0 7.6 fusion.37
  1302.3 4.0 collective-permute-start.42
  1329.9 3.2 collective-permute-start.121
  1335.0 3.0 collective-permute-start.45
  1338.7 2.7 collective-permute-start.118
  1347.3 3.2 fusion.110
  1357.1 3.2 collective-permute-start.54
  1361.0 6.2 collective-permute-done.125
  1370.2 4.3 collective-permute-start.77
  1394.7 4.8 fusion.167
  1405.5 6.3 collective-permute-start.96
  1411.8 3.7 collective-permute-start.89
  1418.9 5.7 collective-permute-done.102
  1431.8 17.6 %collective-permute-done.66 = bf16[2,432,256]{2,1,0:T(8,128)(2,1)S(1)} collective-permute-done((bf16[2,432,256]{2,1,0:T(8,128)(2,1)S(1)}, bf16[2,432,256]{2,1,0:T(8,128)(2,1)S(1)}, u32[]{:S(2)}, u32[]{:S(2)}) %collective-permute-start.66) | collective-permute-done | bytes 442400 | tf_op jit(solution)/shard_map/ppermute | solution.py:53
  1452.5 5.2 fusion.166
  1457.8 29.6 %collective-permute-done.90 = bf16[2,576,256]{2,1,0:T(8,128)(2,1)S(1)} collective-permute-done((bf16[2,576,256]{2,1,0:T(8,128)(2,1)S(1)}, bf16[2,576,256]{2,1,0:T(8,128)(2,1)S(1)}, u32[]{:S(2)}, u32[]{:S(2)}) %collective-permute-start.90) | collective-permute-done | bytes 589856 | tf_op jit(solution)/shard_map/ppermute | solution.py:53
  1490.2 3.9 fusion.168
  1494.6 19.6 %collective-permute-done.98 = bf16[2,576,256]{2,1,0:T(8,128)(2,1)S(1)} collective-permute-done((bf16[2,576,256]{2,1,0:T(8,128)(2,1)S(1)}, bf16[2,576,256]{2,1,0:T(8,128)(2,1)S(1)}, u32[]{:S(2)}, u32[]{:S(2)}) %collective-permute-start.98) | collective-permute-done | bytes 589856 | tf_op jit(solution)/shard_map/ppermute | solution.py:53
  1514.2 3.3 collective-permute-start.93
  1518.2 3.2 fusion.169
  1521.9 3.1 collective-permute-start.105
  1525.4 3.8 collective-permute-done.93
  1529.3 3.3 collective-permute-start.107
  1533.5 23.2 %collective-permute-done.94 = bf16[288,576]{1,0:T(8,128)(2,1)S(1)} collective-permute-done((bf16[288,576]{1,0:T(8,128)(2,1)S(1)}, bf16[288,576]{1,0:T(8,128)(2,1)S(1)}, u32[]{:S(2)}, u32[]{:S(2)}) %collective-permute-start.94) | collective-permute-done | bytes 331808 | tf_op jit(solution)/shard_map/ppermute | solution.py:56
  1557.7 25.9 %collective-permute-done.106 = bf16[144,1152]{1,0:T(8,128)(2,1)S(1)} collective-permute-done((bf16[144,1152]{1,0:T(8,128)(2,1)S(1)}, bf16[144,1152]{1,0:T(8,128)(2,1)S(1)}, u32[]{:S(2)}, u32[]{:S(2)}) %collective-permute-start.106) | collective-permute-done | bytes 331808 | tf_op jit(solution)/shard_map/ppermute | solution.py:56
  1593.5 2.6 collective-permute-done.110
  1596.2 7.4 collective-permute-done.112
  (673 shorter events, 213.6 us)
Async XLA Ops:
  8.6 17.7 %collective-permute-start.6 = (bf16[9,8,4608]{2,1,0:T(8,128)(2,1)S(1)}, bf16[9,8,4608]{2,1,0:T(8,128)(2,1)S(1)}, u32[]{:S(2)}, u32[]{:S(2)}) collective-permute-start(bf16[9,8,4608]{2,1,0:T(8,128)(2,1)S(1)} %pad_maximum_fusion.1), channel_id=1, source_target_pairs={{0,1},{1,2},{2,3},{3,0},{4,5},{5,6},{6,7},{7,4},{8,9},{9,10},{10,1... | collective-permute-start | bytes 1990664 | tf_op jit(solution)/shard_map/ppermute | solution.py:56
  26.4 20.4 %collective-permute-start.10 = (bf16[9,8,4608]{2,1,0:T(8,128)(2,1)S(1)}, bf16[9,8,4608]{2,1,0:T(8,128)(2,1)}, u32[]{:S(2)}, u32[]{:S(2)}) collective-permute-start(bf16[9,8,4608]{2,1,0:T(8,128)(2,1)S(1)} %collective-permute-done.6.refs_2_), channel_id=1, source_target_pairs={{0,1},{1,2},{2,3},{3,0},{4,5},{5,6},{6,7},{7,4},{8,9},{9,10},{10,1... | collective-permute-start | bytes 1990664 | tf_op jit(solution)/shard_map/ppermute | solution.py:56
  34.7 17.3 %collective-permute-start.60 = (bf16[256,1152]{1,0:T(8,128)(2,1)S(1)}, bf16[256,1152]{1,0:T(8,128)(2,1)S(1)}, u32[]{:S(2)}, u32[]{:S(2)}) collective-permute-start(bf16[256,1152]{1,0:T(8,128)(2,1)S(1)} %get-tuple-element.82), channel_id=1, source_target_pairs={{0,8},{4,12},{8,0},{12,4},{16,24},{20,28},{24,16},{28,20},{1,9},{5... | collective-permute-start | bytes 1769480 | tf_op jit(solution)/shard_map/ppermute | solution.py:53
  35.9 18.1 %collective-permute-start.61 = (bf16[256,1152]{1,0:T(8,128)(2,1)S(1)}, bf16[256,1152]{1,0:T(8,128)(2,1)S(1)}, u32[]{:S(2)}, u32[]{:S(2)}) collective-permute-start(bf16[256,1152]{1,0:T(8,128)(2,1)S(1)} %get-tuple-element.82), channel_id=1, source_target_pairs={{0,16},{4,20},{8,24},{12,28},{16,0},{20,4},{24,8},{28,12},{1,17},{... | collective-permute-start | bytes 1769480 | tf_op jit(solution)/shard_map/ppermute | solution.py:53
  46.7 19.8 %collective-permute-start.14 = (bf16[9,8,4608]{2,1,0:T(8,128)(2,1)}, bf16[9,8,4608]{2,1,0:T(8,128)(2,1)}, u32[]{:S(2)}, u32[]{:S(2)}) collective-permute-start(bf16[9,8,4608]{2,1,0:T(8,128)(2,1)} %collective-permute-done.10.refs_6_), channel_id=1, source_target_pairs={{0,1},{1,2},{2,3},{3,0},{4,5},{5,6},{6,7},{7,4},{8,9},{9,10},{10,1... | collective-permute-start | bytes 1990664 | tf_op jit(solution)/shard_map/ppermute | solution.py:56
  58.9 17.3 %collective-permute-start.7 = (bf16[9,8,4608]{2,1,0:T(8,128)(2,1)}, bf16[9,8,4608]{2,1,0:T(8,128)(2,1)}, u32[]{:S(2)}, u32[]{:S(2)}) collective-permute-start(bf16[9,8,4608]{2,1,0:T(8,128)(2,1)} %copy-done.41), channel_id=1, source_target_pairs={{0,8},{4,12},{8,0},{12,4},{16,24},{20,28},{24,16},{28,20},{1,9},{5... | collective-permute-start | bytes 1990664 | tf_op jit(solution)/shard_map/ppermute | solution.py:53
  59.5 21.2 %collective-permute-start.8 = (bf16[9,8,4608]{2,1,0:T(8,128)(2,1)}, bf16[9,8,4608]{2,1,0:T(8,128)(2,1)}, u32[]{:S(2)}, u32[]{:S(2)}) collective-permute-start(bf16[9,8,4608]{2,1,0:T(8,128)(2,1)} %copy-done.41), channel_id=1, source_target_pairs={{0,4},{4,0},{8,12},{12,8},{16,20},{20,16},{24,28},{28,24},{1,5},{5... | collective-permute-start | bytes 1990664 | tf_op jit(solution)/shard_map/ppermute | solution.py:53
  59.9 20.9 %collective-permute-start.11 = (bf16[9,8,4608]{2,1,0:T(8,128)(2,1)}, bf16[9,8,4608]{2,1,0:T(8,128)(2,1)}, u32[]{:S(2)}, u32[]{:S(2)}) collective-permute-start(bf16[9,8,4608]{2,1,0:T(8,128)(2,1)} %collective-permute-done.10.refs_6_), channel_id=1, source_target_pairs={{0,16},{4,20},{8,24},{12,28},{16,0},{20,4},{24,8},{28,12},{1,17},{... | collective-permute-start | bytes 1990664 | tf_op jit(solution)/shard_map/ppermute | solution.py:53
  61.6 19.5 %collective-permute-start.12 = (bf16[9,8,4608]{2,1,0:T(8,128)(2,1)}, bf16[9,8,4608]{2,1,0:T(8,128)(2,1)}, u32[]{:S(2)}, u32[]{:S(2)}) collective-permute-start(bf16[9,8,4608]{2,1,0:T(8,128)(2,1)} %collective-permute-done.10.refs_6_), channel_id=1, source_target_pairs={{0,4},{4,0},{8,12},{12,8},{16,20},{20,16},{24,28},{28,24},{1,5},{5... | collective-permute-start | bytes 1990664 | tf_op jit(solution)/shard_map/ppermute | solution.py:53
  66.5 23.9 %collective-permute-start.15 = (bf16[9,8,4608]{2,1,0:T(8,128)(2,1)}, bf16[9,8,4608]{2,1,0:T(8,128)(2,1)}, u32[]{:S(2)}, u32[]{:S(2)}) collective-permute-start(bf16[9,8,4608]{2,1,0:T(8,128)(2,1)} %collective-permute-done.14.refs_10_), channel_id=1, source_target_pairs={{0,8},{4,12},{8,0},{12,4},{16,24},{20,28},{24,16},{28,20},{1,9},{5... | collective-permute-start | bytes 1990664 | tf_op jit(solution)/shard_map/ppermute | solution.py:53
  76.2 20.1 %collective-permute-start.9 = (bf16[9,8,4608]{2,1,0:T(8,128)(2,1)}, bf16[9,8,4608]{2,1,0:T(8,128)(2,1)S(1)}, u32[]{:S(2)}, u32[]{:S(2)}) collective-permute-start(bf16[9,8,4608]{2,1,0:T(8,128)(2,1)} %collective-permute-done.7.refs_3_), channel_id=1, source_target_pairs={{0,4},{4,0},{8,12},{12,8},{16,20},{20,16},{24,28},{28,24},{1,5},{5... | collective-permute-start | bytes 1990664 | tf_op jit(solution)/shard_map/ppermute | solution.py:53
  80.7 16.8 %collective-permute-start.18 = (bf16[9,8,4608]{2,1,0:T(8,128)(2,1)S(1)}, bf16[9,8,4608]{2,1,0:T(8,128)(2,1)}, u32[]{:S(2)}, u32[]{:S(2)}) collective-permute-start(bf16[9,8,4608]{2,1,0:T(8,128)(2,1)S(1)} %dynamic-slice_bitcast_fusion.4), channel_id=1, source_target_pairs={{0,1},{1,2},{2,3},{3,0},{4,5},{5,6},{6,7},{7,4},{8,9},{9,10},{10,1... | collective-permute-start | bytes 1990664 | tf_op jit(solution)/shard_map/ppermute | solution.py:56
  80.8 19.4 %collective-permute-start.16 = (bf16[9,8,4608]{2,1,0:T(8,128)(2,1)}, bf16[9,8,4608]{2,1,0:T(8,128)(2,1)}, u32[]{:S(2)}, u32[]{:S(2)}) collective-permute-start(bf16[9,8,4608]{2,1,0:T(8,128)(2,1)} %collective-permute-done.14.refs_10_), channel_id=1, source_target_pairs={{0,4},{4,0},{8,12},{12,8},{16,20},{20,16},{24,28},{28,24},{1,5},{5... | collective-permute-start | bytes 1990664 | tf_op jit(solution)/shard_map/ppermute | solution.py:53
  81.1 17.6 %collective-permute-start.13 = (bf16[9,8,4608]{2,1,0:T(8,128)(2,1)}, bf16[9,8,4608]{2,1,0:T(8,128)(2,1)}, u32[]{:S(2)}, u32[]{:S(2)}) collective-permute-start(bf16[9,8,4608]{2,1,0:T(8,128)(2,1)} %collective-permute-done.11.refs_7_), channel_id=1, source_target_pairs={{0,4},{4,0},{8,12},{12,8},{16,20},{20,16},{24,28},{28,24},{1,5},{5... | collective-permute-start | bytes 1990664 | tf_op jit(solution)/shard_map/ppermute | solution.py:53
  96.3 349.5 %collective-permute-start.52 = (bf16[8,288]{1,0:T(8,128)(2,1)}, bf16[8,288]{1,0:T(8,128)(2,1)}, u32[]{:S(2)}, u32[]{:S(2)}) collective-permute-start(bf16[8,288]{1,0:T(8,128)(2,1)} %concatenate.175), channel_id=1, source_target_pairs={{0,8},{4,12},{8,0},{12,4},{16,24},{20,28},{24,16},{28,20},{1,9},{5... | collective-permute-start | bytes 13832 | tf_op jit(solution)/shard_map/ppermute | solution.py:53
  98.6 380.9 %collective-permute-start.64 = (bf16[1024,1152]{1,0:T(8,128)(2,1)}, bf16[1024,1152]{1,0:T(8,128)(2,1)}, u32[]{:S(2)}, u32[]{:S(2)}) collective-permute-start(bf16[1024,1152]{1,0:T(8,128)(2,1)} %get-tuple-element.174), channel_id=1, source_target_pairs={{0,4},{4,0},{8,12},{12,8},{16,20},{20,16},{24,28},{28,24},{1,5},{5... | collective-permute-start | bytes 7077896 | tf_op jit(solution)/shard_map/ppermute | solution.py:53
  98.6 349.2 %collective-permute-start.22 = (bf16[9,8,4608]{2,1,0:T(8,128)(2,1)}, bf16[9,8,4608]{2,1,0:T(8,128)(2,1)}, u32[]{:S(2)}, u32[]{:S(2)}) collective-permute-start(bf16[9,8,4608]{2,1,0:T(8,128)(2,1)} %collective-permute-done.18.refs_1_), channel_id=1, source_target_pairs={{0,1},{1,2},{2,3},{3,0},{4,5},{5,6},{6,7},{7,4},{8,9},{9,10},{10,1... | collective-permute-start | bytes 1990664 | tf_op jit(solution)/shard_map/ppermute | solution.py:56
  447.7 25.9 %collective-permute-start.72 = (bf16[256,1152]{0,1:T(8,128)(2,1)S(1)}, bf16[256,1152]{0,1:T(8,128)(2,1)S(1)}, u32[]{:S(2)}, u32[]{:S(2)}) collective-permute-start(bf16[256,1152]{0,1:T(8,128)(2,1)S(1)} %bitcast.477), channel_id=1, source_target_pairs={{0,8},{4,12},{8,0},{12,4},{16,24},{20,28},{24,16},{28,20},{1,9},{5... | collective-permute-start | bytes 1769480 | tf_op jit(solution)/shard_map/ppermute | solution.py:53
  447.8 27.1 %collective-permute-start.73 = (bf16[256,1152]{0,1:T(8,128)(2,1)S(1)}, bf16[256,1152]{0,1:T(8,128)(2,1)S(1)}, u32[]{:S(2)}, u32[]{:S(2)}) collective-permute-start(bf16[256,1152]{0,1:T(8,128)(2,1)S(1)} %bitcast.478), channel_id=1, source_target_pairs={{0,16},{4,20},{8,24},{12,28},{16,0},{20,4},{24,8},{28,12},{1,17},{... | collective-permute-start | bytes 1769480 | tf_op jit(solution)/shard_map/ppermute | solution.py:53
  457.0 20.0 %collective-permute-start.26 = (bf16[9,8,4608]{2,1,0:T(8,128)(2,1)}, bf16[9,8,4608]{2,1,0:T(8,128)(2,1)S(1)}, u32[]{:S(2)}, u32[]{:S(2)}) collective-permute-start(bf16[9,8,4608]{2,1,0:T(8,128)(2,1)} %collective-permute-done.22.refs_5_), channel_id=1, source_target_pairs={{0,1},{1,2},{2,3},{3,0},{4,5},{5,6},{6,7},{7,4},{8,9},{9,10},{10,1... | collective-permute-start | bytes 1990664 | tf_op jit(solution)/shard_map/ppermute | solution.py:56
  474.9 25.4 %collective-permute-start.20 = (bf16[9,8,4608]{2,1,0:T(8,128)(2,1)}, bf16[9,8,4608]{2,1,0:T(8,128)(2,1)S(1)}, u32[]{:S(2)}, u32[]{:S(2)}) collective-permute-start(bf16[9,8,4608]{2,1,0:T(8,128)(2,1)} %collective-permute-done.18.refs_1_), channel_id=1, source_target_pairs={{0,4},{4,0},{8,12},{12,8},{16,20},{20,16},{24,28},{28,24},{1,5},{5... | collective-permute-start | bytes 1990664 | tf_op jit(solution)/shard_map/ppermute | solution.py:53
  477.0 18.1 %collective-permute-start.87 = (bf16[128,1152]{1,0:T(8,128)(2,1)S(1)}, bf16[128,1152]{1,0:T(8,128)(2,1)S(1)}, u32[]{:S(2)}, u32[]{:S(2)}) collective-permute-start(bf16[128,1152]{1,0:T(8,128)(2,1)S(1)} %slice.310), channel_id=1, source_target_pairs={{0,8},{4,12},{8,0},{12,4},{16,24},{20,28},{24,16},{28,20},{1,9},{5... | collective-permute-start | bytes 884744 | tf_op jit(solution)/shard_map/ppermute | solution.py:53
  479.6 20.8 %collective-permute-start.74 = (bf16[128,1152]{0,1:T(8,128)(2,1)S(1)}, bf16[128,1152]{0,1:T(8,128)(2,1)S(1)}, u32[]{:S(2)}, u32[]{:S(2)}) collective-permute-start(bf16[128,1152]{0,1:T(8,128)(2,1)S(1)} %slice.301), channel_id=1, source_target_pairs={{0,16},{4,20},{8,24},{12,28},{16,0},{20,4},{24,8},{28,12},{1,17},{... | collective-permute-start | bytes 884744 | tf_op jit(solution)/shard_map/ppermute | solution.py:53
  480.9 20.5 %collective-permute-start.75 = (bf16[128,1152]{0,1:T(8,128)(2,1)S(1)}, bf16[128,1152]{0,1:T(8,128)(2,1)S(1)}, u32[]{:S(2)}, u32[]{:S(2)}) collective-permute-start(bf16[128,1152]{0,1:T(8,128)(2,1)S(1)} %slice.302), channel_id=1, source_target_pairs={{0,8},{4,12},{8,0},{12,4},{16,24},{20,28},{24,16},{28,20},{1,9},{5... | collective-permute-start | bytes 884744 | tf_op jit(solution)/shard_map/ppermute | solution.py:53
  500.3 16.2 %collective-permute-start.30 = (bf16[36,8,1152]{2,1,0:T(8,128)(2,1)S(1)}, bf16[36,8,1152]{2,1,0:T(8,128)(2,1)S(1)}, u32[]{:S(2)}, u32[]{:S(2)}) collective-permute-start(bf16[36,8,1152]{2,1,0:T(8,128)(2,1)S(1)} %copy-done.40), channel_id=1, source_target_pairs={{0,1},{1,2},{2,3},{3,0},{4,5},{5,6},{6,7},{7,4},{8,9},{9,10},{10,1... | collective-permute-start | bytes 1990664 | tf_op jit(solution)/shard_map/ppermute | solution.py:56
  501.4 16.3 %collective-permute-start.27 = (bf16[9,8,4608]{2,1,0:T(8,128)(2,1)S(1)}, bf16[9,8,4608]{2,1,0:T(8,128)(2,1)}, u32[]{:S(2)}, u32[]{:S(2)}) collective-permute-start(bf16[9,8,4608]{2,1,0:T(8,128)(2,1)S(1)} %collective-permute-done.26.refs_9_), channel_id=1, source_target_pairs={{0,8},{4,12},{8,0},{12,4},{16,24},{20,28},{24,16},{28,20},{1,9},{5... | collective-permute-start | bytes 1990664 | tf_op jit(solution)/shard_map/ppermute | solution.py:53
  503.5 381.1 %collective-permute-start.88 = (bf16[1024,1152]{1,0:T(8,128)(2,1)}, bf16[1024,1152]{1,0:T(8,128)(2,1)}, u32[]{:S(2)}, u32[]{:S(2)}) collective-permute-start(bf16[1024,1152]{1,0:T(8,128)(2,1)} %get-tuple-element.163), channel_id=1, source_target_pairs={{0,4},{4,0},{8,12},{12,8},{16,20},{20,16},{24,28},{28,24},{1,5},{5... | collective-permute-start | bytes 7077896 | tf_op jit(solution)/shard_map/ppermute | solution.py:53
  506.3 378.7 %collective-permute-start.76 = (bf16[1024,1152]{0,1:T(8,128)(2,1)}, bf16[1024,1152]{0,1:T(8,128)(2,1)}, u32[]{:S(2)}, u32[]{:S(2)}) collective-permute-start(bf16[1024,1152]{0,1:T(8,128)(2,1)} %get-tuple-element.170), channel_id=1, source_target_pairs={{0,4},{4,0},{8,12},{12,8},{16,20},{20,16},{24,28},{28,24},{1,5},{5... | collective-permute-start | bytes 7077896 | tf_op jit(solution)/shard_map/ppermute | solution.py:53
  517.7 16.1 %collective-permute-start.34 = (bf16[36,8,1152]{2,1,0:T(8,128)(2,1)S(1)}, bf16[36,8,1152]{2,1,0:T(8,128)(2,1)}, u32[]{:S(2)}, u32[]{:S(2)}) collective-permute-start(bf16[36,8,1152]{2,1,0:T(8,128)(2,1)S(1)} %collective-permute-done.30.refs_1_), channel_id=1, source_target_pairs={{0,1},{1,2},{2,3},{3,0},{4,5},{5,6},{6,7},{7,4},{8,9},{9,10},{10,1... | collective-permute-start | bytes 1990664 | tf_op jit(solution)/shard_map/ppermute | solution.py:56
  519.6 19.0 %collective-permute-start.31 = (bf16[36,8,1152]{2,1,0:T(8,128)(2,1)S(1)}, bf16[36,8,1152]{2,1,0:T(8,128)(2,1)}, u32[]{:S(2)}, u32[]{:S(2)}) collective-permute-start(bf16[36,8,1152]{2,1,0:T(8,128)(2,1)S(1)} %collective-permute-done.30.refs_1_), channel_id=1, source_target_pairs={{0,8},{4,12},{8,0},{12,4},{16,24},{20,28},{24,16},{28,20},{1,9},{5... | collective-permute-start | bytes 1990664 | tf_op jit(solution)/shard_map/ppermute | solution.py:53
  519.6 20.2 %collective-permute-start.29 = (bf16[9,8,4608]{2,1,0:T(8,128)(2,1)}, bf16[9,8,4608]{2,1,0:T(8,128)(2,1)}, u32[]{:S(2)}, u32[]{:S(2)}) collective-permute-start(bf16[9,8,4608]{2,1,0:T(8,128)(2,1)} %collective-permute-done.27.refs_10_), channel_id=1, source_target_pairs={{0,4},{4,0},{8,12},{12,8},{16,20},{20,16},{24,28},{28,24},{1,5},{5... | collective-permute-start | bytes 1990664 | tf_op jit(solution)/shard_map/ppermute | solution.py:53
  533.9 18.3 %collective-permute-start.38 = (bf16[36,8,1152]{2,1,0:T(8,128)(2,1)}, bf16[36,8,1152]{2,1,0:T(8,128)(2,1)}, u32[]{:S(2)}, u32[]{:S(2)}) collective-permute-start(bf16[36,8,1152]{2,1,0:T(8,128)(2,1)} %collective-permute-done.34.refs_5_), channel_id=1, source_target_pairs={{0,1},{1,2},{2,3},{3,0},{4,5},{5,6},{6,7},{7,4},{8,9},{9,10},{10,1... | collective-permute-start | bytes 1990664 | tf_op jit(solution)/shard_map/ppermute | solution.py:56
  538.6 343.8 %collective-permute-start.32 = (bf16[36,8,1152]{2,1,0:T(8,128)(2,1)S(1)}, bf16[36,8,1152]{2,1,0:T(8,128)(2,1)}, u32[]{:S(2)}, u32[]{:S(2)}) collective-permute-start(bf16[36,8,1152]{2,1,0:T(8,128)(2,1)S(1)} %collective-permute-done.30.refs_1_), channel_id=1, source_target_pairs={{0,4},{4,0},{8,12},{12,8},{16,20},{20,16},{24,28},{28,24},{1,5},{5... | collective-permute-start | bytes 1990664 | tf_op jit(solution)/shard_map/ppermute | solution.py:53
  539.8 344.7 %collective-permute-start.35 = (bf16[36,8,1152]{2,1,0:T(8,128)(2,1)}, bf16[36,8,1152]{2,1,0:T(8,128)(2,1)}, u32[]{:S(2)}, u32[]{:S(2)}) collective-permute-start(bf16[36,8,1152]{2,1,0:T(8,128)(2,1)} %collective-permute-done.34.refs_5_), channel_id=1, source_target_pairs={{0,16},{4,20},{8,24},{12,28},{16,0},{20,4},{24,8},{28,12},{1,17},{... | collective-permute-start | bytes 1990664 | tf_op jit(solution)/shard_map/ppermute | solution.py:53
  552.2 332.9 %collective-permute-start.39 = (bf16[36,8,1152]{2,1,0:T(8,128)(2,1)}, bf16[36,8,1152]{2,1,0:T(8,128)(2,1)}, u32[]{:S(2)}, u32[]{:S(2)}) collective-permute-start(bf16[36,8,1152]{2,1,0:T(8,128)(2,1)} %collective-permute-done.38.refs_9_), channel_id=1, source_target_pairs={{0,8},{4,12},{8,0},{12,4},{16,24},{20,28},{24,16},{28,20},{1,9},{5... | collective-permute-start | bytes 1990664 | tf_op jit(solution)/shard_map/ppermute | solution.py:53
  882.4 17.9 %collective-permute-start.36 = (bf16[36,8,1152]{2,1,0:T(8,128)(2,1)}, bf16[36,8,1152]{2,1,0:T(8,128)(2,1)S(1)}, u32[]{:S(2)}, u32[]{:S(2)}) collective-permute-start(bf16[36,8,1152]{2,1,0:T(8,128)(2,1)} %collective-permute-done.34.refs_5_), channel_id=1, source_target_pairs={{0,4},{4,0},{8,12},{12,8},{16,20},{20,16},{24,28},{28,24},{1,5},{5... | collective-permute-start | bytes 1990664 | tf_op jit(solution)/shard_map/ppermute | solution.py:53
  884.5 15.8 collective-permute-start.33
  884.6 15.8 collective-permute-start.40
  885.1 18.8 %collective-permute-start.41 = (bf16[36,8,1152]{2,1,0:T(8,128)(2,1)}, bf16[36,8,1152]{2,1,0:T(8,128)(2,1)}, u32[]{:S(2)}, u32[]{:S(2)}) collective-permute-start(bf16[36,8,1152]{2,1,0:T(8,128)(2,1)} %collective-permute-done.39.refs_10_), channel_id=1, source_target_pairs={{0,4},{4,0},{8,12},{12,8},{16,20},{20,16},{24,28},{28,24},{1,5},{5... | collective-permute-start | bytes 1990664 | tf_op jit(solution)/shard_map/ppermute | solution.py:53
  1302.3 31.6 %collective-permute-start.42 = (bf16[2304]{0:T(1024)(128)(2,1)}, bf16[2304]{0:T(1024)(128)(2,1)}, u32[]{:S(2)}, u32[]{:S(2)}) collective-permute-start(bf16[2304]{0:T(1024)(128)(2,1)} %pad_maximum_fusion.18), channel_id=1, source_target_pairs={{0,1},{1,2},{2,3},{3,0},{4,5},{5,6},{6,7},{7,4},{8,9},{9,10},{10,1... | collective-permute-start | bytes 13832 | tf_op jit(solution)/shard_map/ppermute | solution.py:56
  1306.3 28.7 %collective-permute-start.43 = (bf16[2304]{0:T(1024)(128)(2,1)}, bf16[2304]{0:T(1024)(128)(2,1)}, u32[]{:S(2)}, u32[]{:S(2)}) collective-permute-start(bf16[2304]{0:T(1024)(128)(2,1)} %pad_maximum_fusion.18), channel_id=1, source_target_pairs={{0,2},{1,3},{2,0},{3,1},{4,6},{5,7},{6,4},{7,5},{8,10},{9,11},{10,... | collective-permute-start | bytes 13832 | tf_op jit(solution)/shard_map/ppermute | solution.py:56
  1344.6 15.8 collective-permute-start.124
  1354.2 62.1 %collective-permute-start.100 = (bf16[256,1152]{1,0:T(8,128)(2,1)}, bf16[256,1152]{1,0:T(8,128)(2,1)S(1)}, u32[]{:S(2)}, u32[]{:S(2)}) collective-permute-start(bf16[256,1152]{1,0:T(8,128)(2,1)} %get-tuple-element.135), channel_id=1, source_target_pairs={{0,8},{4,12},{8,0},{12,4},{16,24},{20,28},{24,16},{28,20},{1,9},{5... | collective-permute-start | bytes 1769480 | tf_op jit(solution)/shard_map/ppermute | solution.py:53
  1356.4 60.6 %collective-permute-start.101 = (bf16[256,1152]{1,0:T(8,128)(2,1)}, bf16[256,1152]{1,0:T(8,128)(2,1)S(1)}, u32[]{:S(2)}, u32[]{:S(2)}) collective-permute-start(bf16[256,1152]{1,0:T(8,128)(2,1)} %get-tuple-element.135), channel_id=1, source_target_pairs={{0,16},{4,20},{8,24},{12,28},{16,0},{20,4},{24,8},{28,12},{1,17},{... | collective-permute-start | bytes 1769480 | tf_op jit(solution)/shard_map/ppermute | solution.py:53
  1370.2 15.4 collective-permute-start.77
  1405.5 23.3 %collective-permute-start.96 = (bf16[4,576,256]{2,1,0:T(8,128)(2,1)S(1)}, bf16[4,576,256]{2,1,0:T(8,128)(2,1)S(1)}, u32[]{:S(2)}, u32[]{:S(2)}) collective-permute-start(bf16[4,576,256]{2,1,0:T(8,128)(2,1)S(1)} %copy-done.17), channel_id=1, source_target_pairs={{0,4},{4,0},{8,12},{12,8},{16,20},{20,16},{24,28},{28,24},{1,5},{5... | collective-permute-start | bytes 3538952 | tf_op jit(solution)/shard_map/ppermute | solution.py:53
  1411.8 18.9 %collective-permute-start.89 = (bf16[4,576,256]{2,1,0:T(8,128)(2,1)S(1)}, bf16[4,576,256]{2,1,0:T(8,128)(2,1)S(1)}, u32[]{:S(2)}, u32[]{:S(2)}) collective-permute-start(bf16[4,576,256]{2,1,0:T(8,128)(2,1)S(1)} %copy-done.16), channel_id=1, source_target_pairs={{0,4},{4,0},{8,12},{12,8},{16,20},{20,16},{24,28},{28,24},{1,5},{5... | collective-permute-start | bytes 3538952 | tf_op jit(solution)/shard_map/ppermute | solution.py:53
  1426.1 91.5 %collective-permute-start.104 = (bf16[1024,1152]{1,0:T(8,128)(2,1)S(1)}, bf16[1024,1152]{1,0:T(8,128)(2,1)S(1)}, u32[]{:S(2)}, u32[]{:S(2)}) collective-permute-start(bf16[1024,1152]{1,0:T(8,128)(2,1)S(1)} %get-tuple-element.159), channel_id=1, source_target_pairs={{0,4},{4,0},{8,12},{12,8},{16,20},{20,16},{24,28},{28,24},{1,5},{5... | collective-permute-start | bytes 7077896 | tf_op jit(solution)/shard_map/ppermute | solution.py:53
  1427.6 23.2 %collective-permute-start.68 = (bf16[2,432,256]{2,1,0:T(8,128)(2,1)S(1)}, bf16[2,432,256]{2,1,0:T(8,128)(2,1)S(1)}, u32[]{:S(2)}, u32[]{:S(2)}) collective-permute-start(bf16[2,432,256]{2,1,0:T(8,128)(2,1)S(1)} %pad_maximum_fusion.11), channel_id=1, source_target_pairs={{0,24},{4,28},{8,16},{12,20},{16,8},{20,12},{24,0},{28,4},{1,25},{... | collective-permute-start | bytes 1327112 | tf_op jit(solution)/shard_map/ppermute | solution.py:53
  1428.2 21.5 %collective-permute-start.67 = (bf16[2,432,256]{2,1,0:T(8,128)(2,1)S(1)}, bf16[2,432,256]{2,1,0:T(8,128)(2,1)S(1)}, u32[]{:S(2)}, u32[]{:S(2)}) collective-permute-start(bf16[2,432,256]{2,1,0:T(8,128)(2,1)S(1)} %pad_maximum_fusion.10), channel_id=1, source_target_pairs={{0,16},{4,20},{8,24},{12,28},{16,0},{20,4},{24,8},{28,12},{1,17},{... | collective-permute-start | bytes 1327112 | tf_op jit(solution)/shard_map/ppermute | solution.py:53
  1428.8 20.7 %collective-permute-start.66 = (bf16[2,432,256]{2,1,0:T(8,128)(2,1)S(1)}, bf16[2,432,256]{2,1,0:T(8,128)(2,1)S(1)}, u32[]{:S(2)}, u32[]{:S(2)}) collective-permute-start(bf16[2,432,256]{2,1,0:T(8,128)(2,1)S(1)} %pad_maximum_fusion.9), channel_id=1, source_target_pairs={{0,8},{4,12},{8,0},{12,4},{16,24},{20,28},{24,16},{28,20},{1,9},{5... | collective-permute-start | bytes 1327112 | tf_op jit(solution)/shard_map/ppermute | solution.py:53
  1430.8 63.5 %collective-permute-start.97 = (bf16[2,576,256]{2,1,0:T(8,128)(2,1)S(1)}, bf16[2,576,256]{2,1,0:T(8,128)(2,1)S(1)}, u32[]{:S(2)}, u32[]{:S(2)}) collective-permute-start(bf16[2,576,256]{2,1,0:T(8,128)(2,1)S(1)} %pad_maximum_fusion.5), channel_id=1, source_target_pairs={{0,8},{4,12},{8,0},{12,4},{16,24},{20,28},{24,16},{28,20},{1,9},{5... | collective-permute-start | bytes 1769480 | tf_op jit(solution)/shard_map/ppermute | solution.py:53
  1449.5 39.3 %collective-permute-start.92 = (bf16[2,576,256]{2,1,0:T(8,128)(2,1)S(1)}, bf16[2,576,256]{2,1,0:T(8,128)(2,1)S(1)}, u32[]{:S(2)}, u32[]{:S(2)}) collective-permute-start(bf16[2,576,256]{2,1,0:T(8,128)(2,1)S(1)} %pad_maximum_fusion.4), channel_id=1, source_target_pairs={{0,24},{4,28},{8,16},{12,20},{16,8},{20,12},{24,0},{28,4},{1,25},{... | collective-permute-start | bytes 1769480 | tf_op jit(solution)/shard_map/ppermute | solution.py:53
  1449.7 38.4 %collective-permute-start.91 = (bf16[2,576,256]{2,1,0:T(8,128)(2,1)S(1)}, bf16[2,576,256]{2,1,0:T(8,128)(2,1)S(1)}, u32[]{:S(2)}, u32[]{:S(2)}) collective-permute-start(bf16[2,576,256]{2,1,0:T(8,128)(2,1)S(1)} %pad_maximum_fusion.3), channel_id=1, source_target_pairs={{0,16},{4,20},{8,24},{12,28},{16,0},{20,4},{24,8},{28,12},{1,17},{... | collective-permute-start | bytes 1769480 | tf_op jit(solution)/shard_map/ppermute | solution.py:53
  1450.8 36.6 %collective-permute-start.90 = (bf16[2,576,256]{2,1,0:T(8,128)(2,1)S(1)}, bf16[2,576,256]{2,1,0:T(8,128)(2,1)S(1)}, u32[]{:S(2)}, u32[]{:S(2)}) collective-permute-start(bf16[2,576,256]{2,1,0:T(8,128)(2,1)S(1)} %pad_maximum_fusion.2), channel_id=1, source_target_pairs={{0,8},{4,12},{8,0},{12,4},{16,24},{20,28},{24,16},{28,20},{1,9},{5... | collective-permute-start | bytes 1769480 | tf_op jit(solution)/shard_map/ppermute | solution.py:53
  1487.4 26.7 %collective-permute-start.98 = (bf16[2,576,256]{2,1,0:T(8,128)(2,1)S(1)}, bf16[2,576,256]{2,1,0:T(8,128)(2,1)S(1)}, u32[]{:S(2)}, u32[]{:S(2)}) collective-permute-start(bf16[2,576,256]{2,1,0:T(8,128)(2,1)S(1)} %pad_maximum_fusion.6), channel_id=1, source_target_pairs={{0,16},{4,20},{8,24},{12,28},{16,0},{20,4},{24,8},{28,12},{1,17},{... | collective-permute-start | bytes 1769480 | tf_op jit(solution)/shard_map/ppermute | solution.py:53
  1488.1 26.0 %collective-permute-start.99 = (bf16[2,576,256]{2,1,0:T(8,128)(2,1)S(1)}, bf16[2,576,256]{2,1,0:T(8,128)(2,1)S(1)}, u32[]{:S(2)}, u32[]{:S(2)}) collective-permute-start(bf16[2,576,256]{2,1,0:T(8,128)(2,1)S(1)} %pad_maximum_fusion.7), channel_id=1, source_target_pairs={{0,24},{4,28},{8,16},{12,20},{16,8},{20,12},{24,0},{28,4},{1,25},{... | collective-permute-start | bytes 1769480 | tf_op jit(solution)/shard_map/ppermute | solution.py:53
  1488.8 32.6 %collective-permute-start.69 = (bf16[288,432]{1,0:T(8,128)(2,1)S(1)}, bf16[288,432]{1,0:T(8,128)(2,1)S(1)}, u32[]{:S(2)}, u32[]{:S(2)}) collective-permute-start(bf16[288,432]{1,0:T(8,128)(2,1)S(1)} %get-tuple-element.101), channel_id=1, source_target_pairs={{0,1},{1,2},{2,3},{3,0},{4,5},{5,6},{6,7},{7,4},{8,9},{9,10},{10,1... | collective-permute-start | bytes 746504 | tf_op jit(solution)/shard_map/ppermute | solution.py:56
  1494.2 27.6 %collective-permute-start.70 = (bf16[288,432]{1,0:T(8,128)(2,1)S(1)}, bf16[288,432]{1,0:T(8,128)(2,1)S(1)}, u32[]{:S(2)}, u32[]{:S(2)}) collective-permute-start(bf16[288,432]{1,0:T(8,128)(2,1)S(1)} %get-tuple-element.103), channel_id=1, source_target_pairs={{0,2},{1,3},{2,0},{3,1},{4,6},{5,7},{6,4},{7,5},{8,10},{9,11},{10,... | collective-permute-start | bytes 746504 | tf_op jit(solution)/shard_map/ppermute | solution.py:56
  1517.7 39.0 %collective-permute-start.94 = (bf16[288,576]{1,0:T(8,128)(2,1)S(1)}, bf16[288,576]{1,0:T(8,128)(2,1)S(1)}, u32[]{:S(2)}, u32[]{:S(2)}) collective-permute-start(bf16[288,576]{1,0:T(8,128)(2,1)S(1)} %get-tuple-element.91), channel_id=1, source_target_pairs={{0,2},{1,3},{2,0},{3,1},{4,6},{5,7},{6,4},{7,5},{8,10},{9,11},{10,... | collective-permute-start | bytes 995336 | tf_op jit(solution)/shard_map/ppermute | solution.py:56
  1521.4 35.3 %collective-permute-start.95 = (bf16[288,576]{1,0:T(8,128)(2,1)S(1)}, bf16[288,576]{1,0:T(8,128)(2,1)S(1)}, u32[]{:S(2)}, u32[]{:S(2)}) collective-permute-start(bf16[288,576]{1,0:T(8,128)(2,1)S(1)} %get-tuple-element.90), channel_id=1, source_target_pairs={{0,3},{1,0},{2,1},{3,2},{4,7},{5,4},{6,5},{7,6},{8,11},{9,8},{10,9... | collective-permute-start | bytes 995336 | tf_op jit(solution)/shard_map/ppermute | solution.py:56
  1521.9 35.9 %collective-permute-start.105 = (bf16[144,1152]{1,0:T(8,128)(2,1)S(1)}, bf16[144,1152]{1,0:T(8,128)(2,1)S(1)}, u32[]{:S(2)}, u32[]{:S(2)}) collective-permute-start(bf16[144,1152]{1,0:T(8,128)(2,1)S(1)} %get-tuple-element.92), channel_id=1, source_target_pairs={{0,1},{1,2},{2,3},{3,0},{4,5},{5,6},{6,7},{7,4},{8,9},{9,10},{10,1... | collective-permute-start | bytes 995336 | tf_op jit(solution)/shard_map/ppermute | solution.py:56
  1524.9 58.7 %collective-permute-start.106 = (bf16[144,1152]{1,0:T(8,128)(2,1)S(1)}, bf16[144,1152]{1,0:T(8,128)(2,1)S(1)}, u32[]{:S(2)}, u32[]{:S(2)}) collective-permute-start(bf16[144,1152]{1,0:T(8,128)(2,1)S(1)} %get-tuple-element.94), channel_id=1, source_target_pairs={{0,2},{1,3},{2,0},{3,1},{4,6},{5,7},{6,4},{7,5},{8,10},{9,11},{10,... | collective-permute-start | bytes 995336 | tf_op jit(solution)/shard_map/ppermute | solution.py:56
  1529.3 54.4 %collective-permute-start.107 = (bf16[144,1152]{1,0:T(8,128)(2,1)S(1)}, bf16[144,1152]{1,0:T(8,128)(2,1)S(1)}, u32[]{:S(2)}, u32[]{:S(2)}) collective-permute-start(bf16[144,1152]{1,0:T(8,128)(2,1)S(1)} %get-tuple-element.93), channel_id=1, source_target_pairs={{0,3},{1,0},{2,1},{3,2},{4,7},{5,4},{6,5},{7,6},{8,11},{9,8},{10,9... | collective-permute-start | bytes 995336 | tf_op jit(solution)/shard_map/ppermute | solution.py:56
  (165 other events, 5507.2 us)

commit v2 on v1

v2 whole, which is shorter than its diff:
```python
import math

import jax
import jax.numpy as jnp
from jax import lax
from jax.experimental import pallas as pl
from jax.experimental.pallas import tpu as pltpu
from jax.sharding import PartitionSpec as P

HEAD_DIM = 72
BOX = 8

epsilon = 1e-06
masked_value = -1e30
gelu_root = math.sqrt(2.0 / math.pi)
f32 = jnp.float32
bf16 = jnp.bfloat16


def norm_parts(values_in):
    centred = values_in - jnp.mean(values_in, axis=-1, keepdims=True)
    spread = jnp.mean(centred * centred, axis=-1, keepdims=True)
    rate = lax.rsqrt(spread + epsilon)
    return centred * rate, rate


def norm_back(normal, rate, grad):
    mean_grad = jnp.mean(grad, axis=-1, keepdims=True)
    mean_both = jnp.mean(grad * normal, axis=-1, keepdims=True)
    return rate * (grad - mean_grad - normal * mean_both)


def gelu_tanh(pre_act):
    return (
        0.5
        * pre_act
        * (1.0 + jnp.tanh(gelu_root * (pre_act + 0.044715 * pre_act * pre_act * pre_act)))
    )


def after(value, other):
    return lax.optimization_barrier((value, other))[0]


def gated(values):
    return lax.optimization_barrier(values)


def pick(array, index, axis=0):
    return lax.dynamic_index_in_dim(array, index, axis, keepdims=False)


def make_body(dp, fs):
    groups = dp // BOX

    def box_send(x, bits):
        return lax.ppermute(x, "dp", [(i, i ^ bits) for i in range(dp)])

    def side_send(x):
        return lax.ppermute(x, "dp", [(i, i ^ (4 if i & 1 else 2)) for i in range(dp)])

    def ring_send(x, hops):
        return lax.ppermute(x, "fsdp", [(i, (i + hops) % fs) for i in range(fs)])

    def group_send(x, hops):
        return lax.ppermute(x, "dp", [(i, (i + hops * BOX) % dp) for i in range(dp)])

    def ring_gather(x):
        return [x] + [ring_send(x, k) for k in range(1, fs)]

    def ring_sorted(blocks, z):
        back = jnp.stack(blocks[::-1] + blocks[::-1])
        return lax.dynamic_slice_in_dim(back, fs - 1 - z, fs, 0)

    def chip_near(x):
        return box_send(x, 2), box_send(x, 4)

    def chip_far(near):
        half = near[0].shape[0] // 2
        return box_send(near[0][:half], 4), box_send(near[1][half:], 2)

    def chip_exchange(blocks, chip):
        return [pick(blocks, chip)] + [
            box_send(pick(blocks, chip ^ k), 2 * k) for k in range(1, BOX // 2)
        ]

    def ring_sum(x, z):
        total = pick(x, z)
        for k in range(1, fs):
            sent = pick(x, lax.rem(z + k, fs)).astype(bf16)
            total = total + ring_send(sent, k).astype(f32)
        return total

    def group_sum(x, group):
        total = pick(x, group)
        for k in range(1, groups):
            total = total + group_send(pick(x, lax.rem(group + k, groups)), k)
        return total

    def assemble(where, owns, pieces):
        arrays = []
        for piece, unused in (each for kind in pieces for each in kind):
            if not any(piece is array for array in arrays):
                arrays.append(piece)
        position = {id(array): i for i, array in enumerate(arrays)}
        plan = [[(position[id(piece)], index) for piece, index in kind] for kind in pieces]
        n_own, n_arrays, n_kinds = len(owns), len(arrays), len(pieces)
        widths = [own.shape[-1] for own in owns]
        starts = [sum(widths[:i]) for i in range(n_own)]
        lead, width = arrays[0].shape[-3], sum(widths)

        def kernel(where_ref, *refs):
            own_refs = refs[:n_own]
            array_refs = refs[n_own : n_own + n_arrays]
            out_refs = refs[n_own + n_arrays : -1]
            sems = refs[-1]
            step = pl.program_id(0)

            def run(copies):
                started = [
                    pltpu.make_async_copy(source, target, sems.at[j])
                    for j, (source, target) in enumerate(copies)
                ]
                for copy in started:
                    copy.start()
                for copy in started:
                    copy.wait()

            @pl.when(step == 0)
            def own_rows():
                run([(own_refs[i], out_refs[i].at[0]) for i in range(n_own)])

            for block in range(1, fs):

                @pl.when(step == block)
                def other_rows(block=block):
                    copies = []
                    for kind in range(n_kinds):
                        which, index = plan[kind][block - 1]
                        source = array_refs[which]
                        source = source if index is None else source.at[index]
                        for i in range(n_own):
                            part = source.at[:, :, pl.ds(starts[i], widths[i])]
                            copies.append((part, out_refs[i].at[0, where_ref[fs + kind]]))
                    run(copies)

        any_spec = pl.BlockSpec(memory_space=pl.ANY)
        outs = pl.pallas_call(
            kernel,
            out_shape=[
                jax.ShapeDtypeStruct((fs, 4, lead, 8, each), bf16) for each in widths
            ],
            grid_spec=pltpu.PrefetchScalarGridSpec(
                num_scalar_prefetch=1,
                grid=(fs,),
                in_specs=[any_spec] * (n_own + n_arrays),
                out_specs=[
                    pl.BlockSpec(
                        (1, 4, lead, 8, each), lambda k, where_ref: (where_ref[k], 0, 0, 0, 0)
                    )
                    for each in widths
                ],
                scratch_shapes=[pltpu.SemaphoreType.DMA((n_own * n_kinds,))],
            ),
            cost_estimate=pl.CostEstimate(
                flops=0, transcendentals=0, bytes_accessed=fs * 4 * lead * 8 * width * 4
            ),
            compiler_params=pltpu.CompilerParams(vmem_limit_bytes=24 << 20),
        )(where, *[own.reshape(4, lead, 8, own.shape[-1]) for own in owns], *arrays)
        return [out.reshape(fs * 4 * lead * 8, out.shape[-1]) for out in outs]

    def assemble_wide(where, owns, mine, got):
        n_own, n_pieces = len(owns), len(mine)
        widths = [own.shape[-1] for own in owns]
        width = sum(widths)
        part = mine[0].shape[-1]
        lead = owns[0].shape[0] // 32
        split = mine[3].shape[0]

        def col_plan(core):
            plan, first = [], 0
            low, high = (0, part) if core == 0 else (part, width)
            offset = 0 if core == 0 else width - part
            for i, each in enumerate(widths):
                start, end = max(low, first), min(high, first + each)
                if start < end:
                    plan.append((start - offset, i, start - first, end - start))
                first += each
            return plan

        def row_plan(block):
            base = (block - 1) * lead
            plan = [(i, base, i, 0, lead) for i in range(3)]
            top = min(max(split - base, 0), lead)
            if top:
                plan.append((3, base, 3, 0, top))
            if top < lead:
                plan.append((4, base + top - split, 3, top, lead - top))
            return plan

        def kernel(where_ref, *refs):
            own_refs = refs[:n_own]
            sets = (refs[n_own : n_own + n_pieces], refs[n_own + n_pieces : n_own + 2 * n_pieces])
            out_refs = refs[n_own + 2 * n_pieces : -1]
            sems = refs[-1]
            step = pl.program_id(0)

            def run(copies):
                started = [
                    pltpu.make_async_copy(source, target, sems.at[j])
                    for j, (source, target) in enumerate(copies)
                ]
                for copy in started:
                    copy.start()
                for copy in started:
                    copy.wait()

            @pl.when(step == 0)
            def own_rows():
                run([(own_refs[i], out_refs[i].at[0]) for i in range(n_own)])

            for block in range(1, fs):
                for core in range(2):

                    @pl.when((step == block) & (where_ref[fs] == core))
                    def other_rows(block=block, core=core):
                        copies = []
                        for side, piece_refs in enumerate(sets):
                            for piece, first, slot, row, rows in row_plan(block):
                                for col, i, target_col, cols in col_plan(core ^ side):
                                    source = piece_refs[piece].at[
                                        first : first + rows, :, col : col + cols
                                    ]
                                    target = out_refs[i].at[
                                        0,
                                        where_ref[fs + 1 + slot],
                                        row : row + rows,
                                        :,
                                        target_col : target_col + cols,
                                    ]
                                    copies.append((source, target))
                        run(copies)

        n_sems = max(
            n_own,
            max(
                len(row_plan(block)) * (len(col_plan(0)) + len(col_plan(1)))
                for block in range(1, fs)
            ),
        )
        any_spec = pl.BlockSpec(memory_space=pl.ANY)
        outs = pl.pallas_call(
            kernel,
            out_shape=[
                jax.ShapeDtypeStruct((fs, 4, lead, 8, each), bf16) for each in widths
            ],
            grid_spec=pltpu.PrefetchScalarGridSpec(
                num_scalar_prefetch=1,
                grid=(fs,),
                in_specs=[any_spec] * (n_own + 2 * n_pieces),
                out_specs=[
                    pl.BlockSpec(
                        (1, 4, lead, 8, each), lambda k, where_ref: (where_ref[k], 0, 0, 0, 0)
                    )
                    for each in widths
                ],
                scratch_shapes=[pltpu.SemaphoreType.DMA((n_sems,))],
            ),
            cost_estimate=pl.CostEstimate(
                flops=0, transcendentals=0, bytes_accessed=fs * 4 * lead * 8 * width * 4
            ),
            compiler_params=pltpu.CompilerParams(vmem_limit_bytes=24 << 20),
        )(where, *[own.reshape(4, lead, 8, own.shape[-1]) for own in owns], *mine, *got)
        return [out.reshape(fs * 4 * lead * 8, out.shape[-1]) for out in outs]

    def column_grad(where, lefts, rights):
        slots, n = rights[0].shape[1], rights[0].shape[0] // 2
        width = lefts[0].shape[1]
        tile = width // 3
        half = slots // 2

        def kernel(where_ref, x0, x1, x2, x3, x4, y0, y1, y2, y3, keep_ref, send_ref):
            core = where_ref[0]
            for out_ref, first in ((keep_ref, core * n), (send_ref, (1 - core) * n)):
                rows = pl.ds(pl.multiple_of(first, 16), n)
                total = None
                for x, y, cols in (
                    (x0, y0, slice(None)),
                    (x1, y1, slice(None)),
                    (x2, y2, slice(None)),
                    (x3, y3, slice(0, half)),
                    (x4, y3, slice(half, slots)),
                ):
                    part = jnp.dot(y[rows, cols], x[...], preferred_element_type=f32)
                    total = part if total is None else total + part
                out_ref[...] = total

        left_specs = [
            pl.BlockSpec((left.shape[0], tile), lambda i, where_ref: (0, i)) for left in lefts
        ]
        right_spec = pl.BlockSpec((2 * n, slots), lambda i, where_ref: (0, 0))
        out_spec = pl.BlockSpec((n, tile), lambda i, where_ref: (0, i))
        return pl.pallas_call(
            kernel,
            out_shape=[jax.ShapeDtypeStruct((n, width), f32)] * 2,
            grid_spec=pltpu.PrefetchScalarGridSpec(
                num_scalar_prefetch=1,
                grid=(width // tile,),
                in_specs=left_specs + [right_spec] * 4,
                out_specs=[out_spec] * 2,
            ),
            cost_estimate=pl.CostEstimate(
                flops=16 * slots * width * n,
                transcendentals=0,
                bytes_accessed=8 * slots * (width + 2 * n) + 8 * width * n,
            ),
            compiler_params=pltpu.CompilerParams(vmem_limit_bytes=32 << 20),
        )(where, *lefts, *rights)

    def split_grad(where, keep, got):
        n, width = keep.shape
        rows = width // fs
        padded = -(-n // 128) * 128

        def kernel(where_ref, keep_ref, got_ref, own_ref, *rest):
            send_refs, turned = rest[:-1], rest[-1]
            for first in range(0, width, 128):
                total = keep_ref[:, first : first + 128] + got_ref[:, first : first + 128]
                if padded > n:
                    total = jnp.concatenate([total, jnp.zeros((padded - n, 128), f32)], axis=0)
                turned[first : first + 128, :] = total.T[:, :n]
            z = where_ref[0]
            own_ref[...] = turned[pl.ds(pl.multiple_of(z * rows, 16), rows), :]
            for k, send_ref in enumerate(send_refs):
                target = lax.rem(z + k + 1, fs)
                block = turned[pl.ds(pl.multiple_of(target * rows, 16), rows), :]
                send_ref[...] = block.astype(bf16)

        whole = pl.BlockSpec(memory_space=pltpu.VMEM)
        return pl.pallas_call(
            kernel,
            out_shape=[jax.ShapeDtypeStruct((rows, n), f32)]
            + [jax.ShapeDtypeStruct((rows, n), bf16)] * (fs - 1),
            in_specs=[pl.BlockSpec(memory_space=pltpu.SMEM), whole, whole],
            out_specs=[whole] * fs,
            scratch_shapes=[pltpu.VMEM((width, n), f32)],
            cost_estimate=pl.CostEstimate(
                flops=width * n, transcendentals=0, bytes_accessed=11 * width * n
            ),
            compiler_params=pltpu.CompilerParams(vmem_limit_bytes=32 << 20),
        )(where, keep, got)

    def row_grad(where, lefts, rights):
        rows = lefts[0].shape[0] // fs
        slots, n = lefts[0].shape[1], rows // 2
        width = rights[0].shape[1]
        half = slots // 2

        def kernel(where_ref, x0, x1, x2, x3, y0, y1, y2, y3, y4, keep_ref, send_ref):
            core = where_ref[0]
            for out_ref, first in ((keep_ref, core * n), (send_ref, (1 - core) * n)):
                lines = pl.ds(pl.multiple_of(first, 16), n)
                total = None
                for x, y, cols in (
                    (x0, y0, slice(None)),
                    (x1, y1, slice(None)),
                    (x2, y2, slice(None)),
                    (x3, y3, slice(0, half)),
                    (x3, y4, slice(half, slots)),
                ):
                    part = jnp.dot(x[lines, cols], y[...], preferred_element_type=f32)
                    total = part if total is None else total + part
                out_ref[0] = total

        left_spec = pl.BlockSpec((rows, slots), lambda i, where_ref: (i, 0))
        right_specs = [
            pl.BlockSpec((right.shape[0], width), lambda i, where_ref: (0, 0))
            for right in rights
        ]
        out_spec = pl.BlockSpec((1, n, width), lambda i, where_ref: (i, 0, 0))
        return pl.pallas_call(
            kernel,
            out_shape=[jax.ShapeDtypeStruct((fs, n, width), f32)] * 2,
            grid_spec=pltpu.PrefetchScalarGridSpec(
                num_scalar_prefetch=1,
                grid=(fs,),
                in_specs=[left_spec] * 4 + right_specs,
                out_specs=[out_spec] * 2,
            ),
            cost_estimate=pl.CostEstimate(
                flops=8 * slots * width * rows * fs,
                transcendentals=0,
                bytes_accessed=8 * slots * (width + rows * fs) + 4 * width * rows * fs,
            ),
            compiler_params=pltpu.CompilerParams(vmem_limit_bytes=32 << 20),
        )(where, *lefts, *rights)

    def body(
        tokens,
        condition,
        grid_sizes,
        w_ada,
        w_qkv,
        w_out,
        w_up,
        w_down,
        b_ada,
        b_qv,
        b_out,
        b_up,
        b_down,
        cotangent,
    ):
        slots, width = tokens.shape[1:]
        heads = width // HEAD_DIM
        hidden = w_up.shape[1]
        rank = lax.axis_index("dp")
        z = lax.axis_index("fsdp")
        place = lax.rem(rank, BOX)
        group = lax.div(rank, BOX)
        core = place & 1
        chip = place >> 1
        side = (chip ^ (chip >> 1)) & 1
        near = 2 * side + core
        far = 2 * (1 - side) + core
        where = jnp.stack(
            [lax.rem(z - k + fs, fs) for k in range(fs)] + [near, far, near ^ 1, far ^ 1]
        ).astype(jnp.int32)
        where_core = core.reshape(1).astype(jnp.int32)
        where_wide = jnp.stack(
            [lax.rem(z - k + fs, fs) for k in range(fs)] + [core] + [chip ^ k for k in range(4)]
        ).astype(jnp.int32)

        cond_wide = condition[0].astype(f32)
        gate = jax.nn.sigmoid(cond_wide)
        cond_act = (cond_wide * gate).astype(bf16)
        row = max(width, b_ada.shape[0])
        small = jnp.stack(
            [
                jnp.pad(each, (0, row - each.shape[0]))
                for each in (cond_act, b_ada, b_qv, b_out, b_up, b_down)
            ]
        )

        def quarter_of(shard):
            rows, cols = shard.shape
            return pick(shard.reshape(4, rows // 32, 8, cols), near)

        def ring_on(held, count):
            helds = []
            for unused in range(count):
                held = ring_send(held, 1)
                helds.append(held)
            return helds

        last = fs - 1
        small_all = ring_gather(small)
        raw = jnp.concatenate([tokens[0], cotangent[0]], axis=1)
        raw_near = chip_near(raw)
        qkv_helds = ring_on(quarter_of(w_qkv), 1)
        def chip_rows_of(shard):
            rows, cols = shard.shape
            return pick(shard.reshape(4, rows // 32, 8, cols), chip)

        mid_rows = jnp.concatenate([chip_rows_of(w_out), chip_rows_of(w_up)], axis=-1)
        mid_width = mid_rows.shape[-1]
        mid_part = -(-mid_width // 256) * 128
        mid_start = jnp.where(core == 0, 0, mid_width - mid_part)
        mid_eighth = lax.dynamic_slice_in_dim(mid_rows, mid_start, mid_part, 2)
        down_quarter = quarter_of(w_down)
        small_all = gated(small_all)

        rows_z = width // fs
        conds = jnp.stack(
            [lax.dynamic_slice_in_dim(each[0], z * rows_z, rows_z, 0) for each in small_all]
        )
        partial = jnp.dot(conds, w_ada, preferred_element_type=f32)
        partials = [partial[0]] + [ring_send(partial[k], fs - k) for k in range(1, fs)]
        qkv_helds += ring_on(qkv_helds[-1], fs - 3)
        tokens_wide = tokens[0].astype(f32)
        norm_one, rate_one = norm_parts(tokens_wide)
        small_all, partials, qkv_helds, raw_near, norm_one, rate_one = gated(
            (small_all, partials, qkv_helds, raw_near, norm_one, rate_one)
        )

        biases = ring_sorted(small_all, z).astype(f32)
        bias_ada, bias_qv, bias_out, bias_up, bias_down = [
            biases[:, i + 1, : each.shape[0]].reshape(-1)
            for i, each in enumerate((b_ada, b_qv, b_out, b_up, b_down))
        ]
        modulation = sum(partials[1:], partials[0] + bias_ada)
        shift_one, scale_one, gate_one, shift_two, scale_two, gate_two = [
            modulation[i * width : (i + 1) * width][None, :] for i in range(6)
        ]
        live = grid_sizes[0, 0] * grid_sizes[0, 1]
        head = jnp.concatenate(
            [shift_one, scale_one, gate_two, jnp.broadcast_to(live.astype(f32), (1, width))]
        )
        heads_got = [box_send(head, bits) for bits in (2, 4, 6)]
        raw_far = chip_far(raw_near)
        qkv_helds += ring_on(qkv_helds[-1], 1)
        live_rows = (lax.broadcasted_iota(jnp.int32, (slots, 1), 0) < live).astype(f32)
        live_keys = lax.broadcasted_iota(jnp.int32, (1, 1, slots), 2) < live
        normed = (norm_one * (1.0 + scale_one) + shift_one).astype(bf16)
        upstream = live_rows * cotangent[0].astype(f32)
        d_mlp = (gate_two * upstream).astype(bf16)
        heads_got, raw_far, qkv_helds, normed, d_mlp = gated(
            (heads_got, raw_far, qkv_helds, normed, d_mlp)
        )

        qkv_mine = jnp.stack(qkv_helds)
        qkv_other = side_send(qkv_mine)
        qkv_mine_got = box_send(qkv_mine, 1)
        mid_helds = ring_on(after(mid_eighth, qkv_mine), fs - 2)

        def head_of(raw_rows, first, got):
            shift, scale, gate_last = got[0:1], got[1:2], got[2:3]
            rows = lax.broadcasted_iota(jnp.int32, (raw_rows.shape[0], 1), 0) + first
            normal = norm_parts(raw_rows[:, :width].astype(f32))[0]
            alive = (rows < got[3, 0].astype(jnp.int32)).astype(f32)
            upstream_rows = alive * raw_rows[:, width:].astype(f32)
            return (
                (normal * (1.0 + scale) + shift).astype(bf16),
                (gate_last * upstream_rows).astype(bf16),
            )

        half = slots // 2
        normed_box, d_mlp_box = [normed], [d_mlp]
        for raw_rows, first, got in zip(
            raw_near + raw_far, (0, 0, 0, half), heads_got + heads_got[2:]
        ):
            one, two = head_of(raw_rows, first, got)
            normed_box.append(one)
            d_mlp_box.append(two)
        normed, qkv_mine, qkv_other, qkv_mine_got, mid_helds, normed_box, d_mlp_box = gated(
            (normed, qkv_mine, qkv_other, qkv_mine_got, mid_helds, normed_box, d_mlp_box)
        )

        def in_order(array):
            return [(array, k) for k in range(last)]

        qkv_other_got = box_send(qkv_other, 1)
        mid_helds += ring_on(mid_helds[-1], 1)
        mid_mine = jnp.concatenate(mid_helds)
        mid_near = chip_near(mid_mine)
        down_helds = ring_on(after(down_quarter, mid_mine), 1)
        (qkv_full,) = assemble(
            where,
            [w_qkv],
            [in_order(each) for each in (qkv_mine, qkv_other, qkv_mine_got, qkv_other_got)],
        )
        projected = jnp.dot(normed, qkv_full, preferred_element_type=f32)
        queries = (projected[:, :width] + bias_qv[:width]).astype(bf16)
        key_part = projected[:, width : 2 * width].astype(bf16)
        values = (projected[:, 2 * width :] + bias_qv[width:]).astype(bf16)
        queries = queries.reshape(slots, heads, HEAD_DIM)
        key_part = key_part.reshape(slots, heads, HEAD_DIM)
        values = values.reshape(slots, heads, HEAD_DIM)
        scores = jnp.einsum("qhe,khe->hqk", queries, key_part, preferred_element_type=f32)
        scores = jnp.where(live_keys, scores * HEAD_DIM ** (-0.5), masked_value)
        highest = jnp.max(scores, axis=-1, keepdims=True)
        lse = highest + jnp.log(jnp.sum(jnp.exp(scores - highest), axis=-1, keepdims=True))
        probs = jnp.exp(scores - lse)
        probs_low = probs.astype(bf16)
        attended = jnp.einsum("hqk,khe->qhe", probs_low, values, preferred_element_type=f32)
        attended = attended.reshape(slots, width).astype(bf16)
        attended, mid_mine, mid_near, down_helds = gated(
            (attended, mid_mine, mid_near, down_helds)
        )

        mid_far = chip_far(mid_near)
        mid_got = [box_send(each, 1) for each in (mid_mine, *mid_near)]
        down_helds += ring_on(down_helds[-1], 1)
        attended, mid_far, mid_got, down_helds = gated((attended, mid_far, mid_got, down_helds))

        mid_got += [box_send(each, 1) for each in mid_far]
        down_others = [side_send(each) for each in down_helds]
        down_helds += ring_on(down_helds[-1], fs - 3)
        attended_near = chip_near(attended)
        attended_far = chip_far(attended_near)
        out_full, up_full = assemble_wide(
            where_wide, [w_out, w_up], (mid_mine, *mid_near, *mid_far), mid_got
        )
        attn_out = jnp.dot(attended, out_full, preferred_element_type=f32) + bias_out
        middle = tokens_wide + gate_one * attn_out
        norm_two, rate_two = norm_parts(middle)
        normed_two = (norm_two * (1.0 + scale_two) + shift_two).astype(bf16)
        pre_act = jnp.dot(normed_two, up_full, preferred_element_type=f32) + bias_up
        activated = gelu_tanh(pre_act).astype(bf16)
        act_blocks = activated.T.reshape(fs, BOX // 2, 2 * hidden // fs // BOX, slots)
        act_blocks = act_blocks.transpose(1, 0, 2, 3).reshape(BOX // 2, -1, slots)
        down_helds, down_others, attended_far, act_blocks, normed_two = gated(
            (down_helds, down_others, attended_far, act_blocks, normed_two)
        )
        attended_box = [attended, *attended_near, *attended_far]

        down_others.append(side_send(down_helds[-1]))
        down_mine = jnp.stack(down_helds)
        down_mine_got = box_send(down_mine, 1)
        down_early = jnp.stack(down_others[:-1])
        down_early_got = box_send(down_early, 1)
        down_others, down_mine, down_mine_got, down_early_got, act_blocks = gated(
            (down_others, down_mine, down_mine_got, down_early_got, act_blocks)
        )

        down_last_got = box_send(down_others[-1], 1)
        act_box = chip_exchange(act_blocks, chip)
        (down_full,) = assemble(
            where,
            [w_down],
            [
                in_order(down_mine),
                [(each, None) for each in down_others],
                in_order(down_mine_got),
                [(down_early_got, k) for k in range(last - 1)] + [(down_last_got, None)],
            ],
        )
        d_act = lax.dot_general(
            d_mlp, down_full, (((1,), (1,)), ((), ())), preferred_element_type=f32
        )
        unused_gelu, gelu_pull = jax.vjp(gelu_tanh, pre_act)
        d_pre = gelu_pull(d_act)[0].astype(bf16)

        def column_blocks(grad_t):
            n = grad_t.shape[0] // dp
            blocks = grad_t.reshape(groups, BOX, n, slots).transpose(1, 0, 2, 3)
            return blocks.reshape(BOX // 2, 2 * groups * n, slots)

        d_pre_blocks = column_blocks(d_pre.T)
        d_pre, d_pre_blocks, act_box, normed_two = gated(
            (d_pre, d_pre_blocks, act_box, normed_two)
        )

        d_pre_box = chip_exchange(d_pre_blocks, chip)
        normed_two_near = chip_near(normed_two)
        keep_down, send_down = row_grad(where_core, act_box, d_mlp_box)
        got_down = box_send(send_down, 1)
        d_normed_two = lax.dot_general(
            d_pre, up_full, (((1,), (1,)), ((), ())), preferred_element_type=f32
        )
        d_shift_two = jnp.sum(d_normed_two, axis=0)
        d_scale_two = jnp.sum(d_normed_two * norm_two, axis=0)
        d_middle = upstream + norm_back(norm_two, rate_two, d_normed_two * (1.0 + scale_two))
        d_gate_one = jnp.sum(d_middle * attn_out, axis=0)
        d_attn = (gate_one * d_middle).astype(bf16)
        d_attn_blocks = column_blocks(d_attn.T)
        d_attended = lax.dot_general(
            d_attn, out_full, (((1,), (1,)), ((), ())), preferred_element_type=f32
        )
        d_attended = d_attended.astype(bf16).reshape(slots, heads, HEAD_DIM)
        d_probs = jnp.einsum("qhe,khe->hqk", d_attended, values, preferred_element_type=f32)
        d_values = jnp.einsum(
            "hqk,qhe->khe", probs_low, d_attended, preferred_element_type=f32
        ).astype(bf16)
        row_inner = jnp.sum(probs * d_probs, axis=-1, keepdims=True)
        d_scores = (probs * (d_probs - row_inner)).astype(bf16)
        d_queries = (
            jnp.einsum("hqk,khe->qhe", d_scores, key_part, preferred_element_type=f32)
            * HEAD_DIM ** (-0.5)
        ).astype(bf16)
        d_keys = (
            jnp.einsum("hqk,qhe->khe", d_scores, queries, preferred_element_type=f32)
            * HEAD_DIM ** (-0.5)
        ).astype(bf16)
        d_projected = jnp.concatenate(
            [
                d_queries.reshape(slots, width),
                d_keys.reshape(slots, width),
                d_values.reshape(slots, width),
            ],
            axis=1,
        )
        d_projected_blocks = column_blocks(d_projected.T)
        (
            d_projected,
            d_projected_blocks,
            d_attn_blocks,
            d_pre_box,
            normed_two_near,
            keep_down,
            got_down,
            activated,
        ) = gated(
            (
                d_projected,
                d_projected_blocks,
                d_attn_blocks,
                d_pre_box,
                normed_two_near,
                keep_down,
                got_down,
                activated,
            )
        )

        d_projected_box = chip_exchange(d_projected_blocks, chip)
        normed_two_far = chip_far(normed_two_near)
        normed_two_box = [normed_two, *normed_two_near, *normed_two_far]
        d_attn_box = chip_exchange(d_attn_blocks, chip)
        d_normed = lax.dot_general(
            d_projected, qkv_full, (((1,), (1,)), ((), ())), preferred_element_type=f32
        )
        d_shift_one = jnp.sum(d_normed, axis=0)
        d_scale_one = jnp.sum(d_normed * norm_one, axis=0)
        grad_tokens = d_middle + norm_back(norm_one, rate_one, d_normed * (1.0 + scale_one))
        mlp_out = jnp.dot(activated, down_full, preferred_element_type=f32) + bias_down
        output = (live_rows * (middle + gate_two * mlp_out)).astype(bf16)
        d_gate_two = jnp.sum(upstream * mlp_out, axis=0)

        def weight_grad(lefts, rights):
            keep, send = column_grad(where_core, lefts, rights)
            grad, *sends = split_grad(where[:1], keep, box_send(send, 1))
            for k, sent in enumerate(sends):
                grad = grad + ring_send(sent, k + 1).astype(f32)
            rows, cols = grad.shape
            grad = grad.reshape(rows, groups, cols // groups)
            return group_sum(grad.transpose(1, 0, 2), group)

        grad_down = ring_sum(keep_down + got_down, z)
        down_rows = grad_down.shape[0]
        grad_down = grad_down.reshape(down_rows, groups, width // groups)
        grad_down = group_sum(grad_down.transpose(1, 0, 2), group)
        down_blocks = grad_down.reshape(down_rows, BOX, width // dp).transpose(1, 0, 2)
        if groups == 1:
            parts = lax.all_to_all(down_blocks, "dp", 0, 0, tiled=True)
        else:
            parts = [pick(down_blocks, place)] + [
                box_send(pick(down_blocks, place ^ k), k) for k in range(1, BOX)
            ]
            parts = jnp.stack(parts)
            parts = jnp.stack([pick(parts, place ^ k) for k in range(BOX)])
        grad_w_down = parts.reshape(BOX * down_rows, width // dp)
        grad_w_up = weight_grad(normed_two_box, d_pre_box)
        grad_w_out = weight_grad(attended_box, d_attn_box)
        grad_w_qkv = weight_grad(normed_box, d_projected_box)

        def row_sum(array):
            return jnp.sum(array.astype(f32), axis=0)

        d_mod = [d_shift_one, d_scale_one, d_gate_one, d_shift_two, d_scale_two, d_gate_two]
        images = jnp.stack(d_mod + [cond_act.astype(f32), cond_act.astype(f32)]).astype(bf16)
        total = [
            row_sum(d_projected[:, :width]),
            row_sum(d_projected[:, 2 * width :]),
            row_sum(d_attn),
            row_sum(d_mlp),
            row_sum(d_pre),
        ]
        total = jnp.concatenate([each.reshape(-1, width) for each in total])
        images_near = jnp.stack(ring_gather(images))
        totals = ring_gather(total)
        total = sum(totals[1:], totals[0])
        images = images_near
        for bits in (1, 2, 4):
            images = jnp.concatenate([images, box_send(images, bits)])
            total = total + box_send(total, bits)
        images_box, total_box = images, total
        for k in range(1, groups):
            images = jnp.concatenate([images, group_send(images_box, k)])
            total = total + group_send(total_box, k)
        conds_all = lax.dynamic_slice_in_dim(images[:, 6], z * rows_z, rows_z, 1)
        d_mod_all = images[:, :6]
        ada_cols = 6 * width // dp
        grad_w_ada = lax.dot_general(
            conds_all,
            lax.dynamic_slice_in_dim(
                d_mod_all.reshape(dp * fs, 6 * width), rank * ada_cols, ada_cols, 1
            ),
            (((0,), (0,)), ((), ())),
            preferred_element_type=f32,
        )
        d_conds = lax.dot_general(
            images_near[:, :6].reshape(fs, 6 * width),
            w_ada,
            (((1,), (1,)), ((), ())),
            preferred_element_type=f32,
        )
        cond_parts = [d_conds[0]] + [ring_send(d_conds[k], fs - k) for k in range(1, fs)]
        twice = jnp.stack(cond_parts + cond_parts)
        d_cond_act = lax.dynamic_slice_in_dim(twice, lax.rem(fs - z, fs), fs, 0).reshape(-1)
        grad_condition = d_cond_act * gate * (1.0 + cond_wide * (1.0 - gate))

        def shard_of(rows):
            return pick(rows.reshape(fs, -1), z)

        grads_bias = [
            shard_of(jnp.sum(d_mod_all.astype(f32), axis=0)),
            shard_of(total[:2]),
            shard_of(total[2]),
            shard_of(total[4:]),
            shard_of(total[3]),
        ]
        return (
            output[None],
            grad_tokens.astype(bf16)[None],
            grad_condition[None],
            grad_w_ada,
            grad_w_qkv,
            grad_w_out,
            grad_w_up,
            grad_w_down,
            *grads_bias,
        )

    return body


def solution(mesh):
    return jax.shard_map(
        make_body(mesh.shape["dp"], mesh.shape["fsdp"]),
        mesh=mesh,
        in_specs=(
            P(("dp", "fsdp"), None, None),
            P(("dp", "fsdp"), None),
            P(("dp", "fsdp"), None),
            P("fsdp", None),
            P("fsdp", None),
            P("fsdp", None),
            P("fsdp", None),
            P("fsdp", None),
            P("fsdp"),
            P("fsdp"),
            P("fsdp"),
            P("fsdp"),
            P("fsdp"),
            P(("dp", "fsdp"), None, None),
        ),
        out_specs=(
            P(("dp", "fsdp"), None, None),
            P(("dp", "fsdp"), None, None),
            P(("dp", "fsdp"), None),
            P("fsdp", "dp"),
            P("fsdp", "dp"),
            P("fsdp", "dp"),
            P("fsdp", "dp"),
            P("fsdp", "dp"),
            P("fsdp"),
            P("fsdp"),
            P("fsdp"),
            P("fsdp"),
            P("fsdp"),
        ),
        check_vma=False,
    )
```

time: 1610 us -> 586 us (0.36)
  Pallas kernels: 971 us -> 48.9 us
  waiting for transfers between devices: 252 us -> 154 us
  matrix products: 90.7 us -> 61.4 us
  other arithmetic: 26 us -> 53.6 us
  starting transfers between devices: 157 us -> 133 us
    pallas_call x3 -> x2, Pallas kernels: 971 us -> 10.7 us  [assemble(): pl.pallas_call(kernel, out_shape=[jax.ShapeDtypeStruct((fs, 4, lead, 8, e...]
    ppermute x85 -> x51, waiting for transfers between devices: 148 us -> 49.9 us  [box_send(): return lax.ppermute(x, 'dp', [(i, i ^ bits) for i in range(dp)])]
    pallas_call x0 -> x8, Pallas kernels: none -> 38.2 us  [the longest x3 16.1 us: column_grad(): pl.pallas_call(kernel, out_shape=[jax.ShapeDtypeStruct((n, width), f32)]...]
    ppermute x85 -> x51, starting transfers between devices: 96.4 us -> 60.9 us  [box_send(): return lax.ppermute(x, 'dp', [(i, i ^ bits) for i in range(dp)])]
    concatenate x27 -> x5, local copies, waits for them, and re-layouts: 25.8 us -> 4.44 us  [the longest x2 3.52 us: body(): images = jnp.concatenate([images, box_send(images, bits)])]
    dot_general x6 -> x2, matrix products: 21.6 us -> 2.43 us  [the longest x1 1.32 us: body(): lax.dot_general(conds_all, lax.dynamic_slice_in_dim(d_mod_all.reshape(dp...]
    unnamed x270 -> x281, local copies, waits for them, and re-layouts: 28.6 us -> 47.4 us
    ppermute x42 -> x36, waiting for transfers between devices: 105 us -> 94.6 us  [ring_send(): return lax.ppermute(x, 'fsdp', [(i, (i + hops) % fs) for i in range(fs)])]
  transfers between devices with their start and end apart: 127 -> 92, of which waited for: 36 -> 24; matrix products, arithmetic and copies ran while one was open for 8% -> 32% of each run, Pallas kernels for 40% -> 9%
where the time goes in v2:
time: 586 us; the launch traced here: 575 us
  waiting for transfers between devices  154 us (26%)
  starting transfers between devices  133 us (23%)
  local copies, waits for them, and re-layouts  117 us (20%)
  matrix products  61.4 us (10%)
  other arithmetic  53.6 us (9%)
  Pallas kernels  48.9 us (8%)
  between operations  6.12 us (1%)
    ppermute x36, waiting for transfers between devices, ring_send(): return lax.ppermute(x, 'fsdp', [(i, (i + hops) % fs) for i in range(fs)])  94.6 us
    ppermute x36, starting transfers between devices, ring_send(): return lax.ppermute(x, 'fsdp', [(i, (i + hops) % fs) for i in range(fs)])  65.6 us
    ppermute x51, starting transfers between devices, box_send(): return lax.ppermute(x, 'dp', [(i, i ^ bits) for i in range(dp)])  60.9 us
    ppermute x51, waiting for transfers between devices, box_send(): return lax.ppermute(x, 'dp', [(i, i ^ bits) for i in range(dp)])  49.9 us
    unnamed x281, local copies, waits for them, and re-layouts  47.4 us
    pallas_call x3, Pallas kernels, column_grad(): pl.pallas_call(kernel, out_shape=[jax.ShapeDtypeStruct((n, width), f32)]...  16.1 us
    squeeze x8, local copies, waits for them, and re-layouts, pick(): return lax.dynamic_index_in_dim(array, index, axis, keepdims=False)  14.6 us
    dot_general x1, matrix products, body(): lax.dot_general(d_mlp, down_full, (((1,), (1,)), ((), ())), preferred_ele...  11.9 us
  transfers between devices with their start and end apart: 92, of which 24 were waited for; matrix products, arithmetic and copies ran while one was open for 32% of the time, Pallas kernels for 9%

profile of v2, /device:TPU:25, one launch (start us, length us, event | category | flops | bytes accessed | tf_op | source)
XLA Modules:
  0.0 574.5 jit_solution(11240178401236016610)
XLA Ops:
  16.7 3.1 collective-permute-start.6
  21.0 7.8 %collective-permute-done.6 = bf16[9,8,3456]{2,1,0:T(8,128)(2,1)S(1)} collective-permute-done((bf16[9,8,3456]{2,1,0:T(8,128)(2,1)}, bf16[9,8,3456]{2,1,0:T(8,128)(2,1)S(1)}, u32[]{:S(2)}, u32[]{:S(2)}) %collective-permute-start.6) | collective-permute-done | bytes 497696 | tf_op jit(solution)/shard_map/ppermute | solution.py:63
  28.8 3.9 collective-permute-start.7
  32.7 2.8 fusion.70
  38.2 3.4 collective-permute-done.3
  41.7 3.9 collective-permute-start.5
  55.9 3.5 collective-permute-start.15
  61.8 3.5 collective-permute-done.12
  71.5 4.4 collective-permute-start.17
  83.6 3.6 collective-permute-start.18
  91.5 4.9 collective-permute-done.18
  96.5 3.9 collective-permute-start.19
  101.5 7.2 %collective-permute-done.19 = bf16[9,8,2944]{2,1,0:T(8,128)(2,1)S(1)} collective-permute-done((bf16[9,8,2944]{2,1,0:T(8,128)(2,1)S(1)}, bf16[9,8,2944]{2,1,0:T(8,128)(2,1)S(1)}, u32[]{:S(2)}, u32[]{:S(2)}) %collective-permute-start.19) | collective-permute-done | bytes 423968 | tf_op jit(solution)/shard_map/ppermute | solution.py:63
  114.6 4.0 collective-permute-start.21
  122.2 5.9 %collective-permute-done.21 = bf16[9,8,2944]{2,1,0:T(8,128)(2,1)S(1)} collective-permute-done((bf16[9,8,2944]{2,1,0:T(8,128)(2,1)}, bf16[9,8,2944]{2,1,0:T(8,128)(2,1)S(1)}, u32[]{:S(2)}, u32[]{:S(2)}) %collective-permute-start.21) | collective-permute-done | bytes 423968 | tf_op jit(solution)/shard_map/ppermute | solution.py:63
  130.4 4.1 collective-permute-start.24
  134.5 6.1 %shard_map.237 = bf16[4,4,9,8,3456]{4,3,2,1,0:T(8,128)(2,1)S(1)} custom-call(s32[8]{0:T(128)S(1)} %stack.228.where_ref, bf16[4,9,8,3456]{3,2,1,0:T(8,128)(2,1)S(1)} %bitcast.243, bf16[3,9,8,3456]{3,2,1,0:T(8,128)(2,1)S(1)} %pad_maximum_fusion.2.refs_1_, bf16[3,9,8,3456]{3,2,1,0:T(8,128)(2,1)} %collective-permute-done.16.refs_2_, ...), custom_call_target="tpu_custom_call" | custom-call | bytes 15925248 | tf_op jit(solution)/shard_map/pallas_call | solution.py:148
  140.6 2.5 fusion.88
  149.0 4.3 convolution_convert_fusion.2
  153.3 4.6 collective-permute-done.22.refs_3_
  163.1 3.9 collective-permute-start.30
  168.1 5.3 collective-permute-done.25.refs_5_
  173.7 13.2 %collective-permute-done.26.refs_6_ = bf16[14,8,2944]{2,1,0:T(8,128)(2,1)} collective-permute-done((bf16[14,8,2944]{2,1,0:T(8,128)(2,1)S(1)}, bf16[14,8,2944]{2,1,0:T(8,128)(2,1)}, u32[]{:S(2)}, u32[]{:S(2)}) %collective-permute-start.26) | collective-permute-done | bytes 659488 | tf_op jit(solution)/shard_map/ppermute | solution.py:57
  190.2 3.8 collective-permute-start.32
  198.7 4.4 collective-permute-start.33
  203.1 6.7 %collective-permute-done.36.x1 = bf16[256,1152]{1,0:T(8,128)(2,1)} collective-permute-done((bf16[256,1152]{1,0:T(8,128)(2,1)}, bf16[256,1152]{1,0:T(8,128)(2,1)}, u32[]{:S(2)}, u32[]{:S(2)}) %collective-permute-start.36) | collective-permute-done | bytes 589856 | tf_op jit(solution)/shard_map/ppermute | solution.py:57
  221.3 5.8 %shard_map.238 = (bf16[4,4,9,8,1152]{4,3,2,1,0:T(8,128)(2,1)S(1)}, bf16[4,4,9,8,4608]{4,3,2,1,0:T(8,128)(2,1)S(1)}) custom-call(s32[9]{0:T(128)S(1)} %stack.234.where_ref, bf16[4,9,8,1152]{3,2,1,0:T(8,128)(2,1)S(1)} %bitcast.248, bf16[4,9,8,4608]{3,2,1,0:T(8,128)(2,1)S(1)} %bitcast.241, bf16[27,8,2944]{2,1,0:T(8,128)(2,1)} %constant_dynamic-update-slice_fusion.8.refs_2_, ...), custom_call_target="tpu_custom_call" | custom-call | bytes 26542080 | tf_op jit(solution)/shard_map/pallas_call | solution.py:252
  227.2 2.7 fusion.86
  231.8 6.0 %multiply_convert_fusion.1 = (bf16[4608,256]{0,1:T(8,128)(2,1)}, f32[256,4608]{1,0:T(8,128)}) fusion(f32[4608]{0:T(1024)S(1)} %add.490, bf16[256,1152]{1,0:T(8,128)(2,1)S(1)} %add_convert_fusion.1.x0, bf16[1152,4608]{1,0:T(8,128)(2,1)S(1)} %bitcast.249), kind=kOutput, calls=%fused_computation.32 | convolution fusion | flops 2729705472 | bytes 18302976 | tf_op jit(solution)/shard_map/dot_general | solution.py:588
  237.8 2.8 copy.105
  243.8 2.9 collective-permute-start.41
  248.3 9.9 %collective-permute-done.40.refs_4_ = bf16[36,8,1152]{2,1,0:T(8,128)(2,1)} collective-permute-done((bf16[36,8,1152]{2,1,0:T(8,128)(2,1)}, bf16[36,8,1152]{2,1,0:T(8,128)(2,1)}, u32[]{:S(2)}, u32[]{:S(2)}) %collective-permute-start.40) | collective-permute-done | bytes 663584 | tf_op jit(solution)/shard_map/ppermute | solution.py:60
  263.2 3.2 dynamic-slice_bitcast_fusion.6
  270.4 4.6 shard_map.239
  275.1 11.9 %multiply_convert_fusion = (bf16[256,4608]{1,0:T(8,128)(2,1)}, bf16[256,4608]{1,0:T(8,128)(2,1)}, f32[256,4608]{1,0:T(8,128)}) fusion(f32[256,4608]{1,0:T(8,128)} %get-tuple-element.407, bf16[256,1152]{1,0:T(8,128)(2,1)S(1)} %copy-done.9, bf16[4608,1152]{1,0:T(8,128)(2,1)S(1)} %bitcast.232), kind=kOutput, calls=%fused_computation.31 | convolution fusion | flops 2748579840 | bytes 25362432 | tf_op jit(solution)/shard_map/dot_general | solution.py:618
  287.0 6.5 %fusion.3 = bf16[4608,256]{0,1:T(8,128)(2,1)} fusion(f32[256,4608]{1,0:T(8,128)} %get-tuple-element.408, f32[256,4608]{1,0:T(8,128)S(1)} %bitcast.262), kind=kLoop, calls=%fused_computation.12 | loop fusion | flops 28311552 | bytes 11796480 | tf_op jit(solution)/shard_map/convert_element_type | solution.py:622
  293.5 4.3 reshape_transpose_reshape.9
  300.2 7.0 %shard_map.240 = (f32[4,144,1152]{2,1,0:T(8,128)S(1)}, f32[4,144,1152]{2,1,0:T(8,128)}) custom-call(s32[1]{0:T(128)} %bitcast.36.where_ref, bf16[1152,256]{1,0:T(8,128)(2,1)S(1)} %copy-done.37, bf16[1152,256]{1,0:T(8,128)(2,1)} %collective-permute-done.44.x1, bf16[1152,256]{1,0:T(8,128)(2,1)} %collective-permute-done.45.x2, ...), custom_call_target="tpu_custom_call" | custom-call | flops 2717908992 | bytes 10027008 | tf_op jit(solution)/shard_map/pallas_call | solution.py:381
  310.1 8.0 %multiply_reduce_fusion.2 = (bf16[1152]{0:T(1024)(128)(2,1)}, f32[256]{0:T(256)S(1)}, f32[256]{0:T(256)S(1)}, bf16[1152]{0:T(1024)(128)(2,1)}, f32[256,1152]{1,0:T(8,128)S(1)}) fusion(f32[256,1152]{1,0:T(8,128)S(1)} %copy-done.59, f32[256]{0:T(256)S(1)} %add_rsqrt_fusion, f32[256]{0:T(256)S(1)} %broadcast_multiply_fusion.4, ...), kind=kOutput, calls=%fused_computation.88 | convolution fusion | flops 2720560640 | bytes 15348736 | tf_op jit(solution)/shard_map/dot_general | solution.py:638
  323.3 3.5 copy.112
  326.9 3.1 dynamic-slice_bitcast_fusion.2
  331.5 2.8 multiply_reduce_fusion
  340.5 4.3 collective-permute-done.47.y1
  350.2 9.8 %collective-permute-done.49.y3 = bf16[1152,256]{1,0:T(8,128)(2,1)S(1)} collective-permute-done((bf16[1152,256]{1,0:T(8,128)(2,1)}, bf16[1152,256]{1,0:T(8,128)(2,1)S(1)}, u32[]{:S(2)}, u32[]{:S(2)}) %collective-permute-start.49) | collective-permute-done | bytes 589856 | tf_op jit(solution)/shard_map/ppermute | solution.py:57
  361.3 4.2 collective-permute-start.85
  365.5 6.8 %multiply_reduce_fusion.4 = (bf16[1152]{0:T(1024)(128)(2,1)S(1)}, f32[256]{0:T(256)S(1)}, f32[256]{0:T(256)S(1)}, bf16[1152]{0:T(1024)(128)(2,1)S(1)}, f32[256,1152]{1,0:T(8,128)S(1)}) fusion(f32[256,1152]{1,0:T(8,128)} %fusion.22, f32[1152]{0:T(1024)S(1)} %copy-done.100, bf16[256,3456]{0,1:T(8,128)(2,1)} %copy-done.64, bf16[1152,3456]{1,0:T(8,128)(2,1)} %bitcast.237), kind=kOutput, calls=%fused_computation.90 | convolution fusion | flops 2040493312 | bytes 12102656 | tf_op jit(solution)/shard_map/dot_general | solution.py:700
  374.8 4.2 multiply_reduce_fusion.1
  383.6 2.7 dynamic-slice_bitcast_fusion.11
  396.7 3.3 collective-permute-start.57
  410.4 9.0 %collective-permute-start.59 = (bf16[4,8,1152]{2,1,0:T(8,128)(2,1)S(1)}, bf16[4,8,1152]{2,1,0:T(8,128)(2,1)}, u32[]{:S(2)}, u32[]{:S(2)}) collective-permute-start(bf16[4,8,1152]{2,1,0:T(8,128)(2,1)S(1)} %pad_maximum_fusion.5), channel_id=1, source_target_pairs={{0,4},{4,0},{8,12},{12,8},{16,20},{20,16},{24,28},{28,24},{1,5},{5... | collective-permute-start | bytes 221192 | tf_op jit(solution)/shard_map/ppermute | solution.py:57
  425.7 7.0 %shard_map.245 = (f32[576,1152]{1,0:T(8,128)S(1)}, f32[576,1152]{1,0:T(8,128)}) custom-call(s32[1]{0:T(128)} %bitcast.36.where_ref, bf16[256,1152]{1,0:T(8,128)(2,1)S(1)} %copy-done.31, bf16[256,1152]{1,0:T(8,128)(2,1)} %collective-permute-done.50.x1, bf16[256,1152]{1,0:T(8,128)(2,1)} %collective-permute-done.51.x2, bf16[128,1152]{1,0:T(8,128)(2,1)S(1)} %copy-done.53, ...), custom_call_target="tpu_custom_call" | custom-call | flops 2717908992 | bytes 10027008 | tf_op jit(solution)/shard_map/pallas_call | solution.py:303
  433.3 5.3 shard_map.241
  447.4 2.8 collective-permute-start.82
  451.1 3.8 shard_map.243
  462.4 4.8 collective-permute-start.72
  467.2 13.2 %collective-permute-done.83 = bf16[144,1152]{1,0:T(8,128)(2,1)} collective-permute-done((bf16[144,1152]{1,0:T(8,128)(2,1)}, bf16[144,1152]{1,0:T(8,128)(2,1)}, u32[]{:S(2)}, u32[]{:S(2)}) %collective-permute-start.83) | collective-permute-done | bytes 331808 | tf_op jit(solution)/shard_map/ppermute | solution.py:63
  483.7 2.9 reshape.458
  486.6 2.7 copy.132
  489.3 4.9 all-to-all-start
  498.5 3.2 shard_map.242
  511.4 3.8 shard_map.246
  517.0 18.2 %collective-permute-done.74 = bf16[288,144]{1,0:T(8,128)(2,1)} collective-permute-done((bf16[288,144]{1,0:T(8,128)(2,1)}, bf16[288,144]{1,0:T(8,128)(2,1)}, u32[]{:S(2)}, u32[]{:S(2)}) %collective-permute-start.74) | collective-permute-done | bytes 82976 | tf_op jit(solution)/shard_map/ppermute | solution.py:63
  543.6 6.3 %collective-permute-done.79 = bf16[288,576]{1,0:T(8,128)(2,1)S(1)} collective-permute-done((bf16[288,576]{1,0:T(8,128)(2,1)}, bf16[288,576]{1,0:T(8,128)(2,1)S(1)}, u32[]{:S(2)}, u32[]{:S(2)}) %collective-permute-start.79) | collective-permute-done | bytes 331808 | tf_op jit(solution)/shard_map/ppermute | solution.py:63
  549.8 23.2 %collective-permute-done.80 = bf16[288,576]{1,0:T(8,128)(2,1)S(1)} collective-permute-done((bf16[288,576]{1,0:T(8,128)(2,1)}, bf16[288,576]{1,0:T(8,128)(2,1)S(1)}, u32[]{:S(2)}, u32[]{:S(2)}) %collective-permute-start.80) | collective-permute-done | bytes 331808 | tf_op jit(solution)/shard_map/ppermute | solution.py:63
  (620 shorter events, 212.2 us)
Async XLA Ops:
  5.7 15.0 %collective-permute-start.1 = (bf16[6,1728]{1,0:T(8,128)(2,1)S(1)}, bf16[6,1728]{1,0:T(8,128)(2,1)S(1)}, u32[]{:S(2)}, u32[]{:S(2)}) collective-permute-start(bf16[6,1728]{1,0:T(8,128)(2,1)S(1)} %stack.209), channel_id=1, source_target_pairs={{0,2},{1,3},{2,0},{3,1},{4,6},{5,7},{6,4},{7,5},{8,10},{9,11},{10,... | collective-permute-start | bytes 62216 | tf_op jit(solution)/shard_map/ppermute | solution.py:63
  7.0 13.7 %collective-permute-start.2 = (bf16[6,1728]{1,0:T(8,128)(2,1)S(1)}, bf16[6,1728]{1,0:T(8,128)(2,1)S(1)}, u32[]{:S(2)}, u32[]{:S(2)}) collective-permute-start(bf16[6,1728]{1,0:T(8,128)(2,1)S(1)} %stack.209), channel_id=1, source_target_pairs={{0,3},{1,0},{2,1},{3,2},{4,7},{5,4},{6,5},{7,6},{8,11},{9,8},{10,9... | collective-permute-start | bytes 62216 | tf_op jit(solution)/shard_map/ppermute | solution.py:63
  9.6 37.0 %collective-permute-start.8 = (bf16[256,2304]{1,0:T(8,128)(2,1)}, bf16[256,2304]{1,0:T(8,128)(2,1)}, u32[]{:S(2)}, u32[]{:S(2)}) collective-permute-start(bf16[256,2304]{1,0:T(8,128)(2,1)} %pad_maximum_fusion.4), channel_id=1, source_target_pairs={{0,8},{4,12},{8,0},{12,4},{16,24},{20,28},{24,16},{28,20},{1,9},{5... | collective-permute-start | bytes 3538952 | tf_op jit(solution)/shard_map/ppermute | solution.py:57
  10.8 35.8 %collective-permute-start.9 = (bf16[256,2304]{1,0:T(8,128)(2,1)}, bf16[256,2304]{1,0:T(8,128)(2,1)}, u32[]{:S(2)}, u32[]{:S(2)}) collective-permute-start(bf16[256,2304]{1,0:T(8,128)(2,1)} %pad_maximum_fusion.4), channel_id=1, source_target_pairs={{0,16},{4,20},{8,24},{12,28},{16,0},{20,4},{24,8},{28,12},{1,17},{... | collective-permute-start | bytes 3538952 | tf_op jit(solution)/shard_map/ppermute | solution.py:57
  28.8 17.8 %collective-permute-start.7 = (bf16[9,8,3456]{2,1,0:T(8,128)(2,1)S(1)}, bf16[9,8,3456]{2,1,0:T(8,128)(2,1)}, u32[]{:S(2)}, u32[]{:S(2)}) collective-permute-start(bf16[9,8,3456]{2,1,0:T(8,128)(2,1)S(1)} %collective-permute-done.6), channel_id=1, source_target_pairs={{0,1},{1,2},{2,3},{3,0},{4,5},{5,6},{6,7},{7,4},{8,9},{9,10},{10,1... | collective-permute-start | bytes 1493000 | tf_op jit(solution)/shard_map/ppermute | solution.py:63
  48.3 13.2 %collective-permute-start.10 = (f32[4,1152]{1,0:T(4,128)S(1)}, f32[4,1152]{1,0:T(4,128)S(1)}, u32[]{:S(2)}, u32[]{:S(2)}) collective-permute-start(f32[4,1152]{1,0:T(4,128)S(1)} %maximum_maximum_fusion), channel_id=1, source_target_pairs={{0,8},{4,12},{8,0},{12,4},{16,24},{20,28},{24,16},{28,20},{1,9},{5... | collective-permute-start | bytes 55304 | tf_op jit(solution)/shard_map/ppermute | solution.py:57
  53.3 14.3 %collective-permute-start.13 = (bf16[128,2304]{1,0:T(8,128)(2,1)S(1)}, bf16[128,2304]{1,0:T(8,128)(2,1)S(1)}, u32[]{:S(2)}, u32[]{:S(2)}) collective-permute-start(bf16[128,2304]{1,0:T(8,128)(2,1)S(1)} %slice.223), channel_id=1, source_target_pairs={{0,16},{4,20},{8,24},{12,28},{16,0},{20,4},{24,8},{28,12},{1,17},{... | collective-permute-start | bytes 1769480 | tf_op jit(solution)/shard_map/ppermute | solution.py:57
  71.2 37.5 %collective-permute-start.16 = (bf16[3,9,8,3456]{3,2,1,0:T(8,128)(2,1)S(1)}, bf16[3,9,8,3456]{3,2,1,0:T(8,128)(2,1)}, u32[]{:S(2)}, u32[]{:S(2)}) collective-permute-start(bf16[3,9,8,3456]{3,2,1,0:T(8,128)(2,1)S(1)} %pad_maximum_fusion.2.refs_1_), channel_id=1, source_target_pairs={{0,8},{4,20},{8,0},{12,28},{16,24},{20,4},{24,16},{28,12},{1,9},{5... | collective-permute-start | bytes 4478984 | tf_op jit(solution)/shard_map/ppermute | solution.py:60
  71.5 37.2 %collective-permute-start.17 = (bf16[3,9,8,3456]{3,2,1,0:T(8,128)(2,1)S(1)}, bf16[3,9,8,3456]{3,2,1,0:T(8,128)(2,1)S(1)}, u32[]{:S(2)}, u32[]{:S(2)}) collective-permute-start(bf16[3,9,8,3456]{3,2,1,0:T(8,128)(2,1)S(1)} %pad_maximum_fusion.2.refs_1_), channel_id=1, source_target_pairs={{0,4},{4,0},{8,12},{12,8},{16,20},{20,16},{24,28},{28,24},{1,5},{5... | collective-permute-start | bytes 4478984 | tf_op jit(solution)/shard_map/ppermute | solution.py:57
  110.0 24.6 %collective-permute-start.20 = (bf16[3,9,8,3456]{3,2,1,0:T(8,128)(2,1)}, bf16[3,9,8,3456]{3,2,1,0:T(8,128)(2,1)}, u32[]{:S(2)}, u32[]{:S(2)}) collective-permute-start(bf16[3,9,8,3456]{3,2,1,0:T(8,128)(2,1)} %collective-permute-done.16.refs_2_), channel_id=1, source_target_pairs={{0,4},{4,0},{8,12},{12,8},{16,20},{20,16},{24,28},{28,24},{1,5},{5... | collective-permute-start | bytes 4478984 | tf_op jit(solution)/shard_map/ppermute | solution.py:57
  114.6 13.5 %collective-permute-start.21 = (bf16[9,8,2944]{2,1,0:T(8,128)(2,1)}, bf16[9,8,2944]{2,1,0:T(8,128)(2,1)S(1)}, u32[]{:S(2)}, u32[]{:S(2)}) collective-permute-start(bf16[9,8,2944]{2,1,0:T(8,128)(2,1)} %copy-done.93), channel_id=1, source_target_pairs={{0,1},{1,2},{2,3},{3,0},{4,5},{5,6},{6,7},{7,4},{8,9},{9,10},{10,1... | collective-permute-start | bytes 1271816 | tf_op jit(solution)/shard_map/ppermute | solution.py:63
  128.9 29.0 %collective-permute-start.22 = (bf16[27,8,2944]{2,1,0:T(8,128)(2,1)}, bf16[27,8,2944]{2,1,0:T(8,128)(2,1)}, u32[]{:S(2)}, u32[]{:S(2)}) collective-permute-start(bf16[27,8,2944]{2,1,0:T(8,128)(2,1)} %constant_dynamic-update-slice_fusion.8.refs_2_), channel_id=1, source_target_pairs={{0,8},{4,12},{8,0},{12,4},{16,24},{20,28},{24,16},{28,20},{1,9},{5... | collective-permute-start | bytes 3815432 | tf_op jit(solution)/shard_map/ppermute | solution.py:57
  130.1 28.7 %collective-permute-start.23 = (bf16[27,8,2944]{2,1,0:T(8,128)(2,1)}, bf16[27,8,2944]{2,1,0:T(8,128)(2,1)}, u32[]{:S(2)}, u32[]{:S(2)}) collective-permute-start(bf16[27,8,2944]{2,1,0:T(8,128)(2,1)} %constant_dynamic-update-slice_fusion.8.refs_2_), channel_id=1, source_target_pairs={{0,16},{4,20},{8,24},{12,28},{16,0},{20,4},{24,8},{28,12},{1,17},{... | collective-permute-start | bytes 3815432 | tf_op jit(solution)/shard_map/ppermute | solution.py:57
  130.4 22.9 %collective-permute-start.24 = (bf16[36,8,1152]{2,1,0:T(8,128)(2,1)}, bf16[36,8,1152]{2,1,0:T(8,128)(2,1)}, u32[]{:S(2)}, u32[]{:S(2)}) collective-permute-start(bf16[36,8,1152]{2,1,0:T(8,128)(2,1)} %dynamic-slice_bitcast_fusion), channel_id=1, source_target_pairs={{0,1},{1,2},{2,3},{3,0},{4,5},{5,6},{6,7},{7,4},{8,9},{9,10},{10,1... | collective-permute-start | bytes 1990664 | tf_op jit(solution)/shard_map/ppermute | solution.py:63
  159.9 13.5 %collective-permute-start.25 = (bf16[13,8,2944]{2,1,0:T(8,128)(2,1)S(1)}, bf16[13,8,2944]{2,1,0:T(8,128)(2,1)}, u32[]{:S(2)}, u32[]{:S(2)}) collective-permute-start(bf16[13,8,2944]{2,1,0:T(8,128)(2,1)S(1)} %slice.250), channel_id=1, source_target_pairs={{0,16},{4,20},{8,24},{12,28},{16,0},{20,4},{24,8},{28,12},{1,17},{... | collective-permute-start | bytes 1837064 | tf_op jit(solution)/shard_map/ppermute | solution.py:57
  160.4 27.7 %collective-permute-start.28 = (bf16[27,8,2944]{2,1,0:T(8,128)(2,1)}, bf16[27,8,2944]{2,1,0:T(8,128)(2,1)S(1)}, u32[]{:S(2)}, u32[]{:S(2)}) collective-permute-start(bf16[27,8,2944]{2,1,0:T(8,128)(2,1)} %collective-permute-done.22.refs_3_), channel_id=1, source_target_pairs={{0,4},{4,0},{8,12},{12,8},{16,20},{20,16},{24,28},{28,24},{1,5},{5... | collective-permute-start | bytes 3815432 | tf_op jit(solution)/shard_map/ppermute | solution.py:57
  162.6 24.3 %collective-permute-start.27 = (bf16[27,8,2944]{2,1,0:T(8,128)(2,1)}, bf16[27,8,2944]{2,1,0:T(8,128)(2,1)S(1)}, u32[]{:S(2)}, u32[]{:S(2)}) collective-permute-start(bf16[27,8,2944]{2,1,0:T(8,128)(2,1)} %constant_dynamic-update-slice_fusion.8.refs_2_), channel_id=1, source_target_pairs={{0,4},{4,0},{8,12},{12,8},{16,20},{20,16},{24,28},{28,24},{1,5},{5... | collective-permute-start | bytes 3815432 | tf_op jit(solution)/shard_map/ppermute | solution.py:57
  162.6 26.6 %collective-permute-start.29 = (bf16[27,8,2944]{2,1,0:T(8,128)(2,1)}, bf16[27,8,2944]{2,1,0:T(8,128)(2,1)S(1)}, u32[]{:S(2)}, u32[]{:S(2)}) collective-permute-start(bf16[27,8,2944]{2,1,0:T(8,128)(2,1)} %collective-permute-done.23.refs_4_), channel_id=1, source_target_pairs={{0,4},{4,0},{8,12},{12,8},{16,20},{20,16},{24,28},{28,24},{1,5},{5... | collective-permute-start | bytes 3815432 | tf_op jit(solution)/shard_map/ppermute | solution.py:57
  163.1 23.8 %collective-permute-start.30 = (bf16[36,8,1152]{2,1,0:T(8,128)(2,1)}, bf16[36,8,1152]{2,1,0:T(8,128)(2,1)S(1)}, u32[]{:S(2)}, u32[]{:S(2)}) collective-permute-start(bf16[36,8,1152]{2,1,0:T(8,128)(2,1)} %collective-permute-done.24), channel_id=1, source_target_pairs={{0,1},{1,2},{2,3},{3,0},{4,5},{5,6},{6,7},{7,4},{8,9},{9,10},{10,1... | collective-permute-start | bytes 1990664 | tf_op jit(solution)/shard_map/ppermute | solution.py:63
  173.4 13.5 %collective-permute-start.26 = (bf16[14,8,2944]{2,1,0:T(8,128)(2,1)S(1)}, bf16[14,8,2944]{2,1,0:T(8,128)(2,1)}, u32[]{:S(2)}, u32[]{:S(2)}) collective-permute-start(bf16[14,8,2944]{2,1,0:T(8,128)(2,1)S(1)} %slice.251), channel_id=1, source_target_pairs={{0,8},{4,12},{8,0},{12,4},{16,24},{20,28},{24,16},{28,20},{1,9},{5... | collective-permute-start | bytes 1978376 | tf_op jit(solution)/shard_map/ppermute | solution.py:57
  190.2 25.0 %collective-permute-start.32 = (bf16[14,8,2944]{2,1,0:T(8,128)(2,1)}, bf16[14,8,2944]{2,1,0:T(8,128)(2,1)}, u32[]{:S(2)}, u32[]{:S(2)}) collective-permute-start(bf16[14,8,2944]{2,1,0:T(8,128)(2,1)} %collective-permute-done.26.refs_6_), channel_id=1, source_target_pairs={{0,4},{4,0},{8,12},{12,8},{16,20},{20,16},{24,28},{28,24},{1,5},{5... | collective-permute-start | bytes 1978376 | tf_op jit(solution)/shard_map/ppermute | solution.py:57
  194.0 20.7 %collective-permute-start.31 = (bf16[13,8,2944]{2,1,0:T(8,128)(2,1)}, bf16[13,8,2944]{2,1,0:T(8,128)(2,1)}, u32[]{:S(2)}, u32[]{:S(2)}) collective-permute-start(bf16[13,8,2944]{2,1,0:T(8,128)(2,1)} %collective-permute-done.25.refs_5_), channel_id=1, source_target_pairs={{0,4},{4,0},{8,12},{12,8},{16,20},{20,16},{24,28},{28,24},{1,5},{5... | collective-permute-start | bytes 1837064 | tf_op jit(solution)/shard_map/ppermute | solution.py:57
  195.1 14.7 %collective-permute-start.36 = (bf16[256,1152]{1,0:T(8,128)(2,1)}, bf16[256,1152]{1,0:T(8,128)(2,1)}, u32[]{:S(2)}, u32[]{:S(2)}) collective-permute-start(bf16[256,1152]{1,0:T(8,128)(2,1)} %copy.103.x0), channel_id=1, source_target_pairs={{0,8},{4,12},{8,0},{12,4},{16,24},{20,28},{24,16},{28,20},{1,9},{5... | collective-permute-start | bytes 1769480 | tf_op jit(solution)/shard_map/ppermute | solution.py:57
  195.4 16.6 %collective-permute-start.38 = (bf16[256,1152]{1,0:T(8,128)(2,1)}, bf16[256,1152]{1,0:T(8,128)(2,1)}, u32[]{:S(2)}, u32[]{:S(2)}) collective-permute-start(bf16[256,1152]{1,0:T(8,128)(2,1)} %copy.103.x0), channel_id=1, source_target_pairs={{0,16},{4,20},{8,24},{12,28},{16,0},{20,4},{24,8},{28,12},{1,17},{... | collective-permute-start | bytes 1769480 | tf_op jit(solution)/shard_map/ppermute | solution.py:57
  198.7 43.5 %collective-permute-start.33 = (bf16[36,8,1152]{2,1,0:T(8,128)(2,1)}, bf16[36,8,1152]{2,1,0:T(8,128)(2,1)}, u32[]{:S(2)}, u32[]{:S(2)}) collective-permute-start(bf16[36,8,1152]{2,1,0:T(8,128)(2,1)} %copy-done.88), channel_id=1, source_target_pairs={{0,1},{1,2},{2,3},{3,0},{4,5},{5,6},{6,7},{7,4},{8,9},{9,10},{10,1... | collective-permute-start | bytes 1990664 | tf_op jit(solution)/shard_map/ppermute | solution.py:63
  209.8 32.4 %collective-permute-start.35 = (bf16[36,8,1152]{2,1,0:T(8,128)(2,1)}, bf16[36,8,1152]{2,1,0:T(8,128)(2,1)S(1)}, u32[]{:S(2)}, u32[]{:S(2)}) collective-permute-start(bf16[36,8,1152]{2,1,0:T(8,128)(2,1)} %copy-done.88), channel_id=1, source_target_pairs={{0,8},{4,20},{8,0},{12,28},{16,24},{20,4},{24,16},{28,12},{1,9},{5... | collective-permute-start | bytes 1990664 | tf_op jit(solution)/shard_map/ppermute | solution.py:60
  212.0 30.3 %collective-permute-start.34 = (bf16[36,8,1152]{2,1,0:T(8,128)(2,1)}, bf16[36,8,1152]{2,1,0:T(8,128)(2,1)}, u32[]{:S(2)}, u32[]{:S(2)}) collective-permute-start(bf16[36,8,1152]{2,1,0:T(8,128)(2,1)} %collective-permute-done.24), channel_id=1, source_target_pairs={{0,8},{4,20},{8,0},{12,28},{16,24},{20,4},{24,16},{28,12},{1,9},{5... | collective-permute-start | bytes 1990664 | tf_op jit(solution)/shard_map/ppermute | solution.py:60
  214.7 27.5 %collective-permute-start.37 = (bf16[128,1152]{1,0:T(8,128)(2,1)}, bf16[128,1152]{1,0:T(8,128)(2,1)}, u32[]{:S(2)}, u32[]{:S(2)}) collective-permute-start(bf16[128,1152]{1,0:T(8,128)(2,1)} %slice.292), channel_id=1, source_target_pairs={{0,16},{4,20},{8,24},{12,28},{16,0},{20,4},{24,8},{28,12},{1,17},{... | collective-permute-start | bytes 884744 | tf_op jit(solution)/shard_map/ppermute | solution.py:57
  215.2 27.1 %collective-permute-start.39 = (bf16[128,1152]{1,0:T(8,128)(2,1)}, bf16[128,1152]{1,0:T(8,128)(2,1)}, u32[]{:S(2)}, u32[]{:S(2)}) collective-permute-start(bf16[128,1152]{1,0:T(8,128)(2,1)} %slice.293), channel_id=1, source_target_pairs={{0,8},{4,12},{8,0},{12,4},{16,24},{20,28},{24,16},{28,20},{1,9},{5... | collective-permute-start | bytes 884744 | tf_op jit(solution)/shard_map/ppermute | solution.py:57
  243.8 15.5 %collective-permute-start.41 = (bf16[3,36,8,1152]{3,2,1,0:T(8,128)(2,1)S(1)}, bf16[3,36,8,1152]{3,2,1,0:T(8,128)(2,1)S(1)}, u32[]{:S(2)}, u32[]{:S(2)}) collective-permute-start(bf16[3,36,8,1152]{3,2,1,0:T(8,128)(2,1)S(1)} %pad_maximum_fusion.refs_1_), channel_id=1, source_target_pairs={{0,4},{4,0},{8,12},{12,8},{16,20},{20,16},{24,28},{28,24},{1,5},{5... | collective-permute-start | bytes 5971976 | tf_op jit(solution)/shard_map/ppermute | solution.py:57
  266.4 31.3 %collective-permute-start.44 = (bf16[1152,256]{1,0:T(8,128)(2,1)}, bf16[1152,256]{1,0:T(8,128)(2,1)}, u32[]{:S(2)}, u32[]{:S(2)}) collective-permute-start(bf16[1152,256]{1,0:T(8,128)(2,1)} %get-tuple-element.349), channel_id=1, source_target_pairs={{0,8},{4,12},{8,0},{12,4},{16,24},{20,28},{24,16},{28,20},{1,9},{5... | collective-permute-start | bytes 1769480 | tf_op jit(solution)/shard_map/ppermute | solution.py:57
  266.8 30.9 %collective-permute-start.45 = (bf16[1152,256]{1,0:T(8,128)(2,1)}, bf16[1152,256]{1,0:T(8,128)(2,1)}, u32[]{:S(2)}, u32[]{:S(2)}) collective-permute-start(bf16[1152,256]{1,0:T(8,128)(2,1)} %get-tuple-element.348), channel_id=1, source_target_pairs={{0,16},{4,20},{8,24},{12,28},{16,0},{20,4},{24,8},{28,12},{1,17},{... | collective-permute-start | bytes 1769480 | tf_op jit(solution)/shard_map/ppermute | solution.py:57
  267.8 29.9 %collective-permute-start.46 = (bf16[1152,256]{1,0:T(8,128)(2,1)}, bf16[1152,256]{1,0:T(8,128)(2,1)}, u32[]{:S(2)}, u32[]{:S(2)}) collective-permute-start(bf16[1152,256]{1,0:T(8,128)(2,1)} %get-tuple-element.347), channel_id=1, source_target_pairs={{0,24},{4,28},{8,16},{12,20},{16,8},{20,12},{24,0},{28,4},{1,25},{... | collective-permute-start | bytes 1769480 | tf_op jit(solution)/shard_map/ppermute | solution.py:57
  297.8 63.0 %collective-permute-start.50 = (bf16[256,1152]{1,0:T(8,128)(2,1)S(1)}, bf16[256,1152]{1,0:T(8,128)(2,1)}, u32[]{:S(2)}, u32[]{:S(2)}) collective-permute-start(bf16[256,1152]{1,0:T(8,128)(2,1)S(1)} %copy-done.30), channel_id=1, source_target_pairs={{0,8},{4,12},{8,0},{12,4},{16,24},{20,28},{24,16},{28,20},{1,9},{5... | collective-permute-start | bytes 1769480 | tf_op jit(solution)/shard_map/ppermute | solution.py:57
  298.2 62.6 %collective-permute-start.51 = (bf16[256,1152]{1,0:T(8,128)(2,1)S(1)}, bf16[256,1152]{1,0:T(8,128)(2,1)}, u32[]{:S(2)}, u32[]{:S(2)}) collective-permute-start(bf16[256,1152]{1,0:T(8,128)(2,1)S(1)} %copy-done.30), channel_id=1, source_target_pairs={{0,16},{4,20},{8,24},{12,28},{16,0},{20,4},{24,8},{28,12},{1,17},{... | collective-permute-start | bytes 1769480 | tf_op jit(solution)/shard_map/ppermute | solution.py:57
  308.7 52.1 %collective-permute-start.52 = (f32[4,144,1152]{2,1,0:T(8,128)}, f32[4,144,1152]{2,1,0:T(8,128)}, u32[]{:S(2)}, u32[]{:S(2)}) collective-permute-start(f32[4,144,1152]{2,1,0:T(8,128)} %get-tuple-element.206), channel_id=1, source_target_pairs={{0,4},{4,0},{8,12},{12,8},{16,20},{20,16},{24,28},{28,24},{1,5},{5... | collective-permute-start | bytes 7962632 | tf_op jit(solution)/shard_map/ppermute | solution.py:57
  330.0 14.9 %collective-permute-start.47 = (bf16[1152,256]{1,0:T(8,128)(2,1)S(1)}, bf16[1152,256]{1,0:T(8,128)(2,1)S(1)}, u32[]{:S(2)}, u32[]{:S(2)}) collective-permute-start(bf16[1152,256]{1,0:T(8,128)(2,1)S(1)} %get-tuple-element.345), channel_id=1, source_target_pairs={{0,8},{4,12},{8,0},{12,4},{16,24},{20,28},{24,16},{28,20},{1,9},{5... | collective-permute-start | bytes 1769480 | tf_op jit(solution)/shard_map/ppermute | solution.py:57
  330.3 19.0 %collective-permute-start.48 = (bf16[1152,256]{1,0:T(8,128)(2,1)}, bf16[1152,256]{1,0:T(8,128)(2,1)S(1)}, u32[]{:S(2)}, u32[]{:S(2)}) collective-permute-start(bf16[1152,256]{1,0:T(8,128)(2,1)} %get-tuple-element.344), channel_id=1, source_target_pairs={{0,16},{4,20},{8,24},{12,28},{16,0},{20,4},{24,8},{28,12},{1,17},{... | collective-permute-start | bytes 1769480 | tf_op jit(solution)/shard_map/ppermute | solution.py:57
  344.8 15.1 %collective-permute-start.49 = (bf16[1152,256]{1,0:T(8,128)(2,1)}, bf16[1152,256]{1,0:T(8,128)(2,1)S(1)}, u32[]{:S(2)}, u32[]{:S(2)}) collective-permute-start(bf16[1152,256]{1,0:T(8,128)(2,1)} %get-tuple-element.343), channel_id=1, source_target_pairs={{0,24},{4,28},{8,16},{12,20},{16,8},{20,12},{24,0},{28,4},{1,25},{... | collective-permute-start | bytes 1769480 | tf_op jit(solution)/shard_map/ppermute | solution.py:57
  361.3 43.1 %collective-permute-start.85 = (f32[8,1152]{1,0:T(8,128)S(1)}, f32[8,1152]{1,0:T(8,128)}, u32[]{:S(2)}, u32[]{:S(2)}) collective-permute-start(f32[8,1152]{1,0:T(8,128)S(1)} %concatenate.46), channel_id=1, source_target_pairs={{0,1},{1,2},{2,3},{3,0},{4,5},{5,6},{6,7},{7,4},{8,9},{9,10},{10,1... | collective-permute-start | bytes 110600 | tf_op jit(solution)/shard_map/ppermute | solution.py:63
  365.5 40.1 %collective-permute-start.86 = (f32[8,1152]{1,0:T(8,128)S(1)}, f32[8,1152]{1,0:T(8,128)}, u32[]{:S(2)}, u32[]{:S(2)}) collective-permute-start(f32[8,1152]{1,0:T(8,128)S(1)} %concatenate.46), channel_id=1, source_target_pairs={{0,2},{1,3},{2,0},{3,1},{4,6},{5,7},{6,4},{7,5},{8,10},{9,11},{10,... | collective-permute-start | bytes 110600 | tf_op jit(solution)/shard_map/ppermute | solution.py:63
  379.7 13.9 %collective-permute-start.53 = (bf16[8,1152]{1,0:T(8,128)(2,1)}, bf16[8,1152]{1,0:T(8,128)(2,1)S(1)}, u32[]{:S(2)}, u32[]{:S(2)}) collective-permute-start(bf16[8,1152]{1,0:T(8,128)(2,1)} %stack.256), channel_id=1, source_target_pairs={{0,1},{1,2},{2,3},{3,0},{4,5},{5,6},{6,7},{7,4},{8,9},{9,10},{10,1... | collective-permute-start | bytes 55304 | tf_op jit(solution)/shard_map/ppermute | solution.py:63
  380.3 13.5 %collective-permute-start.54 = (bf16[8,1152]{1,0:T(8,128)(2,1)}, bf16[8,1152]{1,0:T(8,128)(2,1)S(1)}, u32[]{:S(2)}, u32[]{:S(2)}) collective-permute-start(bf16[8,1152]{1,0:T(8,128)(2,1)} %stack.256), channel_id=1, source_target_pairs={{0,2},{1,3},{2,0},{3,1},{4,6},{5,7},{6,4},{7,5},{8,10},{9,11},{10,... | collective-permute-start | bytes 55304 | tf_op jit(solution)/shard_map/ppermute | solution.py:63
  404.4 28.3 %collective-permute-start.62 = (bf16[864,256]{1,0:T(8,128)(2,1)}, bf16[864,256]{1,0:T(8,128)(2,1)S(1)}, u32[]{:S(2)}, u32[]{:S(2)}) collective-permute-start(bf16[864,256]{1,0:T(8,128)(2,1)} %get-tuple-element.353), channel_id=1, source_target_pairs={{0,8},{4,12},{8,0},{12,4},{16,24},{20,28},{24,16},{28,20},{1,9},{5... | collective-permute-start | bytes 1327112 | tf_op jit(solution)/shard_map/ppermute | solution.py:57
  405.5 27.2 %collective-permute-start.63 = (bf16[864,256]{1,0:T(8,128)(2,1)}, bf16[864,256]{1,0:T(8,128)(2,1)S(1)}, u32[]{:S(2)}, u32[]{:S(2)}) collective-permute-start(bf16[864,256]{1,0:T(8,128)(2,1)} %get-tuple-element.352), channel_id=1, source_target_pairs={{0,16},{4,20},{8,24},{12,28},{16,0},{20,4},{24,8},{28,12},{1,17},{... | collective-permute-start | bytes 1327112 | tf_op jit(solution)/shard_map/ppermute | solution.py:57
  406.0 27.2 %collective-permute-start.64 = (bf16[864,256]{1,0:T(8,128)(2,1)}, bf16[864,256]{1,0:T(8,128)(2,1)S(1)}, u32[]{:S(2)}, u32[]{:S(2)}) collective-permute-start(bf16[864,256]{1,0:T(8,128)(2,1)} %get-tuple-element.351), channel_id=1, source_target_pairs={{0,24},{4,28},{8,16},{12,20},{16,8},{20,12},{24,0},{28,4},{1,25},{... | collective-permute-start | bytes 1327112 | tf_op jit(solution)/shard_map/ppermute | solution.py:57
  409.2 37.3 %collective-permute-start.69 = (bf16[288,256]{1,0:T(8,128)(2,1)}, bf16[288,256]{1,0:T(8,128)(2,1)}, u32[]{:S(2)}, u32[]{:S(2)}) collective-permute-start(bf16[288,256]{1,0:T(8,128)(2,1)} %get-tuple-element.365), channel_id=1, source_target_pairs={{0,8},{4,12},{8,0},{12,4},{16,24},{20,28},{24,16},{28,20},{1,9},{5... | collective-permute-start | bytes 442376 | tf_op jit(solution)/shard_map/ppermute | solution.py:57
  410.4 31.5 %collective-permute-start.59 = (bf16[4,8,1152]{2,1,0:T(8,128)(2,1)S(1)}, bf16[4,8,1152]{2,1,0:T(8,128)(2,1)}, u32[]{:S(2)}, u32[]{:S(2)}) collective-permute-start(bf16[4,8,1152]{2,1,0:T(8,128)(2,1)S(1)} %pad_maximum_fusion.5), channel_id=1, source_target_pairs={{0,4},{4,0},{8,12},{12,8},{16,20},{20,16},{24,28},{28,24},{1,5},{5... | collective-permute-start | bytes 221192 | tf_op jit(solution)/shard_map/ppermute | solution.py:57
  432.7 76.8 %collective-permute-start.78 = (f32[576,1152]{1,0:T(8,128)}, f32[576,1152]{1,0:T(8,128)}, u32[]{:S(2)}, u32[]{:S(2)}) collective-permute-start(f32[576,1152]{1,0:T(8,128)} %get-tuple-element.238), channel_id=1, source_target_pairs={{0,4},{4,0},{8,12},{12,8},{16,20},{20,16},{24,28},{28,24},{1,5},{5... | collective-permute-start | bytes 7962632 | tf_op jit(solution)/shard_map/ppermute | solution.py:57
  439.9 58.6 %collective-permute-start.65 = (f32[432,1152]{1,0:T(8,128)}, f32[432,1152]{1,0:T(8,128)}, u32[]{:S(2)}, u32[]{:S(2)}) collective-permute-start(f32[432,1152]{1,0:T(8,128)} %get-tuple-element.217), channel_id=1, source_target_pairs={{0,4},{4,0},{8,12},{12,8},{16,20},{20,16},{24,28},{28,24},{1,5},{5... | collective-permute-start | bytes 5971976 | tf_op jit(solution)/shard_map/ppermute | solution.py:57
  447.4 15.0 %collective-permute-start.82 = (bf16[144,1152]{1,0:T(8,128)(2,1)}, bf16[144,1152]{1,0:T(8,128)(2,1)}, u32[]{:S(2)}, u32[]{:S(2)}) collective-permute-start(bf16[144,1152]{1,0:T(8,128)(2,1)} %get-tuple-element.340), channel_id=1, source_target_pairs={{0,1},{1,2},{2,3},{3,0},{4,5},{5,6},{6,7},{7,4},{8,9},{9,10},{10,1... | collective-permute-start | bytes 995336 | tf_op jit(solution)/shard_map/ppermute | solution.py:63
  455.8 24.7 %collective-permute-start.83 = (bf16[144,1152]{1,0:T(8,128)(2,1)}, bf16[144,1152]{1,0:T(8,128)(2,1)}, u32[]{:S(2)}, u32[]{:S(2)}) collective-permute-start(bf16[144,1152]{1,0:T(8,128)(2,1)} %get-tuple-element.342), channel_id=1, source_target_pairs={{0,2},{1,3},{2,0},{3,1},{4,6},{5,7},{6,4},{7,5},{8,10},{9,11},{10,... | collective-permute-start | bytes 995336 | tf_op jit(solution)/shard_map/ppermute | solution.py:63
  455.8 25.5 %collective-permute-start.84 = (bf16[144,1152]{1,0:T(8,128)(2,1)}, bf16[144,1152]{1,0:T(8,128)(2,1)}, u32[]{:S(2)}, u32[]{:S(2)}) collective-permute-start(bf16[144,1152]{1,0:T(8,128)(2,1)} %get-tuple-element.341), channel_id=1, source_target_pairs={{0,3},{1,0},{2,1},{3,2},{4,7},{5,4},{6,5},{7,6},{8,11},{9,8},{10,9... | collective-permute-start | bytes 995336 | tf_op jit(solution)/shard_map/ppermute | solution.py:63
  462.4 40.7 %collective-permute-start.72 = (f32[144,1152]{1,0:T(8,128)}, f32[144,1152]{1,0:T(8,128)}, u32[]{:S(2)}, u32[]{:S(2)}) collective-permute-start(f32[144,1152]{1,0:T(8,128)} %copy-done.46), channel_id=1, source_target_pairs={{0,4},{4,0},{8,12},{12,8},{16,20},{20,16},{24,28},{28,24},{1,5},{5... | collective-permute-start | bytes 1990664 | tf_op jit(solution)/shard_map/ppermute | solution.py:57
  480.4 13.7 %collective-permute-start.61 = (bf16[16,8,1152]{2,1,0:T(8,128)(2,1)}, bf16[16,8,1152]{2,1,0:T(8,128)(2,1)}, u32[]{:S(2)}, u32[]{:S(2)}) collective-permute-start(bf16[16,8,1152]{2,1,0:T(8,128)(2,1)} %get-tuple-element.371), channel_id=1, source_target_pairs={{0,16},{4,20},{8,24},{12,28},{16,0},{20,4},{24,8},{28,12},{1,17},{... | collective-permute-start | bytes 884744 | tf_op jit(solution)/shard_map/ppermute | solution.py:57
  489.3 49.3 %all-to-all-start = ((f32[8,144,144]{2,1,0:T(8,128)}), f32[8,144,144]{2,1,0:T(8,128)}, u32[]{:S(2)}, u32[]{:S(2)}) async-start(f32[8,144,144]{2,1,0:T(8,128)} %bitcast.260), calls=%async_computation | async-start | bytes 2359296 | tf_op jit(solution)/shard_map/all_to_all | solution.py:725
  501.7 33.5 %collective-permute-start.66 = (bf16[288,432]{1,0:T(8,128)(2,1)}, bf16[288,432]{1,0:T(8,128)(2,1)}, u32[]{:S(2)}, u32[]{:S(2)}) collective-permute-start(bf16[288,432]{1,0:T(8,128)(2,1)} %get-tuple-element.219), channel_id=1, source_target_pairs={{0,1},{1,2},{2,3},{3,0},{4,5},{5,6},{6,7},{7,4},{8,9},{9,10},{10,1... | collective-permute-start | bytes 746504 | tf_op jit(solution)/shard_map/ppermute | solution.py:63
  508.2 27.0 %collective-permute-start.74 = (bf16[288,144]{1,0:T(8,128)(2,1)}, bf16[288,144]{1,0:T(8,128)(2,1)}, u32[]{:S(2)}, u32[]{:S(2)}) collective-permute-start(bf16[288,144]{1,0:T(8,128)(2,1)} %get-tuple-element.229), channel_id=1, source_target_pairs={{0,2},{1,3},{2,0},{3,1},{4,6},{5,7},{6,4},{7,5},{8,10},{9,11},{10,... | collective-permute-start | bytes 248840 | tf_op jit(solution)/shard_map/ppermute | solution.py:63
  508.7 26.5 %collective-permute-start.75 = (bf16[288,144]{1,0:T(8,128)(2,1)}, bf16[288,144]{1,0:T(8,128)(2,1)}, u32[]{:S(2)}, u32[]{:S(2)}) collective-permute-start(bf16[288,144]{1,0:T(8,128)(2,1)} %get-tuple-element.230), channel_id=1, source_target_pairs={{0,3},{1,0},{2,1},{3,2},{4,7},{5,4},{6,5},{7,6},{8,11},{9,8},{10,9... | collective-permute-start | bytes 248840 | tf_op jit(solution)/shard_map/ppermute | solution.py:63
  509.6 32.0 %collective-permute-start.67 = (bf16[288,432]{1,0:T(8,128)(2,1)}, bf16[288,432]{1,0:T(8,128)(2,1)}, u32[]{:S(2)}, u32[]{:S(2)}) collective-permute-start(bf16[288,432]{1,0:T(8,128)(2,1)} %copy-done.51), channel_id=1, source_target_pairs={{0,2},{1,3},{2,0},{3,1},{4,6},{5,7},{6,4},{7,5},{8,10},{9,11},{10,... | collective-permute-start | bytes 746504 | tf_op jit(solution)/shard_map/ppermute | solution.py:63
  515.2 26.3 %collective-permute-start.68 = (bf16[288,432]{1,0:T(8,128)(2,1)}, bf16[288,432]{1,0:T(8,128)(2,1)S(1)}, u32[]{:S(2)}, u32[]{:S(2)}) collective-permute-start(bf16[288,432]{1,0:T(8,128)(2,1)} %get-tuple-element.221), channel_id=1, source_target_pairs={{0,3},{1,0},{2,1},{3,2},{4,7},{5,4},{6,5},{7,6},{8,11},{9,8},{10,9... | collective-permute-start | bytes 746504 | tf_op jit(solution)/shard_map/ppermute | solution.py:63
  535.2 14.6 %collective-permute-start.79 = (bf16[288,576]{1,0:T(8,128)(2,1)}, bf16[288,576]{1,0:T(8,128)(2,1)S(1)}, u32[]{:S(2)}, u32[]{:S(2)}) collective-permute-start(bf16[288,576]{1,0:T(8,128)(2,1)} %get-tuple-element.240), channel_id=1, source_target_pairs={{0,1},{1,2},{2,3},{3,0},{4,5},{5,6},{6,7},{7,4},{8,9},{9,10},{10,1... | collective-permute-start | bytes 995336 | tf_op jit(solution)/shard_map/ppermute | solution.py:63
  535.2 37.9 %collective-permute-start.80 = (bf16[288,576]{1,0:T(8,128)(2,1)}, bf16[288,576]{1,0:T(8,128)(2,1)S(1)}, u32[]{:S(2)}, u32[]{:S(2)}) collective-permute-start(bf16[288,576]{1,0:T(8,128)(2,1)} %get-tuple-element.241), channel_id=1, source_target_pairs={{0,2},{1,3},{2,0},{3,1},{4,6},{5,7},{6,4},{7,5},{8,10},{9,11},{10,... | collective-permute-start | bytes 995336 | tf_op jit(solution)/shard_map/ppermute | solution.py:63
  535.2 37.8 %collective-permute-start.81 = (bf16[288,576]{1,0:T(8,128)(2,1)}, bf16[288,576]{1,0:T(8,128)(2,1)S(1)}, u32[]{:S(2)}, u32[]{:S(2)}) collective-permute-start(bf16[288,576]{1,0:T(8,128)(2,1)} %get-tuple-element.242), channel_id=1, source_target_pairs={{0,3},{1,0},{2,1},{3,2},{4,7},{5,4},{6,5},{7,6},{8,11},{9,8},{10,9... | collective-permute-start | bytes 995336 | tf_op jit(solution)/shard_map/ppermute | solution.py:63
  (159 other events, 1184.8 us)

commit v3 on v2

v3 whole, which is shorter than its diff:
```python
import math

import jax
import jax.numpy as jnp
from jax import lax
from jax.experimental import pallas as pl
from jax.experimental.pallas import tpu as pltpu
from jax.sharding import PartitionSpec as P

HEAD_DIM = 72
BOX = 8

epsilon = 1e-06
masked_value = -1e30
gelu_root = math.sqrt(2.0 / math.pi)
f32 = jnp.float32
bf16 = jnp.bfloat16


def norm_parts(values_in):
    centred = values_in - jnp.mean(values_in, axis=-1, keepdims=True)
    spread = jnp.mean(centred * centred, axis=-1, keepdims=True)
    rate = lax.rsqrt(spread + epsilon)
    return centred * rate, rate


def norm_back(normal, rate, grad):
    mean_grad = jnp.mean(grad, axis=-1, keepdims=True)
    mean_both = jnp.mean(grad * normal, axis=-1, keepdims=True)
    return rate * (grad - mean_grad - normal * mean_both)


def gelu_tanh(pre_act):
    return (
        0.5
        * pre_act
        * (1.0 + jnp.tanh(gelu_root * (pre_act + 0.044715 * pre_act * pre_act * pre_act)))
    )


def after(value, other):
    return lax.optimization_barrier((value, other))[0]


def gated(values):
    return lax.optimization_barrier(values)


def pick(array, index, axis=0):
    return lax.dynamic_index_in_dim(array, index, axis, keepdims=False)


def make_body(dp, fs):
    groups = dp // BOX

    def box_send(x, bits):
        return lax.ppermute(x, "dp", [(i, i ^ bits) for i in range(dp)])

    def side_send(x):
        return lax.ppermute(x, "dp", [(i, i ^ (4 if i & 1 else 2)) for i in range(dp)])

    def ring_send(x, hops):
        return lax.ppermute(x, "fsdp", [(i, (i + hops) % fs) for i in range(fs)])

    def group_send(x, hops):
        return lax.ppermute(x, "dp", [(i, (i + hops * BOX) % dp) for i in range(dp)])

    def ring_gather(x):
        return [x] + [ring_send(x, k) for k in range(1, fs)]

    def ring_sorted(blocks, z):
        back = jnp.stack(blocks[::-1] + blocks[::-1])
        return lax.dynamic_slice_in_dim(back, fs - 1 - z, fs, 0)

    def chip_near(x):
        return box_send(x, 2), box_send(x, 4)

    def chip_far(near):
        half = near[0].shape[0] // 2
        return box_send(near[0][:half], 4), box_send(near[1][half:], 2)

    def chip_exchange(blocks, chip):
        return [pick(blocks, chip)] + [
            box_send(pick(blocks, chip ^ k), 2 * k) for k in range(1, BOX // 2)
        ]

    def ring_sum(x, z):
        total = pick(x, z)
        for k in range(1, fs):
            sent = pick(x, lax.rem(z + k, fs)).astype(bf16)
            total = total + ring_send(sent, k).astype(f32)
        return total

    def group_sum(x, group):
        total = pick(x, group)
        for k in range(1, groups):
            total = total + group_send(pick(x, lax.rem(group + k, groups)), k)
        return total

    def cost(microseconds):
        return pl.CostEstimate(
            flops=int(microseconds * 5e8),
            transcendentals=0,
            bytes_accessed=int(microseconds * 1.6e6),
        )

    vmem = pl.BlockSpec(memory_space=pltpu.VMEM)
    smem = pl.BlockSpec(memory_space=pltpu.SMEM)

    def params(mebibytes):
        return pltpu.CompilerParams(vmem_limit_bytes=mebibytes << 20)

    def chunks(rows, step, work):
        def one(i, unused):
            work(pl.ds(pl.multiple_of(i * step, step), step), i * step)
            return unused

        lax.fori_loop(0, rows // step, one, 0)

    def alive_rows(first, rows, live):
        return ((lax.broadcasted_iota(jnp.int32, (rows, 1), 0) + first) < live).astype(f32)

    def modulation_parts(conds, w_ada, bias_ada, extra):
        images = conds.shape[0]
        parts, width = bias_ada.shape

        def kernel(cond_ref, w_ref, bias_ref, extra_ref, *out_refs):
            for part in range(parts):
                cols = slice(part * width, (part + 1) * width)
                product = jnp.dot(cond_ref[...], w_ref[:, cols], preferred_element_type=f32)
                product = product + bias_ref[part : part + 1, :]
                for image, out_ref in enumerate(out_refs):
                    out_ref[part : part + 1, :] = product[image : image + 1, :]
            for out_ref in out_refs:
                out_ref[parts:, :] = extra_ref[...]

        rows = parts + extra.shape[0]
        return pl.pallas_call(
            kernel,
            out_shape=[jax.ShapeDtypeStruct((rows, width), f32)] * images,
            in_specs=[vmem] * 4,
            out_specs=[vmem] * images,
            cost_estimate=cost(4),
            compiler_params=params(60),
        )(conds, w_ada, bias_ada, extra)

    def modulation_rows(partials, live):
        rows, width = partials[0].shape

        def kernel(live_ref, *refs):
            mods_ref, head_ref = refs[-2:]
            total = refs[0][...]
            for ref in refs[1:-2]:
                total = total + ref[...]
            mods_ref[...] = total
            head_ref[...] = jnp.full(head_ref.shape, live_ref[0].astype(f32))
            head_ref[0:2, :] = total[0:2, :]
            head_ref[2:3, :] = total[5:6, :]

        return pl.pallas_call(
            kernel,
            out_shape=[jax.ShapeDtypeStruct((rows, width), f32)] * 2,
            in_specs=[smem] + [vmem] * len(partials),
            out_specs=[vmem] * 2,
            cost_estimate=cost(1),
            compiler_params=params(60),
        )(live, *partials)

    def other_heads(raws, firsts, heads):
        n = len(raws)
        width = raws[0].shape[1] // 2

        def kernel(*refs):
            raw_refs, head_refs = refs[:n], refs[n : 2 * n]
            normed_refs, d_mlp_refs = refs[2 * n : 3 * n], refs[3 * n :]
            for raw, head, normed, d_mlp, first in zip(
                raw_refs, head_refs, normed_refs, d_mlp_refs, firsts
            ):
                live = head[3, 0].astype(jnp.int32)

                def work(rows, start):
                    normal = norm_parts(raw[rows, :width].astype(f32))[0]
                    normed[rows, :] = (
                        normal * (1.0 + head[1:2, :]) + head[0:1, :]
                    ).astype(bf16)
                    count = normal.shape[0]
                    up_rows = alive_rows(start + first, count, live) * raw[
                        rows, width:
                    ].astype(f32)
                    d_mlp[rows, :] = (head[2:3, :] * up_rows).astype(bf16)

                chunks(raw.shape[0], 32, work)

        outs = pl.pallas_call(
            kernel,
            out_shape=[jax.ShapeDtypeStruct((raw.shape[0], width), bf16) for raw in raws] * 2,
            in_specs=[vmem] * (2 * n),
            out_specs=[vmem] * (2 * n),
            cost_estimate=cost(8),
            compiler_params=params(60),
        )(*raws, *heads)
        return outs[:n], outs[n:]

    def piece_plan(pieces):
        arrays = []
        for piece, unused in (each for kind in pieces for each in kind):
            if not any(piece is array for array in arrays):
                arrays.append(piece)
        position = {id(array): i for i, array in enumerate(arrays)}
        plan = [[(position[id(piece)], index) for piece, index in kind] for kind in pieces]
        return arrays, plan

    def piece_copies(where_ref, own_ref, array_refs, plan, whole_ref):
        copies = [(own_ref, whole_ref.at[where_ref[0]])]
        for kind, blocks in enumerate(plan):
            for k, (which, index) in enumerate(blocks):
                source = array_refs[which] if index is None else array_refs[which].at[index]
                copies.append((source, whole_ref.at[where_ref[k + 1], where_ref[fs + kind]]))
        return copies

    def wide_copies(core, where_ref, own_refs, sets, whole_refs):
        widths = [ref.shape[-1] for ref in own_refs]
        width, part = sum(widths), sets[0][0].shape[-1]
        lead, split = whole_refs[0].shape[2], sets[0][3].shape[0]
        copies = [(own, whole.at[where_ref[0]]) for own, whole in zip(own_refs, whole_refs)]
        for side, piece_refs in enumerate(sets):
            low, high = (0, part) if core ^ side == 0 else (part, width)
            offset = 0 if core ^ side == 0 else width - part
            for block in range(1, fs):
                base = (block - 1) * lead
                top = min(max(split - base, 0), lead)
                rows = [(i, base, i, 0, lead) for i in range(3)]
                if top:
                    rows.append((3, base, 3, 0, top))
                if top < lead:
                    rows.append((4, base + top - split, 3, top, lead - top))
                for piece, first, slot, row, count in rows:
                    start = 0
                    for i, each in enumerate(widths):
                        left, right = max(low, start), min(high, start + each)
                        if left < right:
                            source = piece_refs[piece].at[
                                first : first + count, :, left - offset : right - offset
                            ]
                            target = whole_refs[i].at[
                                where_ref[block],
                                where_ref[fs + 1 + slot],
                                row : row + count,
                                :,
                                left - start : right - start,
                            ]
                            copies.append((source, target))
                        start += each
        return copies

    def copy_all(copies, sems):
        return [
            pltpu.make_async_copy(source, target, sems.at[j])
            for j, (source, target) in enumerate(copies)
        ]

    def start_all(copies):
        for copy in copies:
            copy.start()

    def wait_all(copies):
        for copy in copies:
            copy.wait()

    def in_blocks(shard):
        rows, cols = shard.shape
        return shard.reshape(4, rows // 32, 8, cols)

    any_spec = pl.BlockSpec(memory_space=pl.ANY)

    def projection(where, normed, own, pieces, biases):
        slots, width = normed.shape
        arrays, plan = piece_plan(pieces)
        own = in_blocks(own)
        shape = (fs,) + own.shape

        def kernel(where_ref, normed_ref, bias_ref, own_ref, *refs):
            array_refs = refs[: len(arrays)]
            turned_ref, whole_ref, scratch, sems, out_sem = refs[len(arrays) :]
            copies = copy_all(
                piece_copies(where_ref, own_ref, array_refs, plan, scratch), sems
            )
            start_all(copies)
            wait_all(copies)
            out = pltpu.make_async_copy(scratch, whole_ref, out_sem)
            out.start()
            w_ref = scratch.reshape(width, 3 * width)
            for part in range(3):
                cols = slice(part * width, (part + 1) * width)
                proj = jnp.dot(normed_ref[...], w_ref[:, cols], preferred_element_type=f32)
                if part != 1:
                    proj = proj + bias_ref[part // 2 : part // 2 + 1, :]
                turned_ref[cols, :] = proj.astype(bf16).astype(f32).T
            out.wait()

        turned, whole = pl.pallas_call(
            kernel,
            out_shape=[
                jax.ShapeDtypeStruct((3 * width, slots), f32),
                jax.ShapeDtypeStruct(shape, bf16),
            ],
            in_specs=[smem, vmem, vmem, any_spec] + [any_spec] * len(arrays),
            out_specs=[vmem, any_spec],
            scratch_shapes=[
                pltpu.VMEM(shape, bf16),
                pltpu.SemaphoreType.DMA((1 + 4 * (fs - 1),)),
                pltpu.SemaphoreType.DMA,
            ],
            cost_estimate=cost(11),
            compiler_params=params(60),
        )(where, normed, biases, own, *arrays)
        return turned, whole.reshape(width, 3 * width)

    def attention(turned, live):
        slots = turned.shape[1]
        width = turned.shape[0] // 3
        count = width // HEAD_DIM
        scale = HEAD_DIM ** (-0.5)

        def kernel(live_ref, turned_ref, attended_ref, out_turned):
            live_keys = lax.broadcasted_iota(jnp.int32, (1, slots), 1) < live_ref[0]

            def head(h, unused):
                def rows(part):
                    first = pl.multiple_of(part * width + h * HEAD_DIM, 8)
                    return turned_ref[pl.ds(first, HEAD_DIM), :].astype(bf16)

                scores = lax.dot_general(
                    rows(0), rows(1), (((0,), (0,)), ((), ())), preferred_element_type=f32
                )
                scores = jnp.where(live_keys, scores * scale, masked_value)
                highest = jnp.max(scores, axis=-1, keepdims=True)
                total = jnp.sum(jnp.exp(scores - highest), axis=-1, keepdims=True)
                probs = jnp.exp(scores - (highest + jnp.log(total)))
                out = lax.dot_general(
                    rows(2),
                    probs.astype(bf16),
                    (((1,), (1,)), ((), ())),
                    preferred_element_type=f32,
                )
                out_turned[pl.ds(pl.multiple_of(h * HEAD_DIM, 8), HEAD_DIM), :] = out
                return unused

            lax.fori_loop(0, count, head, 0)
            attended_ref[...] = out_turned[...].T.astype(bf16)

        return pl.pallas_call(
            kernel,
            out_shape=jax.ShapeDtypeStruct((slots, width), bf16),
            in_specs=[smem, vmem],
            out_specs=vmem,
            scratch_shapes=[pltpu.VMEM((width, slots), f32)],
            cost_estimate=cost(11),
            compiler_params=params(60),
        )(live, turned)

    def attention_back(turned, d_turned, live):
        width, slots = d_turned.shape
        count = width // HEAD_DIM
        scale = HEAD_DIM ** (-0.5)

        def kernel(live_ref, turned_ref, d_ref, out_ref, total_ref):
            live_keys = lax.broadcasted_iota(jnp.int32, (1, slots), 1) < live_ref[0]

            def head(h, unused):
                def place(part):
                    return pl.ds(pl.multiple_of(part * width + h * HEAD_DIM, 8), HEAD_DIM)

                query = turned_ref[place(0), :].astype(bf16)
                key_part = turned_ref[place(1), :].astype(bf16)
                value = turned_ref[place(2), :].astype(bf16)
                d_out = d_ref[place(0), :].astype(bf16)
                both_first = (((0,), (0,)), ((), ()))
                scores = lax.dot_general(
                    query, key_part, both_first, preferred_element_type=f32
                )
                scores = jnp.where(live_keys, scores * scale, masked_value)
                highest = jnp.max(scores, axis=-1, keepdims=True)
                total = jnp.sum(jnp.exp(scores - highest), axis=-1, keepdims=True)
                probs = jnp.exp(scores - (highest + jnp.log(total)))
                d_probs = lax.dot_general(
                    d_out, value, both_first, preferred_element_type=f32
                )
                inner = jnp.sum(probs * d_probs, axis=-1, keepdims=True)
                d_scores = (probs * (d_probs - inner)).astype(bf16)
                total_ref[place(2), :] = jnp.dot(
                    d_out, probs.astype(bf16), preferred_element_type=f32
                )
                total_ref[place(0), :] = scale * lax.dot_general(
                    key_part, d_scores, (((1,), (1,)), ((), ())), preferred_element_type=f32
                )
                total_ref[place(1), :] = scale * jnp.dot(
                    query, d_scores, preferred_element_type=f32
                )
                return unused

            lax.fori_loop(0, count, head, 0)
            out_ref[...] = total_ref[...].astype(bf16)

        return pl.pallas_call(
            kernel,
            out_shape=jax.ShapeDtypeStruct((3 * width, slots), bf16),
            in_specs=[smem, vmem, vmem],
            out_specs=vmem,
            scratch_shapes=[pltpu.VMEM((3 * width, slots), f32)],
            cost_estimate=cost(12),
            compiler_params=params(60),
        )(live, turned, d_turned)

    def middle_forward(where, attended, tokens_own, owns, sets, bias_out, bias_up, mods):
        slots, width = attended.shape
        owns = [in_blocks(own) for own in owns]
        hidden = owns[1].shape[-1]
        tile = hidden // fs
        quarter = tile // 4
        shapes = [(fs,) + own.shape for own in owns]
        n_pieces = len(sets[0])
        n_copies = 2 + 2 * 15 * (fs - 1)

        def kernel(where_ref, attended_ref, tokens_ref, bias_out_ref, bias_up_ref, mods_ref, *refs):
            own_refs = refs[:2]
            set_refs = (refs[2 : 2 + n_pieces], refs[2 + n_pieces : 2 + 2 * n_pieces])
            (
                attn_ref,
                normed_ref,
                pre_ref,
                act_ref,
                turned_ref,
                whole_out,
                whole_up,
                scratch_out,
                scratch_up,
                sems,
                out_sems,
            ) = refs[2 + 2 * n_pieces :]
            step = pl.program_id(0)
            scratches, wholes = (scratch_out, scratch_up), (whole_out, whole_up)

            def outs():
                return [
                    pltpu.make_async_copy(scratch, whole, out_sems.at[i])
                    for i, (scratch, whole) in enumerate(zip(scratches, wholes))
                ]

            @pl.when(step == 0)
            def first():
                for core in range(2):

                    @pl.when(where_ref[fs] == core)
                    def gather(core=core):
                        copies = copy_all(
                            wide_copies(core, where_ref, own_refs, set_refs, scratches), sems
                        )
                        start_all(copies)
                        wait_all(copies)

                start_all(outs())
                attn_ref[...] = (
                    jnp.dot(
                        attended_ref[...],
                        scratch_out.reshape(width, width)[...],
                        preferred_element_type=f32,
                    )
                    + bias_out_ref[...]
                )

                def work(rows, unused):
                    middle = tokens_ref[rows, :].astype(f32) + mods_ref[2:3, :] * attn_ref[rows, :]
                    normal = norm_parts(middle)[0]
                    normed_ref[rows, :] = (
                        normal * (1.0 + mods_ref[4:5, :]) + mods_ref[3:4, :]
                    ).astype(bf16)

                chunks(slots, 32, work)

            cols = pl.ds(pl.multiple_of(step * tile, 128), tile)
            pre_ref[...] = (
                jnp.dot(
                    normed_ref[...],
                    scratch_up.reshape(width, hidden)[:, cols],
                    preferred_element_type=f32,
                )
                + bias_up_ref[0]
            )

            def work(rows, unused):
                act_ref[rows, :] = gelu_tanh(pre_ref[rows, :]).astype(bf16)

            chunks(slots, 32, work)
            for chip in range(4):
                cols = slice(chip * quarter, (chip + 1) * quarter)
                turned_ref[chip, :, :] = act_ref[:, cols].astype(f32).T.astype(bf16)

            @pl.when(step == fs - 1)
            def last():
                wait_all(outs())

        def whole(shape):
            return pl.BlockSpec(shape, lambda j, where_ref: (0,) * len(shape))

        *results, whole_out, whole_up = pl.pallas_call(
            kernel,
            out_shape=[
                jax.ShapeDtypeStruct((slots, width), f32),
                jax.ShapeDtypeStruct((slots, width), bf16),
                jax.ShapeDtypeStruct((slots, hidden), f32),
                jax.ShapeDtypeStruct((slots, hidden), bf16),
                jax.ShapeDtypeStruct((4, fs * quarter, slots), bf16),
            ]
            + [jax.ShapeDtypeStruct(shape, bf16) for shape in shapes],
            grid_spec=pltpu.PrefetchScalarGridSpec(
                num_scalar_prefetch=1,
                grid=(fs,),
                in_specs=[
                    whole((slots, width)),
                    whole((slots, width)),
                    whole((1, width)),
                    pl.BlockSpec((1, 1, tile), lambda j, where_ref: (j, 0, 0)),
                    whole(mods.shape),
                ]
                + [any_spec] * (2 + 2 * n_pieces),
                out_specs=[
                    whole((slots, width)),
                    whole((slots, width)),
                    pl.BlockSpec((slots, tile), lambda j, where_ref: (0, j)),
                    pl.BlockSpec((slots, tile), lambda j, where_ref: (0, j)),
                    pl.BlockSpec((4, quarter, slots), lambda j, where_ref: (0, j, 0)),
                    any_spec,
                    any_spec,
                ],
                scratch_shapes=[pltpu.VMEM(shape, bf16) for shape in shapes]
                + [pltpu.SemaphoreType.DMA((n_copies,)), pltpu.SemaphoreType.DMA((2,))],
            ),
            cost_estimate=cost(20),
            compiler_params=params(60),
        )(
            where,
            attended,
            tokens_own,
            bias_out.reshape(1, width),
            bias_up.reshape(fs, 1, tile),
            mods,
            *owns,
            *sets[0],
            *sets[1],
        )
        return (
            *results,
            whole_out.reshape(width, width),
            whole_up.reshape(width, hidden),
        )

    def hidden_back(where, d_mlp, own, pieces, pre_act):
        slots, width = d_mlp.shape
        hidden = pre_act.shape[1]
        tile = hidden // fs
        arrays, plan = piece_plan(pieces)
        own = in_blocks(own)
        shape = (fs,) + own.shape

        def kernel(where_ref, d_mlp_ref, pre_ref, own_ref, *refs):
            array_refs = refs[: len(arrays)]
            (
                d_pre_ref,
                turned_ref,
                sum_ref,
                whole_ref,
                d_act_ref,
                scratch,
                sems,
                out_sem,
            ) = refs[len(arrays) :]
            step = pl.program_id(0)

            def out():
                return pltpu.make_async_copy(scratch, whole_ref, out_sem)

            @pl.when(step == 0)
            def first():
                copies = copy_all(
                    piece_copies(where_ref, own_ref, array_refs, plan, scratch), sems
                )
                start_all(copies)
                wait_all(copies)
                out().start()

            d_act_ref[...] = lax.dot_general(
                d_mlp_ref[...],
                scratch.at[step].reshape(tile, width)[...],
                (((1,), (1,)), ((), ())),
                preferred_element_type=f32,
            )

            def work(rows, unused):
                pre = pre_ref[rows, :]
                square = pre * pre
                bend = jnp.tanh(gelu_root * (pre + 0.044715 * square * pre))
                slope = 0.5 * (1.0 + bend) + 0.5 * pre * (1.0 - bend * bend) * gelu_root * (
                    1.0 + 3.0 * 0.044715 * square
                )
                d_pre = (d_act_ref[rows, :] * slope).astype(bf16)
                d_pre_ref[rows, :] = d_pre
                d_act_ref[rows, :] = d_pre.astype(f32)

            chunks(slots, 32, work)
            sum_ref[0] = jnp.sum(d_act_ref[...], axis=0, keepdims=True)
            turned_ref[...] = d_act_ref[...].T.astype(bf16)

            @pl.when(step == fs - 1)
            def last():
                out().wait()

        *results, whole = pl.pallas_call(
            kernel,
            out_shape=[
                jax.ShapeDtypeStruct((slots, hidden), bf16),
                jax.ShapeDtypeStruct((hidden, slots), bf16),
                jax.ShapeDtypeStruct((fs, 1, tile), f32),
                jax.ShapeDtypeStruct(shape, bf16),
            ],
            grid_spec=pltpu.PrefetchScalarGridSpec(
                num_scalar_prefetch=1,
                grid=(fs,),
                in_specs=[
                    pl.BlockSpec((slots, width), lambda j, where_ref: (0, 0)),
                    pl.BlockSpec((slots, tile), lambda j, where_ref: (0, j)),
                    any_spec,
                ]
                + [any_spec] * len(arrays),
                out_specs=[
                    pl.BlockSpec((slots, tile), lambda j, where_ref: (0, j)),
                    pl.BlockSpec((tile, slots), lambda j, where_ref: (j, 0)),
                    pl.BlockSpec((1, 1, tile), lambda j, where_ref: (j, 0, 0)),
                    any_spec,
                ],
                scratch_shapes=[
                    pltpu.VMEM((slots, tile), f32),
                    pltpu.VMEM(shape, bf16),
                    pltpu.SemaphoreType.DMA((1 + 4 * (fs - 1),)),
                    pltpu.SemaphoreType.DMA,
                ],
            ),
            cost_estimate=cost(15),
            compiler_params=params(60),
        )(where, d_mlp, pre_act, own, *arrays)
        return (*results, whole.reshape(hidden, width))

    def middle_back(d_pre, up_full, out_full, attn_out, tokens_own, cotangent_own, mods, live):
        slots, hidden = d_pre.shape
        width = attn_out.shape[1]
        tile = hidden // fs

        def kernel(
            live_ref,
            d_pre_ref,
            up_ref,
            out_ref,
            attn_ref,
            tokens_ref,
            cot_ref,
            mods_ref,
            d_middle_ref,
            d_attn_turned_ref,
            d_attended_turned_ref,
            sums_ref,
            total,
            d_attn_ref,
        ):
            step = pl.program_id(0)
            part = lax.dot_general(
                d_pre_ref[...],
                up_ref[...],
                (((1,), (1,)), ((), ())),
                preferred_element_type=f32,
            )

            @pl.when(step == 0)
            def start():
                total[...] = part

            @pl.when(step > 0)
            def add():
                total[...] += part

            @pl.when(step == fs - 1)
            def finish():
                sums_ref[...] = jnp.zeros_like(sums_ref)

                def work(rows, first):
                    grad = total[rows, :]
                    attn = attn_ref[rows, :]
                    middle = tokens_ref[rows, :].astype(f32) + mods_ref[2:3, :] * attn
                    normal, rate = norm_parts(middle)
                    alive = alive_rows(first, grad.shape[0], live_ref[0])
                    d_middle = alive * cot_ref[rows, :].astype(f32) + norm_back(
                        normal, rate, grad * (1.0 + mods_ref[4:5, :])
                    )
                    d_middle_ref[rows, :] = d_middle
                    d_attn = (mods_ref[2:3, :] * d_middle).astype(bf16)
                    d_attn_ref[rows, :] = d_attn
                    for i, each in enumerate(
                        (d_middle * attn, grad, grad * normal, d_attn.astype(f32))
                    ):
                        sums_ref[i : i + 1, :] += jnp.sum(each, axis=0, keepdims=True)

                chunks(slots, 32, work)
                d_attn_turned_ref[...] = d_attn_ref[...].astype(f32).T.astype(bf16)
                d_attended = lax.dot_general(
                    d_attn_ref[...],
                    out_ref[...],
                    (((1,), (1,)), ((), ())),
                    preferred_element_type=f32,
                )
                d_attended_turned_ref[...] = d_attended.astype(bf16).astype(f32).T

        def whole(shape):
            return pl.BlockSpec(shape, lambda j, live_ref: (0,) * len(shape))

        return pl.pallas_call(
            kernel,
            out_shape=[
                jax.ShapeDtypeStruct((slots, width), f32),
                jax.ShapeDtypeStruct((width, slots), bf16),
                jax.ShapeDtypeStruct((width, slots), f32),
                jax.ShapeDtypeStruct((8, width), f32),
            ],
            grid_spec=pltpu.PrefetchScalarGridSpec(
                num_scalar_prefetch=1,
                grid=(fs,),
                in_specs=[
                    pl.BlockSpec((slots, tile), lambda j, live_ref: (0, j)),
                    pl.BlockSpec((width, tile), lambda j, live_ref: (0, j)),
                    whole((width, width)),
                    whole((slots, width)),
                    whole((slots, width)),
                    whole((slots, width)),
                    whole(mods.shape),
                ],
                out_specs=[
                    whole((slots, width)),
                    whole((width, slots)),
                    whole((width, slots)),
                    whole((8, width)),
                ],
                scratch_shapes=[
                    pltpu.VMEM((slots, width), f32),
                    pltpu.VMEM((slots, width), bf16),
                ],
            ),
            cost_estimate=cost(12),
            compiler_params=params(60),
        )(live, d_pre, up_full, out_full, attn_out, tokens_own, cotangent_own, mods)

    def first_back(d_turned, qkv_full, tokens_own, d_middle, mods):
        slots, width = d_middle.shape

        def kernel(d_ref, w_ref, tokens_ref, d_middle_ref, mods_ref, grad_ref, sums_ref, total):
            sums_ref[...] = jnp.zeros_like(sums_ref)
            for part in range(3):
                cols = slice(part * width, (part + 1) * width)
                d_part = d_ref[cols, :].astype(f32).T
                if part != 1:
                    row = 2 + part // 2
                    sums_ref[row : row + 1, :] = jnp.sum(d_part, axis=0, keepdims=True)
                product = lax.dot_general(
                    d_part.astype(bf16),
                    w_ref[:, cols],
                    (((1,), (1,)), ((), ())),
                    preferred_element_type=f32,
                )
                if part == 0:
                    total[...] = product
                else:
                    total[...] += product

            def work(rows, unused):
                grad = total[rows, :]
                normal, rate = norm_parts(tokens_ref[rows, :].astype(f32))
                sums_ref[0:1, :] += jnp.sum(grad, axis=0, keepdims=True)
                sums_ref[1:2, :] += jnp.sum(grad * normal, axis=0, keepdims=True)
                grad_ref[rows, :] = (
                    d_middle_ref[rows, :]
                    + norm_back(normal, rate, grad * (1.0 + mods_ref[1:2, :]))
                ).astype(bf16)

            chunks(slots, 32, work)

        return pl.pallas_call(
            kernel,
            out_shape=[
                jax.ShapeDtypeStruct((slots, width), bf16),
                jax.ShapeDtypeStruct((8, width), f32),
            ],
            in_specs=[vmem] * 5,
            out_specs=[vmem] * 2,
            scratch_shapes=[pltpu.VMEM((slots, width), f32)],
            cost_estimate=cost(9),
            compiler_params=params(60),
        )(d_turned, qkv_full, tokens_own, d_middle, mods)

    def output_rows(
        activated, down_full, bias_down, tokens_own, attn_out, cotangent_own, d_mlp, mods, live
    ):
        slots, hidden = activated.shape
        width = attn_out.shape[1]
        tile = hidden // fs

        def kernel(
            live_ref,
            act_ref,
            down_ref,
            bias_ref,
            tokens_ref,
            attn_ref,
            cot_ref,
            d_mlp_ref,
            mods_ref,
            out_ref,
            sums_ref,
            total,
        ):
            step = pl.program_id(0)
            part = jnp.dot(act_ref[...], down_ref[...], preferred_element_type=f32)

            @pl.when(step == 0)
            def start():
                total[...] = part

            @pl.when(step > 0)
            def add():
                total[...] += part

            @pl.when(step == fs - 1)
            def finish():
                sums_ref[...] = jnp.zeros_like(sums_ref)

                def work(rows, first):
                    mlp_out = total[rows, :] + bias_ref[...]
                    middle = (
                        tokens_ref[rows, :].astype(f32) + mods_ref[2:3, :] * attn_ref[rows, :]
                    )
                    alive = alive_rows(first, mlp_out.shape[0], live_ref[0])
                    out_ref[rows, :] = (alive * (middle + mods_ref[5:6, :] * mlp_out)).astype(bf16)
                    d_gate = alive * cot_ref[rows, :].astype(f32) * mlp_out
                    sums_ref[0:1, :] += jnp.sum(d_gate, axis=0, keepdims=True)
                    sums_ref[1:2, :] += jnp.sum(
                        d_mlp_ref[rows, :].astype(f32), axis=0, keepdims=True
                    )

                chunks(slots, 32, work)

        def whole(shape):
            return pl.BlockSpec(shape, lambda j, live_ref: (0,) * len(shape))

        return pl.pallas_call(
            kernel,
            out_shape=[
                jax.ShapeDtypeStruct((slots, width), bf16),
                jax.ShapeDtypeStruct((8, width), f32),
            ],
            grid_spec=pltpu.PrefetchScalarGridSpec(
                num_scalar_prefetch=1,
                grid=(fs,),
                in_specs=[
                    pl.BlockSpec((slots, tile), lambda j, live_ref: (0, j)),
                    pl.BlockSpec((tile, width), lambda j, live_ref: (j, 0)),
                    whole((1, width)),
                    whole((slots, width)),
                    whole((slots, width)),
                    whole((slots, width)),
                    whole((slots, width)),
                    whole(mods.shape),
                ],
                out_specs=[whole((slots, width)), whole((8, width))],
                scratch_shapes=[pltpu.VMEM((slots, width), f32)],
            ),
            cost_estimate=cost(6),
            compiler_params=params(60),
        )(
            live,
            activated,
            down_full,
            bias_down.reshape(1, width),
            tokens_own,
            attn_out,
            cotangent_own,
            d_mlp,
            mods,
        )

    def column_grad(where, lefts, rights, start, stop):
        slots, n = rights[0].shape[1], (stop - start) // 2
        right_rows = rights[0].shape[0]
        width = lefts[0].shape[1]
        tile = width // 3
        half = slots // 2

        def kernel(where_ref, x0, x1, x2, x3, x4, y0, y1, y2, y3, keep_ref, send_ref):
            core = where_ref[0]
            for out_ref, first in ((keep_ref, core * n), (send_ref, (1 - core) * n)):
                rows = pl.ds(pl.multiple_of(start + first, 16), n)
                total = None
                for x, y, cols in (
                    (x0, y0, slice(None)),
                    (x1, y1, slice(None)),
                    (x2, y2, slice(None)),
                    (x3, y3, slice(0, half)),
                    (x4, y3, slice(half, slots)),
                ):
                    part = jnp.dot(y[rows, cols], x[...], preferred_element_type=f32)
                    total = part if total is None else total + part
                out_ref[...] = total

        left_specs = [
            pl.BlockSpec((left.shape[0], tile), lambda i, where_ref: (0, i)) for left in lefts
        ]
        right_spec = pl.BlockSpec((right_rows, slots), lambda i, where_ref: (0, 0))
        out_spec = pl.BlockSpec((n, tile), lambda i, where_ref: (0, i))
        return pl.pallas_call(
            kernel,
            out_shape=[jax.ShapeDtypeStruct((n, width), f32)] * 2,
            grid_spec=pltpu.PrefetchScalarGridSpec(
                num_scalar_prefetch=1,
                grid=(width // tile,),
                in_specs=left_specs + [right_spec] * 4,
                out_specs=[out_spec] * 2,
            ),
            cost_estimate=cost(7),
            compiler_params=params(60),
        )(where, *lefts, *rights)

    def split_grad(where, keep, got):
        n, width = keep.shape
        rows = width // fs
        padded = -(-n // 128) * 128

        def kernel(where_ref, keep_ref, got_ref, own_ref, *rest):
            send_refs, turned = rest[:-1], rest[-1]
            for first in range(0, width, 128):
                total = keep_ref[:, first : first + 128] + got_ref[:, first : first + 128]
                if padded > n:
                    total = jnp.concatenate([total, jnp.zeros((padded - n, 128), f32)], axis=0)
                turned[first : first + 128, :] = total.T[:, :n]
            z = where_ref[0]
            own_ref[...] = turned[pl.ds(pl.multiple_of(z * rows, 16), rows), :]
            for k, send_ref in enumerate(send_refs):
                target = lax.rem(z + k + 1, fs)
                block = turned[pl.ds(pl.multiple_of(target * rows, 16), rows), :]
                send_ref[...] = block.astype(bf16)

        whole = pl.BlockSpec(memory_space=pltpu.VMEM)
        return pl.pallas_call(
            kernel,
            out_shape=[jax.ShapeDtypeStruct((rows, n), f32)]
            + [jax.ShapeDtypeStruct((rows, n), bf16)] * (fs - 1),
            in_specs=[pl.BlockSpec(memory_space=pltpu.SMEM), whole, whole],
            out_specs=[whole] * fs,
            scratch_shapes=[pltpu.VMEM((width, n), f32)],
            cost_estimate=cost(4),
            compiler_params=params(60),
        )(where, keep, got)

    def split_rows(where, keep, got):
        count, rows, width = keep.shape

        def kernel(where_ref, keep_ref, got_ref, own_ref, *send_refs):
            z = where_ref[0]
            own_ref[...] = keep_ref[z] + got_ref[z]
            for k, send_ref in enumerate(send_refs):
                target = lax.rem(z + k + 1, count)
                send_ref[...] = (keep_ref[target] + got_ref[target]).astype(bf16)

        return pl.pallas_call(
            kernel,
            out_shape=[jax.ShapeDtypeStruct((rows, width), f32)]
            + [jax.ShapeDtypeStruct((rows, width), bf16)] * (count - 1),
            in_specs=[smem, vmem, vmem],
            out_specs=[vmem] * count,
            cost_estimate=cost(3),
            compiler_params=params(60),
        )(where, keep, got)

    def down_columns(parts):
        rows, width = parts[0].shape
        cols = width // BOX

        def kernel(*refs):
            total = refs[0][...]
            for ref in refs[1:-1]:
                total = total + ref[...].astype(f32)
            for block in range(BOX):
                refs[-1][block] = total[:, block * cols : (block + 1) * cols]

        return pl.pallas_call(
            kernel,
            out_shape=jax.ShapeDtypeStruct((BOX, rows, cols), f32),
            in_specs=[vmem] * len(parts),
            out_specs=vmem,
            cost_estimate=cost(2),
            compiler_params=params(60),
        )(*parts)

    def row_grad(where, lefts, rights):
        rows = lefts[0].shape[0] // fs
        slots, n = lefts[0].shape[1], rows // 2
        width = rights[0].shape[1]
        half = slots // 2

        def kernel(where_ref, x0, x1, x2, x3, y0, y1, y2, y3, y4, keep_ref, send_ref):
            core = where_ref[0]
            for out_ref, first in ((keep_ref, core * n), (send_ref, (1 - core) * n)):
                lines = pl.ds(pl.multiple_of(first, 16), n)
                total = None
                for x, y, cols in (
                    (x0, y0, slice(None)),
                    (x1, y1, slice(None)),
                    (x2, y2, slice(None)),
                    (x3, y3, slice(0, half)),
                    (x3, y4, slice(half, slots)),
                ):
                    part = jnp.dot(x[lines, cols], y[...], preferred_element_type=f32)
                    total = part if total is None else total + part
                out_ref[0] = total

        left_spec = pl.BlockSpec((rows, slots), lambda i, where_ref: (i, 0))
        right_specs = [
            pl.BlockSpec((right.shape[0], width), lambda i, where_ref: (0, 0))
            for right in rights
        ]
        out_spec = pl.BlockSpec((1, n, width), lambda i, where_ref: (i, 0, 0))
        return pl.pallas_call(
            kernel,
            out_shape=[jax.ShapeDtypeStruct((fs, n, width), f32)] * 2,
            grid_spec=pltpu.PrefetchScalarGridSpec(
                num_scalar_prefetch=1,
                grid=(fs,),
                in_specs=[left_spec] * 4 + right_specs,
                out_specs=[out_spec] * 2,
            ),
            cost_estimate=cost(6),
            compiler_params=params(60),
        )(where, *lefts, *rights)

    def body(
        tokens,
        condition,
        grid_sizes,
        w_ada,
        w_qkv,
        w_out,
        w_up,
        w_down,
        b_ada,
        b_qv,
        b_out,
        b_up,
        b_down,
        cotangent,
    ):
        slots, width = tokens.shape[1:]
        heads = width // HEAD_DIM
        hidden = w_up.shape[1]
        rank = lax.axis_index("dp")
        z = lax.axis_index("fsdp")
        place = lax.rem(rank, BOX)
        group = lax.div(rank, BOX)
        core = place & 1
        chip = place >> 1
        side = (chip ^ (chip >> 1)) & 1
        near = 2 * side + core
        far = 2 * (1 - side) + core
        where = jnp.stack(
            [lax.rem(z - k + fs, fs) for k in range(fs)] + [near, far, near ^ 1, far ^ 1]
        ).astype(jnp.int32)
        where_core = core.reshape(1).astype(jnp.int32)
        where_wide = jnp.stack(
            [lax.rem(z - k + fs, fs) for k in range(fs)] + [core] + [chip ^ k for k in range(4)]
        ).astype(jnp.int32)

        cond_wide = condition.astype(f32)
        gate = jax.nn.sigmoid(cond_wide)
        cond_act = (cond_wide * gate).astype(bf16)

        def quarter_of(shard):
            return pick(in_blocks(shard), near)

        cond_rows = ring_gather(cond_act)
        raw = jnp.concatenate([tokens[0], cotangent[0]], axis=1)
        raw_near = chip_near(raw)
        qkv_helds = [ring_send(quarter_of(w_qkv), 1)]
        mid_rows = jnp.concatenate(
            [pick(in_blocks(w_out), chip), pick(in_blocks(w_up), chip)], axis=-1
        )
        mid_width = mid_rows.shape[-1]
        mid_part = -(-mid_width // 256) * 128
        mid_start = jnp.where(core == 0, 0, mid_width - mid_part)
        mid_eighth = lax.dynamic_slice_in_dim(mid_rows, mid_start, mid_part, 2)
        down_quarter = quarter_of(w_down)
        ada_shard = b_ada.shape[0]
        bias_ada = lax.dynamic_update_slice_in_dim(
            jnp.zeros((fs * ada_shard,), f32), b_ada.astype(f32), z * ada_shard, 0
        ).reshape(6, width)
        small = jnp.concatenate([b_qv, b_out, b_down, b_up]).astype(f32).reshape(-1, width)
        cond_rows, bias_ada, small, mid_eighth, down_quarter = gated(
            (cond_rows, bias_ada, small, mid_eighth, down_quarter)
        )

        rows_z = width // fs
        conds = jnp.concatenate(cond_rows)
        conds_z = lax.dynamic_slice_in_dim(conds, z * rows_z, rows_z, 1)
        partials = modulation_parts(conds_z, w_ada, bias_ada, small)
        partials = [partials[0]] + [ring_send(partials[k], fs - k) for k in range(1, fs)]
        qkv_helds.append(ring_send(qkv_helds[-1], 1))
        partials, qkv_helds, raw_near = gated((partials, qkv_helds, raw_near))

        live = (grid_sizes[0, 0] * grid_sizes[0, 1]).reshape(1)
        mods, head = modulation_rows(partials, live)
        heads_got = [box_send(head, bits) for bits in (2, 4, 6)]
        raw_far = chip_far(raw_near)
        qkv_helds.append(ring_send(qkv_helds[-1], 1))
        mods, head, heads_got, raw_far, qkv_helds = gated(
            (mods, head, heads_got, raw_far, qkv_helds)
        )

        qkv_mine = jnp.stack(qkv_helds)
        qkv_other = side_send(qkv_mine)
        qkv_mine_got = box_send(qkv_mine, 1)
        qkv_other_got = box_send(qkv_other, 1)
        mid_helds = [ring_send(after(mid_eighth, qkv_mine), 1)]
        mid_helds.append(ring_send(mid_helds[-1], 1))
        (normed,), (d_mlp,) = other_heads((raw,), (0,), (head,))
        bias_rows = [each[6:].reshape(-1) for each in partials]
        bias_rows = jnp.stack(bias_rows + bias_rows)
        biases = lax.dynamic_slice_in_dim(bias_rows, lax.rem(fs - z, fs), fs, 0)
        ends = [0]
        for bias in (b_qv, b_out, b_down, b_up):
            ends.append(ends[-1] + bias.shape[0])
        bias_qv, bias_out, bias_down, bias_up = [
            biases[:, ends[i] : ends[i + 1]].reshape(-1) for i in range(4)
        ]
        (
            qkv_mine,
            qkv_other,
            qkv_mine_got,
            qkv_other_got,
            mid_helds,
            normed,
            d_mlp,
            bias_qv,
            bias_out,
            bias_down,
            bias_up,
        ) = gated(
            (
                qkv_mine,
                qkv_other,
                qkv_mine_got,
                qkv_other_got,
                mid_helds,
                normed,
                d_mlp,
                bias_qv,
                bias_out,
                bias_down,
                bias_up,
            )
        )

        last = fs - 1

        def in_order(array):
            return [(array, k) for k in range(last)]

        mid_helds.append(ring_send(mid_helds[-1], 1))
        turned, qkv_full = projection(
            where,
            normed,
            w_qkv,
            [in_order(each) for each in (qkv_mine, qkv_other, qkv_mine_got, qkv_other_got)],
            bias_qv.reshape(2, width),
        )
        turned, qkv_full, mid_helds = gated((turned, qkv_full, mid_helds))

        mid_mine = jnp.concatenate(mid_helds)
        mid_near = chip_near(mid_mine)
        mid_got = [box_send(mid_mine, 1)]
        down_helds = [ring_send(after(down_quarter, mid_mine), 1)]
        attended = attention(turned, live)
        normed_box, d_mlp_box = other_heads(
            (*raw_near, *raw_far), (0, 0, 0, slots // 2), (*heads_got, heads_got[2])
        )
        normed_box, d_mlp_box = [normed, *normed_box], [d_mlp, *d_mlp_box]
        attended, mid_mine, mid_near, mid_got, down_helds, normed_box, d_mlp_box = gated(
            (attended, mid_mine, mid_near, mid_got, down_helds, normed_box, d_mlp_box)
        )

        mid_far = chip_far(mid_near)
        mid_got += [box_send(each, 1) for each in mid_near]
        down_helds.append(ring_send(down_helds[-1], 1))
        attended, mid_far, mid_got, down_helds = gated((attended, mid_far, mid_got, down_helds))

        mid_got += [box_send(each, 1) for each in mid_far]
        down_helds.append(ring_send(down_helds[-1], 1))
        down_others = [side_send(each) for each in down_helds[:-1]]
        attended_near = chip_near(attended)
        attn_out, normed_two, pre_act, activated, act_blocks, out_full, up_full = middle_forward(
            where_wide,
            attended,
            tokens[0],
            [w_out, w_up],
            ((mid_mine, *mid_near, *mid_far), mid_got),
            bias_out,
            bias_up,
            mods,
        )
        attended_near, down_helds, down_others, act_blocks, normed_two = gated(
            (attended_near, down_helds, down_others, act_blocks, normed_two)
        )

        down_others.append(side_send(down_helds[-1]))
        down_helds_got = [box_send(each, 1) for each in down_helds]
        down_others_got = [box_send(each, 1) for each in down_others]
        act_blocks, down_helds, down_others, down_helds_got, down_others_got = gated(
            (act_blocks, down_helds, down_others, down_helds_got, down_others_got)
        )

        act_box = chip_exchange(act_blocks, chip)
        normed_two_near = chip_near(normed_two)
        d_pre, d_pre_turned, d_pre_sums, down_full = hidden_back(
            where,
            d_mlp,
            w_down,
            [
                [(each, None) for each in kind]
                for kind in (down_helds, down_others, down_helds_got, down_others_got)
            ],
            pre_act,
        )

        def column_blocks(grad_t):
            n = grad_t.shape[0] // dp
            blocks = grad_t.reshape(groups, BOX, n, slots).transpose(1, 0, 2, 3)
            return blocks.reshape(BOX // 2, 2 * groups * n, slots)

        d_pre_blocks = column_blocks(d_pre_turned)
        d_pre, d_pre_blocks, act_box, normed_two_near = gated(
            (d_pre, d_pre_blocks, act_box, normed_two_near)
        )

        d_pre_box = chip_exchange(d_pre_blocks, chip)
        keep_down, send_down = row_grad(where_core, act_box, d_mlp_box)
        got_down = box_send(send_down, 1)
        d_middle, d_attn_turned, d_attended_turned, middle_sums = middle_back(
            d_pre, up_full, out_full, attn_out, tokens[0], cotangent[0], mods, live
        )
        d_attn_blocks = column_blocks(d_attn_turned)
        d_projected = attention_back(turned, d_attended_turned, live)
        d_projected_blocks = column_blocks(d_projected)
        d_projected, d_projected_blocks, d_attn_blocks, d_pre_box, got_down = gated(
            (d_projected, d_projected_blocks, d_attn_blocks, d_pre_box, got_down)
        )

        def after_core(grad_parts):
            grad, *sends = split_grad(where[:1], *grad_parts)
            return [grad] + [ring_send(sent, k + 1) for k, sent in enumerate(sends)]

        def own_block_cols(parts):
            grad = sum((each.astype(f32) for each in parts[1:]), parts[0])
            rows, cols = grad.shape
            grad = grad.reshape(rows, groups, cols // groups)
            return group_sum(grad.transpose(1, 0, 2), group)

        last_blocks = jnp.concatenate([d_projected_blocks, d_attn_blocks], axis=1)
        last_box = chip_exchange(last_blocks, chip)
        normed_two_far = chip_far(normed_two_near)
        attended_far = chip_far(attended_near)
        attended_box = [attended, *attended_near, *attended_far]
        normed_two_box = [normed_two, *normed_two_near, *normed_two_far]
        keep_up, send_up = column_grad(
            where_core, normed_two_box, d_pre_box, 0, d_pre_box[0].shape[0]
        )
        got_up = box_send(send_up, 1)
        down_parts = split_rows(where[:1], keep_down, got_down)
        down_parts = [down_parts[0]] + [
            ring_send(sent, k + 1) for k, sent in enumerate(down_parts[1:])
        ]
        grad_tokens, first_sums = first_back(d_projected, qkv_full, tokens[0], d_middle, mods)
        last_box, attended_box, down_parts, first_sums, keep_up, got_up = gated(
            (last_box, attended_box, down_parts, first_sums, keep_up, got_up)
        )

        cut = d_projected_blocks.shape[1]
        keep_qkv, send_qkv = column_grad(where_core, normed_box, last_box, 0, cut)
        got_qkv = box_send(send_qkv, 1)
        keep_out, send_out = column_grad(
            where_core, attended_box, last_box, cut, last_box[0].shape[0]
        )
        got_out = box_send(send_out, 1)
        up_parts = after_core((keep_up, got_up))
        output, output_sums = output_rows(
            activated,
            down_full,
            bias_down,
            tokens[0],
            attn_out,
            cotangent[0],
            d_mlp,
            mods,
            live,
        )
        d_mod = jnp.concatenate([first_sums[0:2], middle_sums[0:3], output_sums[0:1]])
        cond_row = cond_act.astype(f32)
        images = jnp.concatenate([d_mod, cond_row, cond_row]).astype(bf16)
        total = jnp.concatenate(
            [
                first_sums[2:4],
                middle_sums[3:4],
                output_sums[1:2],
                d_pre_sums.reshape(hidden // width, width),
            ]
        )
        images_near = jnp.stack(ring_gather(images))
        totals = ring_gather(total)
        got_qkv, got_out, up_parts, images_near, totals = gated(
            (got_qkv, got_out, up_parts, images_near, totals)
        )

        qkv_parts = after_core((keep_qkv, got_qkv))
        out_parts = after_core((keep_out, got_out))
        down_rows = down_parts[0].shape[0]
        if groups == 1:
            down_blocks = down_columns(down_parts)
            parts = lax.all_to_all(down_blocks, "dp", 0, 0, tiled=True)
        else:
            grad_down = own_block_cols(down_parts)
            down_blocks = grad_down.reshape(down_rows, BOX, width // dp).transpose(1, 0, 2)
            parts = [pick(down_blocks, place)] + [
                box_send(pick(down_blocks, place ^ k), k) for k in range(1, BOX)
            ]
            parts = jnp.stack(parts)
            parts = jnp.stack([pick(parts, place ^ k) for k in range(BOX)])
        grad_w_down = parts.reshape(BOX * down_rows, width // dp)
        grad_w_up = own_block_cols(up_parts)
        grad_w_out = own_block_cols(out_parts)
        grad_w_qkv = own_block_cols(qkv_parts)

        images, total = images_near, sum(totals[1:], totals[0])
        for bits in (1, 2, 4):
            images = jnp.concatenate([images, box_send(images, bits)])
            total = total + box_send(total, bits)
        images_box, total_box = images, total
        for k in range(1, groups):
            images = jnp.concatenate([images, group_send(images_box, k)])
            total = total + group_send(total_box, k)
        conds_all = lax.dynamic_slice_in_dim(images[:, 6], z * rows_z, rows_z, 1)
        d_mod_all = images[:, :6]
        ada_cols = 6 * width // dp
        grad_w_ada = lax.dot_general(
            conds_all,
            lax.dynamic_slice_in_dim(
                d_mod_all.reshape(dp * fs, 6 * width), rank * ada_cols, ada_cols, 1
            ),
            (((0,), (0,)), ((), ())),
            preferred_element_type=f32,
        )
        d_conds = lax.dot_general(
            images_near[:, :6].reshape(fs, 6 * width),
            w_ada,
            (((1,), (1,)), ((), ())),
            preferred_element_type=f32,
        )
        cond_parts = [d_conds[0]] + [ring_send(d_conds[k], fs - k) for k in range(1, fs)]
        twice = jnp.stack(cond_parts + cond_parts)
        d_cond_act = lax.dynamic_slice_in_dim(twice, lax.rem(fs - z, fs), fs, 0).reshape(-1)
        grad_condition = d_cond_act[None] * gate * (1.0 + cond_wide * (1.0 - gate))

        def shard_of(rows):
            return pick(rows.reshape(fs, -1), z)

        grads_bias = [
            shard_of(jnp.sum(d_mod_all.astype(f32), axis=0)),
            shard_of(total[:2]),
            shard_of(total[2]),
            shard_of(total[4:]),
            shard_of(total[3]),
        ]
        return (
            output[None],
            grad_tokens[None],
            grad_condition,
            grad_w_ada,
            grad_w_qkv,
            grad_w_out,
            grad_w_up,
            grad_w_down,
            *grads_bias,
        )

    return body


def solution(mesh):
    return jax.shard_map(
        make_body(mesh.shape["dp"], mesh.shape["fsdp"]),
        mesh=mesh,
        in_specs=(
            P(("dp", "fsdp"), None, None),
            P(("dp", "fsdp"), None),
            P(("dp", "fsdp"), None),
            P("fsdp", None),
            P("fsdp", None),
            P("fsdp", None),
            P("fsdp", None),
            P("fsdp", None),
            P("fsdp"),
            P("fsdp"),
            P("fsdp"),
            P("fsdp"),
            P("fsdp"),
            P(("dp", "fsdp"), None, None),
        ),
        out_specs=(
            P(("dp", "fsdp"), None, None),
            P(("dp", "fsdp"), None, None),
            P(("dp", "fsdp"), None),
            P("fsdp", "dp"),
            P("fsdp", "dp"),
            P("fsdp", "dp"),
            P("fsdp", "dp"),
            P("fsdp", "dp"),
            P("fsdp"),
            P("fsdp"),
            P("fsdp"),
            P("fsdp"),
            P("fsdp"),
        ),
        check_vma=False,
    )
```

time: 586 us -> 501 us (0.85); the launches traced: 575 us -> 496 us
  Pallas kernels: 48.9 us -> 172 us
  local copies, waits for them, and re-layouts: 117 us -> 37 us
  matrix products: 61.4 us -> 4.56 us
  other arithmetic: 53.6 us -> 8.25 us
  waiting for transfers between devices: 154 us -> 143 us
    pallas_call x3 -> x14, Pallas kernels: 16.5 us -> 132 us  [the longest x1 20.1 us: middle_forward(): pl.pallas_call(kernel, out_shape=[jax.ShapeDtypeStruct((slots, width), f3...]
    dot_general x15 -> x0, matrix products: 58.9 us -> none  [the longest x1 11.9 us: body(): lax.dot_general(d_mlp, down_full, (((1,), (1,)), ((), ())), preferred_ele...]
    unnamed x281 -> x124, local copies, waits for them, and re-layouts: 47.4 us -> 10.7 us
    convert_element_type x18 -> x0, other arithmetic: 21.8 us -> none  [the longest x1 6.48 us: body(): d_pre = gelu_pull(d_act)[0].astype(bf16)]
    ppermute x36, starting transfers between devices: 65.6 us -> 50.7 us  [ring_send(): return lax.ppermute(x, 'fsdp', [(i, (i + hops) % fs) for i in range(fs)])]
    ppermute x4, waiting for transfers between devices: 9.91 us -> 24.2 us  [side_send(): lax.ppermute(x, 'dp', [(i, i ^ (4 if i & 1 else 2)) for i in range(dp)])]
    ppermute x36, waiting for transfers between devices: 94.6 us -> 80.8 us  [ring_send(): return lax.ppermute(x, 'fsdp', [(i, (i + hops) % fs) for i in range(fs)])]
    ppermute x51, waiting for transfers between devices: 49.9 us -> 37.8 us  [box_send(): return lax.ppermute(x, 'dp', [(i, i ^ bits) for i in range(dp)])]
  transfers between devices with their start and end apart: 92 -> 92, of which waited for: 24 -> 23; matrix products, arithmetic and copies ran while one was open for 32% -> 7% of each run, Pallas kernels for 9% -> 30%
where the time goes in v3:
time: 501 us; the launch traced here: 496 us
  Pallas kernels  172 us (34%)
  waiting for transfers between devices  143 us (29%)
  starting transfers between devices  128 us (26%)
  local copies, waits for them, and re-layouts  37 us (7%)
  other arithmetic  8.25 us (2%)
    ppermute x36, waiting for transfers between devices, ring_send(): return lax.ppermute(x, 'fsdp', [(i, (i + hops) % fs) for i in range(fs)])  80.8 us
    ppermute x51, starting transfers between devices, box_send(): return lax.ppermute(x, 'dp', [(i, i ^ bits) for i in range(dp)])  68.5 us
    ppermute x36, starting transfers between devices, ring_send(): return lax.ppermute(x, 'fsdp', [(i, (i + hops) % fs) for i in range(fs)])  50.7 us
    ppermute x51, waiting for transfers between devices, box_send(): return lax.ppermute(x, 'dp', [(i, i ^ bits) for i in range(dp)])  37.8 us
    ppermute x4, waiting for transfers between devices, side_send(): lax.ppermute(x, 'dp', [(i, i ^ (4 if i & 1 else 2)) for i in range(dp)])  24.2 us
    pallas_call x3, Pallas kernels, column_grad(): pl.pallas_call(kernel, out_shape=[jax.ShapeDtypeStruct((n, width), f32)]...  20.2 us
    pallas_call x1, Pallas kernels, middle_forward(): pl.pallas_call(kernel, out_shape=[jax.ShapeDtypeStruct((slots, width), f3...  20.1 us
    pallas_call x1, Pallas kernels, hidden_back(): pl.pallas_call(kernel, out_shape=[jax.ShapeDtypeStruct((slots, hidden), b...  16 us
  transfers between devices with their start and end apart: 92, of which 23 were waited for; matrix products, arithmetic and copies ran while one was open for 7% of the time, Pallas kernels for 30%

profile of v3, /device:TPU:25, one launch (start us, length us, event | category | flops | bytes accessed | tf_op | source)
XLA Modules:
  0.0 495.8 jit_solution(1558462566754716312)
XLA Ops:
  8.2 2.2 collective-permute-start.6
  14.7 4.7 collective-permute-done.6
  19.4 3.9 collective-permute-start.7
  25.5 3.5 shard_map.237
  29.3 4.9 collective-permute-done.3.refs_1_
  34.3 2.4 collective-permute-start.5
  41.0 3.4 collective-permute-start.15
  50.2 1.9 collective-permute-done.10.refs_4_
  52.0 1.7 collective-permute-start.12
  53.8 2.6 collective-permute-done.12.refs_6_.refs_7_
  58.3 5.9 %collective-permute-start.17 = (bf16[3,9,8,3456]{3,2,1,0:T(8,128)(2,1)S(1)}, bf16[3,9,8,3456]{3,2,1,0:T(8,128)(2,1)}, u32[]{:S(2)}, u32[]{:S(2)}) collective-permute-start(bf16[3,9,8,3456]{3,2,1,0:T(8,128)(2,1)S(1)} %pad_maximum_fusion.refs_0_), channel_id=1, source_target_pairs={{0,4},{4,0},{8,12},{12,8},{16,20},{20,16},{24,28},{28,24},{1,5},{5... | collective-permute-start | bytes 4478984 | tf_op jit(solution)/shard_map/ppermute | solution.py:57
  64.3 11.6 %collective-permute-done.16.refs_1_ = bf16[3,9,8,3456]{3,2,1,0:T(8,128)(2,1)} collective-permute-done((bf16[3,9,8,3456]{3,2,1,0:T(8,128)(2,1)S(1)}, bf16[3,9,8,3456]{3,2,1,0:T(8,128)(2,1)}, u32[]{:S(2)}, u32[]{:S(2)}) %collective-permute-start.16) | collective-permute-done | bytes 1493024 | tf_op jit(solution)/shard_map/ppermute | solution.py:60
  75.9 6.9 %collective-permute-start.18 = (bf16[3,9,8,3456]{3,2,1,0:T(8,128)(2,1)}, bf16[3,9,8,3456]{3,2,1,0:T(8,128)(2,1)}, u32[]{:S(2)}, u32[]{:S(2)}) collective-permute-start(bf16[3,9,8,3456]{3,2,1,0:T(8,128)(2,1)} %collective-permute-done.16.refs_1_), channel_id=1, source_target_pairs={{0,4},{4,0},{8,12},{12,8},{16,20},{20,16},{24,28},{28,24},{1,5},{5... | collective-permute-start | bytes 4478984 | tf_op jit(solution)/shard_map/ppermute | solution.py:57
  83.6 3.1 collective-permute-start.19
  87.8 8.5 %collective-permute-done.19 = bf16[9,8,2944]{2,1,0:T(8,128)(2,1)S(1)} collective-permute-done((bf16[9,8,2944]{2,1,0:T(8,128)(2,1)}, bf16[9,8,2944]{2,1,0:T(8,128)(2,1)S(1)}, u32[]{:S(2)}, u32[]{:S(2)}) %collective-permute-start.19) | collective-permute-done | bytes 423968 | tf_op jit(solution)/shard_map/ppermute | solution.py:63
  96.3 3.9 collective-permute-start.20
  101.1 3.9 shard_map.239
  105.0 3.5 collective-permute-done.20
  109.1 4.0 collective-permute-start.21
  113.1 9.4 %shard_map.240 = (f32[3456,256]{1,0:T(8,128)}, bf16[4,4,9,8,3456]{4,3,2,1,0:T(8,128)(2,1)}) custom-call(s32[8]{0:T(128)} %stack.106.where_ref, bf16[256,1152]{1,0:T(8,128)(2,1)} %get-tuple-element.333.normed_ref.x0, f32[2,1152]{1,0:T(2,128)} %reshape.198.bias_ref, bf16[4,9,8,3456]{3,2,1,0:T(8,128)(2,1)} %bitcast.131, bf16[3,9,8,3456]{3,2,1,0:T(8,128)(2,1)} %copy-done.2, ...), custom_call_target="tpu_custom_call" | custom-call | flops 5500000256 | bytes 17600000 | tf_op jit(solution)/shard_map/pallas_call | solution.py:301
  126.2 2.5 collective-permute-start.24
  128.8 2.6 collective-permute-start.25
  131.4 8.8 %shard_map.242 = (bf16[256,1152]{1,0:T(8,128)(2,1)}, bf16[256,1152]{1,0:T(8,128)(2,1)}, bf16[128,1152]{1,0:T(8,128)(2,1)}, bf16[128,1152]{1,0:T(8,128)(2,1)}, bf...) custom-call(bf16[256,2304]{1,0:T(8,128)(2,1)} %collective-permute-do, ...), custom_call_target="tpu_custom_call" | custom-call | flops 4000000000 | bytes 12800000 | tf_op jit(solution)/shard_map/pallas_call | solution.py:194
  140.2 12.5 %shard_map.241.attended_ref.x0 = bf16[256,1152]{1,0:T(8,128)(2,1)} custom-call(s32[1]{0:T(128)} %bitcast.live_ref, f32[3456,256]{1,0:T(8,128)} %get-tuple-element.246.turned_ref), custom_call_target="tpu_custom_call" | custom-call | flops 5500000256 | bytes 17600000 | tf_op jit(solution)/shard_map/pallas_call | solution.py:352
  152.7 3.0 collective-permute-start.28
  155.8 2.0 collective-permute-start.30
  160.3 13.3 %collective-permute-done.26.refs_5_ = bf16[13,8,2944]{2,1,0:T(8,128)(2,1)} collective-permute-done((bf16[13,8,2944]{2,1,0:T(8,128)(2,1)S(1)}, bf16[13,8,2944]{2,1,0:T(8,128)(2,1)}, u32[]{:S(2)}, u32[]{:S(2)}) %collective-permute-start.26) | collective-permute-done | bytes 612384 | tf_op jit(solution)/shard_map/ppermute | solution.py:57
  174.8 1.9 collective-permute-start.32
  184.9 20.1 %shard_map.243 = (f32[256,1152]{1,0:T(8,128)}, bf16[256,1152]{1,0:T(8,128)(2,1)}, f32[256,4608]{1,0:T(8,128)}, bf16[256,4608]{1,0:T(8,128)(2,1)}, bf16[4,1152,25...) custom-call(s32[9]{0:T(128)} %stack.101.where_ref, ...), custom_call_target="tpu_custom_call" | custom-call | flops 10000000000 | bytes 32000000 | tf_op jit(solution)/shard_map/pallas_call | solution.py:506
  205.1 5.7 %collective-permute-done.36.refs_3_ = bf16[36,8,1152]{2,1,0:T(8,128)(2,1)} collective-permute-done((bf16[36,8,1152]{2,1,0:T(8,128)(2,1)}, bf16[36,8,1152]{2,1,0:T(8,128)(2,1)}, u32[]{:S(2)}, u32[]{:S(2)}) %collective-permute-start.36) | collective-permute-done | bytes 663584 | tf_op jit(solution)/shard_map/ppermute | solution.py:60
  213.9 6.9 %collective-permute-done.38.refs_5_ = bf16[36,8,1152]{2,1,0:T(8,128)(2,1)S(1)} collective-permute-done((bf16[36,8,1152]{2,1,0:T(8,128)(2,1)}, bf16[36,8,1152]{2,1,0:T(8,128)(2,1)S(1)}, u32[]{:S(2)}, u32[]{:S(2)}) %collective-permute-start.38) | collective-permute-done | bytes 663584 | tf_op jit(solution)/shard_map/ppermute | solution.py:60
  220.8 2.0 collective-permute-start.43
  225.8 2.6 dynamic-slice_bitcast_fusion.10
  231.0 16.0 %shard_map.244 = (bf16[256,4608]{1,0:T(8,128)(2,1)}, bf16[4608,256]{1,0:T(8,128)(2,1)}, f32[4,1,1152]{2,1,0:T(1,128)}, bf16[4,4,36,8,1152]{4,3,2,1,0:T(8,128)(2,1)}) custom-call(s32[8]{0:T(128)} %stack.106.where_ref, bf16[256,1152]{1,0:T(8,128)(2,1)} %get-tuple-element.323.d_mlp_ref.y0, f32[256,4608]{1,0:T(8,128)} %get-tuple-element.282.pre_ref, ...), custom_call_target="tpu_custom_call" | custom-call | flops 7500000256 | bytes 24000000 | tf_op jit(solution)/shard_map/pallas_call | solution.py:618
  247.1 4.3 collective-permute-done.45.x1
  252.5 12.3 %collective-permute-done.47.x3 = bf16[1152,256]{1,0:T(8,128)(2,1)} collective-permute-done((bf16[1152,256]{1,0:T(8,128)(2,1)S(1)}, bf16[1152,256]{1,0:T(8,128)(2,1)}, u32[]{:S(2)}, u32[]{:S(2)}) %collective-permute-start.47) | collective-permute-done | bytes 589856 | tf_op jit(solution)/shard_map/ppermute | solution.py:57
  264.9 7.8 %shard_map.248 = (f32[4,144,1152]{2,1,0:T(8,128)}, f32[4,144,1152]{2,1,0:T(8,128)}) custom-call(s32[1]{0:T(128)} %bitcast.5.where_ref, bf16[1152,256]{1,0:T(8,128)(2,1)} %get-tuple-element.319.x0, bf16[1152,256]{1,0:T(8,128)(2,1)} %copy-done.41, bf16[1152,256]{1,0:T(8,128)(2,1)} %copy-done.42, bf16[1152,256]{1,0:T(8,128)(2,1)} %collective-permute-done.47.x3, ...), custom_call_target="tpu_custom_call" | custom-call | flops 3000000000 | bytes 9600000 | tf_op jit(solution)/shard_map/pallas_call | solution.py:1036
  272.7 2.0 collective-permute-start.53
  279.4 14.6 %shard_map.246 = (f32[256,1152]{1,0:T(8,128)}, bf16[1152,256]{1,0:T(8,128)(2,1)}, f32[1152,256]{1,0:T(8,128)}, f32[8,1152]{1,0:T(8,128)}) custom-call(s32[1]{0:T(128)} %bitcast.live_ref, bf16[256,4608]{1,0:T(8,128)(2,1)} %get-tuple-element.313.d_pre_ref, bf16[1152,4608]{1,0:T(8,128)(2,1)} %bitcast.147, bf16[1152,1152]{1,0:T(8,128)(2,1)} %bitcast.149, ...), custom_call_target="tpu_custom_call" | custom-call | flops 6000000000 | bytes 19200000 | tf_op jit(solution)/shard_map/pallas_call | solution.py:724
  294.2 15.1 %shard_map.247.d_ref = bf16[3456,256]{1,0:T(8,128)(2,1)} custom-call(s32[1]{0:T(128)} %bitcast.live_ref, f32[3456,256]{1,0:T(8,128)} %get-tuple-element.246.turned_ref, f32[1152,256]{1,0:T(8,128)} %get-tuple-element.316.d_ref), custom_call_target="tpu_custom_call" | custom-call | flops 6000000000 | bytes 19200000 | tf_op jit(solution)/shard_map/pallas_call | solution.py:405
  310.8 7.8 %shard_map.251 = (f32[576,1152]{1,0:T(8,128)}, f32[576,1152]{1,0:T(8,128)}) custom-call(s32[1]{0:T(128)} %bitcast.5.where_ref, bf16[256,1152]{1,0:T(8,128)(2,1)} %get-tuple-element.312.x0, bf16[256,1152]{1,0:T(8,128)(2,1)} %copy-done.12, bf16[256,1152]{1,0:T(8,128)(2,1)} %copy-done.14, bf16[128,1152]{1,0:T(8,128)(2,1)} %collective-permute-done.62.x3, ...), custom_call_target="tpu_custom_call" | custom-call | flops 3500000000 | bytes 11200000 | tf_op jit(solution)/shard_map/pallas_call | solution.py:924
  324.6 4.1 shard_map.250
  332.9 4.8 collective-permute-done.59.refs_1_
  338.5 9.9 %shard_map.245 = (bf16[256,1152]{1,0:T(8,128)(2,1)}, f32[8,1152]{1,0:T(8,128)}) custom-call(s32[1]{0:T(128)} %bitcast.live_ref, bf16[256,4608]{1,0:T(8,128)(2,1)} %get-tuple-element.281.act_ref, bf16[4608,1152]{1,0:T(8,128)(2,1)} %bitcast.105, f32[1,1152]{1,0:T(1,128)} %reshape.203.bias_ref, bf16[256,1152]{1,0:T(8,128)(2,1)} %bitcast.114, ...), custom_call_target="tpu_custom_call" | custom-call | flops 3000000000 | bytes 9600000 | tf_op jit(solution)/shard_map/pallas_call | solution.py:860
  348.4 2.9 collective-permute-done.60.refs_2_
  352.0 10.3 %shard_map.249 = (bf16[256,1152]{1,0:T(8,128)(2,1)}, f32[8,1152]{1,0:T(8,128)}) custom-call(bf16[3456,256]{1,0:T(8,128)(2,1)} %shard_map.247.d_ref, bf16[1152,3456]{1,0:T(8,128)(2,1)} %bitcast.148, bf16[256,1152]{1,0:T(8,128)(2,1)} %bitcast.115, f32[256,1152]{1,0:T(8,128)} %get-tuple-element.331.d_middle_ref, f32[8,1152]{1,0:T(8,128)} %get-tuple-element.274.mods_ref), custom_call_target="tpu_custom_call" | custom-call | flops 4499999744 | bytes 14400000 | tf_op jit(solution)/shard_map/pallas_call | solution.py:793
  363.6 7.1 %shard_map.252 = (f32[432,1152]{1,0:T(8,128)}, f32[432,1152]{1,0:T(8,128)}) custom-call(s32[1]{0:T(128)} %bitcast.5.where_ref, bf16[256,1152]{1,0:T(8,128)(2,1)} %get-tuple-element.333.normed_ref.x0, bf16[256,1152]{1,0:T(8,128)(2,1)} %get-tuple-element.334.x1, bf16[256,1152]{1,0:T(8,128)(2,1)} %get-tuple-element.335.x2, ...), custom_call_target="tpu_custom_call" | custom-call | flops 3500000000 | bytes 11200000 | tf_op jit(solution)/shard_map/pallas_call | solution.py:924
  370.7 6.8 %collective-permute-start.65 = (f32[432,1152]{1,0:T(8,128)}, f32[432,1152]{1,0:T(8,128)}, u32[]{:S(2)}, u32[]{:S(2)}) collective-permute-start(f32[432,1152]{1,0:T(8,128)} %get-tuple-element.361), channel_id=1, source_target_pairs={{0,4},{4,0},{8,12},{12,8},{16,20},{20,16},{24,28},{28,24},{1,5},{5... | collective-permute-start | bytes 5971976 | tf_op jit(solution)/shard_map/ppermute | solution.py:57
  380.2 2.7 collective-permute-start.70
  382.8 2.7 shard_map.257
  385.6 4.3 all-to-all-start
  389.9 5.3 %shard_map.253 = (f32[144,1152]{1,0:T(8,128)}, f32[144,1152]{1,0:T(8,128)}) custom-call(s32[1]{0:T(128)} %bitcast.5.where_ref, bf16[256,1152]{1,0:T(8,128)(2,1)} %shard_map.241.attended_ref.x0, bf16[256,1152]{1,0:T(8,128)(2,1)} %collective-permute-done.33.x1, bf16[256,1152]{1,0:T(8,128)(2,1)} %collective-permute-done.34.x2, bf16[128,1152]{1,0:T(8,128)(2,1)} %copy-done.45, ...), custom_call_target="tpu_custom_call" | custom-call | flops 3500000000 | bytes 11200000 | tf_op jit(solution)/shard_map/pallas_call | solution.py:924
  395.6 2.6 collective-permute-start.72
  398.2 5.0 %shard_map.254 = (f32[288,576]{1,0:T(8,128)}, bf16[288,576]{1,0:T(8,128)(2,1)}, bf16[288,576]{1,0:T(8,128)(2,1)}, bf16[288,576]{1,0:T(8,128)(2,1)}) custom-call(s32[1]{0:T(128)} %bitcast.1.where_ref, f32[576,1152]{1,0:T(8,128)} %get-tuple-element.368.keep_ref, f32[576,1152]{1,0:T(8,128)} %collective-permute-done.64.got_ref), custom_call_target="tpu_custom_call" | custom-call | flops 2000000000 | bytes 6400000 | tf_op jit(solution)/shard_map/pallas_call | solution.py:957
  408.1 4.7 collective-permute-done.67
  412.8 23.8 %collective-permute-done.68 = bf16[288,576]{1,0:T(8,128)(2,1)S(1)} collective-permute-done((bf16[288,576]{1,0:T(8,128)(2,1)}, bf16[288,576]{1,0:T(8,128)(2,1)S(1)}, u32[]{:S(2)}, u32[]{:S(2)}) %collective-permute-start.68) | collective-permute-done | bytes 331808 | tf_op jit(solution)/shard_map/ppermute | solution.py:63
  438.1 3.2 fusion.17
  441.5 1.8 collective-permute-start.77
  443.3 2.3 collective-permute-start.78
  445.6 2.7 shard_map.256
  449.4 4.3 shard_map.255
  456.6 1.9 collective-permute-start.82
  463.2 3.2 collective-permute-done.86
  473.9 18.4 %collective-permute-done.83 = bf16[288,432]{1,0:T(8,128)(2,1)S(1)} collective-permute-done((bf16[288,432]{1,0:T(8,128)(2,1)}, bf16[288,432]{1,0:T(8,128)(2,1)S(1)}, u32[]{:S(2)}, u32[]{:S(2)}) %collective-permute-start.83) | collective-permute-done | bytes 248864 | tf_op jit(solution)/shard_map/ppermute | solution.py:63
  (354 shorter events, 102.3 us)
Async XLA Ops:
  1.9 12.7 %collective-permute-start = (bf16[1,1152]{1,0:T(2,128)(2,1)S(1)}, bf16[1,1152]{1,0:T(2,128)(2,1)S(1)}, u32[]{:S(2)}, u32[]{:S(2)}) collective-permute-start(bf16[1,1152]{1,0:T(2,128)(2,1)S(1)} %get-tuple-element.208), channel_id=1, source_target_pairs={{0,1},{1,2},{2,3},{3,0},{4,5},{5,6},{6,7},{7,4},{8,9},{9,10},{10,1... | collective-permute-start | bytes 6920 | tf_op jit(solution)/shard_map/ppermute | solution.py:63
  2.0 22.9 %collective-permute-start.1 = (bf16[1,1152]{1,0:T(2,128)(2,1)S(1)}, bf16[1,1152]{1,0:T(2,128)(2,1)S(1)}, u32[]{:S(2)}, u32[]{:S(2)}) collective-permute-start(bf16[1,1152]{1,0:T(2,128)(2,1)S(1)} %get-tuple-element.208), channel_id=1, source_target_pairs={{0,2},{1,3},{2,0},{3,1},{4,6},{5,7},{6,4},{7,5},{8,10},{9,11},{10,... | collective-permute-start | bytes 6920 | tf_op jit(solution)/shard_map/ppermute | solution.py:63
  4.6 33.4 %collective-permute-start.8 = (bf16[256,2304]{1,0:T(8,128)(2,1)S(1)}, bf16[256,2304]{1,0:T(8,128)(2,1)}, u32[]{:S(2)}, u32[]{:S(2)}) collective-permute-start(bf16[256,2304]{1,0:T(8,128)(2,1)S(1)} %pad_maximum_fusion.1.refs_0_), channel_id=1, source_target_pairs={{0,8},{4,12},{8,0},{12,4},{16,24},{20,28},{24,16},{28,20},{1,9},{5... | collective-permute-start | bytes 3538952 | tf_op jit(solution)/shard_map/ppermute | solution.py:57
  5.9 32.2 %collective-permute-start.9 = (bf16[256,2304]{1,0:T(8,128)(2,1)S(1)}, bf16[256,2304]{1,0:T(8,128)(2,1)}, u32[]{:S(2)}, u32[]{:S(2)}) collective-permute-start(bf16[256,2304]{1,0:T(8,128)(2,1)S(1)} %pad_maximum_fusion.1.refs_0_), channel_id=1, source_target_pairs={{0,16},{4,20},{8,24},{12,28},{16,0},{20,4},{24,8},{28,12},{1,17},{... | collective-permute-start | bytes 3538952 | tf_op jit(solution)/shard_map/ppermute | solution.py:57
  19.4 18.6 %collective-permute-start.7 = (bf16[9,8,3456]{2,1,0:T(8,128)(2,1)S(1)}, bf16[9,8,3456]{2,1,0:T(8,128)(2,1)S(1)}, u32[]{:S(2)}, u32[]{:S(2)}) collective-permute-start(bf16[9,8,3456]{2,1,0:T(8,128)(2,1)S(1)} %collective-permute-done.6), channel_id=1, source_target_pairs={{0,1},{1,2},{2,3},{3,0},{4,5},{5,6},{6,7},{7,4},{8,9},{9,10},{10,1... | collective-permute-start | bytes 1493000 | tf_op jit(solution)/shard_map/ppermute | solution.py:63
  39.2 17.2 %collective-permute-start.13 = (bf16[128,2304]{1,0:T(8,128)(2,1)S(1)}, bf16[128,2304]{1,0:T(8,128)(2,1)}, u32[]{:S(2)}, u32[]{:S(2)}) collective-permute-start(bf16[128,2304]{1,0:T(8,128)(2,1)S(1)} %slice.107), channel_id=1, source_target_pairs={{0,16},{4,20},{8,24},{12,28},{16,0},{20,4},{24,8},{28,12},{1,17},{... | collective-permute-start | bytes 1769480 | tf_op jit(solution)/shard_map/ppermute | solution.py:57
  40.7 15.7 %collective-permute-start.14 = (bf16[128,2304]{1,0:T(8,128)(2,1)S(1)}, bf16[128,2304]{1,0:T(8,128)(2,1)}, u32[]{:S(2)}, u32[]{:S(2)}) collective-permute-start(bf16[128,2304]{1,0:T(8,128)(2,1)S(1)} %slice.108), channel_id=1, source_target_pairs={{0,8},{4,12},{8,0},{12,4},{16,24},{20,28},{24,16},{28,20},{1,9},{5... | collective-permute-start | bytes 1769480 | tf_op jit(solution)/shard_map/ppermute | solution.py:57
  41.0 15.4 %collective-permute-start.15 = (bf16[9,8,3456]{2,1,0:T(8,128)(2,1)S(1)}, bf16[9,8,3456]{2,1,0:T(8,128)(2,1)S(1)}, u32[]{:S(2)}, u32[]{:S(2)}) collective-permute-start(bf16[9,8,3456]{2,1,0:T(8,128)(2,1)S(1)} %collective-permute-done.7), channel_id=1, source_target_pairs={{0,1},{1,2},{2,3},{3,0},{4,5},{5,6},{6,7},{7,4},{8,9},{9,10},{10,1... | collective-permute-start | bytes 1493000 | tf_op jit(solution)/shard_map/ppermute | solution.py:63
  56.6 19.3 %collective-permute-start.16 = (bf16[3,9,8,3456]{3,2,1,0:T(8,128)(2,1)S(1)}, bf16[3,9,8,3456]{3,2,1,0:T(8,128)(2,1)}, u32[]{:S(2)}, u32[]{:S(2)}) collective-permute-start(bf16[3,9,8,3456]{3,2,1,0:T(8,128)(2,1)S(1)} %pad_maximum_fusion.refs_0_), channel_id=1, source_target_pairs={{0,8},{4,20},{8,0},{12,28},{16,24},{20,4},{24,16},{28,12},{1,9},{5... | collective-permute-start | bytes 4478984 | tf_op jit(solution)/shard_map/ppermute | solution.py:60
  58.3 50.1 %collective-permute-start.17 = (bf16[3,9,8,3456]{3,2,1,0:T(8,128)(2,1)S(1)}, bf16[3,9,8,3456]{3,2,1,0:T(8,128)(2,1)}, u32[]{:S(2)}, u32[]{:S(2)}) collective-permute-start(bf16[3,9,8,3456]{3,2,1,0:T(8,128)(2,1)S(1)} %pad_maximum_fusion.refs_0_), channel_id=1, source_target_pairs={{0,4},{4,0},{8,12},{12,8},{16,20},{20,16},{24,28},{28,24},{1,5},{5... | collective-permute-start | bytes 4478984 | tf_op jit(solution)/shard_map/ppermute | solution.py:57
  75.9 32.6 %collective-permute-start.18 = (bf16[3,9,8,3456]{3,2,1,0:T(8,128)(2,1)}, bf16[3,9,8,3456]{3,2,1,0:T(8,128)(2,1)}, u32[]{:S(2)}, u32[]{:S(2)}) collective-permute-start(bf16[3,9,8,3456]{3,2,1,0:T(8,128)(2,1)} %collective-permute-done.16.refs_1_), channel_id=1, source_target_pairs={{0,4},{4,0},{8,12},{12,8},{16,20},{20,16},{24,28},{28,24},{1,5},{5... | collective-permute-start | bytes 4478984 | tf_op jit(solution)/shard_map/ppermute | solution.py:57
  83.6 12.6 %collective-permute-start.19 = (bf16[9,8,2944]{2,1,0:T(8,128)(2,1)}, bf16[9,8,2944]{2,1,0:T(8,128)(2,1)S(1)}, u32[]{:S(2)}, u32[]{:S(2)}) collective-permute-start(bf16[9,8,2944]{2,1,0:T(8,128)(2,1)} %fusion), channel_id=1, source_target_pairs={{0,1},{1,2},{2,3},{3,0},{4,5},{5,6},{6,7},{7,4},{8,9},{9,10},{10,1... | collective-permute-start | bytes 1271816 | tf_op jit(solution)/shard_map/ppermute | solution.py:63
  96.3 12.2 %collective-permute-start.20 = (bf16[9,8,2944]{2,1,0:T(8,128)(2,1)S(1)}, bf16[9,8,2944]{2,1,0:T(8,128)(2,1)S(1)}, u32[]{:S(2)}, u32[]{:S(2)}) collective-permute-start(bf16[9,8,2944]{2,1,0:T(8,128)(2,1)S(1)} %collective-permute-done.19), channel_id=1, source_target_pairs={{0,1},{1,2},{2,3},{3,0},{4,5},{5,6},{6,7},{7,4},{8,9},{9,10},{10,1... | collective-permute-start | bytes 1271816 | tf_op jit(solution)/shard_map/ppermute | solution.py:63
  109.1 13.4 %collective-permute-start.21 = (bf16[9,8,2944]{2,1,0:T(8,128)(2,1)S(1)}, bf16[9,8,2944]{2,1,0:T(8,128)(2,1)S(1)}, u32[]{:S(2)}, u32[]{:S(2)}) collective-permute-start(bf16[9,8,2944]{2,1,0:T(8,128)(2,1)S(1)} %collective-permute-done.20), channel_id=1, source_target_pairs={{0,1},{1,2},{2,3},{3,0},{4,5},{5,6},{6,7},{7,4},{8,9},{9,10},{10,1... | collective-permute-start | bytes 1271816 | tf_op jit(solution)/shard_map/ppermute | solution.py:63
  124.9 27.8 %collective-permute-start.22 = (bf16[27,8,2944]{2,1,0:T(8,128)(2,1)}, bf16[27,8,2944]{2,1,0:T(8,128)(2,1)S(1)}, u32[]{:S(2)}, u32[]{:S(2)}) collective-permute-start(bf16[27,8,2944]{2,1,0:T(8,128)(2,1)} %constant_dynamic-update-slice_fusion.refs_2_), channel_id=1, source_target_pairs={{0,8},{4,12},{8,0},{12,4},{16,24},{20,28},{24,16},{28,20},{1,9},{5... | collective-permute-start | bytes 3815432 | tf_op jit(solution)/shard_map/ppermute | solution.py:57
  125.1 27.5 %collective-permute-start.23 = (bf16[27,8,2944]{2,1,0:T(8,128)(2,1)}, bf16[27,8,2944]{2,1,0:T(8,128)(2,1)S(1)}, u32[]{:S(2)}, u32[]{:S(2)}) collective-permute-start(bf16[27,8,2944]{2,1,0:T(8,128)(2,1)} %constant_dynamic-update-slice_fusion.refs_2_), channel_id=1, source_target_pairs={{0,16},{4,20},{8,24},{12,28},{16,0},{20,4},{24,8},{28,12},{1,17},{... | collective-permute-start | bytes 3815432 | tf_op jit(solution)/shard_map/ppermute | solution.py:57
  126.2 26.4 %collective-permute-start.24 = (bf16[27,8,2944]{2,1,0:T(8,128)(2,1)}, bf16[27,8,2944]{2,1,0:T(8,128)(2,1)}, u32[]{:S(2)}, u32[]{:S(2)}) collective-permute-start(bf16[27,8,2944]{2,1,0:T(8,128)(2,1)} %constant_dynamic-update-slice_fusion.refs_2_), channel_id=1, source_target_pairs={{0,4},{4,0},{8,12},{12,8},{16,20},{20,16},{24,28},{28,24},{1,5},{5... | collective-permute-start | bytes 3815432 | tf_op jit(solution)/shard_map/ppermute | solution.py:57
  128.8 23.9 %collective-permute-start.25 = (bf16[36,8,1152]{2,1,0:T(8,128)(2,1)S(1)}, bf16[36,8,1152]{2,1,0:T(8,128)(2,1)}, u32[]{:S(2)}, u32[]{:S(2)}) collective-permute-start(bf16[36,8,1152]{2,1,0:T(8,128)(2,1)S(1)} %dynamic-slice_bitcast_fusion), channel_id=1, source_target_pairs={{0,1},{1,2},{2,3},{3,0},{4,5},{5,6},{6,7},{7,4},{8,9},{9,10},{10,1... | collective-permute-start | bytes 1990664 | tf_op jit(solution)/shard_map/ppermute | solution.py:63
  152.7 20.9 %collective-permute-start.28 = (bf16[27,8,2944]{2,1,0:T(8,128)(2,1)S(1)}, bf16[27,8,2944]{2,1,0:T(8,128)(2,1)S(1)}, u32[]{:S(2)}, u32[]{:S(2)}) collective-permute-start(bf16[27,8,2944]{2,1,0:T(8,128)(2,1)S(1)} %collective-permute-done.22.refs_3_), channel_id=1, source_target_pairs={{0,4},{4,0},{8,12},{12,8},{16,20},{20,16},{24,28},{28,24},{1,5},{5... | collective-permute-start | bytes 3815432 | tf_op jit(solution)/shard_map/ppermute | solution.py:57
  155.7 17.9 %collective-permute-start.29 = (bf16[27,8,2944]{2,1,0:T(8,128)(2,1)S(1)}, bf16[27,8,2944]{2,1,0:T(8,128)(2,1)S(1)}, u32[]{:S(2)}, u32[]{:S(2)}) collective-permute-start(bf16[27,8,2944]{2,1,0:T(8,128)(2,1)S(1)} %collective-permute-done.23.refs_4_), channel_id=1, source_target_pairs={{0,4},{4,0},{8,12},{12,8},{16,20},{20,16},{24,28},{28,24},{1,5},{5... | collective-permute-start | bytes 3815432 | tf_op jit(solution)/shard_map/ppermute | solution.py:57
  155.8 17.8 %collective-permute-start.30 = (bf16[36,8,1152]{2,1,0:T(8,128)(2,1)}, bf16[36,8,1152]{2,1,0:T(8,128)(2,1)S(1)}, u32[]{:S(2)}, u32[]{:S(2)}) collective-permute-start(bf16[36,8,1152]{2,1,0:T(8,128)(2,1)} %collective-permute-done.25.refs_0_), channel_id=1, source_target_pairs={{0,1},{1,2},{2,3},{3,0},{4,5},{5,6},{6,7},{7,4},{8,9},{9,10},{10,1... | collective-permute-start | bytes 1990664 | tf_op jit(solution)/shard_map/ppermute | solution.py:63
  157.8 15.8 %collective-permute-start.27 = (bf16[14,8,2944]{2,1,0:T(8,128)(2,1)S(1)}, bf16[14,8,2944]{2,1,0:T(8,128)(2,1)}, u32[]{:S(2)}, u32[]{:S(2)}) collective-permute-start(bf16[14,8,2944]{2,1,0:T(8,128)(2,1)S(1)} %slice.118), channel_id=1, source_target_pairs={{0,8},{4,12},{8,0},{12,4},{16,24},{20,28},{24,16},{28,20},{1,9},{5... | collective-permute-start | bytes 1978376 | tf_op jit(solution)/shard_map/ppermute | solution.py:57
  159.1 14.5 %collective-permute-start.26 = (bf16[13,8,2944]{2,1,0:T(8,128)(2,1)S(1)}, bf16[13,8,2944]{2,1,0:T(8,128)(2,1)}, u32[]{:S(2)}, u32[]{:S(2)}) collective-permute-start(bf16[13,8,2944]{2,1,0:T(8,128)(2,1)S(1)} %slice.117), channel_id=1, source_target_pairs={{0,16},{4,20},{8,24},{12,28},{16,0},{20,4},{24,8},{28,12},{1,17},{... | collective-permute-start | bytes 1837064 | tf_op jit(solution)/shard_map/ppermute | solution.py:57
  179.5 25.5 %collective-permute-start.35 = (bf16[36,8,1152]{2,1,0:T(8,128)(2,1)S(1)}, bf16[36,8,1152]{2,1,0:T(8,128)(2,1)}, u32[]{:S(2)}, u32[]{:S(2)}) collective-permute-start(bf16[36,8,1152]{2,1,0:T(8,128)(2,1)S(1)} %collective-permute-done.30.refs_1_), channel_id=1, source_target_pairs={{0,1},{1,2},{2,3},{3,0},{4,5},{5,6},{6,7},{7,4},{8,9},{9,10},{10,1... | collective-permute-start | bytes 1990664 | tf_op jit(solution)/shard_map/ppermute | solution.py:63
  181.1 29.7 %collective-permute-start.37 = (bf16[36,8,1152]{2,1,0:T(8,128)(2,1)S(1)}, bf16[36,8,1152]{2,1,0:T(8,128)(2,1)}, u32[]{:S(2)}, u32[]{:S(2)}) collective-permute-start(bf16[36,8,1152]{2,1,0:T(8,128)(2,1)S(1)} %collective-permute-done.30.refs_1_), channel_id=1, source_target_pairs={{0,8},{4,20},{8,0},{12,28},{16,24},{20,4},{24,16},{28,12},{1,9},{5... | collective-permute-start | bytes 1990664 | tf_op jit(solution)/shard_map/ppermute | solution.py:60
  182.2 22.8 %collective-permute-start.33 = (bf16[256,1152]{1,0:T(8,128)(2,1)}, bf16[256,1152]{1,0:T(8,128)(2,1)}, u32[]{:S(2)}, u32[]{:S(2)}) collective-permute-start(bf16[256,1152]{1,0:T(8,128)(2,1)} %shard_map.241.attended_ref.x0), channel_id=1, source_target_pairs={{0,8},{4,12},{8,0},{12,4},{16,24},{20,28},{24,16},{28,20},{1,9},{5... | collective-permute-start | bytes 1769480 | tf_op jit(solution)/shard_map/ppermute | solution.py:57
  183.4 21.6 %collective-permute-start.34 = (bf16[256,1152]{1,0:T(8,128)(2,1)}, bf16[256,1152]{1,0:T(8,128)(2,1)}, u32[]{:S(2)}, u32[]{:S(2)}) collective-permute-start(bf16[256,1152]{1,0:T(8,128)(2,1)} %shard_map.241.attended_ref.x0), channel_id=1, source_target_pairs={{0,16},{4,20},{8,24},{12,28},{16,0},{20,4},{24,8},{28,12},{1,17},{... | collective-permute-start | bytes 1769480 | tf_op jit(solution)/shard_map/ppermute | solution.py:57
  183.8 27.0 %collective-permute-start.36 = (bf16[36,8,1152]{2,1,0:T(8,128)(2,1)}, bf16[36,8,1152]{2,1,0:T(8,128)(2,1)}, u32[]{:S(2)}, u32[]{:S(2)}) collective-permute-start(bf16[36,8,1152]{2,1,0:T(8,128)(2,1)} %collective-permute-done.25.refs_0_), channel_id=1, source_target_pairs={{0,8},{4,20},{8,0},{12,28},{16,24},{20,4},{24,16},{28,12},{1,9},{5... | collective-permute-start | bytes 1990664 | tf_op jit(solution)/shard_map/ppermute | solution.py:60
  213.9 11.9 %collective-permute-start.42 = (bf16[36,8,1152]{2,1,0:T(8,128)(2,1)}, bf16[36,8,1152]{2,1,0:T(8,128)(2,1)}, u32[]{:S(2)}, u32[]{:S(2)}) collective-permute-start(bf16[36,8,1152]{2,1,0:T(8,128)(2,1)} %collective-permute-done.36.refs_3_), channel_id=1, source_target_pairs={{0,4},{4,0},{8,12},{12,8},{16,20},{20,16},{24,28},{28,24},{1,5},{5... | collective-permute-start | bytes 1990664 | tf_op jit(solution)/shard_map/ppermute | solution.py:57
  223.6 23.4 %collective-permute-start.48 = (bf16[256,1152]{1,0:T(8,128)(2,1)}, bf16[256,1152]{1,0:T(8,128)(2,1)S(1)}, u32[]{:S(2)}, u32[]{:S(2)}) collective-permute-start(bf16[256,1152]{1,0:T(8,128)(2,1)} %get-tuple-element.312.x0), channel_id=1, source_target_pairs={{0,8},{4,12},{8,0},{12,4},{16,24},{20,28},{24,16},{28,20},{1,9},{5... | collective-permute-start | bytes 1769480 | tf_op jit(solution)/shard_map/ppermute | solution.py:57
  224.8 22.2 %collective-permute-start.49 = (bf16[256,1152]{1,0:T(8,128)(2,1)}, bf16[256,1152]{1,0:T(8,128)(2,1)S(1)}, u32[]{:S(2)}, u32[]{:S(2)}) collective-permute-start(bf16[256,1152]{1,0:T(8,128)(2,1)} %get-tuple-element.312.x0), channel_id=1, source_target_pairs={{0,16},{4,20},{8,24},{12,28},{16,0},{20,4},{24,8},{28,12},{1,17},{... | collective-permute-start | bytes 1769480 | tf_op jit(solution)/shard_map/ppermute | solution.py:57
  228.4 23.0 %collective-permute-start.45 = (bf16[1152,256]{1,0:T(8,128)(2,1)S(1)}, bf16[1152,256]{1,0:T(8,128)(2,1)S(1)}, u32[]{:S(2)}, u32[]{:S(2)}) collective-permute-start(bf16[1152,256]{1,0:T(8,128)(2,1)S(1)} %get-tuple-element.446), channel_id=1, source_target_pairs={{0,8},{4,12},{8,0},{12,4},{16,24},{20,28},{24,16},{28,20},{1,9},{5... | collective-permute-start | bytes 1769480 | tf_op jit(solution)/shard_map/ppermute | solution.py:57
  229.4 23.2 %collective-permute-start.46 = (bf16[1152,256]{1,0:T(8,128)(2,1)S(1)}, bf16[1152,256]{1,0:T(8,128)(2,1)S(1)}, u32[]{:S(2)}, u32[]{:S(2)}) collective-permute-start(bf16[1152,256]{1,0:T(8,128)(2,1)S(1)} %get-tuple-element.445), channel_id=1, source_target_pairs={{0,16},{4,20},{8,24},{12,28},{16,0},{20,4},{24,8},{28,12},{1,17},{... | collective-permute-start | bytes 1769480 | tf_op jit(solution)/shard_map/ppermute | solution.py:57
  230.3 34.5 %collective-permute-start.47 = (bf16[1152,256]{1,0:T(8,128)(2,1)S(1)}, bf16[1152,256]{1,0:T(8,128)(2,1)}, u32[]{:S(2)}, u32[]{:S(2)}) collective-permute-start(bf16[1152,256]{1,0:T(8,128)(2,1)S(1)} %get-tuple-element.444), channel_id=1, source_target_pairs={{0,24},{4,28},{8,16},{12,20},{16,8},{20,12},{24,0},{28,4},{1,25},{... | collective-permute-start | bytes 1769480 | tf_op jit(solution)/shard_map/ppermute | solution.py:57
  272.7 36.6 %collective-permute-start.53 = (f32[4,144,1152]{2,1,0:T(8,128)}, f32[4,144,1152]{2,1,0:T(8,128)}, u32[]{:S(2)}, u32[]{:S(2)}) collective-permute-start(f32[4,144,1152]{2,1,0:T(8,128)} %get-tuple-element.328), channel_id=1, source_target_pairs={{0,4},{4,0},{8,12},{12,8},{16,20},{20,16},{24,28},{28,24},{1,5},{5... | collective-permute-start | bytes 7962632 | tf_op jit(solution)/shard_map/ppermute | solution.py:57
  275.8 18.4 %collective-permute-start.50 = (bf16[1152,256]{1,0:T(8,128)(2,1)S(1)}, bf16[1152,256]{1,0:T(8,128)(2,1)S(1)}, u32[]{:S(2)}, u32[]{:S(2)}) collective-permute-start(bf16[1152,256]{1,0:T(8,128)(2,1)S(1)} %get-tuple-element.442), channel_id=1, source_target_pairs={{0,8},{4,12},{8,0},{12,4},{16,24},{20,28},{24,16},{28,20},{1,9},{5... | collective-permute-start | bytes 1769480 | tf_op jit(solution)/shard_map/ppermute | solution.py:57
  275.8 33.5 %collective-permute-start.51 = (bf16[1152,256]{1,0:T(8,128)(2,1)S(1)}, bf16[1152,256]{1,0:T(8,128)(2,1)S(1)}, u32[]{:S(2)}, u32[]{:S(2)}) collective-permute-start(bf16[1152,256]{1,0:T(8,128)(2,1)S(1)} %get-tuple-element.441), channel_id=1, source_target_pairs={{0,16},{4,20},{8,24},{12,28},{16,0},{20,4},{24,8},{28,12},{1,17},{... | collective-permute-start | bytes 1769480 | tf_op jit(solution)/shard_map/ppermute | solution.py:57
  276.7 32.6 %collective-permute-start.52 = (bf16[1152,256]{1,0:T(8,128)(2,1)S(1)}, bf16[1152,256]{1,0:T(8,128)(2,1)}, u32[]{:S(2)}, u32[]{:S(2)}) collective-permute-start(bf16[1152,256]{1,0:T(8,128)(2,1)S(1)} %get-tuple-element.440), channel_id=1, source_target_pairs={{0,24},{4,28},{8,16},{12,20},{16,8},{20,12},{24,0},{28,4},{1,25},{... | collective-permute-start | bytes 1769480 | tf_op jit(solution)/shard_map/ppermute | solution.py:57
  278.4 31.0 %collective-permute-start.62 = (bf16[128,1152]{1,0:T(8,128)(2,1)S(1)}, bf16[128,1152]{1,0:T(8,128)(2,1)}, u32[]{:S(2)}, u32[]{:S(2)}) collective-permute-start(bf16[128,1152]{1,0:T(8,128)(2,1)S(1)} %slice.121), channel_id=1, source_target_pairs={{0,16},{4,20},{8,24},{12,28},{16,0},{20,4},{24,8},{28,12},{1,17},{... | collective-permute-start | bytes 884744 | tf_op jit(solution)/shard_map/ppermute | solution.py:57
  294.1 15.6 %collective-permute-start.63 = (bf16[128,1152]{1,0:T(8,128)(2,1)S(1)}, bf16[128,1152]{1,0:T(8,128)(2,1)S(1)}, u32[]{:S(2)}, u32[]{:S(2)}) collective-permute-start(bf16[128,1152]{1,0:T(8,128)(2,1)S(1)} %slice.122), channel_id=1, source_target_pairs={{0,8},{4,12},{8,0},{12,4},{16,24},{20,28},{24,16},{28,20},{1,9},{5... | collective-permute-start | bytes 884744 | tf_op jit(solution)/shard_map/ppermute | solution.py:57
  318.6 43.7 %collective-permute-start.64 = (f32[576,1152]{1,0:T(8,128)}, f32[576,1152]{1,0:T(8,128)}, u32[]{:S(2)}, u32[]{:S(2)}) collective-permute-start(f32[576,1152]{1,0:T(8,128)} %get-tuple-element.356), channel_id=1, source_target_pairs={{0,4},{4,0},{8,12},{12,8},{16,20},{20,16},{24,28},{28,24},{1,5},{5... | collective-permute-start | bytes 7962632 | tf_op jit(solution)/shard_map/ppermute | solution.py:57
  328.7 22.6 %collective-permute-start.60 = (bf16[144,1152]{1,0:T(8,128)(2,1)}, bf16[144,1152]{1,0:T(8,128)(2,1)}, u32[]{:S(2)}, u32[]{:S(2)}) collective-permute-start(bf16[144,1152]{1,0:T(8,128)(2,1)} %get-tuple-element.346), channel_id=1, source_target_pairs={{0,2},{1,3},{2,0},{3,1},{4,6},{5,7},{6,4},{7,5},{8,10},{9,11},{10,... | collective-permute-start | bytes 995336 | tf_op jit(solution)/shard_map/ppermute | solution.py:63
  331.5 30.8 %collective-permute-start.54 = (bf16[1152,256]{1,0:T(8,128)(2,1)S(1)}, bf16[1152,256]{1,0:T(8,128)(2,1)S(1)}, u32[]{:S(2)}, u32[]{:S(2)}) collective-permute-start(bf16[1152,256]{1,0:T(8,128)(2,1)S(1)} %get-tuple-element.438), channel_id=1, source_target_pairs={{0,8},{4,12},{8,0},{12,4},{16,24},{20,28},{24,16},{28,20},{1,9},{5... | collective-permute-start | bytes 1769480 | tf_op jit(solution)/shard_map/ppermute | solution.py:57
  332.3 30.0 %collective-permute-start.55 = (bf16[1152,256]{1,0:T(8,128)(2,1)S(1)}, bf16[1152,256]{1,0:T(8,128)(2,1)S(1)}, u32[]{:S(2)}, u32[]{:S(2)}) collective-permute-start(bf16[1152,256]{1,0:T(8,128)(2,1)S(1)} %get-tuple-element.437), channel_id=1, source_target_pairs={{0,16},{4,20},{8,24},{12,28},{16,0},{20,4},{24,8},{28,12},{1,17},{... | collective-permute-start | bytes 1769480 | tf_op jit(solution)/shard_map/ppermute | solution.py:57
  337.7 24.6 %collective-permute-start.56 = (bf16[1152,256]{1,0:T(8,128)(2,1)S(1)}, bf16[1152,256]{1,0:T(8,128)(2,1)S(1)}, u32[]{:S(2)}, u32[]{:S(2)}) collective-permute-start(bf16[1152,256]{1,0:T(8,128)(2,1)S(1)} %get-tuple-element.436), channel_id=1, source_target_pairs={{0,24},{4,28},{8,16},{12,20},{16,8},{20,12},{24,0},{28,4},{1,25},{... | collective-permute-start | bytes 1769480 | tf_op jit(solution)/shard_map/ppermute | solution.py:57
  370.7 65.9 %collective-permute-start.65 = (f32[432,1152]{1,0:T(8,128)}, f32[432,1152]{1,0:T(8,128)}, u32[]{:S(2)}, u32[]{:S(2)}) collective-permute-start(f32[432,1152]{1,0:T(8,128)} %get-tuple-element.361), channel_id=1, source_target_pairs={{0,4},{4,0},{8,12},{12,8},{16,20},{20,16},{24,28},{28,24},{1,5},{5... | collective-permute-start | bytes 5971976 | tf_op jit(solution)/shard_map/ppermute | solution.py:57
  379.1 24.7 %collective-permute-start.73 = (f32[8,1152]{1,0:T(8,128)S(1)}, f32[8,1152]{1,0:T(8,128)S(1)}, u32[]{:S(2)}, u32[]{:S(2)}) collective-permute-start(f32[8,1152]{1,0:T(8,128)S(1)} %pad_maximum_fusion.5), channel_id=1, source_target_pairs={{0,1},{1,2},{2,3},{3,0},{4,5},{5,6},{6,7},{7,4},{8,9},{9,10},{10,1... | collective-permute-start | bytes 110600 | tf_op jit(solution)/shard_map/ppermute | solution.py:63
  379.2 25.2 %collective-permute-start.74 = (f32[8,1152]{1,0:T(8,128)S(1)}, f32[8,1152]{1,0:T(8,128)S(1)}, u32[]{:S(2)}, u32[]{:S(2)}) collective-permute-start(f32[8,1152]{1,0:T(8,128)S(1)} %pad_maximum_fusion.5), channel_id=1, source_target_pairs={{0,2},{1,3},{2,0},{3,1},{4,6},{5,7},{6,4},{7,5},{8,10},{9,11},{10,... | collective-permute-start | bytes 110600 | tf_op jit(solution)/shard_map/ppermute | solution.py:63
  380.2 15.0 %collective-permute-start.70 = (bf16[8,1152]{1,0:T(8,128)(2,1)S(1)}, bf16[8,1152]{1,0:T(8,128)(2,1)S(1)}, u32[]{:S(2)}, u32[]{:S(2)}) collective-permute-start(bf16[8,1152]{1,0:T(8,128)(2,1)S(1)} %concatenate.65), channel_id=1, source_target_pairs={{0,1},{1,2},{2,3},{3,0},{4,5},{5,6},{6,7},{7,4},{8,9},{9,10},{10,1... | collective-permute-start | bytes 55304 | tf_op jit(solution)/shard_map/ppermute | solution.py:63
  382.8 12.8 %collective-permute-start.71 = (bf16[8,1152]{1,0:T(8,128)(2,1)S(1)}, bf16[8,1152]{1,0:T(8,128)(2,1)S(1)}, u32[]{:S(2)}, u32[]{:S(2)}) collective-permute-start(bf16[8,1152]{1,0:T(8,128)(2,1)S(1)} %concatenate.65), channel_id=1, source_target_pairs={{0,2},{1,3},{2,0},{3,1},{4,6},{5,7},{6,4},{7,5},{8,10},{9,11},{10,... | collective-permute-start | bytes 55304 | tf_op jit(solution)/shard_map/ppermute | solution.py:63
  385.6 21.3 %all-to-all-start = ((f32[8,144,144]{2,1,0:T(8,128)}), f32[8,144,144]{2,1,0:T(8,128)S(1)}, u32[]{:S(2)}, u32[]{:S(2)}) async-start(f32[8,144,144]{2,1,0:T(8,128)} %shard_map.257), calls=%async_computation | async-start | bytes 2359296 | tf_op jit(solution)/shard_map/all_to_all | solution.py:1338
  403.9 32.7 %collective-permute-start.68 = (bf16[288,576]{1,0:T(8,128)(2,1)}, bf16[288,576]{1,0:T(8,128)(2,1)S(1)}, u32[]{:S(2)}, u32[]{:S(2)}) collective-permute-start(bf16[288,576]{1,0:T(8,128)(2,1)} %get-tuple-element.372), channel_id=1, source_target_pairs={{0,2},{1,3},{2,0},{3,1},{4,6},{5,7},{6,4},{7,5},{8,10},{9,11},{10,... | collective-permute-start | bytes 995336 | tf_op jit(solution)/shard_map/ppermute | solution.py:63
  404.4 32.2 %collective-permute-start.69 = (bf16[288,576]{1,0:T(8,128)(2,1)}, bf16[288,576]{1,0:T(8,128)(2,1)S(1)}, u32[]{:S(2)}, u32[]{:S(2)}) collective-permute-start(bf16[288,576]{1,0:T(8,128)(2,1)} %get-tuple-element.373), channel_id=1, source_target_pairs={{0,3},{1,0},{2,1},{3,2},{4,7},{5,4},{6,5},{7,6},{8,11},{9,8},{10,9... | collective-permute-start | bytes 995336 | tf_op jit(solution)/shard_map/ppermute | solution.py:63
  405.3 31.3 %collective-permute-start.66 = (f32[144,1152]{1,0:T(8,128)}, f32[144,1152]{1,0:T(8,128)}, u32[]{:S(2)}, u32[]{:S(2)}) collective-permute-start(f32[144,1152]{1,0:T(8,128)} %get-tuple-element.367), channel_id=1, source_target_pairs={{0,4},{4,0},{8,12},{12,8},{16,20},{20,16},{24,28},{28,24},{1,5},{5... | collective-permute-start | bytes 1990664 | tf_op jit(solution)/shard_map/ppermute | solution.py:57
  436.6 21.9 %collective-permute-start.79 = (bf16[4,8,1152]{2,1,0:T(8,128)(2,1)S(1)}, bf16[4,8,1152]{2,1,0:T(8,128)(2,1)S(1)}, u32[]{:S(2)}, u32[]{:S(2)}) collective-permute-start(bf16[4,8,1152]{2,1,0:T(8,128)(2,1)S(1)} %pad_maximum_fusion.4), channel_id=1, source_target_pairs={{0,4},{4,0},{8,12},{12,8},{16,20},{20,16},{24,28},{28,24},{1,5},{5... | collective-permute-start | bytes 221192 | tf_op jit(solution)/shard_map/ppermute | solution.py:57
  438.0 18.6 %collective-permute-start.88 = (f32[8,1152]{1,0:T(8,128)S(1)}, f32[8,1152]{1,0:T(8,128)S(1)}, u32[]{:S(2)}, u32[]{:S(2)}) collective-permute-start(f32[8,1152]{1,0:T(8,128)S(1)} %add_add_fusion), channel_id=1, source_target_pairs={{0,4},{4,0},{8,12},{12,8},{16,20},{20,16},{24,28},{28,24},{1,5},{5... | collective-permute-start | bytes 110600 | tf_op jit(solution)/shard_map/ppermute | solution.py:57
  441.4 12.2 %collective-permute-start.76 = (f32[288]{0:T(512)S(1)}, f32[288]{0:T(512)S(1)}, u32[]{:S(2)}, u32[]{:S(2)}) collective-permute-start(f32[288]{0:T(512)S(1)} %get-tuple-element.433), channel_id=1, source_target_pairs={{0,3},{1,0},{2,1},{3,2},{4,7},{5,4},{6,5},{7,6},{8,11},{9,8},{10,9... | collective-permute-start | bytes 3464 | tf_op jit(solution)/shard_map/ppermute | solution.py:63
  441.5 12.3 %collective-permute-start.77 = (f32[288]{0:T(512)S(1)}, f32[288]{0:T(512)S(1)}, u32[]{:S(2)}, u32[]{:S(2)}) collective-permute-start(f32[288]{0:T(512)S(1)} %get-tuple-element.432), channel_id=1, source_target_pairs={{0,2},{1,3},{2,0},{3,1},{4,6},{5,7},{6,4},{7,5},{8,10},{9,11},{10,... | collective-permute-start | bytes 3464 | tf_op jit(solution)/shard_map/ppermute | solution.py:63
  453.7 12.6 %collective-permute-start.86 = (bf16[288,144]{1,0:T(8,128)(2,1)}, bf16[288,144]{1,0:T(8,128)(2,1)S(1)}, u32[]{:S(2)}, u32[]{:S(2)}) collective-permute-start(bf16[288,144]{1,0:T(8,128)(2,1)} %get-tuple-element.389), channel_id=1, source_target_pairs={{0,2},{1,3},{2,0},{3,1},{4,6},{5,7},{6,4},{7,5},{8,10},{9,11},{10,... | collective-permute-start | bytes 248840 | tf_op jit(solution)/shard_map/ppermute | solution.py:63
  454.4 13.3 %collective-permute-start.87 = (bf16[288,144]{1,0:T(8,128)(2,1)S(1)}, bf16[288,144]{1,0:T(8,128)(2,1)}, u32[]{:S(2)}, u32[]{:S(2)}) collective-permute-start(bf16[288,144]{1,0:T(8,128)(2,1)S(1)} %copy-done.48), channel_id=1, source_target_pairs={{0,3},{1,0},{2,1},{3,2},{4,7},{5,4},{6,5},{7,6},{8,11},{9,8},{10,9... | collective-permute-start | bytes 248840 | tf_op jit(solution)/shard_map/ppermute | solution.py:63
  456.6 17.3 %collective-permute-start.82 = (bf16[288,432]{1,0:T(8,128)(2,1)}, bf16[288,432]{1,0:T(8,128)(2,1)S(1)}, u32[]{:S(2)}, u32[]{:S(2)}) collective-permute-start(bf16[288,432]{1,0:T(8,128)(2,1)} %get-tuple-element.382), channel_id=1, source_target_pairs={{0,1},{1,2},{2,3},{3,0},{4,5},{5,6},{6,7},{7,4},{8,9},{9,10},{10,1... | collective-permute-start | bytes 746504 | tf_op jit(solution)/shard_map/ppermute | solution.py:63
  461.7 30.6 %collective-permute-start.83 = (bf16[288,432]{1,0:T(8,128)(2,1)}, bf16[288,432]{1,0:T(8,128)(2,1)S(1)}, u32[]{:S(2)}, u32[]{:S(2)}) collective-permute-start(bf16[288,432]{1,0:T(8,128)(2,1)} %get-tuple-element.383), channel_id=1, source_target_pairs={{0,2},{1,3},{2,0},{3,1},{4,6},{5,7},{6,4},{7,5},{8,10},{9,11},{10,... | collective-permute-start | bytes 746504 | tf_op jit(solution)/shard_map/ppermute | solution.py:63
  461.7 30.6 %collective-permute-start.84 = (bf16[288,432]{1,0:T(8,128)(2,1)}, bf16[288,432]{1,0:T(8,128)(2,1)S(1)}, u32[]{:S(2)}, u32[]{:S(2)}) collective-permute-start(bf16[288,432]{1,0:T(8,128)(2,1)} %get-tuple-element.384), channel_id=1, source_target_pairs={{0,3},{1,0},{2,1},{3,2},{4,7},{5,4},{6,5},{7,6},{8,11},{9,8},{10,9... | collective-permute-start | bytes 746504 | tf_op jit(solution)/shard_map/ppermute | solution.py:63
  473.5 19.7 %collective-permute-start.81 = (bf16[16,8,1152]{2,1,0:T(8,128)(2,1)S(1)}, bf16[16,8,1152]{2,1,0:T(8,128)(2,1)S(1)}, u32[]{:S(2)}, u32[]{:S(2)}) collective-permute-start(bf16[16,8,1152]{2,1,0:T(8,128)(2,1)S(1)} %pad_maximum_fusion.2), channel_id=1, source_target_pairs={{0,16},{4,20},{8,24},{12,28},{16,0},{20,4},{24,8},{28,12},{1,17},{... | collective-permute-start | bytes 884744 | tf_op jit(solution)/shard_map/ppermute | solution.py:57
  (81 other events, 978.1 us)

commit v4 on v3

--- a/solution.py
+++ b/solution.py
@@ -79,10 +79,8 @@
         half = near[0].shape[0] // 2
         return box_send(near[0][:half], 4), box_send(near[1][half:], 2)
 
-    def chip_exchange(blocks, chip):
-        return [pick(blocks, chip)] + [
-            box_send(pick(blocks, chip ^ k), 2 * k) for k in range(1, BOX // 2)
-        ]
+    def chip_exchange(blocks):
+        return [blocks[0]] + [box_send(blocks[k], 2 * k) for k in range(1, BOX // 2)]
 
     def ring_sum(x, z):
         total = pick(x, z)
@@ -99,9 +97,9 @@
 
     def cost(microseconds):
         return pl.CostEstimate(
-            flops=int(microseconds * 5e8),
+            flops=int(microseconds * 1e8),
             transcendentals=0,
-            bytes_accessed=int(microseconds * 1.6e6),
+            bytes_accessed=int(microseconds * 3.2e5),
         )
 
     vmem = pl.BlockSpec(memory_space=pltpu.VMEM)
@@ -320,12 +318,13 @@
         slots = turned.shape[1]
         width = turned.shape[0] // 3
         count = width // HEAD_DIM
+        heads_at_once = 2 if count % 2 == 0 else 1
         scale = HEAD_DIM ** (-0.5)
 
         def kernel(live_ref, turned_ref, attended_ref, out_turned):
             live_keys = lax.broadcasted_iota(jnp.int32, (1, slots), 1) < live_ref[0]
 
-            def head(h, unused):
+            def head(h):
                 def rows(part):
                     first = pl.multiple_of(part * width + h * HEAD_DIM, 8)
                     return turned_ref[pl.ds(first, HEAD_DIM), :].astype(bf16)
@@ -337,16 +336,21 @@
                 highest = jnp.max(scores, axis=-1, keepdims=True)
                 total = jnp.sum(jnp.exp(scores - highest), axis=-1, keepdims=True)
                 probs = jnp.exp(scores - (highest + jnp.log(total)))
-                out = lax.dot_general(
+                return lax.dot_general(
                     rows(2),
                     probs.astype(bf16),
                     (((1,), (1,)), ((), ())),
                     preferred_element_type=f32,
                 )
-                out_turned[pl.ds(pl.multiple_of(h * HEAD_DIM, 8), HEAD_DIM), :] = out
+
+            def some_heads(i, unused):
+                outs = [head(i * heads_at_once + j) for j in range(heads_at_once)]
+                for j, out in enumerate(outs):
+                    first = pl.multiple_of((i * heads_at_once + j) * HEAD_DIM, 8)
+                    out_turned[pl.ds(first, HEAD_DIM), :] = out
                 return unused
 
-            lax.fori_loop(0, count, head, 0)
+            lax.fori_loop(0, count // heads_at_once, some_heads, 0)
             attended_ref[...] = out_turned[...].T.astype(bf16)
 
         return pl.pallas_call(
@@ -359,17 +363,23 @@
             compiler_params=params(60),
         )(live, turned)
 
-    def attention_back(turned, d_turned, live):
+    def attention_back(turned, d_turned, d_attn_turned, live, where_chip):
         width, slots = d_turned.shape
+        parts = (3 * width // 4, width // 4)
         count = width // HEAD_DIM
+        heads_at_once = 2 if count % 2 == 0 else 1
         scale = HEAD_DIM ** (-0.5)
 
-        def kernel(live_ref, turned_ref, d_ref, out_ref, total_ref):
+        def kernel(live_ref, chip_ref, turned_ref, d_ref, d_attn_ref, out_ref, *rest):
+            block_refs, total_ref = rest[:-1], rest[-1]
             live_keys = lax.broadcasted_iota(jnp.int32, (1, slots), 1) < live_ref[0]
 
-            def head(h, unused):
+            def place_of(h, part):
+                return pl.ds(pl.multiple_of(part * width + h * HEAD_DIM, 8), HEAD_DIM)
+
+            def head(h):
                 def place(part):
-                    return pl.ds(pl.multiple_of(part * width + h * HEAD_DIM, 8), HEAD_DIM)
+                    return place_of(h, part)
 
                 query = turned_ref[place(0), :].astype(bf16)
                 key_part = turned_ref[place(1), :].astype(bf16)
@@ -388,29 +398,39 @@
                 )
                 inner = jnp.sum(probs * d_probs, axis=-1, keepdims=True)
                 d_scores = (probs * (d_probs - inner)).astype(bf16)
-                total_ref[place(2), :] = jnp.dot(
-                    d_out, probs.astype(bf16), preferred_element_type=f32
-                )
-                total_ref[place(0), :] = scale * lax.dot_general(
+                d_value = jnp.dot(d_out, probs.astype(bf16), preferred_element_type=f32)
+                d_query = scale * lax.dot_general(
                     key_part, d_scores, (((1,), (1,)), ((), ())), preferred_element_type=f32
                 )
-                total_ref[place(1), :] = scale * jnp.dot(
-                    query, d_scores, preferred_element_type=f32
-                )
+                d_key = scale * jnp.dot(query, d_scores, preferred_element_type=f32)
+                return d_query, d_key, d_value
+
+            def some_heads(i, unused):
+                outs = [head(i * heads_at_once + j) for j in range(heads_at_once)]
+                for j, parts in enumerate(outs):
+                    for part, out in enumerate(parts):
+                        total_ref[place_of(i * heads_at_once + j, part), :] = out
                 return unused
 
-            lax.fori_loop(0, count, head, 0)
+            lax.fori_loop(0, count // heads_at_once, some_heads, 0)
             out_ref[...] = total_ref[...].astype(bf16)
-
+            for k, block in enumerate(block_refs):
+                first = pl.multiple_of(chip_ref[k] * parts[0], 16)
+                block[: parts[0], :] = total_ref[pl.ds(first, parts[0]), :].astype(bf16)
+                first = pl.multiple_of(chip_ref[k] * parts[1], 16)
+                block[parts[0] :, :] = d_attn_ref[pl.ds(first, parts[1]), :]
+
+        n_blocks = 4 if groups == 1 else 0
         return pl.pallas_call(
             kernel,
-            out_shape=jax.ShapeDtypeStruct((3 * width, slots), bf16),
-            in_specs=[smem, vmem, vmem],
-            out_specs=vmem,
+            out_shape=[jax.ShapeDtypeStruct((3 * width, slots), bf16)]
+            + [jax.ShapeDtypeStruct((width, slots), bf16)] * n_blocks,
+            in_specs=[smem, smem, vmem, vmem, vmem],
+            out_specs=[vmem] * (1 + n_blocks),
             scratch_shapes=[pltpu.VMEM((3 * width, slots), f32)],
             cost_estimate=cost(12),
             compiler_params=params(60),
-        )(live, turned, d_turned)
+        )(live, where_chip, turned, d_turned, d_attn_turned)
 
     def middle_forward(where, attended, tokens_own, owns, sets, bias_out, bias_up, mods):
         slots, width = attended.shape
@@ -430,11 +450,15 @@
                 normed_ref,
                 pre_ref,
                 act_ref,
-                turned_ref,
+                block0,
+                block1,
+                block2,
+                block3,
                 whole_out,
                 whole_up,
                 scratch_out,
                 scratch_up,
+                turned,
                 sems,
                 out_sems,
             ) = refs[2 + 2 * n_pieces :]
@@ -492,9 +516,10 @@
                 act_ref[rows, :] = gelu_tanh(pre_ref[rows, :]).astype(bf16)
 
             chunks(slots, 32, work)
-            for chip in range(4):
-                cols = slice(chip * quarter, (chip + 1) * quarter)
-                turned_ref[chip, :, :] = act_ref[:, cols].astype(f32).T.astype(bf16)
+            turned[...] = act_ref[...].astype(f32).T
+            for k, block in enumerate((block0, block1, block2, block3)):
+                first = pl.multiple_of(where_ref[fs + 1 + k] * quarter, 16)
+                block[...] = turned[pl.ds(first, quarter), :].astype(bf16)
 
             @pl.when(step == fs - 1)
             def last():
@@ -510,8 +535,8 @@
                 jax.ShapeDtypeStruct((slots, width), bf16),
                 jax.ShapeDtypeStruct((slots, hidden), f32),
                 jax.ShapeDtypeStruct((slots, hidden), bf16),
-                jax.ShapeDtypeStruct((4, fs * quarter, slots), bf16),
             ]
+            + [jax.ShapeDtypeStruct((fs * quarter, slots), bf16)] * 4
             + [jax.ShapeDtypeStruct(shape, bf16) for shape in shapes],
             grid_spec=pltpu.PrefetchScalarGridSpec(
                 num_scalar_prefetch=1,
@@ -529,12 +554,15 @@
                     whole((slots, width)),
                     pl.BlockSpec((slots, tile), lambda j, where_ref: (0, j)),
                     pl.BlockSpec((slots, tile), lambda j, where_ref: (0, j)),
-                    pl.BlockSpec((4, quarter, slots), lambda j, where_ref: (0, j, 0)),
-                    any_spec,
-                    any_spec,
+                ]
+                + [pl.BlockSpec((quarter, slots), lambda j, where_ref: (j, 0))] * 4
+                + [any_spec, any_spec],
+                scratch_shapes=[pltpu.VMEM(shape, bf16) for shape in shapes]
+                + [
+                    pltpu.VMEM((tile, slots), f32),
+                    pltpu.SemaphoreType.DMA((n_copies,)),
+                    pltpu.SemaphoreType.DMA((2,)),
                 ],
-                scratch_shapes=[pltpu.VMEM(shape, bf16) for shape in shapes]
-                + [pltpu.SemaphoreType.DMA((n_copies,)), pltpu.SemaphoreType.DMA((2,))],
             ),
             cost_estimate=cost(20),
             compiler_params=params(60),
@@ -559,22 +587,20 @@
         slots, width = d_mlp.shape
         hidden = pre_act.shape[1]
         tile = hidden // fs
+        if groups == 1:
+            turned_shapes = [jax.ShapeDtypeStruct((tile, slots), bf16)] * 4
+            turned_specs = [pl.BlockSpec((tile, slots), lambda j, where_ref: (0, 0))] * 4
+        else:
+            turned_shapes = [jax.ShapeDtypeStruct((hidden, slots), bf16)]
+            turned_specs = [pl.BlockSpec((tile, slots), lambda j, where_ref: (j, 0))]
         arrays, plan = piece_plan(pieces)
         own = in_blocks(own)
         shape = (fs,) + own.shape
 
         def kernel(where_ref, d_mlp_ref, pre_ref, own_ref, *refs):
             array_refs = refs[: len(arrays)]
-            (
-                d_pre_ref,
-                turned_ref,
-                sum_ref,
-                whole_ref,
-                d_act_ref,
-                scratch,
-                sems,
-                out_sem,
-            ) = refs[len(arrays) :]
+            d_pre_ref, *turned_refs, sum_ref, whole_ref = refs[len(arrays) : -4]
+            d_act_ref, scratch, sems, out_sem = refs[-4:]
             step = pl.program_id(0)
 
             def out():
@@ -609,7 +635,14 @@
 
             chunks(slots, 32, work)
             sum_ref[0] = jnp.sum(d_act_ref[...], axis=0, keepdims=True)
-            turned_ref[...] = d_act_ref[...].T.astype(bf16)
+            if groups == 1:
+                for k, turned_ref in enumerate(turned_refs):
+
+                    @pl.when(step == where_ref[fs + 4 + k])
+                    def block(turned_ref=turned_ref):
+                        turned_ref[...] = d_act_ref[...].T.astype(bf16)
+            else:
+                turned_refs[0][...] = d_act_ref[...].T.astype(bf16)
 
             @pl.when(step == fs - 1)
             def last():
@@ -619,7 +652,7 @@
             kernel,
             out_shape=[
                 jax.ShapeDtypeStruct((slots, hidden), bf16),
-                jax.ShapeDtypeStruct((hidden, slots), bf16),
+                *turned_shapes,
                 jax.ShapeDtypeStruct((fs, 1, tile), f32),
                 jax.ShapeDtypeStruct(shape, bf16),
             ],
@@ -634,7 +667,7 @@
                 + [any_spec] * len(arrays),
                 out_specs=[
                     pl.BlockSpec((slots, tile), lambda j, where_ref: (0, j)),
-                    pl.BlockSpec((tile, slots), lambda j, where_ref: (j, 0)),
+                    *turned_specs,
                     pl.BlockSpec((1, 1, tile), lambda j, where_ref: (j, 0, 0)),
                     any_spec,
                 ],
@@ -893,117 +926,119 @@
             mods,
         )
 
-    def column_grad(where, lefts, rights, start, stop):
-        slots, n = rights[0].shape[1], (stop - start) // 2
-        right_rows = rights[0].shape[0]
-        width = lefts[0].shape[1]
+    def column_grad(where, items, rights):
+        slots = rights[0].shape[1]
+        width = items[0][0][0].shape[1]
         tile = width // 3
         half = slots // 2
-
-        def kernel(where_ref, x0, x1, x2, x3, x4, y0, y1, y2, y3, keep_ref, send_ref):
+        counts = [(stop - start) // 2 for unused, start, stop in items]
+        n_out = sum(counts)
+        lefts = [left for box, unused, unused_stop in items for left in box]
+
+        def kernel(where_ref, *refs):
             core = where_ref[0]
-            for out_ref, first in ((keep_ref, core * n), (send_ref, (1 - core) * n)):
-                rows = pl.ds(pl.multiple_of(start + first, 16), n)
-                total = None
-                for x, y, cols in (
-                    (x0, y0, slice(None)),
-                    (x1, y1, slice(None)),
-                    (x2, y2, slice(None)),
-                    (x3, y3, slice(0, half)),
-                    (x4, y3, slice(half, slots)),
-                ):
-                    part = jnp.dot(y[rows, cols], x[...], preferred_element_type=f32)
-                    total = part if total is None else total + part
-                out_ref[...] = total
+            y0, y1, y2, y3, keep_ref, send_ref = refs[len(lefts) :]
+            for i, (unused, start, unused_stop) in enumerate(items):
+                x0, x1, x2, x3, x4 = refs[5 * i : 5 * i + 5]
+                n = counts[i]
+                below = sum(counts[:i])
+                for out_ref, first in ((keep_ref, core * n), (send_ref, (1 - core) * n)):
+                    rows = pl.ds(pl.multiple_of(start + first, 16), n)
+                    total = None
+                    for x, y, cols in (
+                        (x0, y0, slice(None)),
+                        (x1, y1, slice(None)),
+                        (x2, y2, slice(None)),
+                        (x3, y3, slice(0, half)),
+                        (x4, y3, slice(half, slots)),
+                    ):
+                        part = jnp.dot(y[rows, cols], x[...], preferred_element_type=f32)
+                        total = part if total is None else total + part
+                    out_ref[below : below + n, :] = total
 
         left_specs = [
             pl.BlockSpec((left.shape[0], tile), lambda i, where_ref: (0, i)) for left in lefts
         ]
-        right_spec = pl.BlockSpec((right_rows, slots), lambda i, where_ref: (0, 0))
-        out_spec = pl.BlockSpec((n, tile), lambda i, where_ref: (0, i))
+        right_spec = pl.BlockSpec(rights[0].shape, lambda i, where_ref: (0, 0))
+        out_spec = pl.BlockSpec((n_out, tile), lambda i, where_ref: (0, i))
         return pl.pallas_call(
             kernel,
-            out_shape=[jax.ShapeDtypeStruct((n, width), f32)] * 2,
+            out_shape=[jax.ShapeDtypeStruct((n_out, width), f32)] * 2,
             grid_spec=pltpu.PrefetchScalarGridSpec(
                 num_scalar_prefetch=1,
                 grid=(width // tile,),
                 in_specs=left_specs + [right_spec] * 4,
                 out_specs=[out_spec] * 2,
             ),
-            cost_estimate=cost(7),
+            cost_estimate=cost(8),
             compiler_params=params(60),
         )(where, *lefts, *rights)
 
-    def split_grad(where, keep, got):
-        n, width = keep.shape
-        rows = width // fs
+    def sums_message(first_sums, middle_sums, output_sums, d_pre_sums, cond_act):
+        width = cond_act.shape[1]
+        extra = d_pre_sums.shape[0]
+
+        def kernel(first_ref, middle_ref, output_ref, d_pre_ref, cond_ref, out_ref):
+            out_ref[0:2, :] = first_ref[0:2, :].astype(bf16).astype(f32)
+            out_ref[2:5, :] = middle_ref[0:3, :].astype(bf16).astype(f32)
+            out_ref[5:6, :] = output_ref[0:1, :].astype(bf16).astype(f32)
+            for row in (6, 7):
+                out_ref[row : row + 1, :] = cond_ref[...].astype(f32)
+            out_ref[8:10, :] = first_ref[2:4, :]
+            out_ref[10:11, :] = middle_ref[3:4, :]
+            out_ref[11:12, :] = output_ref[1:2, :]
+            out_ref[12:, :] = d_pre_ref[...]
+
+        return pl.pallas_call(
+            kernel,
+            out_shape=jax.ShapeDtypeStruct((12 + extra, width), f32),
+            in_specs=[vmem] * 5,
+            out_specs=vmem,
+            cost_estimate=cost(1),
+            compiler_params=params(60),
+        )(first_sums, middle_sums, output_sums, d_pre_sums, cond_act)
+
+    def column_total(pairs):
+        width = pairs[0][0].shape[1]
+        n = sum(keep.shape[0] for keep, unused in pairs)
         padded = -(-n // 128) * 128
 
-        def kernel(where_ref, keep_ref, got_ref, own_ref, *rest):
-            send_refs, turned = rest[:-1], rest[-1]
+        def kernel(*refs):
             for first in range(0, width, 128):
-                total = keep_ref[:, first : first + 128] + got_ref[:, first : first + 128]
+                cols = slice(first, first + 128)
+                totals = [
+                    refs[2 * i][:, cols] + refs[2 * i + 1][:, cols] for i in range(len(pairs))
+                ]
                 if padded > n:
-                    total = jnp.concatenate([total, jnp.zeros((padded - n, 128), f32)], axis=0)
-                turned[first : first + 128, :] = total.T[:, :n]
-            z = where_ref[0]
-            own_ref[...] = turned[pl.ds(pl.multiple_of(z * rows, 16), rows), :]
-            for k, send_ref in enumerate(send_refs):
-                target = lax.rem(z + k + 1, fs)
-                block = turned[pl.ds(pl.multiple_of(target * rows, 16), rows), :]
-                send_ref[...] = block.astype(bf16)
-
-        whole = pl.BlockSpec(memory_space=pltpu.VMEM)
+                    totals.append(jnp.zeros((padded - n, 128), f32))
+                total = jnp.concatenate(totals, axis=0) if len(totals) > 1 else totals[0]
+                refs[-1][cols, :] = total.T.astype(bf16)
+
         return pl.pallas_call(
             kernel,
-            out_shape=[jax.ShapeDtypeStruct((rows, n), f32)]
-            + [jax.ShapeDtypeStruct((rows, n), bf16)] * (fs - 1),
-            in_specs=[pl.BlockSpec(memory_space=pltpu.SMEM), whole, whole],
-            out_specs=[whole] * fs,
-            scratch_shapes=[pltpu.VMEM((width, n), f32)],
+            out_shape=jax.ShapeDtypeStruct((width, padded), bf16),
+            in_specs=[vmem] * (2 * len(pairs)),
+            out_specs=vmem,
             cost_estimate=cost(4),
             compiler_params=params(60),
-        )(where, keep, got)
-
-    def split_rows(where, keep, got):
-        count, rows, width = keep.shape
-
-        def kernel(where_ref, keep_ref, got_ref, own_ref, *send_refs):
-            z = where_ref[0]
-            own_ref[...] = keep_ref[z] + got_ref[z]
-            for k, send_ref in enumerate(send_refs):
-                target = lax.rem(z + k + 1, count)
-                send_ref[...] = (keep_ref[target] + got_ref[target]).astype(bf16)
-
-        return pl.pallas_call(
-            kernel,
-            out_shape=[jax.ShapeDtypeStruct((rows, width), f32)]
-            + [jax.ShapeDtypeStruct((rows, width), bf16)] * (count - 1),
-            in_specs=[smem, vmem, vmem],
-            out_specs=[vmem] * count,
+        )(*[each for pair in pairs for each in pair])
+
+    def row_total(keep, got):
+        def kernel(keep_ref, got_ref, out_ref):
+            out_ref[...] = (keep_ref[...] + got_ref[...]).astype(bf16)
+
+        total = pl.pallas_call(
+            kernel,
+            out_shape=jax.ShapeDtypeStruct(keep.shape, bf16),
+            in_specs=[vmem] * 2,
+            out_specs=vmem,
             cost_estimate=cost(3),
             compiler_params=params(60),
-        )(where, keep, got)
-
-    def down_columns(parts):
-        rows, width = parts[0].shape
-        cols = width // BOX
-
-        def kernel(*refs):
-            total = refs[0][...]
-            for ref in refs[1:-1]:
-                total = total + ref[...].astype(f32)
-            for block in range(BOX):
-                refs[-1][block] = total[:, block * cols : (block + 1) * cols]
-
-        return pl.pallas_call(
-            kernel,
-            out_shape=jax.ShapeDtypeStruct((BOX, rows, cols), f32),
-            in_specs=[vmem] * len(parts),
-            out_specs=vmem,
-            cost_estimate=cost(2),
-            compiler_params=params(60),
-        )(*parts)
+        )(keep, got)
+        return total.reshape(-1, keep.shape[2])
+
+    def fsdp_sum(x):
+        return lax.psum_scatter(x, "fsdp", scatter_dimension=0, tiled=True)
 
     def row_grad(where, lefts, rights):
         rows = lefts[0].shape[0] // fs
@@ -1075,7 +1110,9 @@
         near = 2 * side + core
         far = 2 * (1 - side) + core
         where = jnp.stack(
-            [lax.rem(z - k + fs, fs) for k in range(fs)] + [near, far, near ^ 1, far ^ 1]
+            [lax.rem(z - k + fs, fs) for k in range(fs)]
+            + [near, far, near ^ 1, far ^ 1]
+            + [chip ^ k for k in range(4)]
         ).astype(jnp.int32)
         where_core = core.reshape(1).astype(jnp.int32)
         where_wide = jnp.stack(
@@ -1089,10 +1126,10 @@
         def quarter_of(shard):
             return pick(in_blocks(shard), near)
 
-        cond_rows = ring_gather(cond_act)
+        qkv_quarter = quarter_of(w_qkv)
+        cond_rows = ring_gather(after(cond_act, qkv_quarter))
         raw = jnp.concatenate([tokens[0], cotangent[0]], axis=1)
-        raw_near = chip_near(raw)
-        qkv_helds = [ring_send(quarter_of(w_qkv), 1)]
+        qkv_helds = [ring_send(qkv_quarter, 1)]
         mid_rows = jnp.concatenate(
             [pick(in_blocks(w_out), chip), pick(in_blocks(w_up), chip)], axis=-1
         )
@@ -1106,8 +1143,8 @@
             jnp.zeros((fs * ada_shard,), f32), b_ada.astype(f32), z * ada_shard, 0
         ).reshape(6, width)
         small = jnp.concatenate([b_qv, b_out, b_down, b_up]).astype(f32).reshape(-1, width)
-        cond_rows, bias_ada, small, mid_eighth, down_quarter = gated(
-            (cond_rows, bias_ada, small, mid_eighth, down_quarter)
+        cond_rows, qkv_helds, bias_ada, small, mid_eighth, down_quarter = gated(
+            (cond_rows, qkv_helds, bias_ada, small, mid_eighth, down_quarter)
         )
 
         rows_z = width // fs
@@ -1115,67 +1152,41 @@
         conds_z = lax.dynamic_slice_in_dim(conds, z * rows_z, rows_z, 1)
         partials = modulation_parts(conds_z, w_ada, bias_ada, small)
         partials = [partials[0]] + [ring_send(partials[k], fs - k) for k in range(1, fs)]
+        raw_near = chip_near(after(raw, conds_z))
         qkv_helds.append(ring_send(qkv_helds[-1], 1))
-        partials, qkv_helds, raw_near = gated((partials, qkv_helds, raw_near))
+        partials, qkv_helds = gated((partials, qkv_helds))
 
         live = (grid_sizes[0, 0] * grid_sizes[0, 1]).reshape(1)
         mods, head = modulation_rows(partials, live)
-        heads_got = [box_send(head, bits) for bits in (2, 4, 6)]
-        raw_far = chip_far(raw_near)
+        (normed,), (d_mlp,) = other_heads((raw,), (0,), (head,))
         qkv_helds.append(ring_send(qkv_helds[-1], 1))
-        mods, head, heads_got, raw_far, qkv_helds = gated(
-            (mods, head, heads_got, raw_far, qkv_helds)
+        mods, head, normed, d_mlp, raw_near, qkv_helds = gated(
+            (mods, head, normed, d_mlp, raw_near, qkv_helds)
         )
 
         qkv_mine = jnp.stack(qkv_helds)
         qkv_other = side_send(qkv_mine)
         qkv_mine_got = box_send(qkv_mine, 1)
-        qkv_other_got = box_send(qkv_other, 1)
         mid_helds = [ring_send(after(mid_eighth, qkv_mine), 1)]
-        mid_helds.append(ring_send(mid_helds[-1], 1))
-        (normed,), (d_mlp,) = other_heads((raw,), (0,), (head,))
         bias_rows = [each[6:].reshape(-1) for each in partials]
         bias_rows = jnp.stack(bias_rows + bias_rows)
         biases = lax.dynamic_slice_in_dim(bias_rows, lax.rem(fs - z, fs), fs, 0)
         ends = [0]
         for bias in (b_qv, b_out, b_down, b_up):
             ends.append(ends[-1] + bias.shape[0])
-        bias_qv, bias_out, bias_down, bias_up = [
-            biases[:, ends[i] : ends[i + 1]].reshape(-1) for i in range(4)
-        ]
-        (
-            qkv_mine,
-            qkv_other,
-            qkv_mine_got,
-            qkv_other_got,
-            mid_helds,
-            normed,
-            d_mlp,
-            bias_qv,
-            bias_out,
-            bias_down,
-            bias_up,
-        ) = gated(
-            (
-                qkv_mine,
-                qkv_other,
-                qkv_mine_got,
-                qkv_other_got,
-                mid_helds,
-                normed,
-                d_mlp,
-                bias_qv,
-                bias_out,
-                bias_down,
-                bias_up,
-            )
-        )
+        biases = [biases[:, ends[i] : ends[i + 1]].reshape(-1) for i in range(4)]
+        qkv_mine, qkv_other, qkv_mine_got, mid_helds, biases = gated(
+            (qkv_mine, qkv_other, qkv_mine_got, mid_helds, biases)
+        )
+        bias_qv, bias_out, bias_down, bias_up = biases
 
         last = fs - 1
 
         def in_order(array):
             return [(array, k) for k in range(last)]
 
+        qkv_other_got = box_send(qkv_other, 1)
+        raw_far = chip_far([after(each, qkv_other) for each in raw_near])
         mid_helds.append(ring_send(mid_helds[-1], 1))
         turned, qkv_full = projection(
             where,
@@ -1184,13 +1195,18 @@
             [in_order(each) for each in (qkv_mine, qkv_other, qkv_mine_got, qkv_other_got)],
             bias_qv.reshape(2, width),
         )
-        turned, qkv_full, mid_helds = gated((turned, qkv_full, mid_helds))
+        turned, qkv_full, mid_helds, raw_far = gated((turned, qkv_full, mid_helds, raw_far))
+
+        heads_got = [box_send(after(head, turned), bits) for bits in (2, 4, 6)]
+        mid_helds.append(ring_send(mid_helds[-1], 1))
+        attended = attention(turned, live)
+        attended, mid_helds, heads_got = gated((attended, mid_helds, heads_got))
 
         mid_mine = jnp.concatenate(mid_helds)
         mid_near = chip_near(mid_mine)
         mid_got = [box_send(mid_mine, 1)]
         down_helds = [ring_send(after(down_quarter, mid_mine), 1)]
-        attended = attention(turned, live)
+        down_helds.append(ring_send(down_helds[-1], 1))
         normed_box, d_mlp_box = other_heads(
             (*raw_near, *raw_far), (0, 0, 0, slots // 2), (*heads_got, heads_got[2])
         )
@@ -1205,10 +1221,8 @@
         attended, mid_far, mid_got, down_helds = gated((attended, mid_far, mid_got, down_helds))
 
         mid_got += [box_send(each, 1) for each in mid_far]
-        down_helds.append(ring_send(down_helds[-1], 1))
-        down_others = [side_send(each) for each in down_helds[:-1]]
-        attended_near = chip_near(attended)
-        attn_out, normed_two, pre_act, activated, act_blocks, out_full, up_full = middle_forward(
+        down_others = [side_send(each) for each in down_helds]
+        attn_out, normed_two, pre_act, activated, *act_blocks, out_full, up_full = middle_forward(
             where_wide,
             attended,
             tokens[0],
@@ -1218,90 +1232,29 @@
             bias_up,
             mods,
         )
-        attended_near, down_helds, down_others, act_blocks, normed_two = gated(
-            (attended_near, down_helds, down_others, act_blocks, normed_two)
-        )
-
-        down_others.append(side_send(down_helds[-1]))
-        down_helds_got = [box_send(each, 1) for each in down_helds]
-        down_others_got = [box_send(each, 1) for each in down_others]
-        act_blocks, down_helds, down_others, down_helds_got, down_others_got = gated(
-            (act_blocks, down_helds, down_others, down_helds_got, down_others_got)
-        )
-
-        act_box = chip_exchange(act_blocks, chip)
-        normed_two_near = chip_near(normed_two)
-        d_pre, d_pre_turned, d_pre_sums, down_full = hidden_back(
+        down_helds, down_others, act_blocks, normed_two = gated(
+            (down_helds, down_others, act_blocks, normed_two)
+        )
+
+        down_got = [[box_send(each, 1) for each in kind] for kind in (down_helds, down_others)]
+        act_blocks, down_got = gated((act_blocks, down_got))
+
+        act_box = chip_exchange(act_blocks)
+        d_pre, *d_pre_turned, d_pre_sums, down_full = hidden_back(
             where,
             d_mlp,
             w_down,
-            [
-                [(each, None) for each in kind]
-                for kind in (down_helds, down_others, down_helds_got, down_others_got)
-            ],
+            [[(each, None) for each in kind] for kind in (down_helds, down_others, *down_got)],
             pre_act,
         )
 
         def column_blocks(grad_t):
             n = grad_t.shape[0] // dp
             blocks = grad_t.reshape(groups, BOX, n, slots).transpose(1, 0, 2, 3)
-            return blocks.reshape(BOX // 2, 2 * groups * n, slots)
-
-        d_pre_blocks = column_blocks(d_pre_turned)
-        d_pre, d_pre_blocks, act_box, normed_two_near = gated(
-            (d_pre, d_pre_blocks, act_box, normed_two_near)
-        )
-
-        d_pre_box = chip_exchange(d_pre_blocks, chip)
-        keep_down, send_down = row_grad(where_core, act_box, d_mlp_box)
-        got_down = box_send(send_down, 1)
-        d_middle, d_attn_turned, d_attended_turned, middle_sums = middle_back(
-            d_pre, up_full, out_full, attn_out, tokens[0], cotangent[0], mods, live
-        )
-        d_attn_blocks = column_blocks(d_attn_turned)
-        d_projected = attention_back(turned, d_attended_turned, live)
-        d_projected_blocks = column_blocks(d_projected)
-        d_projected, d_projected_blocks, d_attn_blocks, d_pre_box, got_down = gated(
-            (d_projected, d_projected_blocks, d_attn_blocks, d_pre_box, got_down)
-        )
-
-        def after_core(grad_parts):
-            grad, *sends = split_grad(where[:1], *grad_parts)
-            return [grad] + [ring_send(sent, k + 1) for k, sent in enumerate(sends)]
-
-        def own_block_cols(parts):
-            grad = sum((each.astype(f32) for each in parts[1:]), parts[0])
-            rows, cols = grad.shape
-            grad = grad.reshape(rows, groups, cols // groups)
-            return group_sum(grad.transpose(1, 0, 2), group)
-
-        last_blocks = jnp.concatenate([d_projected_blocks, d_attn_blocks], axis=1)
-        last_box = chip_exchange(last_blocks, chip)
-        normed_two_far = chip_far(normed_two_near)
-        attended_far = chip_far(attended_near)
-        attended_box = [attended, *attended_near, *attended_far]
-        normed_two_box = [normed_two, *normed_two_near, *normed_two_far]
-        keep_up, send_up = column_grad(
-            where_core, normed_two_box, d_pre_box, 0, d_pre_box[0].shape[0]
-        )
-        got_up = box_send(send_up, 1)
-        down_parts = split_rows(where[:1], keep_down, got_down)
-        down_parts = [down_parts[0]] + [
-            ring_send(sent, k + 1) for k, sent in enumerate(down_parts[1:])
-        ]
-        grad_tokens, first_sums = first_back(d_projected, qkv_full, tokens[0], d_middle, mods)
-        last_box, attended_box, down_parts, first_sums, keep_up, got_up = gated(
-            (last_box, attended_box, down_parts, first_sums, keep_up, got_up)
-        )
-
-        cut = d_projected_blocks.shape[1]
-        keep_qkv, send_qkv = column_grad(where_core, normed_box, last_box, 0, cut)
-        got_qkv = box_send(send_qkv, 1)
-        keep_out, send_out = column_grad(
-            where_core, attended_box, last_box, cut, last_box[0].shape[0]
-        )
-        got_out = box_send(send_out, 1)
-        up_parts = after_core((keep_up, got_up))
+            blocks = blocks.reshape(BOX // 2, 2 * groups * n, slots)
+            return [pick(blocks, chip ^ k) for k in range(BOX // 2)]
+
+        d_pre_blocks = d_pre_turned if groups == 1 else column_blocks(d_pre_turned[0])
         output, output_sums = output_rows(
             activated,
             down_full,
@@ -1313,41 +1266,75 @@
             mods,
             live,
         )
-        d_mod = jnp.concatenate([first_sums[0:2], middle_sums[0:3], output_sums[0:1]])
-        cond_row = cond_act.astype(f32)
-        images = jnp.concatenate([d_mod, cond_row, cond_row]).astype(bf16)
-        total = jnp.concatenate(
-            [
-                first_sums[2:4],
-                middle_sums[3:4],
-                output_sums[1:2],
-                d_pre_sums.reshape(hidden // width, width),
+        d_pre, d_pre_blocks, act_box, normed_two, output_sums = gated(
+            (d_pre, d_pre_blocks, act_box, normed_two, output_sums)
+        )
+
+        d_pre_box = chip_exchange(d_pre_blocks)
+        keep_down, send_down = row_grad(where_core, act_box, d_mlp_box)
+        d_middle, d_attn_turned, d_attended_turned, middle_sums = middle_back(
+            d_pre, up_full, out_full, attn_out, tokens[0], cotangent[0], mods, live
+        )
+        d_attended_turned, d_attn_turned, d_pre_box, keep_down, send_down, normed_two = gated(
+            (d_attended_turned, d_attn_turned, d_pre_box, keep_down, send_down, normed_two)
+        )
+
+        normed_two_near = chip_near(normed_two)
+        total_down = row_total(keep_down, box_send(send_down, 1))
+        d_projected, *last_blocks = attention_back(
+            turned, d_attended_turned, d_attn_turned, live, where[fs + 4 :]
+        )
+        if groups > 1:
+            last_blocks = [
+                jnp.concatenate(pair)
+                for pair in zip(column_blocks(d_projected), column_blocks(d_attn_turned))
             ]
-        )
-        images_near = jnp.stack(ring_gather(images))
-        totals = ring_gather(total)
-        got_qkv, got_out, up_parts, images_near, totals = gated(
-            (got_qkv, got_out, up_parts, images_near, totals)
-        )
-
-        qkv_parts = after_core((keep_qkv, got_qkv))
-        out_parts = after_core((keep_out, got_out))
-        down_rows = down_parts[0].shape[0]
-        if groups == 1:
-            down_blocks = down_columns(down_parts)
-            parts = lax.all_to_all(down_blocks, "dp", 0, 0, tiled=True)
-        else:
-            grad_down = own_block_cols(down_parts)
-            down_blocks = grad_down.reshape(down_rows, BOX, width // dp).transpose(1, 0, 2)
-            parts = [pick(down_blocks, place)] + [
-                box_send(pick(down_blocks, place ^ k), k) for k in range(1, BOX)
-            ]
-            parts = jnp.stack(parts)
-            parts = jnp.stack([pick(parts, place ^ k) for k in range(BOX)])
-        grad_w_down = parts.reshape(BOX * down_rows, width // dp)
-        grad_w_up = own_block_cols(up_parts)
-        grad_w_out = own_block_cols(out_parts)
-        grad_w_qkv = own_block_cols(qkv_parts)
+        normed_two_far = chip_far([after(each, d_projected) for each in normed_two_near])
+        normed_two_box = [normed_two, *normed_two_near, *normed_two_far]
+        d_projected, last_blocks, normed_two_box, total_down = gated(
+            (d_projected, last_blocks, normed_two_box, total_down)
+        )
+        grad_down = fsdp_sum(total_down)
+
+        last_box = chip_exchange(last_blocks)
+        grad_tokens, first_sums = first_back(d_projected, qkv_full, tokens[0], d_middle, mods)
+        keep_up, send_up = column_grad(
+            after(where_core, first_sums), [(normed_two_box, 0, d_pre_box[0].shape[0])], d_pre_box
+        )
+        last_box, first_sums, keep_up, send_up = gated((last_box, first_sums, keep_up, send_up))
+
+        total_up = column_total([(keep_up, box_send(send_up, 1))])
+        attended_near = chip_near(attended)
+        cut = 3 * last_box[0].shape[0] // 4
+        keep_qkv, send_qkv = column_grad(where_core, [(normed_box, 0, cut)], last_box)
+        attended_far = chip_far([after(each, (keep_qkv, total_up)) for each in attended_near])
+        attended_box = [attended, *attended_near, *attended_far]
+        message = sums_message(
+            first_sums, middle_sums, output_sums, d_pre_sums.reshape(-1, width), cond_act
+        )
+        messages = ring_gather(message)
+        total_up, keep_qkv, send_qkv, messages, attended_box = gated(
+            (total_up, keep_qkv, send_qkv, messages, attended_box)
+        )
+        grad_up = fsdp_sum(total_up)
+
+        got_qkv = box_send(send_qkv, 1)
+        keep_out, send_out = column_grad(
+            where_core, [(attended_box, cut, last_box[0].shape[0])], last_box
+        )
+        got_out = box_send(send_out, 1)
+        grad_last = fsdp_sum(column_total([(keep_qkv, got_qkv), (keep_out, got_out)]))
+        images_near = jnp.stack([each[:8] for each in messages]).astype(bf16)
+        totals = [each[8:] for each in messages]
+
+        def over_groups(grad):
+            rows, cols = grad.shape
+            return group_sum(grad.reshape(rows, groups, -1).transpose(1, 0, 2), group)
+
+        cut_cols, last_cols = cut // 2, last_box[0].shape[0] // 2
+        grad_w_up = over_groups(grad_up[:, : d_pre_box[0].shape[0] // 2].astype(f32))
+        grad_w_qkv = over_groups(grad_last[:, :cut_cols].astype(f32))
+        grad_w_out = over_groups(grad_last[:, cut_cols:last_cols].astype(f32))
 
         images, total = images_near, sum(totals[1:], totals[0])
         for bits in (1, 2, 4):
@@ -1357,6 +1344,18 @@
         for k in range(1, groups):
             images = jnp.concatenate([images, group_send(images_box, k)])
             total = total + group_send(total_box, k)
+        grad_down = over_groups(after(grad_down, got_qkv).astype(f32))
+        down_rows = grad_down.shape[0]
+        down_blocks = grad_down.reshape(down_rows, BOX, -1).transpose(1, 0, 2)
+        if groups == 1:
+            parts = lax.all_to_all(down_blocks, "dp", 0, 0, tiled=True)
+        else:
+            parts = [pick(down_blocks, place)] + [
+                box_send(pick(down_blocks, place ^ k), k) for k in range(1, BOX)
+            ]
+            parts = jnp.stack(parts)
+            parts = jnp.stack([pick(parts, place ^ k) for k in range(BOX)])
+        grad_w_down = parts.reshape(BOX * down_rows, width // dp)
         conds_all = lax.dynamic_slice_in_dim(images[:, 6], z * rows_z, rows_z, 1)
         d_mod_all = images[:, :6]
         ada_cols = 6 * width // dp

time: 501 us -> 448 us (0.89)
  waiting for transfers between devices: 143 us -> 107 us
  starting transfers between devices: 128 us -> 100 us
  between operations: 2.85 us -> 15.9 us
  Pallas kernels: 172 us -> 163 us
    ppermute x36 -> x21, waiting for transfers between devices: 80.8 us -> 41.4 us  [ring_send(): return lax.ppermute(x, 'fsdp', [(i, (i + hops) % fs) for i in range(fs)])]
    ppermute x4, waiting for transfers between devices: 24.2 us -> 1.57 us  [side_send(): lax.ppermute(x, 'dp', [(i, i ^ (4 if i & 1 else 2)) for i in range(dp)])]
    ppermute x51, starting transfers between devices: 68.5 us -> 49.9 us  [box_send(): return lax.ppermute(x, 'dp', [(i, i ^ bits) for i in range(dp)])]
    reduce_scatter x0 -> x3, waiting for transfers between devices: none -> 14.9 us  [fsdp_sum(): return lax.psum_scatter(x, 'fsdp', scatter_dimension=0, tiled=True)]
    all_to_all x1, waiting for transfers between devices: 0.01 us -> 10.8 us  [body(): parts = lax.all_to_all(down_blocks, 'dp', 0, 0, tiled=True)]
    ppermute x36 -> x21, starting transfers between devices: 50.7 us -> 41 us  [ring_send(): return lax.ppermute(x, 'fsdp', [(i, (i + hops) % fs) for i in range(fs)])]
    pallas_call x9 -> x8, Pallas kernels: 54.1 us -> 48.5 us  [the longest x3 20.3 us: column_grad(): pl.pallas_call(kernel, out_shape=[jax.ShapeDtypeStruct((n_out, width), f3...]
    unnamed x124 -> x128, local copies, waits for them, and re-layouts: 10.7 us -> 15.5 us
  transfers between devices with their start and end apart: 92 -> 80, of which waited for: 23 -> 30; matrix products, arithmetic and copies ran while one was open for 7% -> 8% of each run, Pallas kernels for 30% -> 37%
where the time goes in v4:
time: 448 us; the launch traced here: 443 us
  Pallas kernels  163 us (36%)
  waiting for transfers between devices  107 us (24%)
  starting transfers between devices  100 us (22%)
  local copies, waits for them, and re-layouts  40.2 us (9%)
  between operations  15.9 us (4%)
  other arithmetic  11.8 us (3%)
  matrix products  4.63 us (1%)
    ppermute x51, starting transfers between devices, box_send(): return lax.ppermute(x, 'dp', [(i, i ^ bits) for i in range(dp)])  49.9 us
    ppermute x21, waiting for transfers between devices, ring_send(): return lax.ppermute(x, 'fsdp', [(i, (i + hops) % fs) for i in range(fs)])  41.4 us
    ppermute x21, starting transfers between devices, ring_send(): return lax.ppermute(x, 'fsdp', [(i, (i + hops) % fs) for i in range(fs)])  41 us
    ppermute x51, waiting for transfers between devices, box_send(): return lax.ppermute(x, 'dp', [(i, i ^ bits) for i in range(dp)])  38.2 us
    pallas_call x3, Pallas kernels, column_grad(): pl.pallas_call(kernel, out_shape=[jax.ShapeDtypeStruct((n_out, width), f3...  20.3 us
    pallas_call x1, Pallas kernels, middle_forward(): pl.pallas_call(kernel, out_shape=[jax.ShapeDtypeStruct((slots, width), f3...  19.6 us
    pallas_call x1, Pallas kernels, hidden_back(): pl.pallas_call(kernel, out_shape=[jax.ShapeDtypeStruct((slots, hidden), b...  17.1 us
    unnamed x128, local copies, waits for them, and re-layouts  15.5 us
  transfers between devices with their start and end apart: 80, of which 30 were waited for; matrix products, arithmetic and copies ran while one was open for 8% of the time, Pallas kernels for 37%

profile of v4, /device:TPU:25, one launch (start us, length us, event | category | flops | bytes accessed | tf_op | source)
XLA Modules:
  0.0 442.8 jit_solution(7504213619725734968)
XLA Ops:
  10.7 3.1 collective-permute-start.3
  17.9 2.0 dynamic-slice_bitcast_fusion
  21.3 1.6 collective-permute-done.3
  26.1 4.0 collective-permute-start.7
  30.1 3.5 shard_map.237
  33.9 5.4 %collective-permute-done.4.refs_1_ = f32[8,1152]{1,0:T(8,128)S(1)} collective-permute-done((f32[8,1152]{1,0:T(8,128)}, f32[8,1152]{1,0:T(8,128)S(1)}, u32[]{:S(2)}, u32[]{:S(2)}) %collective-permute-start.4) | collective-permute-done | bytes 36896 | tf_op jit(solution)/shard_map/ppermute | solution.py:63
  39.2 4.0 collective-permute-start.6
  44.6 3.5 collective-permute-start.10
  51.4 3.9 shard_map.239
  55.3 2.1 collective-permute-done.10
  60.2 2.9 collective-permute-start.12
  63.9 3.8 collective-permute-start.13
  69.1 8.1 %collective-permute-done.13 = bf16[9,8,2944]{2,1,0:T(8,128)(2,1)} collective-permute-done((bf16[9,8,2944]{2,1,0:T(8,128)(2,1)}, bf16[9,8,2944]{2,1,0:T(8,128)(2,1)}, u32[]{:S(2)}, u32[]{:S(2)}) %collective-permute-start.13) | collective-permute-done | bytes 423968 | tf_op jit(solution)/shard_map/ppermute | solution.py:63
  77.2 1.6 collective-permute-done.11.refs_1_
  78.8 3.4 collective-permute-start.14
  83.7 3.8 collective-permute-start.15
  88.6 9.4 %shard_map.240 = (f32[3456,256]{1,0:T(8,128)}, bf16[4,4,9,8,3456]{4,3,2,1,0:T(8,128)(2,1)}) custom-call(s32[12]{0:T(128)} %stack.119.where_ref, bf16[256,1152]{1,0:T(8,128)(2,1)} %get-tuple-element.402.normed_ref.refs_0_, f32[2,1152]{1,0:T(2,128)} %reshape.136.bias_ref, bf16[4,9,8,3456]{3,2,1,0:T(8,128)(2,1)} %bitcast.102, ...), custom_call_target="tpu_custom_call" | custom-call | flops 1100000000 | bytes 3520000 | tf_op jit(solution)/shard_map/pallas_call | solution.py:299
  98.2 3.8 collective-permute-start.18
  104.6 8.7 %shard_map.241.attended_ref.refs_0_ = bf16[256,1152]{1,0:T(8,128)(2,1)} custom-call(s32[1]{0:T(128)} %bitcast.live_ref, f32[3456,256]{1,0:T(8,128)} %get-tuple-element.264.turned_ref), custom_call_target="tpu_custom_call" | custom-call | flops 1100000000 | bytes 3520000 | tf_op jit(solution)/shard_map/pallas_call | solution.py:356
  113.4 1.9 constant_dynamic-update-slice_fusion.2
  115.3 1.8 constant_dynamic-update-slice_fusion.1
  120.3 2.8 collective-permute-start.24
  123.0 9.0 %collective-permute-done.25.refs_0_ = bf16[36,8,1152]{2,1,0:T(8,128)(2,1)S(1)} collective-permute-done((bf16[36,8,1152]{2,1,0:T(8,128)(2,1)S(1)}, bf16[36,8,1152]{2,1,0:T(8,128)(2,1)S(1)}, u32[]{:S(2)}, u32[]{:S(2)}) %collective-permute-start.25) | collective-permute-done | bytes 663584 | tf_op jit(solution)/shard_map/ppermute | solution.py:63
  132.0 2.7 collective-permute-start.26
  134.7 8.9 %shard_map.242 = (bf16[256,1152]{1,0:T(8,128)(2,1)}, bf16[256,1152]{1,0:T(8,128)(2,1)}, bf16[128,1152]{1,0:T(8,128)(2,1)}, bf16[128,1152]{1,0:T(8,128)(2,1)}, bf...) custom-call(bf16[256,2304]{1,0:T(8,128)(2,1)} %copy-done.6, ...), custom_call_target="tpu_custom_call" | custom-call | flops 800000000 | bytes 2560000 | tf_op jit(solution)/shard_map/pallas_call | solution.py:192
  143.6 2.4 collective-permute-done.22.refs_3_
  146.3 3.5 collective-permute-start.29
  149.8 4.1 collective-permute-start.31
  156.0 13.1 %collective-permute-done.27.refs_5_ = bf16[13,8,2944]{2,1,0:T(8,128)(2,1)} collective-permute-done((bf16[13,8,2944]{2,1,0:T(8,128)(2,1)S(1)}, bf16[13,8,2944]{2,1,0:T(8,128)(2,1)}, u32[]{:S(2)}, u32[]{:S(2)}) %collective-permute-start.27) | collective-permute-done | bytes 612384 | tf_op jit(solution)/shard_map/ppermute | solution.py:57
  170.8 1.7 collective-permute-start.33
  178.1 19.6 %shard_map.243 = (f32[256,1152]{1,0:T(8,128)}, bf16[256,1152]{1,0:T(8,128)(2,1)}, f32[256,4608]{1,0:T(8,128)}, bf16[256,4608]{1,0:T(8,128)(2,1)}, bf16[1152,256]...) custom-call(s32[9]{0:T(128)} %stack.114.where_ref, ...), custom_call_target="tpu_custom_call" | custom-call | flops 2000000000 | bytes 6400000 | tf_op jit(solution)/shard_map/pallas_call | solution.py:531
  199.6 1.6 collective-permute-done.37.refs_6_
  201.6 1.8 collective-permute-done.39.refs_8_
  208.5 17.1 %shard_map.244 = (bf16[256,4608]{1,0:T(8,128)(2,1)}, bf16[1152,256]{1,0:T(8,128)(2,1)}, bf16[1152,256]{1,0:T(8,128)(2,1)}, bf16[1152,256]{1,0:T(8,128)(2,1)}, bf...) custom-call(s32[12]{0:T(128)} %stack.119.where_ref, ...), custom_call_target="tpu_custom_call" | custom-call | flops 1500000000 | bytes 4800000 | tf_op jit(solution)/shard_map/pallas_call | solution.py:651
  225.6 10.0 %shard_map.245 = (bf16[256,1152]{1,0:T(8,128)(2,1)}, f32[8,1152]{1,0:T(8,128)}) custom-call(s32[1]{0:T(128)} %bitcast.live_ref, bf16[256,4608]{1,0:T(8,128)(2,1)} %get-tuple-element.305.act_ref, bf16[4608,1152]{1,0:T(8,128)(2,1)} %bitcast.90, f32[1,1152]{1,0:T(1,128)} %reshape.141.bias_ref, bf16[256,1152]{1,0:T(8,128)(2,1)} %bitcast.86, ...), custom_call_target="tpu_custom_call" | custom-call | flops 600000000 | bytes 1920000 | tf_op jit(solution)/shard_map/pallas_call | solution.py:893
  238.4 7.7 %shard_map.247 = (f32[4,144,1152]{2,1,0:T(8,128)}, f32[4,144,1152]{2,1,0:T(8,128)}) custom-call(s32[1]{0:T(128)} %bitcast.5.where_ref, bf16[1152,256]{1,0:T(8,128)(2,1)} %get-tuple-element.355.x0, bf16[1152,256]{1,0:T(8,128)(2,1)} %copy-done.29, bf16[1152,256]{1,0:T(8,128)(2,1)} %collective-permute-done.44.x2, bf16[1152,256]{1,0:T(8,128)(2,1)} %collective-permute-done.45.x3, ...), custom_call_target="tpu_custom_call" | custom-call | flops 600000000 | bytes 1920000 | tf_op jit(solution)/shard_map/pallas_call | solution.py:1071
  246.1 14.6 %shard_map.246 = (f32[256,1152]{1,0:T(8,128)}, bf16[1152,256]{1,0:T(8,128)(2,1)}, f32[1152,256]{1,0:T(8,128)}, f32[8,1152]{1,0:T(8,128)}) custom-call(s32[1]{0:T(128)} %bitcast.live_ref, bf16[256,4608]{1,0:T(8,128)(2,1)} %get-tuple-element.346.d_pre_ref, bf16[1152,4608]{1,0:T(8,128)(2,1)} %bitcast.91, bf16[1152,1152]{1,0:T(8,128)(2,1)} %bitcast.104, ...), custom_call_target="tpu_custom_call" | custom-call | flops 1200000000 | bytes 3840000 | tf_op jit(solution)/shard_map/pallas_call | solution.py:757
  260.7 2.5 collective-permute-done.48.refs_8_
  264.0 2.1 collective-permute-start.53
  268.5 14.5 %shard_map.248 = (bf16[3456,256]{1,0:T(8,128)(2,1)}, bf16[1152,256]{1,0:T(8,128)(2,1)}, bf16[1152,256]{1,0:T(8,128)(2,1)}, bf16[1152,256]{1,0:T(8,128)(2,1)}, bf16[1152,256]{1,0:T(8,128)(2,1)}) custom-call(s32[1]{0:T(128)} %bitcast.live_ref, s32[4]{0:T(128)} %pad_add_fusion.chip_ref, f32[3456,256]{1,0:T(8,128)} %get-tuple-element.264.turned_ref, ...), custom_call_target="tpu_custom_call" | custom-call | flops 1200000000 | bytes 3840000 | tf_op jit(solution)/shard_map/pallas_call | solution.py:424
  285.8 1.5 copy-done.9
  287.2 3.9 shard_map.249
  295.8 10.1 %shard_map.250 = (bf16[256,1152]{1,0:T(8,128)(2,1)}, f32[8,1152]{1,0:T(8,128)}) custom-call(bf16[3456,256]{1,0:T(8,128)(2,1)} %get-tuple-element.379.d_ref, bf16[1152,3456]{1,0:T(8,128)(2,1)} %bitcast.92, bf16[256,1152]{1,0:T(8,128)(2,1)} %bitcast.88, f32[256,1152]{1,0:T(8,128)} %get-tuple-element.381.d_middle_ref, f32[8,1152]{1,0:T(8,128)} %get-tuple-element.298.mods_ref), custom_call_target="tpu_custom_call" | custom-call | flops 900000000 | bytes 2880000 | tf_op jit(solution)/shard_map/pallas_call | solution.py:826
  305.9 7.8 %shard_map.251 = (f32[576,1152]{1,0:T(8,128)}, f32[576,1152]{1,0:T(8,128)}) custom-call(s32[1]{0:T(128)} %bitcast.5.where_ref, bf16[256,1152]{1,0:T(8,128)(2,1)} %get-tuple-element.389.refs_0_, bf16[256,1152]{1,0:T(8,128)(2,1)} %copy-done.15, bf16[256,1152]{1,0:T(8,128)(2,1)} %copy-done.14, bf16[128,1152]{1,0:T(8,128)(2,1)} %collective-permute-done.51.refs_3_, ...), custom_call_target="tpu_custom_call" | custom-call | flops 800000000 | bytes 2560000 | tf_op jit(solution)/shard_map/pallas_call | solution.py:964
  313.7 5.7 %collective-permute-done.56.refs_8_ = bf16[1152,256]{1,0:T(8,128)(2,1)S(1)} collective-permute-done((bf16[1152,256]{1,0:T(8,128)(2,1)}, bf16[1152,256]{1,0:T(8,128)(2,1)S(1)}, u32[]{:S(2)}, u32[]{:S(2)}) %collective-permute-start.56) | collective-permute-done | bytes 589856 | tf_op jit(solution)/shard_map/ppermute | solution.py:57
  320.3 3.4 collective-permute-start.57
  324.8 7.2 %shard_map.253 = (f32[432,1152]{1,0:T(8,128)}, f32[432,1152]{1,0:T(8,128)}) custom-call(s32[1]{0:T(128)} %bitcast.5.where_ref, bf16[256,1152]{1,0:T(8,128)(2,1)} %get-tuple-element.402.normed_ref.refs_0_, bf16[256,1152]{1,0:T(8,128)(2,1)} %get-tuple-element.403.refs_1_, bf16[256,1152]{1,0:T(8,128)(2,1)} %get-tuple-element.404.refs_2_, ...), custom_call_target="tpu_custom_call" | custom-call | flops 800000000 | bytes 2560000 | tf_op jit(solution)/shard_map/pallas_call | solution.py:964
  332.0 1.5 copy-done.10
  333.5 4.2 shard_map.252
  344.1 2.0 collective-permute-start.58
  346.3 5.9 %collective-permute-done.58 = f32[16,1152]{1,0:T(8,128)S(1)} collective-permute-done((f32[16,1152]{1,0:T(8,128)}, f32[16,1152]{1,0:T(8,128)S(1)}, u32[]{:S(2)}, u32[]{:S(2)}) %collective-permute-start.58) | collective-permute-done | bytes 73760 | tf_op jit(solution)/shard_map/ppermute | solution.py:63
  352.2 5.3 %collective-permute-done.59 = f32[16,1152]{1,0:T(8,128)S(1)} collective-permute-done((f32[16,1152]{1,0:T(8,128)}, f32[16,1152]{1,0:T(8,128)S(1)}, u32[]{:S(2)}, u32[]{:S(2)}) %collective-permute-start.59) | collective-permute-done | bytes 73760 | tf_op jit(solution)/shard_map/ppermute | solution.py:63
  359.3 5.3 %shard_map.255 = (f32[144,1152]{1,0:T(8,128)}, f32[144,1152]{1,0:T(8,128)}) custom-call(s32[1]{0:T(128)} %bitcast.5.where_ref, bf16[256,1152]{1,0:T(8,128)(2,1)} %shard_map.241.attended_ref.refs_0_, bf16[256,1152]{1,0:T(8,128)(2,1)} %collective-permute-done.61.refs_1_, bf16[256,1152]{1,0:T(8,128)(2,1)} %collective-permute-done.62.refs_2_, ...), custom_call_target="tpu_custom_call" | custom-call | flops 800000000 | bytes 2560000 | tf_op jit(solution)/shard_map/pallas_call | solution.py:964
  367.8 4.1 shard_map.256
  372.0 3.3 fusion.23
  377.9 2.3 collective-permute-start.67
  381.2 1.7 collective-permute-done.67
  383.1 3.1 collective-permute-done.74
  392.2 2.3 copy.33
  394.4 6.1 %all-to-all-start = ((f32[8,144,144]{1,2,0:T(8,128)}), f32[8,144,144]{1,2,0:T(8,128)S(1)}, u32[]{:S(2)}, u32[]{:S(2)}) async-start(f32[8,144,144]{1,2,0:T(8,128)} %bitcast.39), calls=%async_computation.3 | async-start | bytes 2359296 | tf_op jit(solution)/shard_map/all_to_all | solution.py:1351
  403.0 10.8 %all-to-all-done = f32[8,144,144]{1,2,0:T(8,128)S(1)} async-done(((f32[8,144,144]{1,2,0:T(8,128)}), f32[8,144,144]{1,2,0:T(8,128)S(1)}, u32[]{:S(2)}, u32[]{:S(2)}) %all-to-all-start) | async-done | bytes 663584 | tf_op jit(solution)/shard_map/all_to_all | solution.py:1351
  415.8 1.9 slice_convert_fusion
  417.7 14.9 %reduce-scatter.4.cloned.1.call-done = bf16[288,640]{1,0:T(8,128)(2,1)} async-done(((bf16[1152,640]{1,0:T(8,128)(2,1)}), bf16[288,640]{1,0:T(8,128)(2,1)}) %reduce-scatter.4.cloned.1.call-update) | async-done | bytes 368656 | tf_op jit(solution)/shard_map/reduce_scatter | solution.py:1041
  434.4 1.8 slice_convert_fusion.1
  (324 shorter events, 89.4 us)
Async XLA Ops:
  7.2 385.0 %reduce-scatter.8.cloned.1.call-start = ((), (), s32[]{:S(2)}) async-start(), calls=%async_computation.6 | async-start | bytes 1658880 | tf_op jit(solution)/shard_map/reduce_scatter | solution.py:1041
  9.1 12.2 %collective-permute-start = (bf16[1,1152]{1,0:T(2,128)(2,1)S(1)}, bf16[1,1152]{1,0:T(2,128)(2,1)S(1)}, u32[]{:S(2)}, u32[]{:S(2)}) collective-permute-start(bf16[1,1152]{1,0:T(2,128)(2,1)S(1)} %get-tuple-element.225.cond_ref), channel_id=1, source_target_pairs={{0,1},{1,2},{2,3},{3,0},{4,5},{5,6},{6,7},{7,4},{8,9},{9,10},{10,1... | collective-permute-start | bytes 6920 | tf_op jit(solution)/shard_map/ppermute | solution.py:63
  9.2 12.1 %collective-permute-start.1 = (bf16[1,1152]{1,0:T(2,128)(2,1)S(1)}, bf16[1,1152]{1,0:T(2,128)(2,1)S(1)}, u32[]{:S(2)}, u32[]{:S(2)}) collective-permute-start(bf16[1,1152]{1,0:T(2,128)(2,1)S(1)} %get-tuple-element.225.cond_ref), channel_id=1, source_target_pairs={{0,2},{1,3},{2,0},{3,1},{4,6},{5,7},{6,4},{7,5},{8,10},{9,11},{10,... | collective-permute-start | bytes 6920 | tf_op jit(solution)/shard_map/ppermute | solution.py:63
  10.6 10.8 %collective-permute-start.2 = (bf16[1,1152]{1,0:T(2,128)(2,1)S(1)}, bf16[1,1152]{1,0:T(2,128)(2,1)S(1)}, u32[]{:S(2)}, u32[]{:S(2)}) collective-permute-start(bf16[1,1152]{1,0:T(2,128)(2,1)S(1)} %get-tuple-element.225.cond_ref), channel_id=1, source_target_pairs={{0,3},{1,0},{2,1},{3,2},{4,7},{5,4},{6,5},{7,6},{8,11},{9,8},{10,9... | collective-permute-start | bytes 6920 | tf_op jit(solution)/shard_map/ppermute | solution.py:63
  10.7 12.2 %collective-permute-start.3 = (bf16[9,8,3456]{2,1,0:T(8,128)(2,1)S(1)}, bf16[9,8,3456]{2,1,0:T(8,128)(2,1)S(1)}, u32[]{:S(2)}, u32[]{:S(2)}) collective-permute-start(bf16[9,8,3456]{2,1,0:T(8,128)(2,1)S(1)} %dynamic-slice_bitcast_fusion.2), channel_id=1, source_target_pairs={{0,1},{1,2},{2,3},{3,0},{4,5},{5,6},{6,7},{7,4},{8,9},{9,10},{10,1... | collective-permute-start | bytes 1493000 | tf_op jit(solution)/shard_map/ppermute | solution.py:63
  23.6 33.8 %collective-permute-start.8 = (bf16[256,2304]{1,0:T(8,128)(2,1)}, bf16[256,2304]{1,0:T(8,128)(2,1)S(1)}, u32[]{:S(2)}, u32[]{:S(2)}) collective-permute-start(bf16[256,2304]{1,0:T(8,128)(2,1)} %pad_maximum_fusion.1.refs_0_), channel_id=1, source_target_pairs={{0,8},{4,12},{8,0},{12,4},{16,24},{20,28},{24,16},{28,20},{1,9},{5... | collective-permute-start | bytes 3538952 | tf_op jit(solution)/shard_map/ppermute | solution.py:57
  24.8 32.6 %collective-permute-start.9 = (bf16[256,2304]{1,0:T(8,128)(2,1)}, bf16[256,2304]{1,0:T(8,128)(2,1)S(1)}, u32[]{:S(2)}, u32[]{:S(2)}) collective-permute-start(bf16[256,2304]{1,0:T(8,128)(2,1)} %pad_maximum_fusion.1.refs_0_), channel_id=1, source_target_pairs={{0,16},{4,20},{8,24},{12,28},{16,0},{20,4},{24,8},{28,12},{1,17},{... | collective-permute-start | bytes 3538952 | tf_op jit(solution)/shard_map/ppermute | solution.py:57
  26.1 18.5 %collective-permute-start.7 = (bf16[9,8,3456]{2,1,0:T(8,128)(2,1)S(1)}, bf16[9,8,3456]{2,1,0:T(8,128)(2,1)S(1)}, u32[]{:S(2)}, u32[]{:S(2)}) collective-permute-start(bf16[9,8,3456]{2,1,0:T(8,128)(2,1)S(1)} %collective-permute-done.3), channel_id=1, source_target_pairs={{0,1},{1,2},{2,3},{3,0},{4,5},{5,6},{6,7},{7,4},{8,9},{9,10},{10,1... | collective-permute-start | bytes 1493000 | tf_op jit(solution)/shard_map/ppermute | solution.py:63
  33.6 9.6 %collective-permute-start.5 = (f32[8,1152]{1,0:T(8,128)}, f32[8,1152]{1,0:T(8,128)S(1)}, u32[]{:S(2)}, u32[]{:S(2)}) collective-permute-start(f32[8,1152]{1,0:T(8,128)} %get-tuple-element.233), channel_id=1, source_target_pairs={{0,2},{1,3},{2,0},{3,1},{4,6},{5,7},{6,4},{7,5},{8,10},{9,11},{10,... | collective-permute-start | bytes 110600 | tf_op jit(solution)/shard_map/ppermute | solution.py:63
  44.6 12.8 %collective-permute-start.10 = (bf16[9,8,3456]{2,1,0:T(8,128)(2,1)S(1)}, bf16[9,8,3456]{2,1,0:T(8,128)(2,1)}, u32[]{:S(2)}, u32[]{:S(2)}) collective-permute-start(bf16[9,8,3456]{2,1,0:T(8,128)(2,1)S(1)} %collective-permute-done.7), channel_id=1, source_target_pairs={{0,1},{1,2},{2,3},{3,0},{4,5},{5,6},{6,7},{7,4},{8,9},{9,10},{10,1... | collective-permute-start | bytes 1493000 | tf_op jit(solution)/shard_map/ppermute | solution.py:63
  59.9 18.9 %collective-permute-start.11 = (bf16[3,9,8,3456]{3,2,1,0:T(8,128)(2,1)S(1)}, bf16[3,9,8,3456]{3,2,1,0:T(8,128)(2,1)}, u32[]{:S(2)}, u32[]{:S(2)}) collective-permute-start(bf16[3,9,8,3456]{3,2,1,0:T(8,128)(2,1)S(1)} %pad_maximum_fusion.refs_0_), channel_id=1, source_target_pairs={{0,8},{4,20},{8,0},{12,28},{16,24},{20,4},{24,16},{28,12},{1,9},{5... | collective-permute-start | bytes 4478984 | tf_op jit(solution)/shard_map/ppermute | solution.py:60
  60.2 18.6 %collective-permute-start.12 = (bf16[3,9,8,3456]{3,2,1,0:T(8,128)(2,1)S(1)}, bf16[3,9,8,3456]{3,2,1,0:T(8,128)(2,1)}, u32[]{:S(2)}, u32[]{:S(2)}) collective-permute-start(bf16[3,9,8,3456]{3,2,1,0:T(8,128)(2,1)S(1)} %pad_maximum_fusion.refs_0_), channel_id=1, source_target_pairs={{0,4},{4,0},{8,12},{12,8},{16,20},{20,16},{24,28},{28,24},{1,5},{5... | collective-permute-start | bytes 4478984 | tf_op jit(solution)/shard_map/ppermute | solution.py:57
  63.9 13.3 %collective-permute-start.13 = (bf16[9,8,2944]{2,1,0:T(8,128)(2,1)}, bf16[9,8,2944]{2,1,0:T(8,128)(2,1)}, u32[]{:S(2)}, u32[]{:S(2)}) collective-permute-start(bf16[9,8,2944]{2,1,0:T(8,128)(2,1)} %fusion), channel_id=1, source_target_pairs={{0,1},{1,2},{2,3},{3,0},{4,5},{5,6},{6,7},{7,4},{8,9},{9,10},{10,1... | collective-permute-start | bytes 1271816 | tf_op jit(solution)/shard_map/ppermute | solution.py:63
  78.8 9.9 %collective-permute-start.14 = (bf16[3,9,8,3456]{3,2,1,0:T(8,128)(2,1)}, bf16[3,9,8,3456]{3,2,1,0:T(8,128)(2,1)}, u32[]{:S(2)}, u32[]{:S(2)}) collective-permute-start(bf16[3,9,8,3456]{3,2,1,0:T(8,128)(2,1)} %collective-permute-done.11.refs_1_), channel_id=1, source_target_pairs={{0,4},{4,0},{8,12},{12,8},{16,20},{20,16},{24,28},{28,24},{1,5},{5... | collective-permute-start | bytes 4478984 | tf_op jit(solution)/shard_map/ppermute | solution.py:57
  82.2 15.8 %collective-permute-start.16 = (bf16[128,2304]{1,0:T(8,128)(2,1)S(1)}, bf16[128,2304]{1,0:T(8,128)(2,1)S(1)}, u32[]{:S(2)}, u32[]{:S(2)}) collective-permute-start(bf16[128,2304]{1,0:T(8,128)(2,1)S(1)} %slice.136), channel_id=1, source_target_pairs={{0,16},{4,20},{8,24},{12,28},{16,0},{20,4},{24,8},{28,12},{1,17},{... | collective-permute-start | bytes 1769480 | tf_op jit(solution)/shard_map/ppermute | solution.py:57
  83.4 14.8 %collective-permute-start.17 = (bf16[128,2304]{1,0:T(8,128)(2,1)}, bf16[128,2304]{1,0:T(8,128)(2,1)S(1)}, u32[]{:S(2)}, u32[]{:S(2)}) collective-permute-start(bf16[128,2304]{1,0:T(8,128)(2,1)} %slice.137), channel_id=1, source_target_pairs={{0,8},{4,12},{8,0},{12,4},{16,24},{20,28},{24,16},{28,20},{1,9},{5... | collective-permute-start | bytes 1769480 | tf_op jit(solution)/shard_map/ppermute | solution.py:57
  83.7 14.4 %collective-permute-start.15 = (bf16[9,8,2944]{2,1,0:T(8,128)(2,1)}, bf16[9,8,2944]{2,1,0:T(8,128)(2,1)}, u32[]{:S(2)}, u32[]{:S(2)}) collective-permute-start(bf16[9,8,2944]{2,1,0:T(8,128)(2,1)} %collective-permute-done.13), channel_id=1, source_target_pairs={{0,1},{1,2},{2,3},{3,0},{4,5},{5,6},{6,7},{7,4},{8,9},{9,10},{10,1... | collective-permute-start | bytes 1271816 | tf_op jit(solution)/shard_map/ppermute | solution.py:63
  98.2 15.2 %collective-permute-start.18 = (bf16[9,8,2944]{2,1,0:T(8,128)(2,1)}, bf16[9,8,2944]{2,1,0:T(8,128)(2,1)S(1)}, u32[]{:S(2)}, u32[]{:S(2)}) collective-permute-start(bf16[9,8,2944]{2,1,0:T(8,128)(2,1)} %collective-permute-done.15), channel_id=1, source_target_pairs={{0,1},{1,2},{2,3},{3,0},{4,5},{5,6},{6,7},{7,4},{8,9},{9,10},{10,1... | collective-permute-start | bytes 1271816 | tf_op jit(solution)/shard_map/ppermute | solution.py:63
  102.0 11.3 %collective-permute-start.19 = (f32[8,1152]{1,0:T(8,128)S(1)}, f32[8,1152]{1,0:T(8,128)S(1)}, u32[]{:S(2)}, u32[]{:S(2)}) collective-permute-start(f32[8,1152]{1,0:T(8,128)S(1)} %copy-done.52), channel_id=1, source_target_pairs={{0,8},{4,12},{8,0},{12,4},{16,24},{20,28},{24,16},{28,20},{1,9},{5... | collective-permute-start | bytes 110600 | tf_op jit(solution)/shard_map/ppermute | solution.py:57
  102.4 11.0 %collective-permute-start.20 = (f32[8,1152]{1,0:T(8,128)S(1)}, f32[8,1152]{1,0:T(8,128)S(1)}, u32[]{:S(2)}, u32[]{:S(2)}) collective-permute-start(f32[8,1152]{1,0:T(8,128)S(1)} %copy-done.52), channel_id=1, source_target_pairs={{0,16},{4,20},{8,24},{12,28},{16,0},{20,4},{24,8},{28,12},{1,17},{... | collective-permute-start | bytes 110600 | tf_op jit(solution)/shard_map/ppermute | solution.py:57
  103.6 9.8 %collective-permute-start.21 = (f32[8,1152]{1,0:T(8,128)S(1)}, f32[8,1152]{1,0:T(8,128)S(1)}, u32[]{:S(2)}, u32[]{:S(2)}) collective-permute-start(f32[8,1152]{1,0:T(8,128)S(1)} %copy-done.52), channel_id=1, source_target_pairs={{0,24},{4,28},{8,16},{12,20},{16,8},{20,12},{24,0},{28,4},{1,25},{... | collective-permute-start | bytes 110600 | tf_op jit(solution)/shard_map/ppermute | solution.py:57
  117.9 14.2 %collective-permute-start.25 = (bf16[36,8,1152]{2,1,0:T(8,128)(2,1)S(1)}, bf16[36,8,1152]{2,1,0:T(8,128)(2,1)S(1)}, u32[]{:S(2)}, u32[]{:S(2)}) collective-permute-start(bf16[36,8,1152]{2,1,0:T(8,128)(2,1)S(1)} %copy-done.25), channel_id=1, source_target_pairs={{0,1},{1,2},{2,3},{3,0},{4,5},{5,6},{6,7},{7,4},{8,9},{9,10},{10,1... | collective-permute-start | bytes 1990664 | tf_op jit(solution)/shard_map/ppermute | solution.py:63
  118.5 27.4 %collective-permute-start.22 = (bf16[27,8,2944]{2,1,0:T(8,128)(2,1)}, bf16[27,8,2944]{2,1,0:T(8,128)(2,1)S(1)}, u32[]{:S(2)}, u32[]{:S(2)}) collective-permute-start(bf16[27,8,2944]{2,1,0:T(8,128)(2,1)} %constant_dynamic-update-slice_fusion.refs_2_), channel_id=1, source_target_pairs={{0,8},{4,12},{8,0},{12,4},{16,24},{20,28},{24,16},{28,20},{1,9},{5... | collective-permute-start | bytes 3815432 | tf_op jit(solution)/shard_map/ppermute | solution.py:57
  119.0 27.3 %collective-permute-start.23 = (bf16[27,8,2944]{2,1,0:T(8,128)(2,1)}, bf16[27,8,2944]{2,1,0:T(8,128)(2,1)S(1)}, u32[]{:S(2)}, u32[]{:S(2)}) collective-permute-start(bf16[27,8,2944]{2,1,0:T(8,128)(2,1)} %constant_dynamic-update-slice_fusion.refs_2_), channel_id=1, source_target_pairs={{0,16},{4,20},{8,24},{12,28},{16,0},{20,4},{24,8},{28,12},{1,17},{... | collective-permute-start | bytes 3815432 | tf_op jit(solution)/shard_map/ppermute | solution.py:57
  120.3 26.0 %collective-permute-start.24 = (bf16[27,8,2944]{2,1,0:T(8,128)(2,1)}, bf16[27,8,2944]{2,1,0:T(8,128)(2,1)}, u32[]{:S(2)}, u32[]{:S(2)}) collective-permute-start(bf16[27,8,2944]{2,1,0:T(8,128)(2,1)} %constant_dynamic-update-slice_fusion.refs_2_), channel_id=1, source_target_pairs={{0,4},{4,0},{8,12},{12,8},{16,20},{20,16},{24,28},{28,24},{1,5},{5... | collective-permute-start | bytes 3815432 | tf_op jit(solution)/shard_map/ppermute | solution.py:57
  132.0 14.3 %collective-permute-start.26 = (bf16[36,8,1152]{2,1,0:T(8,128)(2,1)S(1)}, bf16[36,8,1152]{2,1,0:T(8,128)(2,1)}, u32[]{:S(2)}, u32[]{:S(2)}) collective-permute-start(bf16[36,8,1152]{2,1,0:T(8,128)(2,1)S(1)} %collective-permute-done.25.refs_0_), channel_id=1, source_target_pairs={{0,1},{1,2},{2,3},{3,0},{4,5},{5,6},{6,7},{7,4},{8,9},{9,10},{10,1... | collective-permute-start | bytes 1990664 | tf_op jit(solution)/shard_map/ppermute | solution.py:63
  146.3 23.4 %collective-permute-start.29 = (bf16[27,8,2944]{2,1,0:T(8,128)(2,1)S(1)}, bf16[27,8,2944]{2,1,0:T(8,128)(2,1)S(1)}, u32[]{:S(2)}, u32[]{:S(2)}) collective-permute-start(bf16[27,8,2944]{2,1,0:T(8,128)(2,1)S(1)} %collective-permute-done.22.refs_3_), channel_id=1, source_target_pairs={{0,4},{4,0},{8,12},{12,8},{16,20},{20,16},{24,28},{28,24},{1,5},{5... | collective-permute-start | bytes 3815432 | tf_op jit(solution)/shard_map/ppermute | solution.py:57
  149.8 19.9 %collective-permute-start.30 = (bf16[27,8,2944]{2,1,0:T(8,128)(2,1)S(1)}, bf16[27,8,2944]{2,1,0:T(8,128)(2,1)S(1)}, u32[]{:S(2)}, u32[]{:S(2)}) collective-permute-start(bf16[27,8,2944]{2,1,0:T(8,128)(2,1)S(1)} %collective-permute-done.23.refs_4_), channel_id=1, source_target_pairs={{0,4},{4,0},{8,12},{12,8},{16,20},{20,16},{24,28},{28,24},{1,5},{5... | collective-permute-start | bytes 3815432 | tf_op jit(solution)/shard_map/ppermute | solution.py:57
  149.8 19.9 %collective-permute-start.31 = (bf16[36,8,1152]{2,1,0:T(8,128)(2,1)}, bf16[36,8,1152]{2,1,0:T(8,128)(2,1)}, u32[]{:S(2)}, u32[]{:S(2)}) collective-permute-start(bf16[36,8,1152]{2,1,0:T(8,128)(2,1)} %collective-permute-done.26.refs_1_), channel_id=1, source_target_pairs={{0,1},{1,2},{2,3},{3,0},{4,5},{5,6},{6,7},{7,4},{8,9},{9,10},{10,1... | collective-permute-start | bytes 1990664 | tf_op jit(solution)/shard_map/ppermute | solution.py:63
  154.0 15.7 %collective-permute-start.28 = (bf16[14,8,2944]{2,1,0:T(8,128)(2,1)S(1)}, bf16[14,8,2944]{2,1,0:T(8,128)(2,1)}, u32[]{:S(2)}, u32[]{:S(2)}) collective-permute-start(bf16[14,8,2944]{2,1,0:T(8,128)(2,1)S(1)} %slice.139), channel_id=1, source_target_pairs={{0,8},{4,12},{8,0},{12,4},{16,24},{20,28},{24,16},{28,20},{1,9},{5... | collective-permute-start | bytes 1978376 | tf_op jit(solution)/shard_map/ppermute | solution.py:57
  154.7 14.4 %collective-permute-start.27 = (bf16[13,8,2944]{2,1,0:T(8,128)(2,1)S(1)}, bf16[13,8,2944]{2,1,0:T(8,128)(2,1)}, u32[]{:S(2)}, u32[]{:S(2)}) collective-permute-start(bf16[13,8,2944]{2,1,0:T(8,128)(2,1)S(1)} %slice.138), channel_id=1, source_target_pairs={{0,16},{4,20},{8,24},{12,28},{16,0},{20,4},{24,8},{28,12},{1,17},{... | collective-permute-start | bytes 1837064 | tf_op jit(solution)/shard_map/ppermute | solution.py:57
  173.5 24.1 %collective-permute-start.34 = (bf16[36,8,1152]{2,1,0:T(8,128)(2,1)S(1)}, bf16[36,8,1152]{2,1,0:T(8,128)(2,1)}, u32[]{:S(2)}, u32[]{:S(2)}) collective-permute-start(bf16[36,8,1152]{2,1,0:T(8,128)(2,1)S(1)} %collective-permute-done.25.refs_0_), channel_id=1, source_target_pairs={{0,8},{4,20},{8,0},{12,28},{16,24},{20,4},{24,16},{28,12},{1,9},{5... | collective-permute-start | bytes 1990664 | tf_op jit(solution)/shard_map/ppermute | solution.py:60
  174.8 22.9 %collective-permute-start.35 = (bf16[36,8,1152]{2,1,0:T(8,128)(2,1)}, bf16[36,8,1152]{2,1,0:T(8,128)(2,1)}, u32[]{:S(2)}, u32[]{:S(2)}) collective-permute-start(bf16[36,8,1152]{2,1,0:T(8,128)(2,1)} %collective-permute-done.26.refs_1_), channel_id=1, source_target_pairs={{0,8},{4,20},{8,0},{12,28},{16,24},{20,4},{24,16},{28,12},{1,9},{5... | collective-permute-start | bytes 1990664 | tf_op jit(solution)/shard_map/ppermute | solution.py:60
  175.0 22.7 %collective-permute-start.36 = (bf16[36,8,1152]{2,1,0:T(8,128)(2,1)}, bf16[36,8,1152]{2,1,0:T(8,128)(2,1)}, u32[]{:S(2)}, u32[]{:S(2)}) collective-permute-start(bf16[36,8,1152]{2,1,0:T(8,128)(2,1)} %collective-permute-done.31.refs_2_), channel_id=1, source_target_pairs={{0,8},{4,20},{8,0},{12,28},{16,24},{20,4},{24,16},{28,12},{1,9},{5... | collective-permute-start | bytes 1990664 | tf_op jit(solution)/shard_map/ppermute | solution.py:60
  205.2 30.4 %collective-permute-start.43 = (bf16[1152,256]{1,0:T(8,128)(2,1)}, bf16[1152,256]{1,0:T(8,128)(2,1)S(1)}, u32[]{:S(2)}, u32[]{:S(2)}) collective-permute-start(bf16[1152,256]{1,0:T(8,128)(2,1)} %get-tuple-element.341), channel_id=1, source_target_pairs={{0,8},{4,12},{8,0},{12,4},{16,24},{20,28},{24,16},{28,20},{1,9},{5... | collective-permute-start | bytes 1769480 | tf_op jit(solution)/shard_map/ppermute | solution.py:57
  205.8 29.8 %collective-permute-start.44 = (bf16[1152,256]{1,0:T(8,128)(2,1)}, bf16[1152,256]{1,0:T(8,128)(2,1)}, u32[]{:S(2)}, u32[]{:S(2)}) collective-permute-start(bf16[1152,256]{1,0:T(8,128)(2,1)} %get-tuple-element.342), channel_id=1, source_target_pairs={{0,16},{4,20},{8,24},{12,28},{16,0},{20,4},{24,8},{28,12},{1,17},{... | collective-permute-start | bytes 1769480 | tf_op jit(solution)/shard_map/ppermute | solution.py:57
  207.1 28.6 %collective-permute-start.45 = (bf16[1152,256]{1,0:T(8,128)(2,1)}, bf16[1152,256]{1,0:T(8,128)(2,1)}, u32[]{:S(2)}, u32[]{:S(2)}) collective-permute-start(bf16[1152,256]{1,0:T(8,128)(2,1)} %get-tuple-element.343), channel_id=1, source_target_pairs={{0,24},{4,28},{8,16},{12,20},{16,8},{20,12},{24,0},{28,4},{1,25},{... | collective-permute-start | bytes 1769480 | tf_op jit(solution)/shard_map/ppermute | solution.py:57
  235.7 25.0 %collective-permute-start.46 = (bf16[1152,256]{1,0:T(8,128)(2,1)}, bf16[1152,256]{1,0:T(8,128)(2,1)S(1)}, u32[]{:S(2)}, u32[]{:S(2)}) collective-permute-start(bf16[1152,256]{1,0:T(8,128)(2,1)} %get-tuple-element.352), channel_id=1, source_target_pairs={{0,8},{4,12},{8,0},{12,4},{16,24},{20,28},{24,16},{28,20},{1,9},{5... | collective-permute-start | bytes 1769480 | tf_op jit(solution)/shard_map/ppermute | solution.py:57
  236.3 24.4 %collective-permute-start.47 = (bf16[1152,256]{1,0:T(8,128)(2,1)S(1)}, bf16[1152,256]{1,0:T(8,128)(2,1)S(1)}, u32[]{:S(2)}, u32[]{:S(2)}) collective-permute-start(bf16[1152,256]{1,0:T(8,128)(2,1)S(1)} %copy-done.51), channel_id=1, source_target_pairs={{0,16},{4,20},{8,24},{12,28},{16,0},{20,4},{24,8},{28,12},{1,17},{... | collective-permute-start | bytes 1769480 | tf_op jit(solution)/shard_map/ppermute | solution.py:57
  237.6 25.6 %collective-permute-start.48 = (bf16[1152,256]{1,0:T(8,128)(2,1)S(1)}, bf16[1152,256]{1,0:T(8,128)(2,1)S(1)}, u32[]{:S(2)}, u32[]{:S(2)}) collective-permute-start(bf16[1152,256]{1,0:T(8,128)(2,1)S(1)} %copy-done.50), channel_id=1, source_target_pairs={{0,24},{4,28},{8,16},{12,20},{16,8},{20,12},{24,0},{28,4},{1,25},{... | collective-permute-start | bytes 1769480 | tf_op jit(solution)/shard_map/ppermute | solution.py:57
  264.0 21.8 %collective-permute-start.53 = (f32[4,144,1152]{2,1,0:T(8,128)}, f32[4,144,1152]{2,1,0:T(8,128)S(1)}, u32[]{:S(2)}, u32[]{:S(2)}) collective-permute-start(f32[4,144,1152]{2,1,0:T(8,128)} %get-tuple-element.378), channel_id=1, source_target_pairs={{0,4},{4,0},{8,12},{12,8},{16,20},{20,16},{24,28},{28,24},{1,5},{5... | collective-permute-start | bytes 7962632 | tf_op jit(solution)/shard_map/ppermute | solution.py:57
  266.1 16.8 %collective-permute-start.50 = (bf16[256,1152]{1,0:T(8,128)(2,1)}, bf16[256,1152]{1,0:T(8,128)(2,1)S(1)}, u32[]{:S(2)}, u32[]{:S(2)}) collective-permute-start(bf16[256,1152]{1,0:T(8,128)(2,1)} %get-tuple-element.389.refs_0_), channel_id=1, source_target_pairs={{0,16},{4,20},{8,24},{12,28},{16,0},{20,4},{24,8},{28,12},{1,17},{... | collective-permute-start | bytes 1769480 | tf_op jit(solution)/shard_map/ppermute | solution.py:57
  267.0 17.4 %collective-permute-start.49 = (bf16[256,1152]{1,0:T(8,128)(2,1)}, bf16[256,1152]{1,0:T(8,128)(2,1)S(1)}, u32[]{:S(2)}, u32[]{:S(2)}) collective-permute-start(bf16[256,1152]{1,0:T(8,128)(2,1)} %get-tuple-element.389.refs_0_), channel_id=1, source_target_pairs={{0,8},{4,12},{8,0},{12,4},{16,24},{20,28},{24,16},{28,20},{1,9},{5... | collective-permute-start | bytes 1769480 | tf_op jit(solution)/shard_map/ppermute | solution.py:57
  283.8 8.3 %collective-permute-start.52 = (bf16[128,1152]{1,0:T(8,128)(2,1)}, bf16[128,1152]{1,0:T(8,128)(2,1)}, u32[]{:S(2)}, u32[]{:S(2)}) collective-permute-start(bf16[128,1152]{1,0:T(8,128)(2,1)} %slice.141), channel_id=1, source_target_pairs={{0,8},{4,12},{8,0},{12,4},{16,24},{20,28},{24,16},{28,20},{1,9},{5... | collective-permute-start | bytes 884744 | tf_op jit(solution)/shard_map/ppermute | solution.py:57
  285.1 8.0 %collective-permute-start.51 = (bf16[128,1152]{1,0:T(8,128)(2,1)}, bf16[128,1152]{1,0:T(8,128)(2,1)}, u32[]{:S(2)}, u32[]{:S(2)}) collective-permute-start(bf16[128,1152]{1,0:T(8,128)(2,1)} %slice.140), channel_id=1, source_target_pairs={{0,16},{4,20},{8,24},{12,28},{16,0},{20,4},{24,8},{28,12},{1,17},{... | collective-permute-start | bytes 884744 | tf_op jit(solution)/shard_map/ppermute | solution.py:57
  293.1 20.6 %collective-permute-start.54 = (bf16[1152,256]{1,0:T(8,128)(2,1)}, bf16[1152,256]{1,0:T(8,128)(2,1)S(1)}, u32[]{:S(2)}, u32[]{:S(2)}) collective-permute-start(bf16[1152,256]{1,0:T(8,128)(2,1)} %get-tuple-element.384), channel_id=1, source_target_pairs={{0,8},{4,12},{8,0},{12,4},{16,24},{20,28},{24,16},{28,20},{1,9},{5... | collective-permute-start | bytes 1769480 | tf_op jit(solution)/shard_map/ppermute | solution.py:57
  294.0 19.7 %collective-permute-start.55 = (bf16[1152,256]{1,0:T(8,128)(2,1)}, bf16[1152,256]{1,0:T(8,128)(2,1)S(1)}, u32[]{:S(2)}, u32[]{:S(2)}) collective-permute-start(bf16[1152,256]{1,0:T(8,128)(2,1)} %get-tuple-element.385), channel_id=1, source_target_pairs={{0,16},{4,20},{8,24},{12,28},{16,0},{20,4},{24,8},{28,12},{1,17},{... | collective-permute-start | bytes 1769480 | tf_op jit(solution)/shard_map/ppermute | solution.py:57
  294.3 25.1 %collective-permute-start.56 = (bf16[1152,256]{1,0:T(8,128)(2,1)}, bf16[1152,256]{1,0:T(8,128)(2,1)S(1)}, u32[]{:S(2)}, u32[]{:S(2)}) collective-permute-start(bf16[1152,256]{1,0:T(8,128)(2,1)} %get-tuple-element.386), channel_id=1, source_target_pairs={{0,24},{4,28},{8,16},{12,20},{16,8},{20,12},{24,0},{28,4},{1,25},{... | collective-permute-start | bytes 1769480 | tf_op jit(solution)/shard_map/ppermute | solution.py:57
  320.3 11.7 %collective-permute-start.57 = (f32[576,1152]{1,0:T(8,128)}, f32[576,1152]{1,0:T(8,128)S(1)}, u32[]{:S(2)}, u32[]{:S(2)}) collective-permute-start(f32[576,1152]{1,0:T(8,128)} %get-tuple-element.401), channel_id=1, source_target_pairs={{0,4},{4,0},{8,12},{12,8},{16,20},{20,16},{24,28},{28,24},{1,5},{5... | collective-permute-start | bytes 7962632 | tf_op jit(solution)/shard_map/ppermute | solution.py:57
  323.7 92.1 %reduce-scatter.6.cloned.1.call-start = ((), (), s32[]{:S(2)}) async-start(), calls=%async_computation.5 | async-start | bytes 1843200 | tf_op jit(solution)/shard_map/reduce_scatter | solution.py:1041
  323.7 15.1 %collective-permute-start.62 = (bf16[256,1152]{1,0:T(8,128)(2,1)S(1)}, bf16[256,1152]{1,0:T(8,128)(2,1)}, u32[]{:S(2)}, u32[]{:S(2)}) collective-permute-start(bf16[256,1152]{1,0:T(8,128)(2,1)S(1)} %copy-done.2), channel_id=1, source_target_pairs={{0,16},{4,20},{8,24},{12,28},{16,0},{20,4},{24,8},{28,12},{1,17},{... | collective-permute-start | bytes 1769480 | tf_op jit(solution)/shard_map/ppermute | solution.py:57
  323.9 16.6 %collective-permute-start.61 = (bf16[256,1152]{1,0:T(8,128)(2,1)S(1)}, bf16[256,1152]{1,0:T(8,128)(2,1)}, u32[]{:S(2)}, u32[]{:S(2)}) collective-permute-start(bf16[256,1152]{1,0:T(8,128)(2,1)S(1)} %copy-done.2), channel_id=1, source_target_pairs={{0,8},{4,12},{8,0},{12,4},{16,24},{20,28},{24,16},{28,20},{1,9},{5... | collective-permute-start | bytes 1769480 | tf_op jit(solution)/shard_map/ppermute | solution.py:57
  339.8 17.7 %collective-permute-start.64 = (bf16[128,1152]{1,0:T(8,128)(2,1)S(1)}, bf16[128,1152]{1,0:T(8,128)(2,1)S(1)}, u32[]{:S(2)}, u32[]{:S(2)}) collective-permute-start(bf16[128,1152]{1,0:T(8,128)(2,1)S(1)} %slice.143), channel_id=1, source_target_pairs={{0,8},{4,12},{8,0},{12,4},{16,24},{20,28},{24,16},{28,20},{1,9},{5... | collective-permute-start | bytes 884744 | tf_op jit(solution)/shard_map/ppermute | solution.py:57
  341.5 16.0 %collective-permute-start.63 = (bf16[128,1152]{1,0:T(8,128)(2,1)S(1)}, bf16[128,1152]{1,0:T(8,128)(2,1)S(1)}, u32[]{:S(2)}, u32[]{:S(2)}) collective-permute-start(bf16[128,1152]{1,0:T(8,128)(2,1)S(1)} %slice.142), channel_id=1, source_target_pairs={{0,16},{4,20},{8,24},{12,28},{16,0},{20,4},{24,8},{28,12},{1,17},{... | collective-permute-start | bytes 884744 | tf_op jit(solution)/shard_map/ppermute | solution.py:57
  344.1 8.2 %collective-permute-start.58 = (f32[16,1152]{1,0:T(8,128)}, f32[16,1152]{1,0:T(8,128)S(1)}, u32[]{:S(2)}, u32[]{:S(2)}) collective-permute-start(f32[16,1152]{1,0:T(8,128)} %shard_map.254), channel_id=1, source_target_pairs={{0,1},{1,2},{2,3},{3,0},{4,5},{5,6},{6,7},{7,4},{8,9},{9,10},{10,1... | collective-permute-start | bytes 221192 | tf_op jit(solution)/shard_map/ppermute | solution.py:63
  346.0 11.5 %collective-permute-start.59 = (f32[16,1152]{1,0:T(8,128)}, f32[16,1152]{1,0:T(8,128)S(1)}, u32[]{:S(2)}, u32[]{:S(2)}) collective-permute-start(f32[16,1152]{1,0:T(8,128)} %shard_map.254), channel_id=1, source_target_pairs={{0,2},{1,3},{2,0},{3,1},{4,6},{5,7},{6,4},{7,5},{8,10},{9,11},{10,... | collective-permute-start | bytes 221192 | tf_op jit(solution)/shard_map/ppermute | solution.py:63
  346.0 11.5 %collective-permute-start.60 = (f32[16,1152]{1,0:T(8,128)}, f32[16,1152]{1,0:T(8,128)S(1)}, u32[]{:S(2)}, u32[]{:S(2)}) collective-permute-start(f32[16,1152]{1,0:T(8,128)} %shard_map.254), channel_id=1, source_target_pairs={{0,3},{1,0},{2,1},{3,2},{4,7},{5,4},{6,5},{7,6},{8,11},{9,8},{10,9... | collective-permute-start | bytes 221192 | tf_op jit(solution)/shard_map/ppermute | solution.py:63
  358.4 24.5 %collective-permute-start.73 = (f32[8,1152]{1,0:T(8,128)S(1)}, f32[8,1152]{1,0:T(8,128)S(1)}, u32[]{:S(2)}, u32[]{:S(2)}) collective-permute-start(f32[8,1152]{1,0:T(8,128)S(1)} %slice_add_fusion), channel_id=1, source_target_pairs={{0,4},{4,0},{8,12},{12,8},{16,20},{20,16},{24,28},{28,24},{1,5},{5... | collective-permute-start | bytes 110600 | tf_op jit(solution)/shard_map/ppermute | solution.py:57
  359.3 7.7 %collective-permute-start.71 = (f32[432,1152]{1,0:T(8,128)}, f32[432,1152]{1,0:T(8,128)}, u32[]{:S(2)}, u32[]{:S(2)}) collective-permute-start(f32[432,1152]{1,0:T(8,128)} %get-tuple-element.424), channel_id=1, source_target_pairs={{0,4},{4,0},{8,12},{12,8},{16,20},{20,16},{24,28},{28,24},{1,5},{5... | collective-permute-start | bytes 5971976 | tf_op jit(solution)/shard_map/ppermute | solution.py:57
  365.1 67.5 %reduce-scatter.4.cloned.1.call-start = ((), (), s32[]{:S(2)}) async-start(), calls=%async_computation.4 | async-start | bytes 1843200 | tf_op jit(solution)/shard_map/reduce_scatter | solution.py:1041
  366.0 9.4 %collective-permute-start.68 = (bf16[4,8,1152]{2,1,0:T(8,128)(2,1)S(1)}, bf16[4,8,1152]{2,1,0:T(8,128)(2,1)S(1)}, u32[]{:S(2)}, u32[]{:S(2)}) collective-permute-start(bf16[4,8,1152]{2,1,0:T(8,128)(2,1)S(1)} %pad_maximum_fusion.2), channel_id=1, source_target_pairs={{0,4},{4,0},{8,12},{12,8},{16,20},{20,16},{24,28},{28,24},{1,5},{5... | collective-permute-start | bytes 221192 | tf_op jit(solution)/shard_map/ppermute | solution.py:57
  375.4 11.1 %collective-permute-start.69 = (bf16[8,8,1152]{2,1,0:T(8,128)(2,1)S(1)}, bf16[8,8,1152]{2,1,0:T(8,128)(2,1)S(1)}, u32[]{:S(2)}, u32[]{:S(2)}) collective-permute-start(bf16[8,8,1152]{2,1,0:T(8,128)(2,1)S(1)} %get-tuple-element.506), channel_id=1, source_target_pairs={{0,8},{4,12},{8,0},{12,4},{16,24},{20,28},{24,16},{28,20},{1,9},{5... | collective-permute-start | bytes 442376 | tf_op jit(solution)/shard_map/ppermute | solution.py:57
  386.6 13.9 %collective-permute-start.70 = (bf16[16,8,1152]{2,1,0:T(8,128)(2,1)S(1)}, bf16[16,8,1152]{2,1,0:T(8,128)(2,1)S(1)}, u32[]{:S(2)}, u32[]{:S(2)}) collective-permute-start(bf16[16,8,1152]{2,1,0:T(8,128)(2,1)S(1)} %get-tuple-element.502), channel_id=1, source_target_pairs={{0,16},{4,20},{8,24},{12,28},{16,0},{20,4},{24,8},{28,12},{1,17},{... | collective-permute-start | bytes 884744 | tf_op jit(solution)/shard_map/ppermute | solution.py:57
  394.4 19.4 %all-to-all-start = ((f32[8,144,144]{1,2,0:T(8,128)}), f32[8,144,144]{1,2,0:T(8,128)S(1)}, u32[]{:S(2)}, u32[]{:S(2)}) async-start(f32[8,144,144]{1,2,0:T(8,128)} %bitcast.39), calls=%async_computation.3 | async-start | bytes 2359296 | tf_op jit(solution)/shard_map/all_to_all | solution.py:1351
  (69 other events, 629.1 us)
Sparse Core Ops, SparseCore 0:
  323.8 31.5 reduce-scatter.7
  365.2 32.1 reduce-scatter.5
  399.8 32.6 reduce-scatter.3

commit v5 on v4

--- a/solution.py
+++ b/solution.py
@@ -363,14 +363,14 @@
             compiler_params=params(60),
         )(live, turned)
 
-    def attention_back(turned, d_turned, d_attn_turned, live, where_chip):
+    def attention_back(turned, d_turned, live, where_chip):
         width, slots = d_turned.shape
-        parts = (3 * width // 4, width // 4)
+        part = 3 * width // 4
         count = width // HEAD_DIM
-        heads_at_once = 2 if count % 2 == 0 else 1
+        heads_at_once = 1
         scale = HEAD_DIM ** (-0.5)
 
-        def kernel(live_ref, chip_ref, turned_ref, d_ref, d_attn_ref, out_ref, *rest):
+        def kernel(live_ref, chip_ref, turned_ref, d_ref, out_ref, *rest):
             block_refs, total_ref = rest[:-1], rest[-1]
             live_keys = lax.broadcasted_iota(jnp.int32, (1, slots), 1) < live_ref[0]
 
@@ -415,22 +415,20 @@
             lax.fori_loop(0, count // heads_at_once, some_heads, 0)
             out_ref[...] = total_ref[...].astype(bf16)
             for k, block in enumerate(block_refs):
-                first = pl.multiple_of(chip_ref[k] * parts[0], 16)
-                block[: parts[0], :] = total_ref[pl.ds(first, parts[0]), :].astype(bf16)
-                first = pl.multiple_of(chip_ref[k] * parts[1], 16)
-                block[parts[0] :, :] = d_attn_ref[pl.ds(first, parts[1]), :]
+                first = pl.multiple_of(chip_ref[k] * part, 16)
+                block[...] = total_ref[pl.ds(first, part), :].astype(bf16)
 
         n_blocks = 4 if groups == 1 else 0
         return pl.pallas_call(
             kernel,
             out_shape=[jax.ShapeDtypeStruct((3 * width, slots), bf16)]
-            + [jax.ShapeDtypeStruct((width, slots), bf16)] * n_blocks,
-            in_specs=[smem, smem, vmem, vmem, vmem],
+            + [jax.ShapeDtypeStruct((part, slots), bf16)] * n_blocks,
+            in_specs=[smem, smem, vmem, vmem],
             out_specs=[vmem] * (1 + n_blocks),
             scratch_shapes=[pltpu.VMEM((3 * width, slots), f32)],
             cost_estimate=cost(12),
             compiler_params=params(60),
-        )(live, where_chip, turned, d_turned, d_attn_turned)
+        )(live, where_chip, turned, d_turned)
 
     def middle_forward(where, attended, tokens_own, owns, sets, bias_out, bias_up, mods):
         slots, width = attended.shape
@@ -998,30 +996,32 @@
             compiler_params=params(60),
         )(first_sums, middle_sums, output_sums, d_pre_sums, cond_act)
 
-    def column_total(pairs):
-        width = pairs[0][0].shape[1]
-        n = sum(keep.shape[0] for keep, unused in pairs)
+    def column_total(items):
+        width = items[0][0].shape[1]
+        n = sum(item[0].shape[0] for item in items)
         padded = -(-n // 128) * 128
+        arrays = [array for item in items for array in item]
 
         def kernel(*refs):
             for first in range(0, width, 128):
-                cols = slice(first, first + 128)
-                totals = [
-                    refs[2 * i][:, cols] + refs[2 * i + 1][:, cols] for i in range(len(pairs))
-                ]
+                totals, used = [], 0
+                for item in items:
+                    parts = [ref[:, first : first + 128] for ref in refs[used : used + len(item)]]
+                    totals.append(sum((part.astype(f32) for part in parts[1:]), parts[0]))
+                    used += len(item)
                 if padded > n:
                     totals.append(jnp.zeros((padded - n, 128), f32))
                 total = jnp.concatenate(totals, axis=0) if len(totals) > 1 else totals[0]
-                refs[-1][cols, :] = total.T.astype(bf16)
+                refs[-1][first : first + 128, :] = total.T.astype(bf16)
 
         return pl.pallas_call(
             kernel,
             out_shape=jax.ShapeDtypeStruct((width, padded), bf16),
-            in_specs=[vmem] * (2 * len(pairs)),
+            in_specs=[vmem] * len(arrays),
             out_specs=vmem,
-            cost_estimate=cost(4),
-            compiler_params=params(60),
-        )(*[each for pair in pairs for each in pair])
+            cost_estimate=cost(5),
+            compiler_params=params(60),
+        )(*arrays)
 
     def row_total(keep, got):
         def kernel(keep_ref, got_ref, out_ref):
@@ -1039,6 +1039,52 @@
 
     def fsdp_sum(x):
         return lax.psum_scatter(x, "fsdp", scatter_dimension=0, tiled=True)
+
+    def out_grad(where, d_attn_turned, attended):
+        width, slots = d_attn_turned.shape
+        n = width // BOX
+
+        def kernel(where_ref, d_ref, x_ref, keep_ref, send_ref):
+            step = pl.program_id(0)
+            core = where_ref[0]
+            for out_ref, which in ((keep_ref, core), (send_ref, 1 - core)):
+                first = (where_ref[step + 1] * 2 + which) * n
+                rows = pl.ds(pl.multiple_of(first, 16), n)
+                out_ref[0] = jnp.dot(d_ref[rows, :], x_ref[...], preferred_element_type=f32)
+
+        out_spec = pl.BlockSpec((1, n, width), lambda i, where_ref: (i, 0, 0))
+        return pl.pallas_call(
+            kernel,
+            out_shape=[jax.ShapeDtypeStruct((BOX // 2, n, width), f32)] * 2,
+            grid_spec=pltpu.PrefetchScalarGridSpec(
+                num_scalar_prefetch=1,
+                grid=(BOX // 2,),
+                in_specs=[
+                    pl.BlockSpec((width, slots), lambda i, where_ref: (0, 0)),
+                    pl.BlockSpec((slots, width), lambda i, where_ref: (0, 0)),
+                ],
+                out_specs=[out_spec] * 2,
+            ),
+            cost_estimate=cost(5),
+            compiler_params=params(60),
+        )(where, d_attn_turned, attended)
+
+    def chip_split(keep, got):
+        count, rows, width = keep.shape
+
+        def kernel(keep_ref, got_ref, *outs):
+            for k, out_ref in enumerate(outs):
+                out_ref[...] = (keep_ref[k] + got_ref[k]).astype(out_ref.dtype)
+
+        return pl.pallas_call(
+            kernel,
+            out_shape=[jax.ShapeDtypeStruct((rows, width), f32)]
+            + [jax.ShapeDtypeStruct((rows, width), bf16)] * (count - 1),
+            in_specs=[vmem] * 2,
+            out_specs=[vmem] * count,
+            cost_estimate=cost(3),
+            compiler_params=params(60),
+        )(keep, got)
 
     def row_grad(where, lefts, rights):
         rows = lefts[0].shape[0] // fs
@@ -1281,61 +1327,67 @@
 
         normed_two_near = chip_near(normed_two)
         total_down = row_total(keep_down, box_send(send_down, 1))
+        grad_down = fsdp_sum(total_down)
         d_projected, *last_blocks = attention_back(
-            turned, d_attended_turned, d_attn_turned, live, where[fs + 4 :]
+            turned, after(d_attended_turned, total_down), live, where[fs + 4 :]
         )
         if groups > 1:
-            last_blocks = [
-                jnp.concatenate(pair)
-                for pair in zip(column_blocks(d_projected), column_blocks(d_attn_turned))
-            ]
+            last_blocks = column_blocks(d_projected)
+            d_attn_turned = d_attn_turned.reshape(groups, BOX, -1, slots)
+            d_attn_turned = d_attn_turned.transpose(1, 0, 2, 3).reshape(width, slots)
+        keep_out, send_out = out_grad(
+            jnp.concatenate([where_core, where[fs + 4 :]]), d_attn_turned, attended
+        )
+        got_out = box_send(send_out, 1)
         normed_two_far = chip_far([after(each, d_projected) for each in normed_two_near])
         normed_two_box = [normed_two, *normed_two_near, *normed_two_far]
-        d_projected, last_blocks, normed_two_box, total_down = gated(
-            (d_projected, last_blocks, normed_two_box, total_down)
-        )
-        grad_down = fsdp_sum(total_down)
-
-        last_box = chip_exchange(last_blocks)
-        grad_tokens, first_sums = first_back(d_projected, qkv_full, tokens[0], d_middle, mods)
-        keep_up, send_up = column_grad(
-            after(where_core, first_sums), [(normed_two_box, 0, d_pre_box[0].shape[0])], d_pre_box
-        )
-        last_box, first_sums, keep_up, send_up = gated((last_box, first_sums, keep_up, send_up))
-
-        total_up = column_total([(keep_up, box_send(send_up, 1))])
-        attended_near = chip_near(attended)
-        cut = 3 * last_box[0].shape[0] // 4
-        keep_qkv, send_qkv = column_grad(where_core, [(normed_box, 0, cut)], last_box)
-        attended_far = chip_far([after(each, (keep_qkv, total_up)) for each in attended_near])
-        attended_box = [attended, *attended_near, *attended_far]
-        message = sums_message(
-            first_sums, middle_sums, output_sums, d_pre_sums.reshape(-1, width), cond_act
-        )
-        messages = ring_gather(message)
-        total_up, keep_qkv, send_qkv, messages, attended_box = gated(
-            (total_up, keep_qkv, send_qkv, messages, attended_box)
-        )
-        grad_up = fsdp_sum(total_up)
-
-        got_qkv = box_send(send_qkv, 1)
-        keep_out, send_out = column_grad(
-            where_core, [(attended_box, cut, last_box[0].shape[0])], last_box
-        )
-        got_out = box_send(send_out, 1)
-        grad_last = fsdp_sum(column_total([(keep_qkv, got_qkv), (keep_out, got_out)]))
-        images_near = jnp.stack([each[:8] for each in messages]).astype(bf16)
-        totals = [each[8:] for each in messages]
+        d_projected, last_blocks, normed_two_box, grad_down, keep_out, got_out = gated(
+            (d_projected, last_blocks, normed_two_box, grad_down, keep_out, got_out)
+        )
 
         def over_groups(grad):
             rows, cols = grad.shape
             return group_sum(grad.reshape(rows, groups, -1).transpose(1, 0, 2), group)
 
-        cut_cols, last_cols = cut // 2, last_box[0].shape[0] // 2
-        grad_w_up = over_groups(grad_up[:, : d_pre_box[0].shape[0] // 2].astype(f32))
-        grad_w_qkv = over_groups(grad_last[:, :cut_cols].astype(f32))
-        grad_w_out = over_groups(grad_last[:, cut_cols:last_cols].astype(f32))
-
+        last_box = chip_exchange(last_blocks)
+        grad_tokens, first_sums = first_back(d_projected, qkv_full, tokens[0], d_middle, mods)
+        out_blocks = chip_split(keep_out, got_out)
+        keep_up, send_up = column_grad(
+            where_core, [(normed_two_box, 0, d_pre_box[0].shape[0])], d_pre_box
+        )
+        total_up = column_total([(keep_up, box_send(send_up, 1))])
+        last_box, first_sums, total_up, out_blocks = gated(
+            (last_box, first_sums, total_up, out_blocks)
+        )
+
+        grad_up = fsdp_sum(total_up)
+        keep_qkv, send_qkv = column_grad(
+            where_core, [(normed_box, 0, last_box[0].shape[0])], last_box
+        )
+        message = sums_message(
+            first_sums, middle_sums, output_sums, d_pre_sums.reshape(-1, width), cond_act
+        )
+        out_parts = chip_exchange(out_blocks)
+        messages = ring_gather(message)
+        total_last = column_total([(keep_qkv, box_send(send_qkv, 1)), tuple(out_parts)])
+        grad_down = after(grad_down, keep_qkv)
+        if groups > 1:
+            grad_down = over_groups(grad_down.astype(f32))
+        down_rows = grad_down.shape[0]
+        down_cols = grad_down.reshape(down_rows, BOX, -1).transpose(1, 0, 2)
+        if groups == 1:
+            parts = lax.all_to_all(down_cols, "dp", 0, 0, tiled=True)
+        else:
+            parts = [pick(down_cols, place)] + [
+                box_send(pick(down_cols, place ^ k), k) for k in range(1, BOX)
+            ]
+            parts = jnp.stack(parts)
+            parts = jnp.stack([pick(parts, place ^ k) for k in range(BOX)])
+        total_last, messages, grad_up, parts = gated((total_last, messages, grad_up, parts))
+
+        grad_last = fsdp_sum(total_last)
+        images_near = jnp.stack([each[:8] for each in messages]).astype(bf16)
+        totals = [each[8:] for each in messages]
         images, total = images_near, sum(totals[1:], totals[0])
         for bits in (1, 2, 4):
             images = jnp.concatenate([images, box_send(images, bits)])
@@ -1344,18 +1396,11 @@
         for k in range(1, groups):
             images = jnp.concatenate([images, group_send(images_box, k)])
             total = total + group_send(total_box, k)
-        grad_down = over_groups(after(grad_down, got_qkv).astype(f32))
-        down_rows = grad_down.shape[0]
-        down_blocks = grad_down.reshape(down_rows, BOX, -1).transpose(1, 0, 2)
-        if groups == 1:
-            parts = lax.all_to_all(down_blocks, "dp", 0, 0, tiled=True)
-        else:
-            parts = [pick(down_blocks, place)] + [
-                box_send(pick(down_blocks, place ^ k), k) for k in range(1, BOX)
-            ]
-            parts = jnp.stack(parts)
-            parts = jnp.stack([pick(parts, place ^ k) for k in range(BOX)])
-        grad_w_down = parts.reshape(BOX * down_rows, width // dp)
+        grad_w_down = parts.reshape(BOX * down_rows, width // dp).astype(f32)
+        grad_w_up = over_groups(grad_up[:, : keep_up.shape[0]].astype(f32))
+        cut_cols, last_cols = keep_qkv.shape[0], keep_qkv.shape[0] + keep_out.shape[1]
+        grad_w_qkv = over_groups(grad_last[:, :cut_cols].astype(f32))
+        grad_w_out = over_groups(grad_last[:, cut_cols:last_cols].astype(f32))
         conds_all = lax.dynamic_slice_in_dim(images[:, 6], z * rows_z, rows_z, 1)
         d_mod_all = images[:, :6]
         ada_cols = 6 * width // dp

time: 448 us -> 427 us (0.953)
  starting transfers between devices: 100 us -> 87.9 us
  waiting for transfers between devices: 107 us -> 99.7 us
  Pallas kernels: 163 us -> 168 us
    all_to_all x1, waiting for transfers between devices: 10.8 us -> 0.01 us  [body(): parts = lax.all_to_all(down_cols, 'dp', 0, 0, tiled=True)]
    ppermute x21, waiting for transfers between devices: 41.4 us -> 31 us  [ring_send(): return lax.ppermute(x, 'fsdp', [(i, (i + hops) % fs) for i in range(fs)])]
    pallas_call x0 -> x2, Pallas kernels: none -> 8.91 us  [the longest x1 5.13 us: out_grad(): pl.pallas_call(kernel, out_shape=[jax.ShapeDtypeStruct((BOX // 2, n, widt...]
    ppermute x51 -> x50, starting transfers between devices: 49.9 us -> 41.7 us  [box_send(): return lax.ppermute(x, 'dp', [(i, i ^ bits) for i in range(dp)])]
    ppermute x51 -> x50, waiting for transfers between devices: 38.2 us -> 45.1 us  [box_send(): return lax.ppermute(x, 'dp', [(i, i ^ bits) for i in range(dp)])]
    pallas_call x3 -> x2, Pallas kernels: 20.3 us -> 14.8 us  [column_grad(): pl.pallas_call(kernel, out_shape=[jax.ShapeDtypeStruct((n_out, width), f3...]
    unnamed x128 -> x138, local copies, waits for them, and re-layouts: 15.5 us -> 14.8 us
  transfers between devices with their start and end apart: 80 -> 79, of which waited for: 30 -> 28; matrix products, arithmetic and copies ran while one was open for 8% -> 7% of each run, Pallas kernels for 37% -> 38%
where the time goes in v5:
time: 427 us; the launch traced here: 422 us
  Pallas kernels  168 us (39%)
  waiting for transfers between devices  99.7 us (23%)
  starting transfers between devices  87.9 us (21%)
  local copies, waits for them, and re-layouts  36 us (8%)
  between operations  15.9 us (4%)
  other arithmetic  9.99 us (2%)
  matrix products  4.61 us (1%)
    ppermute x50, waiting for transfers between devices, box_send(): return lax.ppermute(x, 'dp', [(i, i ^ bits) for i in range(dp)])  45.1 us
    ppermute x50, starting transfers between devices, box_send(): return lax.ppermute(x, 'dp', [(i, i ^ bits) for i in range(dp)])  41.7 us
    ppermute x21, starting transfers between devices, ring_send(): return lax.ppermute(x, 'fsdp', [(i, (i + hops) % fs) for i in range(fs)])  39.3 us
    ppermute x21, waiting for transfers between devices, ring_send(): return lax.ppermute(x, 'fsdp', [(i, (i + hops) % fs) for i in range(fs)])  31 us
    pallas_call x1, Pallas kernels, middle_forward(): pl.pallas_call(kernel, out_shape=[jax.ShapeDtypeStruct((slots, width), f3...  19.5 us
    reduce_scatter x3, waiting for transfers between devices, fsdp_sum(): return lax.psum_scatter(x, 'fsdp', scatter_dimension=0, tiled=True)  17.8 us
    pallas_call x1, Pallas kernels, hidden_back(): pl.pallas_call(kernel, out_shape=[jax.ShapeDtypeStruct((slots, hidden), b...  17.1 us
    pallas_call x1, Pallas kernels, attention_back(): pl.pallas_call(kernel, out_shape=[jax.ShapeDtypeStruct((3 * width, slots)...  15.5 us
  transfers between devices with their start and end apart: 79, of which 28 were waited for; matrix products, arithmetic and copies ran while one was open for 7% of the time, Pallas kernels for 38%

profile of v5, /device:TPU:25, one launch (start us, length us, event | category | flops | bytes accessed | tf_op | source)
XLA Modules:
  0.0 421.9 jit_solution(12313494790373755446)
XLA Ops:
  9.4 3.1 collective-permute-start
  17.0 2.0 dynamic-slice_bitcast_fusion
  20.4 3.7 collective-permute-done.3
  27.3 2.0 collective-permute-start.7
  29.3 3.5 shard_map.237
  33.4 5.1 %collective-permute-done.4.refs_1_ = f32[8,1152]{1,0:T(8,128)S(1)} collective-permute-done((f32[8,1152]{1,0:T(8,128)}, f32[8,1152]{1,0:T(8,128)S(1)}, u32[]{:S(2)}, u32[]{:S(2)}) %collective-permute-start.4) | collective-permute-done | bytes 36896 | tf_op jit(solution)/shard_map/ppermute | solution.py:63
  38.4 3.7 collective-permute-start.6
  43.5 3.7 collective-permute-start.10
  49.1 1.5 shard_map.238
  50.6 3.9 shard_map.239
  54.4 2.0 collective-permute-done.10
  58.9 2.9 collective-permute-start.12
  62.8 3.7 collective-permute-start.13
  67.9 7.6 %collective-permute-done.13 = bf16[9,8,2944]{2,1,0:T(8,128)(2,1)} collective-permute-done((bf16[9,8,2944]{2,1,0:T(8,128)(2,1)}, bf16[9,8,2944]{2,1,0:T(8,128)(2,1)}, u32[]{:S(2)}, u32[]{:S(2)}) %collective-permute-start.13) | collective-permute-done | bytes 423968 | tf_op jit(solution)/shard_map/ppermute | solution.py:63
  75.6 5.0 %collective-permute-done.11.refs_1_ = bf16[3,9,8,3456]{3,2,1,0:T(8,128)(2,1)} collective-permute-done((bf16[3,9,8,3456]{3,2,1,0:T(8,128)(2,1)S(1)}, bf16[3,9,8,3456]{3,2,1,0:T(8,128)(2,1)}, u32[]{:S(2)}, u32[]{:S(2)}) %collective-permute-start.11) | collective-permute-done | bytes 1493024 | tf_op jit(solution)/shard_map/ppermute | solution.py:60
  84.0 3.6 collective-permute-start.15
  88.9 9.4 %shard_map.240 = (f32[3456,256]{1,0:T(8,128)}, bf16[4,4,9,8,3456]{4,3,2,1,0:T(8,128)(2,1)}) custom-call(s32[12]{0:T(128)} %stack.119.where_ref, bf16[256,1152]{1,0:T(8,128)(2,1)} %get-tuple-element.388.normed_ref.refs_0_, f32[2,1152]{1,0:T(2,128)} %reshape.132.bias_ref, bf16[4,9,8,3456]{3,2,1,0:T(8,128)(2,1)} %bitcast.102, ...), custom_call_target="tpu_custom_call" | custom-call | flops 1100000000 | bytes 3520000 | tf_op jit(solution)/shard_map/pallas_call | solution.py:299
  98.7 3.7 collective-permute-start.18
  105.0 8.7 %shard_map.241.attended_ref.x_ref = bf16[256,1152]{1,0:T(8,128)(2,1)} custom-call(s32[1]{0:T(128)} %bitcast.live_ref, f32[3456,256]{1,0:T(8,128)} %get-tuple-element.266.turned_ref), custom_call_target="tpu_custom_call" | custom-call | flops 1100000000 | bytes 3520000 | tf_op jit(solution)/shard_map/pallas_call | solution.py:356
  113.8 1.9 constant_dynamic-update-slice_fusion.2
  115.7 1.8 constant_dynamic-update-slice_fusion.1
  119.3 2.0 collective-permute-start.24
  122.5 10.3 %collective-permute-done.25.refs_0_ = bf16[36,8,1152]{2,1,0:T(8,128)(2,1)S(1)} collective-permute-done((bf16[36,8,1152]{2,1,0:T(8,128)(2,1)S(1)}, bf16[36,8,1152]{2,1,0:T(8,128)(2,1)S(1)}, u32[]{:S(2)}, u32[]{:S(2)}) %collective-permute-start.25) | collective-permute-done | bytes 663584 | tf_op jit(solution)/shard_map/ppermute | solution.py:63
  132.8 3.1 collective-permute-start.26
  135.8 8.9 %shard_map.242 = (bf16[256,1152]{1,0:T(8,128)(2,1)}, bf16[256,1152]{1,0:T(8,128)(2,1)}, bf16[128,1152]{1,0:T(8,128)(2,1)}, bf16[128,1152]{1,0:T(8,128)(2,1)}, bf...) custom-call(bf16[256,2304]{1,0:T(8,128)(2,1)} %copy-done.6, ...), custom_call_target="tpu_custom_call" | custom-call | flops 800000000 | bytes 2560000 | tf_op jit(solution)/shard_map/pallas_call | solution.py:192
  144.7 6.3 %collective-permute-done.23.refs_4_ = bf16[27,8,2944]{2,1,0:T(8,128)(2,1)S(1)} collective-permute-done((bf16[27,8,2944]{2,1,0:T(8,128)(2,1)}, bf16[27,8,2944]{2,1,0:T(8,128)(2,1)S(1)}, u32[]{:S(2)}, u32[]{:S(2)}) %collective-permute-start.23) | collective-permute-done | bytes 1271840 | tf_op jit(solution)/shard_map/ppermute | solution.py:57
  152.2 2.8 collective-permute-start.31
  156.0 13.8 %collective-permute-done.27.refs_5_ = bf16[13,8,2944]{2,1,0:T(8,128)(2,1)} collective-permute-done((bf16[13,8,2944]{2,1,0:T(8,128)(2,1)S(1)}, bf16[13,8,2944]{2,1,0:T(8,128)(2,1)}, u32[]{:S(2)}, u32[]{:S(2)}) %collective-permute-start.27) | collective-permute-done | bytes 612384 | tf_op jit(solution)/shard_map/ppermute | solution.py:57
  171.9 1.7 collective-permute-start.33
  178.5 19.5 %shard_map.243 = (f32[256,1152]{1,0:T(8,128)}, bf16[256,1152]{1,0:T(8,128)(2,1)}, f32[256,4608]{1,0:T(8,128)}, bf16[256,4608]{1,0:T(8,128)(2,1)}, bf16[1152,256]...) custom-call(s32[9]{0:T(128)} %stack.114.where_ref, ...), custom_call_target="tpu_custom_call" | custom-call | flops 2000000000 | bytes 6400000 | tf_op jit(solution)/shard_map/pallas_call | solution.py:529
  200.7 1.6 collective-permute-done.37.refs_6_
  202.7 1.8 collective-permute-done.39.refs_8_
  207.5 1.5 collective-permute-start.45
  209.6 17.1 %shard_map.244 = (bf16[256,4608]{1,0:T(8,128)(2,1)}, bf16[1152,256]{1,0:T(8,128)(2,1)}, bf16[1152,256]{1,0:T(8,128)(2,1)}, bf16[1152,256]{1,0:T(8,128)(2,1)}, bf...) custom-call(s32[12]{0:T(128)} %stack.119.where_ref, ...), custom_call_target="tpu_custom_call" | custom-call | flops 1500000000 | bytes 4800000 | tf_op jit(solution)/shard_map/pallas_call | solution.py:649
  226.7 10.0 %shard_map.245 = (bf16[256,1152]{1,0:T(8,128)(2,1)}, f32[8,1152]{1,0:T(8,128)}) custom-call(s32[1]{0:T(128)} %bitcast.live_ref, bf16[256,4608]{1,0:T(8,128)(2,1)} %get-tuple-element.307.act_ref, bf16[4608,1152]{1,0:T(8,128)(2,1)} %bitcast.90, f32[1,1152]{1,0:T(1,128)} %reshape.137.bias_ref, bf16[256,1152]{1,0:T(8,128)(2,1)} %bitcast.86, ...), custom_call_target="tpu_custom_call" | custom-call | flops 600000000 | bytes 1920000 | tf_op jit(solution)/shard_map/pallas_call | solution.py:891
  238.0 1.5 collective-permute-start.48
  239.5 7.7 %shard_map.247 = (f32[4,144,1152]{2,1,0:T(8,128)}, f32[4,144,1152]{2,1,0:T(8,128)}) custom-call(s32[1]{0:T(128)} %bitcast.5.where_ref, bf16[1152,256]{1,0:T(8,128)(2,1)} %get-tuple-element.357.x0, bf16[1152,256]{1,0:T(8,128)(2,1)} %copy-done.24, bf16[1152,256]{1,0:T(8,128)(2,1)} %collective-permute-done.44.x2, bf16[1152,256]{1,0:T(8,128)(2,1)} %collective-permute-done.45.x3, ...), custom_call_target="tpu_custom_call" | custom-call | flops 600000000 | bytes 1920000 | tf_op jit(solution)/shard_map/pallas_call | solution.py:1117
  247.2 14.6 %shard_map.246 = (f32[256,1152]{1,0:T(8,128)}, bf16[1152,256]{1,0:T(8,128)(2,1)}, f32[1152,256]{1,0:T(8,128)}, f32[8,1152]{1,0:T(8,128)}) custom-call(s32[1]{0:T(128)} %bitcast.live_ref, bf16[256,4608]{1,0:T(8,128)(2,1)} %get-tuple-element.348.d_pre_ref, bf16[1152,4608]{1,0:T(8,128)(2,1)} %bitcast.91, bf16[1152,1152]{1,0:T(8,128)(2,1)} %bitcast.104, ...), custom_call_target="tpu_custom_call" | custom-call | flops 1200000000 | bytes 3840000 | tf_op jit(solution)/shard_map/pallas_call | solution.py:755
  261.8 1.8 collective-permute-done.48.refs_8_
  264.5 2.2 collective-permute-start.49
  267.3 5.1 %shard_map.250 = (f32[4,144,1152]{2,1,0:T(8,128)}, f32[4,144,1152]{2,1,0:T(8,128)}) custom-call(s32[5]{0:T(128)} %concatenate.39.where_ref, bf16[1152,256]{1,0:T(8,128)(2,1)} %get-tuple-element.381.d_ref, bf16[256,1152]{1,0:T(8,128)(2,1)} %shard_map.241.attended_ref.x_ref), custom_call_target="tpu_custom_call" | custom-call | flops 500000000 | bytes 1600000 | tf_op jit(solution)/shard_map/pallas_call | solution.py:1056
  272.4 1.5 copy-done.8
  273.9 3.8 shard_map.248
  280.1 15.5 %shard_map.249 = (bf16[3456,256]{1,0:T(8,128)(2,1)}, bf16[864,256]{1,0:T(8,128)(2,1)}, bf16[864,256]{1,0:T(8,128)(2,1)}, bf16[864,256]{1,0:T(8,128)(2,1)}, bf16[864,256]{1,0:T(8,128)(2,1)}) custom-call(s32[1]{0:T(128)} %bitcast.live_ref, s32[4]{0:T(128)} %pad_add_fusion.chip_ref, f32[3456,256]{1,0:T(8,128)} %get-tuple-element.266.turned_ref, ...), custom_call_target="tpu_custom_call" | custom-call | flops 1200000000 | bytes 3840000 | tf_op jit(solution)/shard_map/pallas_call | solution.py:422
  297.2 6.0 %collective-permute-done.53.refs_4_ = bf16[128,1152]{1,0:T(8,128)(2,1)S(1)} collective-permute-done((bf16[128,1152]{1,0:T(8,128)(2,1)S(1)}, bf16[128,1152]{1,0:T(8,128)(2,1)S(1)}, u32[]{:S(2)}, u32[]{:S(2)}) %collective-permute-start.53) | collective-permute-done | bytes 294944 | tf_op jit(solution)/shard_map/ppermute | solution.py:57
  303.8 3.3 reduce-scatter.4.cloned.1.call-done
  307.2 7.8 %shard_map.252 = (f32[576,1152]{1,0:T(8,128)}, f32[576,1152]{1,0:T(8,128)}) custom-call(s32[1]{0:T(128)} %bitcast.5.where_ref, bf16[256,1152]{1,0:T(8,128)(2,1)} %get-tuple-element.398.refs_0_, bf16[256,1152]{1,0:T(8,128)(2,1)} %copy-done.10, bf16[256,1152]{1,0:T(8,128)(2,1)} %copy-done.9, bf16[128,1152]{1,0:T(8,128)(2,1)} %copy-done.37, ...), custom_call_target="tpu_custom_call" | custom-call | flops 800000000 | bytes 2560000 | tf_op jit(solution)/shard_map/pallas_call | solution.py:962
  318.4 3.8 shard_map.254
  322.2 10.1 %shard_map.251 = (bf16[256,1152]{1,0:T(8,128)(2,1)}, f32[8,1152]{1,0:T(8,128)}) custom-call(bf16[3456,256]{1,0:T(8,128)(2,1)} %get-tuple-element.384.d_ref, bf16[1152,3456]{1,0:T(8,128)(2,1)} %bitcast.92, bf16[256,1152]{1,0:T(8,128)(2,1)} %bitcast.88, f32[256,1152]{1,0:T(8,128)} %get-tuple-element.386.d_middle_ref, f32[8,1152]{1,0:T(8,128)} %get-tuple-element.300.mods_ref), custom_call_target="tpu_custom_call" | custom-call | flops 900000000 | bytes 2880000 | tf_op jit(solution)/shard_map/pallas_call | solution.py:824
  332.3 1.5 copy-done.7
  333.8 4.2 %shard_map.253 = bf16[1152,640]{1,0:T(8,128)(2,1)} custom-call(f32[576,1152]{1,0:T(8,128)} %get-tuple-element.407.refs_0_, f32[576,1152]{1,0:T(8,128)} %copy-done.7), custom_call_target="tpu_custom_call" | custom-call | flops 500000000 | bytes 1600000 | tf_op jit(solution)/shard_map/pallas_call | solution.py:1017
  339.1 7.0 %shard_map.255 = (f32[432,1152]{1,0:T(8,128)}, f32[432,1152]{1,0:T(8,128)}) custom-call(s32[1]{0:T(128)} %bitcast.5.where_ref, bf16[256,1152]{1,0:T(8,128)(2,1)} %get-tuple-element.388.normed_ref.refs_0_, bf16[256,1152]{1,0:T(8,128)(2,1)} %get-tuple-element.389.refs_1_, bf16[256,1152]{1,0:T(8,128)(2,1)} %get-tuple-element.390.refs_2_, ...), custom_call_target="tpu_custom_call" | custom-call | flops 800000000 | bytes 2560000 | tf_op jit(solution)/shard_map/pallas_call | solution.py:962
  350.9 4.4 %all-to-all-start = ((bf16[8,144,144]{1,2,0:T(8,128)(2,1)}), bf16[8,144,144]{1,2,0:T(8,128)(2,1)S(1)}, u32[]{:S(2)}, u32[]{:S(2)}) async-start(bf16[8,144,144]{1,2,0:T(8,128)(2,1)} %bitcast.35), calls=%async_computation.2 | async-start | bytes 1179648 | tf_op jit(solution)/shard_map/all_to_all | solution.py:1379
  356.0 1.5 shard_map.257
  358.7 1.6 collective-permute-start.64
  360.8 4.2 collective-permute-done.62.refs_5_
  365.7 4.2 shard_map.256
  370.8 5.0 %reduce-scatter.6.cloned.1.call-done = bf16[288,640]{1,0:T(8,128)(2,1)} async-done(((bf16[1152,640]{1,0:T(8,128)(2,1)}), bf16[288,640]{1,0:T(8,128)(2,1)}) %reduce-scatter.6.cloned.1.call-update) | async-done | bytes 368656 | tf_op jit(solution)/shard_map/reduce_scatter | solution.py:1041
  376.9 3.3 fusion.23
  380.2 2.3 collective-permute-start.68
  389.1 2.5 collective-permute-done.73
  397.6 2.1 collective-permute-done.71
  402.2 9.4 %reduce-scatter.8.cloned.1.call-done = bf16[288,640]{1,0:T(8,128)(2,1)} async-done(((bf16[1152,640]{1,0:T(8,128)(2,1)}), bf16[288,640]{1,0:T(8,128)(2,1)}) %reduce-scatter.8.cloned.1.call-update) | async-done | bytes 368656 | tf_op jit(solution)/shard_map/reduce_scatter | solution.py:1041
  413.5 1.8 slice_convert_fusion.1
  (332 shorter events, 83.5 us)
Async XLA Ops:
  7.2 300.0 %reduce-scatter.4.cloned.1.call-start = ((), (), s32[]{:S(2)}) async-start(), calls=%async_computation.4 | async-start | bytes 1658880 | tf_op jit(solution)/shard_map/reduce_scatter | solution.py:1041
  9.1 11.3 %collective-permute-start.2 = (bf16[1,1152]{1,0:T(2,128)(2,1)S(1)}, bf16[1,1152]{1,0:T(2,128)(2,1)S(1)}, u32[]{:S(2)}, u32[]{:S(2)}) collective-permute-start(bf16[1,1152]{1,0:T(2,128)(2,1)S(1)} %get-tuple-element.227.cond_ref), channel_id=1, source_target_pairs={{0,3},{1,0},{2,1},{3,2},{4,7},{5,4},{6,5},{7,6},{8,11},{9,8},{10,9... | collective-permute-start | bytes 6920 | tf_op jit(solution)/shard_map/ppermute | solution.py:63
  9.4 11.1 %collective-permute-start.1 = (bf16[1,1152]{1,0:T(2,128)(2,1)S(1)}, bf16[1,1152]{1,0:T(2,128)(2,1)S(1)}, u32[]{:S(2)}, u32[]{:S(2)}) collective-permute-start(bf16[1,1152]{1,0:T(2,128)(2,1)S(1)} %get-tuple-element.227.cond_ref), channel_id=1, source_target_pairs={{0,2},{1,3},{2,0},{3,1},{4,6},{5,7},{6,4},{7,5},{8,10},{9,11},{10,... | collective-permute-start | bytes 6920 | tf_op jit(solution)/shard_map/ppermute | solution.py:63
  9.4 11.1 %collective-permute-start = (bf16[1,1152]{1,0:T(2,128)(2,1)S(1)}, bf16[1,1152]{1,0:T(2,128)(2,1)S(1)}, u32[]{:S(2)}, u32[]{:S(2)}) collective-permute-start(bf16[1,1152]{1,0:T(2,128)(2,1)S(1)} %get-tuple-element.227.cond_ref), channel_id=1, source_target_pairs={{0,1},{1,2},{2,3},{3,0},{4,5},{5,6},{6,7},{7,4},{8,9},{9,10},{10,1... | collective-permute-start | bytes 6920 | tf_op jit(solution)/shard_map/ppermute | solution.py:63
  12.5 11.7 %collective-permute-start.3 = (bf16[9,8,3456]{2,1,0:T(8,128)(2,1)S(1)}, bf16[9,8,3456]{2,1,0:T(8,128)(2,1)S(1)}, u32[]{:S(2)}, u32[]{:S(2)}) collective-permute-start(bf16[9,8,3456]{2,1,0:T(8,128)(2,1)S(1)} %dynamic-slice_bitcast_fusion.2), channel_id=1, source_target_pairs={{0,1},{1,2},{2,3},{3,0},{4,5},{5,6},{6,7},{7,4},{8,9},{9,10},{10,1... | collective-permute-start | bytes 1493000 | tf_op jit(solution)/shard_map/ppermute | solution.py:63
  24.8 31.5 %collective-permute-start.9 = (bf16[256,2304]{1,0:T(8,128)(2,1)}, bf16[256,2304]{1,0:T(8,128)(2,1)S(1)}, u32[]{:S(2)}, u32[]{:S(2)}) collective-permute-start(bf16[256,2304]{1,0:T(8,128)(2,1)} %pad_maximum_fusion.1.refs_0_), channel_id=1, source_target_pairs={{0,16},{4,20},{8,24},{12,28},{16,0},{20,4},{24,8},{28,12},{1,17},{... | collective-permute-start | bytes 3538952 | tf_op jit(solution)/shard_map/ppermute | solution.py:57
  26.1 30.3 %collective-permute-start.8 = (bf16[256,2304]{1,0:T(8,128)(2,1)}, bf16[256,2304]{1,0:T(8,128)(2,1)S(1)}, u32[]{:S(2)}, u32[]{:S(2)}) collective-permute-start(bf16[256,2304]{1,0:T(8,128)(2,1)} %pad_maximum_fusion.1.refs_0_), channel_id=1, source_target_pairs={{0,8},{4,12},{8,0},{12,4},{16,24},{20,28},{24,16},{28,20},{1,9},{5... | collective-permute-start | bytes 3538952 | tf_op jit(solution)/shard_map/ppermute | solution.py:57
  27.3 16.2 %collective-permute-start.7 = (bf16[9,8,3456]{2,1,0:T(8,128)(2,1)S(1)}, bf16[9,8,3456]{2,1,0:T(8,128)(2,1)S(1)}, u32[]{:S(2)}, u32[]{:S(2)}) collective-permute-start(bf16[9,8,3456]{2,1,0:T(8,128)(2,1)S(1)} %collective-permute-done.3), channel_id=1, source_target_pairs={{0,1},{1,2},{2,3},{3,0},{4,5},{5,6},{6,7},{7,4},{8,9},{9,10},{10,1... | collective-permute-start | bytes 1493000 | tf_op jit(solution)/shard_map/ppermute | solution.py:63
  32.8 9.3 %collective-permute-start.5 = (f32[8,1152]{1,0:T(8,128)}, f32[8,1152]{1,0:T(8,128)S(1)}, u32[]{:S(2)}, u32[]{:S(2)}) collective-permute-start(f32[8,1152]{1,0:T(8,128)} %get-tuple-element.235), channel_id=1, source_target_pairs={{0,2},{1,3},{2,0},{3,1},{4,6},{5,7},{6,4},{7,5},{8,10},{9,11},{10,... | collective-permute-start | bytes 110600 | tf_op jit(solution)/shard_map/ppermute | solution.py:63
  43.5 12.9 %collective-permute-start.10 = (bf16[9,8,3456]{2,1,0:T(8,128)(2,1)S(1)}, bf16[9,8,3456]{2,1,0:T(8,128)(2,1)}, u32[]{:S(2)}, u32[]{:S(2)}) collective-permute-start(bf16[9,8,3456]{2,1,0:T(8,128)(2,1)S(1)} %collective-permute-done.7), channel_id=1, source_target_pairs={{0,1},{1,2},{2,3},{3,0},{4,5},{5,6},{6,7},{7,4},{8,9},{9,10},{10,1... | collective-permute-start | bytes 1493000 | tf_op jit(solution)/shard_map/ppermute | solution.py:63
  58.9 16.7 %collective-permute-start.12 = (bf16[3,9,8,3456]{3,2,1,0:T(8,128)(2,1)S(1)}, bf16[3,9,8,3456]{3,2,1,0:T(8,128)(2,1)}, u32[]{:S(2)}, u32[]{:S(2)}) collective-permute-start(bf16[3,9,8,3456]{3,2,1,0:T(8,128)(2,1)S(1)} %pad_maximum_fusion.refs_0_), channel_id=1, source_target_pairs={{0,4},{4,0},{8,12},{12,8},{16,20},{20,16},{24,28},{28,24},{1,5},{5... | collective-permute-start | bytes 4478984 | tf_op jit(solution)/shard_map/ppermute | solution.py:57
  61.8 18.8 %collective-permute-start.11 = (bf16[3,9,8,3456]{3,2,1,0:T(8,128)(2,1)S(1)}, bf16[3,9,8,3456]{3,2,1,0:T(8,128)(2,1)}, u32[]{:S(2)}, u32[]{:S(2)}) collective-permute-start(bf16[3,9,8,3456]{3,2,1,0:T(8,128)(2,1)S(1)} %pad_maximum_fusion.refs_0_), channel_id=1, source_target_pairs={{0,8},{4,20},{8,0},{12,28},{16,24},{20,4},{24,16},{28,12},{1,9},{5... | collective-permute-start | bytes 4478984 | tf_op jit(solution)/shard_map/ppermute | solution.py:60
  62.8 12.8 %collective-permute-start.13 = (bf16[9,8,2944]{2,1,0:T(8,128)(2,1)}, bf16[9,8,2944]{2,1,0:T(8,128)(2,1)}, u32[]{:S(2)}, u32[]{:S(2)}) collective-permute-start(bf16[9,8,2944]{2,1,0:T(8,128)(2,1)} %fusion), channel_id=1, source_target_pairs={{0,1},{1,2},{2,3},{3,0},{4,5},{5,6},{6,7},{7,4},{8,9},{9,10},{10,1... | collective-permute-start | bytes 1271816 | tf_op jit(solution)/shard_map/ppermute | solution.py:63
  80.6 8.3 %collective-permute-start.14 = (bf16[3,9,8,3456]{3,2,1,0:T(8,128)(2,1)}, bf16[3,9,8,3456]{3,2,1,0:T(8,128)(2,1)}, u32[]{:S(2)}, u32[]{:S(2)}) collective-permute-start(bf16[3,9,8,3456]{3,2,1,0:T(8,128)(2,1)} %collective-permute-done.11.refs_1_), channel_id=1, source_target_pairs={{0,4},{4,0},{8,12},{12,8},{16,20},{20,16},{24,28},{28,24},{1,5},{5... | collective-permute-start | bytes 4478984 | tf_op jit(solution)/shard_map/ppermute | solution.py:57
  83.5 15.2 %collective-permute-start.17 = (bf16[128,2304]{1,0:T(8,128)(2,1)}, bf16[128,2304]{1,0:T(8,128)(2,1)S(1)}, u32[]{:S(2)}, u32[]{:S(2)}) collective-permute-start(bf16[128,2304]{1,0:T(8,128)(2,1)} %slice.132), channel_id=1, source_target_pairs={{0,8},{4,12},{8,0},{12,4},{16,24},{20,28},{24,16},{28,20},{1,9},{5... | collective-permute-start | bytes 1769480 | tf_op jit(solution)/shard_map/ppermute | solution.py:57
  83.8 14.9 %collective-permute-start.16 = (bf16[128,2304]{1,0:T(8,128)(2,1)S(1)}, bf16[128,2304]{1,0:T(8,128)(2,1)S(1)}, u32[]{:S(2)}, u32[]{:S(2)}) collective-permute-start(bf16[128,2304]{1,0:T(8,128)(2,1)S(1)} %slice.131), channel_id=1, source_target_pairs={{0,16},{4,20},{8,24},{12,28},{16,0},{20,4},{24,8},{28,12},{1,17},{... | collective-permute-start | bytes 1769480 | tf_op jit(solution)/shard_map/ppermute | solution.py:57
  84.0 14.4 %collective-permute-start.15 = (bf16[9,8,2944]{2,1,0:T(8,128)(2,1)}, bf16[9,8,2944]{2,1,0:T(8,128)(2,1)}, u32[]{:S(2)}, u32[]{:S(2)}) collective-permute-start(bf16[9,8,2944]{2,1,0:T(8,128)(2,1)} %collective-permute-done.13), channel_id=1, source_target_pairs={{0,1},{1,2},{2,3},{3,0},{4,5},{5,6},{6,7},{7,4},{8,9},{9,10},{10,1... | collective-permute-start | bytes 1271816 | tf_op jit(solution)/shard_map/ppermute | solution.py:63
  98.7 15.1 %collective-permute-start.18 = (bf16[9,8,2944]{2,1,0:T(8,128)(2,1)}, bf16[9,8,2944]{2,1,0:T(8,128)(2,1)S(1)}, u32[]{:S(2)}, u32[]{:S(2)}) collective-permute-start(bf16[9,8,2944]{2,1,0:T(8,128)(2,1)} %collective-permute-done.15), channel_id=1, source_target_pairs={{0,1},{1,2},{2,3},{3,0},{4,5},{5,6},{6,7},{7,4},{8,9},{9,10},{10,1... | collective-permute-start | bytes 1271816 | tf_op jit(solution)/shard_map/ppermute | solution.py:63
  102.4 11.3 %collective-permute-start.21 = (f32[8,1152]{1,0:T(8,128)S(1)}, f32[8,1152]{1,0:T(8,128)S(1)}, u32[]{:S(2)}, u32[]{:S(2)}) collective-permute-start(f32[8,1152]{1,0:T(8,128)S(1)} %copy-done.57), channel_id=1, source_target_pairs={{0,24},{4,28},{8,16},{12,20},{16,8},{20,12},{24,0},{28,4},{1,25},{... | collective-permute-start | bytes 110600 | tf_op jit(solution)/shard_map/ppermute | solution.py:57
  103.3 10.4 %collective-permute-start.20 = (f32[8,1152]{1,0:T(8,128)S(1)}, f32[8,1152]{1,0:T(8,128)S(1)}, u32[]{:S(2)}, u32[]{:S(2)}) collective-permute-start(f32[8,1152]{1,0:T(8,128)S(1)} %copy-done.57), channel_id=1, source_target_pairs={{0,16},{4,20},{8,24},{12,28},{16,0},{20,4},{24,8},{28,12},{1,17},{... | collective-permute-start | bytes 110600 | tf_op jit(solution)/shard_map/ppermute | solution.py:57
  104.4 9.3 %collective-permute-start.19 = (f32[8,1152]{1,0:T(8,128)S(1)}, f32[8,1152]{1,0:T(8,128)S(1)}, u32[]{:S(2)}, u32[]{:S(2)}) collective-permute-start(f32[8,1152]{1,0:T(8,128)S(1)} %copy-done.57), channel_id=1, source_target_pairs={{0,8},{4,12},{8,0},{12,4},{16,24},{20,28},{24,16},{28,20},{1,9},{5... | collective-permute-start | bytes 110600 | tf_op jit(solution)/shard_map/ppermute | solution.py:57
  118.3 14.5 %collective-permute-start.25 = (bf16[36,8,1152]{2,1,0:T(8,128)(2,1)S(1)}, bf16[36,8,1152]{2,1,0:T(8,128)(2,1)S(1)}, u32[]{:S(2)}, u32[]{:S(2)}) collective-permute-start(bf16[36,8,1152]{2,1,0:T(8,128)(2,1)S(1)} %copy-done.19), channel_id=1, source_target_pairs={{0,1},{1,2},{2,3},{3,0},{4,5},{5,6},{6,7},{7,4},{8,9},{9,10},{10,1... | collective-permute-start | bytes 1990664 | tf_op jit(solution)/shard_map/ppermute | solution.py:63
  119.3 25.4 %collective-permute-start.24 = (bf16[27,8,2944]{2,1,0:T(8,128)(2,1)}, bf16[27,8,2944]{2,1,0:T(8,128)(2,1)}, u32[]{:S(2)}, u32[]{:S(2)}) collective-permute-start(bf16[27,8,2944]{2,1,0:T(8,128)(2,1)} %constant_dynamic-update-slice_fusion.refs_2_), channel_id=1, source_target_pairs={{0,4},{4,0},{8,12},{12,8},{16,20},{20,16},{24,28},{28,24},{1,5},{5... | collective-permute-start | bytes 3815432 | tf_op jit(solution)/shard_map/ppermute | solution.py:57
  121.2 29.8 %collective-permute-start.23 = (bf16[27,8,2944]{2,1,0:T(8,128)(2,1)}, bf16[27,8,2944]{2,1,0:T(8,128)(2,1)S(1)}, u32[]{:S(2)}, u32[]{:S(2)}) collective-permute-start(bf16[27,8,2944]{2,1,0:T(8,128)(2,1)} %constant_dynamic-update-slice_fusion.refs_2_), channel_id=1, source_target_pairs={{0,16},{4,20},{8,24},{12,28},{16,0},{20,4},{24,8},{28,12},{1,17},{... | collective-permute-start | bytes 3815432 | tf_op jit(solution)/shard_map/ppermute | solution.py:57
  121.6 29.5 %collective-permute-start.22 = (bf16[27,8,2944]{2,1,0:T(8,128)(2,1)}, bf16[27,8,2944]{2,1,0:T(8,128)(2,1)S(1)}, u32[]{:S(2)}, u32[]{:S(2)}) collective-permute-start(bf16[27,8,2944]{2,1,0:T(8,128)(2,1)} %constant_dynamic-update-slice_fusion.refs_2_), channel_id=1, source_target_pairs={{0,8},{4,12},{8,0},{12,4},{16,24},{20,28},{24,16},{28,20},{1,9},{5... | collective-permute-start | bytes 3815432 | tf_op jit(solution)/shard_map/ppermute | solution.py:57
  132.8 18.3 %collective-permute-start.26 = (bf16[36,8,1152]{2,1,0:T(8,128)(2,1)S(1)}, bf16[36,8,1152]{2,1,0:T(8,128)(2,1)}, u32[]{:S(2)}, u32[]{:S(2)}) collective-permute-start(bf16[36,8,1152]{2,1,0:T(8,128)(2,1)S(1)} %collective-permute-done.25.refs_0_), channel_id=1, source_target_pairs={{0,1},{1,2},{2,3},{3,0},{4,5},{5,6},{6,7},{7,4},{8,9},{9,10},{10,1... | collective-permute-start | bytes 1990664 | tf_op jit(solution)/shard_map/ppermute | solution.py:63
  151.0 19.8 %collective-permute-start.29 = (bf16[27,8,2944]{2,1,0:T(8,128)(2,1)S(1)}, bf16[27,8,2944]{2,1,0:T(8,128)(2,1)S(1)}, u32[]{:S(2)}, u32[]{:S(2)}) collective-permute-start(bf16[27,8,2944]{2,1,0:T(8,128)(2,1)S(1)} %collective-permute-done.22.refs_3_), channel_id=1, source_target_pairs={{0,4},{4,0},{8,12},{12,8},{16,20},{20,16},{24,28},{28,24},{1,5},{5... | collective-permute-start | bytes 3815432 | tf_op jit(solution)/shard_map/ppermute | solution.py:57
  152.1 18.7 %collective-permute-start.30 = (bf16[27,8,2944]{2,1,0:T(8,128)(2,1)S(1)}, bf16[27,8,2944]{2,1,0:T(8,128)(2,1)S(1)}, u32[]{:S(2)}, u32[]{:S(2)}) collective-permute-start(bf16[27,8,2944]{2,1,0:T(8,128)(2,1)S(1)} %collective-permute-done.23.refs_4_), channel_id=1, source_target_pairs={{0,4},{4,0},{8,12},{12,8},{16,20},{20,16},{24,28},{28,24},{1,5},{5... | collective-permute-start | bytes 3815432 | tf_op jit(solution)/shard_map/ppermute | solution.py:57
  152.2 18.6 %collective-permute-start.31 = (bf16[36,8,1152]{2,1,0:T(8,128)(2,1)}, bf16[36,8,1152]{2,1,0:T(8,128)(2,1)}, u32[]{:S(2)}, u32[]{:S(2)}) collective-permute-start(bf16[36,8,1152]{2,1,0:T(8,128)(2,1)} %collective-permute-done.26.refs_1_), channel_id=1, source_target_pairs={{0,1},{1,2},{2,3},{3,0},{4,5},{5,6},{6,7},{7,4},{8,9},{9,10},{10,1... | collective-permute-start | bytes 1990664 | tf_op jit(solution)/shard_map/ppermute | solution.py:63
  155.1 15.7 %collective-permute-start.28 = (bf16[14,8,2944]{2,1,0:T(8,128)(2,1)S(1)}, bf16[14,8,2944]{2,1,0:T(8,128)(2,1)}, u32[]{:S(2)}, u32[]{:S(2)}) collective-permute-start(bf16[14,8,2944]{2,1,0:T(8,128)(2,1)S(1)} %slice.134), channel_id=1, source_target_pairs={{0,8},{4,12},{8,0},{12,4},{16,24},{20,28},{24,16},{28,20},{1,9},{5... | collective-permute-start | bytes 1978376 | tf_op jit(solution)/shard_map/ppermute | solution.py:57
  155.4 14.4 %collective-permute-start.27 = (bf16[13,8,2944]{2,1,0:T(8,128)(2,1)S(1)}, bf16[13,8,2944]{2,1,0:T(8,128)(2,1)}, u32[]{:S(2)}, u32[]{:S(2)}) collective-permute-start(bf16[13,8,2944]{2,1,0:T(8,128)(2,1)S(1)} %slice.133), channel_id=1, source_target_pairs={{0,16},{4,20},{8,24},{12,28},{16,0},{20,4},{24,8},{28,12},{1,17},{... | collective-permute-start | bytes 1837064 | tf_op jit(solution)/shard_map/ppermute | solution.py:57
  174.6 23.4 %collective-permute-start.34 = (bf16[36,8,1152]{2,1,0:T(8,128)(2,1)S(1)}, bf16[36,8,1152]{2,1,0:T(8,128)(2,1)}, u32[]{:S(2)}, u32[]{:S(2)}) collective-permute-start(bf16[36,8,1152]{2,1,0:T(8,128)(2,1)S(1)} %collective-permute-done.25.refs_0_), channel_id=1, source_target_pairs={{0,8},{4,20},{8,0},{12,28},{16,24},{20,4},{24,16},{28,12},{1,9},{5... | collective-permute-start | bytes 1990664 | tf_op jit(solution)/shard_map/ppermute | solution.py:60
  175.2 22.9 %collective-permute-start.35 = (bf16[36,8,1152]{2,1,0:T(8,128)(2,1)}, bf16[36,8,1152]{2,1,0:T(8,128)(2,1)}, u32[]{:S(2)}, u32[]{:S(2)}) collective-permute-start(bf16[36,8,1152]{2,1,0:T(8,128)(2,1)} %collective-permute-done.26.refs_1_), channel_id=1, source_target_pairs={{0,8},{4,20},{8,0},{12,28},{16,24},{20,4},{24,16},{28,12},{1,9},{5... | collective-permute-start | bytes 1990664 | tf_op jit(solution)/shard_map/ppermute | solution.py:60
  176.1 22.7 %collective-permute-start.36 = (bf16[36,8,1152]{2,1,0:T(8,128)(2,1)}, bf16[36,8,1152]{2,1,0:T(8,128)(2,1)}, u32[]{:S(2)}, u32[]{:S(2)}) collective-permute-start(bf16[36,8,1152]{2,1,0:T(8,128)(2,1)} %collective-permute-done.31.refs_2_), channel_id=1, source_target_pairs={{0,8},{4,20},{8,0},{12,28},{16,24},{20,4},{24,16},{28,12},{1,9},{5... | collective-permute-start | bytes 1990664 | tf_op jit(solution)/shard_map/ppermute | solution.py:60
  206.3 30.4 %collective-permute-start.43 = (bf16[1152,256]{1,0:T(8,128)(2,1)}, bf16[1152,256]{1,0:T(8,128)(2,1)S(1)}, u32[]{:S(2)}, u32[]{:S(2)}) collective-permute-start(bf16[1152,256]{1,0:T(8,128)(2,1)} %get-tuple-element.343), channel_id=1, source_target_pairs={{0,8},{4,12},{8,0},{12,4},{16,24},{20,28},{24,16},{28,20},{1,9},{5... | collective-permute-start | bytes 1769480 | tf_op jit(solution)/shard_map/ppermute | solution.py:57
  206.9 29.9 %collective-permute-start.44 = (bf16[1152,256]{1,0:T(8,128)(2,1)}, bf16[1152,256]{1,0:T(8,128)(2,1)}, u32[]{:S(2)}, u32[]{:S(2)}) collective-permute-start(bf16[1152,256]{1,0:T(8,128)(2,1)} %get-tuple-element.344), channel_id=1, source_target_pairs={{0,16},{4,20},{8,24},{12,28},{16,0},{20,4},{24,8},{28,12},{1,17},{... | collective-permute-start | bytes 1769480 | tf_op jit(solution)/shard_map/ppermute | solution.py:57
  207.5 29.3 %collective-permute-start.45 = (bf16[1152,256]{1,0:T(8,128)(2,1)}, bf16[1152,256]{1,0:T(8,128)(2,1)}, u32[]{:S(2)}, u32[]{:S(2)}) collective-permute-start(bf16[1152,256]{1,0:T(8,128)(2,1)} %get-tuple-element.345), channel_id=1, source_target_pairs={{0,24},{4,28},{8,16},{12,20},{16,8},{20,12},{24,0},{28,4},{1,25},{... | collective-permute-start | bytes 1769480 | tf_op jit(solution)/shard_map/ppermute | solution.py:57
  236.8 25.0 %collective-permute-start.46 = (bf16[1152,256]{1,0:T(8,128)(2,1)}, bf16[1152,256]{1,0:T(8,128)(2,1)S(1)}, u32[]{:S(2)}, u32[]{:S(2)}) collective-permute-start(bf16[1152,256]{1,0:T(8,128)(2,1)} %get-tuple-element.354), channel_id=1, source_target_pairs={{0,8},{4,12},{8,0},{12,4},{16,24},{20,28},{24,16},{28,20},{1,9},{5... | collective-permute-start | bytes 1769480 | tf_op jit(solution)/shard_map/ppermute | solution.py:57
  237.4 24.4 %collective-permute-start.47 = (bf16[1152,256]{1,0:T(8,128)(2,1)S(1)}, bf16[1152,256]{1,0:T(8,128)(2,1)S(1)}, u32[]{:S(2)}, u32[]{:S(2)}) collective-permute-start(bf16[1152,256]{1,0:T(8,128)(2,1)S(1)} %copy-done.55), channel_id=1, source_target_pairs={{0,16},{4,20},{8,24},{12,28},{16,0},{20,4},{24,8},{28,12},{1,17},{... | collective-permute-start | bytes 1769480 | tf_op jit(solution)/shard_map/ppermute | solution.py:57
  238.0 25.6 %collective-permute-start.48 = (bf16[1152,256]{1,0:T(8,128)(2,1)S(1)}, bf16[1152,256]{1,0:T(8,128)(2,1)S(1)}, u32[]{:S(2)}, u32[]{:S(2)}) collective-permute-start(bf16[1152,256]{1,0:T(8,128)(2,1)S(1)} %copy-done.54), channel_id=1, source_target_pairs={{0,24},{4,28},{8,16},{12,20},{16,8},{20,12},{24,0},{28,4},{1,25},{... | collective-permute-start | bytes 1769480 | tf_op jit(solution)/shard_map/ppermute | solution.py:57
  264.5 7.9 %collective-permute-start.49 = (f32[4,144,1152]{2,1,0:T(8,128)}, f32[4,144,1152]{2,1,0:T(8,128)S(1)}, u32[]{:S(2)}, u32[]{:S(2)}) collective-permute-start(f32[4,144,1152]{2,1,0:T(8,128)} %get-tuple-element.371), channel_id=1, source_target_pairs={{0,4},{4,0},{8,12},{12,8},{16,20},{20,16},{24,28},{28,24},{1,5},{5... | collective-permute-start | bytes 7962632 | tf_op jit(solution)/shard_map/ppermute | solution.py:57
  272.4 24.8 %collective-permute-start.54 = (f32[4,144,1152]{2,1,0:T(8,128)}, f32[4,144,1152]{2,1,0:T(8,128)}, u32[]{:S(2)}, u32[]{:S(2)}) collective-permute-start(f32[4,144,1152]{2,1,0:T(8,128)} %get-tuple-element.383), channel_id=1, source_target_pairs={{0,4},{4,0},{8,12},{12,8},{16,20},{20,16},{24,28},{28,24},{1,5},{5... | collective-permute-start | bytes 7962632 | tf_op jit(solution)/shard_map/ppermute | solution.py:57
  277.7 98.1 %reduce-scatter.6.cloned.1.call-start = ((), (), s32[]{:S(2)}) async-start(), calls=%async_computation.5 | async-start | bytes 1843200 | tf_op jit(solution)/shard_map/reduce_scatter | solution.py:1041
  278.0 17.6 %collective-permute-start.51 = (bf16[256,1152]{1,0:T(8,128)(2,1)S(1)}, bf16[256,1152]{1,0:T(8,128)(2,1)S(1)}, u32[]{:S(2)}, u32[]{:S(2)}) collective-permute-start(bf16[256,1152]{1,0:T(8,128)(2,1)S(1)} %copy-done.20), channel_id=1, source_target_pairs={{0,16},{4,20},{8,24},{12,28},{16,0},{20,4},{24,8},{28,12},{1,17},{... | collective-permute-start | bytes 1769480 | tf_op jit(solution)/shard_map/ppermute | solution.py:57
  278.9 16.7 %collective-permute-start.50 = (bf16[256,1152]{1,0:T(8,128)(2,1)S(1)}, bf16[256,1152]{1,0:T(8,128)(2,1)S(1)}, u32[]{:S(2)}, u32[]{:S(2)}) collective-permute-start(bf16[256,1152]{1,0:T(8,128)(2,1)S(1)} %copy-done.20), channel_id=1, source_target_pairs={{0,8},{4,12},{8,0},{12,4},{16,24},{20,28},{24,16},{28,20},{1,9},{5... | collective-permute-start | bytes 1769480 | tf_op jit(solution)/shard_map/ppermute | solution.py:57
  295.7 7.5 %collective-permute-start.53 = (bf16[128,1152]{1,0:T(8,128)(2,1)S(1)}, bf16[128,1152]{1,0:T(8,128)(2,1)S(1)}, u32[]{:S(2)}, u32[]{:S(2)}) collective-permute-start(bf16[128,1152]{1,0:T(8,128)(2,1)S(1)} %slice.136), channel_id=1, source_target_pairs={{0,8},{4,12},{8,0},{12,4},{16,24},{20,28},{24,16},{28,20},{1,9},{5... | collective-permute-start | bytes 884744 | tf_op jit(solution)/shard_map/ppermute | solution.py:57
  296.6 7.3 %collective-permute-start.52 = (bf16[128,1152]{1,0:T(8,128)(2,1)S(1)}, bf16[128,1152]{1,0:T(8,128)(2,1)S(1)}, u32[]{:S(2)}, u32[]{:S(2)}) collective-permute-start(bf16[128,1152]{1,0:T(8,128)(2,1)S(1)} %slice.135), channel_id=1, source_target_pairs={{0,16},{4,20},{8,24},{12,28},{16,0},{20,4},{24,8},{28,12},{1,17},{... | collective-permute-start | bytes 884744 | tf_op jit(solution)/shard_map/ppermute | solution.py:57
  315.0 17.3 %collective-permute-start.58 = (f32[576,1152]{1,0:T(8,128)}, f32[576,1152]{1,0:T(8,128)S(1)}, u32[]{:S(2)}, u32[]{:S(2)}) collective-permute-start(f32[576,1152]{1,0:T(8,128)} %get-tuple-element.408), channel_id=1, source_target_pairs={{0,4},{4,0},{8,12},{12,8},{16,20},{20,16},{24,28},{28,24},{1,5},{5... | collective-permute-start | bytes 7962632 | tf_op jit(solution)/shard_map/ppermute | solution.py:57
  315.8 22.3 %collective-permute-start.55 = (bf16[864,256]{1,0:T(8,128)(2,1)}, bf16[864,256]{1,0:T(8,128)(2,1)S(1)}, u32[]{:S(2)}, u32[]{:S(2)}) collective-permute-start(bf16[864,256]{1,0:T(8,128)(2,1)} %get-tuple-element.394), channel_id=1, source_target_pairs={{0,8},{4,12},{8,0},{12,4},{16,24},{20,28},{24,16},{28,20},{1,9},{5... | collective-permute-start | bytes 1327112 | tf_op jit(solution)/shard_map/ppermute | solution.py:57
  316.9 21.1 %collective-permute-start.56 = (bf16[864,256]{1,0:T(8,128)(2,1)}, bf16[864,256]{1,0:T(8,128)(2,1)S(1)}, u32[]{:S(2)}, u32[]{:S(2)}) collective-permute-start(bf16[864,256]{1,0:T(8,128)(2,1)} %get-tuple-element.395), channel_id=1, source_target_pairs={{0,16},{4,20},{8,24},{12,28},{16,0},{20,4},{24,8},{28,12},{1,17},{... | collective-permute-start | bytes 1327112 | tf_op jit(solution)/shard_map/ppermute | solution.py:57
  318.1 20.0 %collective-permute-start.57 = (bf16[864,256]{1,0:T(8,128)(2,1)}, bf16[864,256]{1,0:T(8,128)(2,1)S(1)}, u32[]{:S(2)}, u32[]{:S(2)}) collective-permute-start(bf16[864,256]{1,0:T(8,128)(2,1)} %get-tuple-element.396), channel_id=1, source_target_pairs={{0,24},{4,28},{8,16},{12,20},{16,8},{20,12},{24,0},{28,4},{1,25},{... | collective-permute-start | bytes 1327112 | tf_op jit(solution)/shard_map/ppermute | solution.py:57
  346.1 18.9 %collective-permute-start.59 = (f32[432,1152]{1,0:T(8,128)}, f32[432,1152]{1,0:T(8,128)}, u32[]{:S(2)}, u32[]{:S(2)}) collective-permute-start(f32[432,1152]{1,0:T(8,128)} %get-tuple-element.420), channel_id=1, source_target_pairs={{0,4},{4,0},{8,12},{12,8},{16,20},{20,16},{24,28},{28,24},{1,5},{5... | collective-permute-start | bytes 5971976 | tf_op jit(solution)/shard_map/ppermute | solution.py:57
  347.2 11.5 %collective-permute-start.60 = (bf16[144,1152]{1,0:T(8,128)(2,1)}, bf16[144,1152]{1,0:T(8,128)(2,1)S(1)}, u32[]{:S(2)}, u32[]{:S(2)}) collective-permute-start(bf16[144,1152]{1,0:T(8,128)(2,1)} %get-tuple-element.422), channel_id=1, source_target_pairs={{0,8},{4,12},{8,0},{12,4},{16,24},{20,28},{24,16},{28,20},{1,9},{5... | collective-permute-start | bytes 995336 | tf_op jit(solution)/shard_map/ppermute | solution.py:57
  348.3 12.0 %collective-permute-start.61 = (bf16[144,1152]{1,0:T(8,128)(2,1)}, bf16[144,1152]{1,0:T(8,128)(2,1)S(1)}, u32[]{:S(2)}, u32[]{:S(2)}) collective-permute-start(bf16[144,1152]{1,0:T(8,128)(2,1)} %get-tuple-element.423), channel_id=1, source_target_pairs={{0,16},{4,20},{8,24},{12,28},{16,0},{20,4},{24,8},{28,12},{1,17},{... | collective-permute-start | bytes 995336 | tf_op jit(solution)/shard_map/ppermute | solution.py:57
  349.5 15.5 %collective-permute-start.62 = (bf16[144,1152]{1,0:T(8,128)(2,1)S(1)}, bf16[144,1152]{1,0:T(8,128)(2,1)S(1)}, u32[]{:S(2)}, u32[]{:S(2)}) collective-permute-start(bf16[144,1152]{1,0:T(8,128)(2,1)S(1)} %copy-done.56), channel_id=1, source_target_pairs={{0,24},{4,28},{8,16},{12,20},{16,8},{20,12},{24,0},{28,4},{1,25},{... | collective-permute-start | bytes 995336 | tf_op jit(solution)/shard_map/ppermute | solution.py:57
  350.9 19.9 %all-to-all-start = ((bf16[8,144,144]{1,2,0:T(8,128)(2,1)}), bf16[8,144,144]{1,2,0:T(8,128)(2,1)S(1)}, u32[]{:S(2)}, u32[]{:S(2)}) async-start(bf16[8,144,144]{1,2,0:T(8,128)(2,1)} %bitcast.35), calls=%async_computation.2 | async-start | bytes 1179648 | tf_op jit(solution)/shard_map/all_to_all | solution.py:1379
  355.4 56.3 %reduce-scatter.8.cloned.1.call-start = ((), (), s32[]{:S(2)}) async-start(), calls=%async_computation.6 | async-start | bytes 1843200 | tf_op jit(solution)/shard_map/reduce_scatter | solution.py:1041
  357.5 12.5 %collective-permute-start.65 = (f32[16,1152]{1,0:T(8,128)}, f32[16,1152]{1,0:T(8,128)S(1)}, u32[]{:S(2)}, u32[]{:S(2)}) collective-permute-start(f32[16,1152]{1,0:T(8,128)} %shard_map.257), channel_id=1, source_target_pairs={{0,3},{1,0},{2,1},{3,2},{4,7},{5,4},{6,5},{7,6},{8,11},{9,8},{10,9... | collective-permute-start | bytes 221192 | tf_op jit(solution)/shard_map/ppermute | solution.py:63
  358.7 12.1 %collective-permute-start.64 = (f32[16,1152]{1,0:T(8,128)}, f32[16,1152]{1,0:T(8,128)S(1)}, u32[]{:S(2)}, u32[]{:S(2)}) collective-permute-start(f32[16,1152]{1,0:T(8,128)} %shard_map.257), channel_id=1, source_target_pairs={{0,2},{1,3},{2,0},{3,1},{4,6},{5,7},{6,4},{7,5},{8,10},{9,11},{10,... | collective-permute-start | bytes 221192 | tf_op jit(solution)/shard_map/ppermute | solution.py:63
  360.2 10.6 %collective-permute-start.63 = (f32[16,1152]{1,0:T(8,128)}, f32[16,1152]{1,0:T(8,128)S(1)}, u32[]{:S(2)}, u32[]{:S(2)}) collective-permute-start(f32[16,1152]{1,0:T(8,128)} %shard_map.257), channel_id=1, source_target_pairs={{0,1},{1,2},{2,3},{3,0},{4,5},{5,6},{6,7},{7,4},{8,9},{9,10},{10,1... | collective-permute-start | bytes 221192 | tf_op jit(solution)/shard_map/ppermute | solution.py:63
  375.9 8.6 %collective-permute-start.69 = (bf16[4,8,1152]{2,1,0:T(8,128)(2,1)S(1)}, bf16[4,8,1152]{2,1,0:T(8,128)(2,1)S(1)}, u32[]{:S(2)}, u32[]{:S(2)}) collective-permute-start(bf16[4,8,1152]{2,1,0:T(8,128)(2,1)S(1)} %pad_maximum_fusion.2), channel_id=1, source_target_pairs={{0,4},{4,0},{8,12},{12,8},{16,20},{20,16},{24,28},{28,24},{1,5},{5... | collective-permute-start | bytes 221192 | tf_op jit(solution)/shard_map/ppermute | solution.py:57
  376.8 11.6 %collective-permute-start.72 = (f32[8,1152]{1,0:T(8,128)S(1)}, f32[8,1152]{1,0:T(8,128)S(1)}, u32[]{:S(2)}, u32[]{:S(2)}) collective-permute-start(f32[8,1152]{1,0:T(8,128)S(1)} %slice_add_fusion), channel_id=1, source_target_pairs={{0,4},{4,0},{8,12},{12,8},{16,20},{20,16},{24,28},{28,24},{1,5},{5... | collective-permute-start | bytes 110600 | tf_op jit(solution)/shard_map/ppermute | solution.py:57
  380.2 8.0 %collective-permute-start.68 = (f32[288]{0:T(512)S(1)}, f32[288]{0:T(512)S(1)}, u32[]{:S(2)}, u32[]{:S(2)}) collective-permute-start(f32[288]{0:T(512)S(1)} %get-tuple-element.493), channel_id=1, source_target_pairs={{0,1},{1,2},{2,3},{3,0},{4,5},{5,6},{6,7},{7,4},{8,9},{9,10},{10,1... | collective-permute-start | bytes 3464 | tf_op jit(solution)/shard_map/ppermute | solution.py:63
  384.6 8.2 %collective-permute-start.70 = (bf16[8,8,1152]{2,1,0:T(8,128)(2,1)S(1)}, bf16[8,8,1152]{2,1,0:T(8,128)(2,1)S(1)}, u32[]{:S(2)}, u32[]{:S(2)}) collective-permute-start(bf16[8,8,1152]{2,1,0:T(8,128)(2,1)S(1)} %get-tuple-element.510), channel_id=1, source_target_pairs={{0,8},{4,12},{8,0},{12,4},{16,24},{20,28},{24,16},{28,20},{1,9},{5... | collective-permute-start | bytes 442376 | tf_op jit(solution)/shard_map/ppermute | solution.py:57
  (73 other events, 640.8 us)
Sparse Core Ops, SparseCore 0:
  277.9 29.2 reduce-scatter.3
  338.3 37.5 reduce-scatter.5
  378.3 33.3 reduce-scatter.7

commit v6 on v5

--- a/solution.py
+++ b/solution.py
@@ -219,7 +219,7 @@
     def wide_copies(core, where_ref, own_refs, sets, whole_refs):
         widths = [ref.shape[-1] for ref in own_refs]
         width, part = sum(widths), sets[0][0].shape[-1]
-        lead, split = whole_refs[0].shape[2], sets[0][3].shape[0]
+        lead, split = whole_refs[0].shape[2], sets[0][6].shape[0]
         copies = [(own, whole.at[where_ref[0]]) for own, whole in zip(own_refs, whole_refs)]
         for side, piece_refs in enumerate(sets):
             low, high = (0, part) if core ^ side == 0 else (part, width)
@@ -227,11 +227,12 @@
             for block in range(1, fs):
                 base = (block - 1) * lead
                 top = min(max(split - base, 0), lead)
-                rows = [(i, base, i, 0, lead) for i in range(3)]
+                late = int(block == fs - 1)
+                rows = [(2 * i + late, 0 if late else base, i, 0, lead) for i in range(3)]
                 if top:
-                    rows.append((3, base, 3, 0, top))
+                    rows.append((6, base, 3, 0, top))
                 if top < lead:
-                    rows.append((4, base + top - split, 3, top, lead - top))
+                    rows.append((7, base + top - split, 3, top, lead - top))
                 for piece, first, slot, row, count in rows:
                     start = 0
                     for i, each in enumerate(widths):
@@ -1214,6 +1215,7 @@
         qkv_other = side_send(qkv_mine)
         qkv_mine_got = box_send(qkv_mine, 1)
         mid_helds = [ring_send(after(mid_eighth, qkv_mine), 1)]
+        heads_got = [box_send(after(head, qkv_mine), bits) for bits in (2, 4)]
         bias_rows = [each[6:].reshape(-1) for each in partials]
         bias_rows = jnp.stack(bias_rows + bias_rows)
         biases = lax.dynamic_slice_in_dim(bias_rows, lax.rem(fs - z, fs), fs, 0)
@@ -1221,8 +1223,8 @@
         for bias in (b_qv, b_out, b_down, b_up):
             ends.append(ends[-1] + bias.shape[0])
         biases = [biases[:, ends[i] : ends[i + 1]].reshape(-1) for i in range(4)]
-        qkv_mine, qkv_other, qkv_mine_got, mid_helds, biases = gated(
-            (qkv_mine, qkv_other, qkv_mine_got, mid_helds, biases)
+        qkv_mine, qkv_other, qkv_mine_got, mid_helds, biases, heads_got = gated(
+            (qkv_mine, qkv_other, qkv_mine_got, mid_helds, biases, heads_got)
         )
         bias_qv, bias_out, bias_down, bias_up = biases
 
@@ -1232,6 +1234,7 @@
             return [(array, k) for k in range(last)]
 
         qkv_other_got = box_send(qkv_other, 1)
+        heads_got.append(box_send(after(head, qkv_other), 6))
         raw_far = chip_far([after(each, qkv_other) for each in raw_near])
         mid_helds.append(ring_send(mid_helds[-1], 1))
         turned, qkv_full = projection(
@@ -1241,39 +1244,58 @@
             [in_order(each) for each in (qkv_mine, qkv_other, qkv_mine_got, qkv_other_got)],
             bias_qv.reshape(2, width),
         )
-        turned, qkv_full, mid_helds, raw_far = gated((turned, qkv_full, mid_helds, raw_far))
-
-        heads_got = [box_send(after(head, turned), bits) for bits in (2, 4, 6)]
-        mid_helds.append(ring_send(mid_helds[-1], 1))
+        turned, qkv_full, mid_helds, raw_far, heads_got = gated(
+            (turned, qkv_full, mid_helds, raw_far, heads_got)
+        )
+
+        mid_first = jnp.concatenate(mid_helds)
+        first_near = chip_near(mid_first)
+        mid_last = ring_send(mid_helds[-1], 1)
+        down_helds = [ring_send(after(down_quarter, mid_first), 1)]
         attended = attention(turned, live)
-        attended, mid_helds, heads_got = gated((attended, mid_helds, heads_got))
-
-        mid_mine = jnp.concatenate(mid_helds)
-        mid_near = chip_near(mid_mine)
-        mid_got = [box_send(mid_mine, 1)]
-        down_helds = [ring_send(after(down_quarter, mid_mine), 1)]
-        down_helds.append(ring_send(down_helds[-1], 1))
+        attended, mid_first, first_near, mid_last = gated(
+            (attended, mid_first, first_near, mid_last)
+        )
+
+        last_near = chip_near(mid_last)
+        first_got = [box_send(mid_first, 1)]
         normed_box, d_mlp_box = other_heads(
             (*raw_near, *raw_far), (0, 0, 0, slots // 2), (*heads_got, heads_got[2])
         )
         normed_box, d_mlp_box = [normed, *normed_box], [d_mlp, *d_mlp_box]
-        attended, mid_mine, mid_near, mid_got, down_helds, normed_box, d_mlp_box = gated(
-            (attended, mid_mine, mid_near, mid_got, down_helds, normed_box, d_mlp_box)
-        )
-
-        mid_far = chip_far(mid_near)
-        mid_got += [box_send(each, 1) for each in mid_near]
+        first_near, last_near, first_got, down_helds, normed_box, d_mlp_box = gated(
+            (first_near, last_near, first_got, down_helds, normed_box, d_mlp_box)
+        )
+
+        split = (mid_first.shape[0] + mid_last.shape[0]) // 2
+        mid_far = (
+            box_send(first_near[0][:split], 4),
+            box_send(jnp.concatenate([first_near[1][split:], last_near[1]]), 2),
+        )
+        first_got += [box_send(each, 1) for each in first_near]
         down_helds.append(ring_send(down_helds[-1], 1))
-        attended, mid_far, mid_got, down_helds = gated((attended, mid_far, mid_got, down_helds))
-
-        mid_got += [box_send(each, 1) for each in mid_far]
-        down_others = [side_send(each) for each in down_helds]
+        attended, mid_far, first_got, down_helds = gated(
+            (attended, mid_far, first_got, down_helds)
+        )
+
+        last_got = [box_send(each, 1) for each in (mid_last, *last_near)]
+        far_got = [box_send(each, 1) for each in mid_far]
+        down_helds.append(ring_send(down_helds[-1], 1))
+        down_others = [side_send(each) for each in down_helds[:-1]]
+
+        def paired(first, last_ones, far):
+            pairs = [each for pair in zip(first, last_ones) for each in pair]
+            return [*pairs, *far]
+
         attn_out, normed_two, pre_act, activated, *act_blocks, out_full, up_full = middle_forward(
             where_wide,
             attended,
             tokens[0],
             [w_out, w_up],
-            ((mid_mine, *mid_near, *mid_far), mid_got),
+            (
+                paired((mid_first, *first_near), (mid_last, *last_near), mid_far),
+                paired(first_got, last_got, far_got),
+            ),
             bias_out,
             bias_up,
             mods,
@@ -1282,8 +1304,9 @@
             (down_helds, down_others, act_blocks, normed_two)
         )
 
+        down_others.append(side_send(down_helds[-1]))
         down_got = [[box_send(each, 1) for each in kind] for kind in (down_helds, down_others)]
-        act_blocks, down_got = gated((act_blocks, down_got))
+        act_blocks, down_others, down_got = gated((act_blocks, down_others, down_got))
 
         act_box = chip_exchange(act_blocks)
         d_pre, *d_pre_turned, d_pre_sums, down_full = hidden_back(

time: 427 us -> 425 us (level)
  starting transfers between devices: 87.9 us -> 93.7 us
  waiting for transfers between devices: 99.7 us -> 94.5 us
    ppermute x21, waiting for transfers between devices: 31 us -> 17.9 us  [ring_send(): return lax.ppermute(x, 'fsdp', [(i, (i + hops) % fs) for i in range(fs)])]
    ppermute x50 -> x55, waiting for transfers between devices: 45.1 us -> 51.1 us  [box_send(): return lax.ppermute(x, 'dp', [(i, i ^ bits) for i in range(dp)])]
    ppermute x50 -> x55, starting transfers between devices: 41.7 us -> 46.2 us  [box_send(): return lax.ppermute(x, 'dp', [(i, i ^ bits) for i in range(dp)])]
    unnamed x138 -> x157, local copies, waits for them, and re-layouts: 14.8 us -> 12 us
  transfers between devices with their start and end apart: 79 -> 84, of which waited for: 28 -> 24; matrix products, arithmetic and copies ran while one was open for 7% -> 7% of each run, Pallas kernels for 38% -> 38%
where the time goes in v6:
time: 425 us; the launch traced here: 420 us
  Pallas kernels  168 us (40%)
  waiting for transfers between devices  94.5 us (22%)
  starting transfers between devices  93.7 us (22%)
  local copies, waits for them, and re-layouts  33.5 us (8%)
  between operations  16.1 us (4%)
  other arithmetic  10.1 us (2%)
  matrix products  4.61 us (1%)
    ppermute x55, waiting for transfers between devices, box_send(): return lax.ppermute(x, 'dp', [(i, i ^ bits) for i in range(dp)])  51.1 us
    ppermute x55, starting transfers between devices, box_send(): return lax.ppermute(x, 'dp', [(i, i ^ bits) for i in range(dp)])  46.2 us
    ppermute x21, starting transfers between devices, ring_send(): return lax.ppermute(x, 'fsdp', [(i, (i + hops) % fs) for i in range(fs)])  40.8 us
    pallas_call x1, Pallas kernels, middle_forward(): pl.pallas_call(kernel, out_shape=[jax.ShapeDtypeStruct((slots, width), f3...  19.6 us
    reduce_scatter x3, waiting for transfers between devices, fsdp_sum(): return lax.psum_scatter(x, 'fsdp', scatter_dimension=0, tiled=True)  18 us
    ppermute x21, waiting for transfers between devices, ring_send(): return lax.ppermute(x, 'fsdp', [(i, (i + hops) % fs) for i in range(fs)])  17.9 us
    pallas_call x1, Pallas kernels, hidden_back(): pl.pallas_call(kernel, out_shape=[jax.ShapeDtypeStruct((slots, hidden), b...  17.1 us
    pallas_call x1, Pallas kernels, attention_back(): pl.pallas_call(kernel, out_shape=[jax.ShapeDtypeStruct((3 * width, slots)...  15.4 us
  transfers between devices with their start and end apart: 84, of which 24 were waited for; matrix products, arithmetic and copies ran while one was open for 7% of the time, Pallas kernels for 38%

profile of v6, /device:TPU:25, one launch (start us, length us, event | category | flops | bytes accessed | tf_op | source)
XLA Modules:
  0.0 420.2 jit_solution(14165327508593714198)
XLA Ops:
  9.4 3.1 collective-permute-start
  17.0 2.0 dynamic-slice_bitcast_fusion
  20.5 3.7 collective-permute-done.3
  27.3 2.0 collective-permute-start.7
  29.3 3.5 shard_map.237
  33.4 5.1 %collective-permute-done.4.refs_1_ = f32[8,1152]{1,0:T(8,128)S(1)} collective-permute-done((f32[8,1152]{1,0:T(8,128)}, f32[8,1152]{1,0:T(8,128)S(1)}, u32[]{:S(2)}, u32[]{:S(2)}) %collective-permute-start.4) | collective-permute-done | bytes 36896 | tf_op jit(solution)/shard_map/ppermute | solution.py:63
  38.4 3.7 collective-permute-start.6
  42.1 1.4 collective-permute-done.6.refs_3_
  43.5 3.7 collective-permute-start.10
  49.1 1.5 shard_map.238
  50.6 3.9 shard_map.239
  54.4 2.0 collective-permute-done.10
  58.8 2.9 collective-permute-start.12
  62.8 3.7 collective-permute-start.13
  69.4 11.9 %collective-permute-done.15.refs_5_ = f32[8,1152]{1,0:T(8,128)S(1)} collective-permute-done((f32[8,1152]{1,0:T(8,128)S(1)}, f32[8,1152]{1,0:T(8,128)S(1)}, u32[]{:S(2)}, u32[]{:S(2)}) %collective-permute-start.15) | collective-permute-done | bytes 36896 | tf_op jit(solution)/shard_map/ppermute | solution.py:57
  84.7 3.6 collective-permute-start.17
  89.6 2.2 collective-permute-start.20
  91.8 9.4 %shard_map.240 = (f32[3456,256]{1,0:T(8,128)}, bf16[4,4,9,8,3456]{4,3,2,1,0:T(8,128)(2,1)}) custom-call(s32[12]{0:T(128)} %stack.119.where_ref, bf16[256,1152]{1,0:T(8,128)(2,1)} %get-tuple-element.396.normed_ref.refs_0_, f32[2,1152]{1,0:T(2,128)} %reshape.132.bias_ref, bf16[4,9,8,3456]{3,2,1,0:T(8,128)(2,1)} %bitcast.102, ...), custom_call_target="tpu_custom_call" | custom-call | flops 1100000000 | bytes 3520000 | tf_op jit(solution)/shard_map/pallas_call | solution.py:300
  104.8 3.2 collective-permute-start.23
  108.0 8.7 %shard_map.241.attended_ref.x_ref = bf16[256,1152]{1,0:T(8,128)(2,1)} custom-call(s32[1]{0:T(128)} %bitcast.live_ref, f32[3456,256]{1,0:T(8,128)} %get-tuple-element.275.turned_ref), custom_call_target="tpu_custom_call" | custom-call | flops 1100000000 | bytes 3520000 | tf_op jit(solution)/shard_map/pallas_call | solution.py:357
  116.6 6.8 %collective-permute-done.22.refs_6_ = bf16[18,8,2944]{2,1,0:T(8,128)(2,1)S(1)} collective-permute-done((bf16[18,8,2944]{2,1,0:T(8,128)(2,1)S(1)}, bf16[18,8,2944]{2,1,0:T(8,128)(2,1)S(1)}, u32[]{:S(2)}, u32[]{:S(2)}) %collective-permute-start.22) | collective-permute-done | bytes 847904 | tf_op jit(solution)/shard_map/ppermute | solution.py:57
  123.5 2.3 collective-permute-start.26
  125.8 3.2 collective-permute-start.27
  129.9 8.8 %shard_map.242 = (bf16[256,1152]{1,0:T(8,128)(2,1)}, bf16[256,1152]{1,0:T(8,128)(2,1)}, bf16[128,1152]{1,0:T(8,128)(2,1)}, bf16[128,1152]{1,0:T(8,128)(2,1)}, bf...) custom-call(bf16[256,2304]{1,0:T(8,128)(2,1)} %copy-done.4, ...), custom_call_target="tpu_custom_call" | custom-call | flops 800000000 | bytes 2560000 | tf_op jit(solution)/shard_map/pallas_call | solution.py:192
  138.7 4.8 %collective-permute-done.27.refs_0_ = bf16[36,8,1152]{2,1,0:T(8,128)(2,1)} collective-permute-done((bf16[36,8,1152]{2,1,0:T(8,128)(2,1)}, bf16[36,8,1152]{2,1,0:T(8,128)(2,1)}, u32[]{:S(2)}, u32[]{:S(2)}) %collective-permute-start.27) | collective-permute-done | bytes 663584 | tf_op jit(solution)/shard_map/ppermute | solution.py:63
  143.6 4.1 collective-permute-start.32
  148.8 1.7 collective-permute-start.30
  150.6 11.6 %collective-permute-done.28.refs_8_ = bf16[13,8,2944]{2,1,0:T(8,128)(2,1)} collective-permute-done((bf16[13,8,2944]{2,1,0:T(8,128)(2,1)S(1)}, bf16[13,8,2944]{2,1,0:T(8,128)(2,1)}, u32[]{:S(2)}, u32[]{:S(2)}) %collective-permute-start.28) | collective-permute-done | bytes 612384 | tf_op jit(solution)/shard_map/ppermute | solution.py:57
  162.2 2.3 collective-permute-start.33
  167.8 1.7 collective-permute-start.38
  171.3 19.6 %shard_map.243 = (f32[256,1152]{1,0:T(8,128)}, bf16[256,1152]{1,0:T(8,128)(2,1)}, f32[256,4608]{1,0:T(8,128)}, bf16[256,4608]{1,0:T(8,128)(2,1)}, bf16[1152,256]...) custom-call(s32[9]{0:T(128)} %stack.114.where_ref, ...), custom_call_target="tpu_custom_call" | custom-call | flops 2000000000 | bytes 6400000 | tf_op jit(solution)/shard_map/pallas_call | solution.py:530
  194.4 7.5 %collective-permute-done.41.refs_5_ = bf16[36,8,1152]{2,1,0:T(8,128)(2,1)S(1)} collective-permute-done((bf16[36,8,1152]{2,1,0:T(8,128)(2,1)S(1)}, bf16[36,8,1152]{2,1,0:T(8,128)(2,1)S(1)}, u32[]{:S(2)}, u32[]{:S(2)}) %collective-permute-start.41) | collective-permute-done | bytes 663584 | tf_op jit(solution)/shard_map/ppermute | solution.py:60
  202.8 1.7 collective-permute-done.47.refs_11_
  205.4 1.8 collective-permute-start.50
  207.9 17.1 %shard_map.244 = (bf16[256,4608]{1,0:T(8,128)(2,1)}, bf16[1152,256]{1,0:T(8,128)(2,1)}, bf16[1152,256]{1,0:T(8,128)(2,1)}, bf16[1152,256]{1,0:T(8,128)(2,1)}, bf...) custom-call(s32[12]{0:T(128)} %stack.119.where_ref, ...), custom_call_target="tpu_custom_call" | custom-call | flops 1500000000 | bytes 4800000 | tf_op jit(solution)/shard_map/pallas_call | solution.py:650
  225.0 10.1 %shard_map.245 = (bf16[256,1152]{1,0:T(8,128)(2,1)}, f32[8,1152]{1,0:T(8,128)}) custom-call(s32[1]{0:T(128)} %bitcast.live_ref, bf16[256,4608]{1,0:T(8,128)(2,1)} %get-tuple-element.314.act_ref, bf16[4608,1152]{1,0:T(8,128)(2,1)} %bitcast.90, f32[1,1152]{1,0:T(1,128)} %reshape.137.bias_ref, bf16[256,1152]{1,0:T(8,128)(2,1)} %bitcast.86, ...), custom_call_target="tpu_custom_call" | custom-call | flops 600000000 | bytes 1920000 | tf_op jit(solution)/shard_map/pallas_call | solution.py:892
  236.1 1.8 collective-permute-start.53
  237.8 7.7 %shard_map.247 = (f32[4,144,1152]{2,1,0:T(8,128)}, f32[4,144,1152]{2,1,0:T(8,128)}) custom-call(s32[1]{0:T(128)} %bitcast.5.where_ref, bf16[1152,256]{1,0:T(8,128)(2,1)} %get-tuple-element.365.x0, bf16[1152,256]{1,0:T(8,128)(2,1)} %collective-permute-done.48.x1, bf16[1152,256]{1,0:T(8,128)(2,1)} %collective-permute-done.49.x2, ...), custom_call_target="tpu_custom_call" | custom-call | flops 600000000 | bytes 1920000 | tf_op jit(solution)/shard_map/pallas_call | solution.py:1118
  245.5 14.6 %shard_map.246 = (f32[256,1152]{1,0:T(8,128)}, bf16[1152,256]{1,0:T(8,128)(2,1)}, f32[1152,256]{1,0:T(8,128)}, f32[8,1152]{1,0:T(8,128)}) custom-call(s32[1]{0:T(128)} %bitcast.live_ref, bf16[256,4608]{1,0:T(8,128)(2,1)} %get-tuple-element.356.d_pre_ref, bf16[1152,4608]{1,0:T(8,128)(2,1)} %bitcast.91, bf16[1152,1152]{1,0:T(8,128)(2,1)} %bitcast.104, ...), custom_call_target="tpu_custom_call" | custom-call | flops 1200000000 | bytes 3840000 | tf_op jit(solution)/shard_map/pallas_call | solution.py:756
  262.3 2.6 collective-permute-start.54
  265.5 5.1 %shard_map.250 = (f32[4,144,1152]{2,1,0:T(8,128)}, f32[4,144,1152]{2,1,0:T(8,128)}) custom-call(s32[5]{0:T(128)} %concatenate.43.where_ref, bf16[1152,256]{1,0:T(8,128)(2,1)} %get-tuple-element.389.d_ref, bf16[256,1152]{1,0:T(8,128)(2,1)} %shard_map.241.attended_ref.x_ref), custom_call_target="tpu_custom_call" | custom-call | flops 500000000 | bytes 1600000 | tf_op jit(solution)/shard_map/pallas_call | solution.py:1057
  270.6 1.5 copy-done.6
  272.1 3.8 shard_map.248
  278.4 15.4 %shard_map.249 = (bf16[3456,256]{1,0:T(8,128)(2,1)}, bf16[864,256]{1,0:T(8,128)(2,1)}, bf16[864,256]{1,0:T(8,128)(2,1)}, bf16[864,256]{1,0:T(8,128)(2,1)}, bf16[864,256]{1,0:T(8,128)(2,1)}) custom-call(s32[1]{0:T(128)} %bitcast.live_ref, s32[4]{0:T(128)} %pad_add_fusion.chip_ref, f32[3456,256]{1,0:T(8,128)} %get-tuple-element.275.turned_ref, ...), custom_call_target="tpu_custom_call" | custom-call | flops 1200000000 | bytes 3840000 | tf_op jit(solution)/shard_map/pallas_call | solution.py:423
  295.4 6.0 %collective-permute-done.58.refs_4_ = bf16[128,1152]{1,0:T(8,128)(2,1)S(1)} collective-permute-done((bf16[128,1152]{1,0:T(8,128)(2,1)S(1)}, bf16[128,1152]{1,0:T(8,128)(2,1)S(1)}, u32[]{:S(2)}, u32[]{:S(2)}) %collective-permute-start.58) | collective-permute-done | bytes 294944 | tf_op jit(solution)/shard_map/ppermute | solution.py:57
  301.9 3.5 reduce-scatter.4.cloned.1.call-done
  305.5 7.8 %shard_map.252 = (f32[576,1152]{1,0:T(8,128)}, f32[576,1152]{1,0:T(8,128)}) custom-call(s32[1]{0:T(128)} %bitcast.5.where_ref, bf16[256,1152]{1,0:T(8,128)(2,1)} %get-tuple-element.406.refs_0_, bf16[256,1152]{1,0:T(8,128)(2,1)} %copy-done.12, bf16[256,1152]{1,0:T(8,128)(2,1)} %copy-done.11, bf16[128,1152]{1,0:T(8,128)(2,1)} %copy-done.46, ...), custom_call_target="tpu_custom_call" | custom-call | flops 800000000 | bytes 2560000 | tf_op jit(solution)/shard_map/pallas_call | solution.py:963
  316.7 3.8 shard_map.254
  320.6 10.1 %shard_map.251 = (bf16[256,1152]{1,0:T(8,128)(2,1)}, f32[8,1152]{1,0:T(8,128)}) custom-call(bf16[3456,256]{1,0:T(8,128)(2,1)} %get-tuple-element.392.d_ref, bf16[1152,3456]{1,0:T(8,128)(2,1)} %bitcast.92, bf16[256,1152]{1,0:T(8,128)(2,1)} %bitcast.88, f32[256,1152]{1,0:T(8,128)} %get-tuple-element.394.d_middle_ref, f32[8,1152]{1,0:T(8,128)} %get-tuple-element.307.mods_ref), custom_call_target="tpu_custom_call" | custom-call | flops 900000000 | bytes 2880000 | tf_op jit(solution)/shard_map/pallas_call | solution.py:825
  330.6 1.5 copy-done.5
  332.2 4.2 %shard_map.253 = bf16[1152,640]{1,0:T(8,128)(2,1)} custom-call(f32[576,1152]{1,0:T(8,128)} %get-tuple-element.415.refs_0_, f32[576,1152]{1,0:T(8,128)} %copy-done.5), custom_call_target="tpu_custom_call" | custom-call | flops 500000000 | bytes 1600000 | tf_op jit(solution)/shard_map/pallas_call | solution.py:1018
  337.5 6.9 %shard_map.255 = (f32[432,1152]{1,0:T(8,128)}, f32[432,1152]{1,0:T(8,128)}) custom-call(s32[1]{0:T(128)} %bitcast.5.where_ref, bf16[256,1152]{1,0:T(8,128)(2,1)} %get-tuple-element.396.normed_ref.refs_0_, bf16[256,1152]{1,0:T(8,128)(2,1)} %get-tuple-element.397.refs_1_, bf16[256,1152]{1,0:T(8,128)(2,1)} %get-tuple-element.398.refs_2_, ...), custom_call_target="tpu_custom_call" | custom-call | flops 800000000 | bytes 2560000 | tf_op jit(solution)/shard_map/pallas_call | solution.py:963
  349.2 4.5 %all-to-all-start = ((bf16[8,144,144]{1,2,0:T(8,128)(2,1)}), bf16[8,144,144]{1,2,0:T(8,128)(2,1)S(1)}, u32[]{:S(2)}, u32[]{:S(2)}) async-start(bf16[8,144,144]{1,2,0:T(8,128)(2,1)} %bitcast.35), calls=%async_computation.2 | async-start | bytes 1179648 | tf_op jit(solution)/shard_map/all_to_all | solution.py:1402
  354.3 1.5 shard_map.257
  356.9 1.5 collective-permute-start.69
  359.1 4.1 collective-permute-done.67.refs_5_
  363.9 4.2 %shard_map.256 = bf16[1152,640]{1,0:T(8,128)(2,1)} custom-call(f32[432,1152]{1,0:T(8,128)} %get-tuple-element.427.refs_0_, f32[432,1152]{1,0:T(8,128)} %collective-permute-done.64.refs_1_, f32[144,1152]{1,0:T(8,128)} %get-tuple-element.429.refs_2_, bf16[144,1152]{1,0:T(8,128)(2,1)} %copy-done.42, bf16[144,1152]{1,0:T(8,128)(2,1)} %copy-done.43, ...), custom_call_target="tpu_custom_call" | custom-call | flops 500000000 | bytes 1600000 | tf_op jit(solution)/shard_map/pallas_call | solution.py:1018
  369.1 5.0 %reduce-scatter.6.cloned.1.call-done = bf16[288,640]{1,0:T(8,128)(2,1)} async-done(((bf16[1152,640]{1,0:T(8,128)(2,1)}), bf16[288,640]{1,0:T(8,128)(2,1)}) %reduce-scatter.6.cloned.1.call-update) | async-done | bytes 368656 | tf_op jit(solution)/shard_map/reduce_scatter | solution.py:1042
  375.2 3.3 fusion.23
  378.5 2.3 collective-permute-start.73
  387.4 2.6 collective-permute-done.78
  395.9 2.1 collective-permute-done.76
  400.5 9.4 %reduce-scatter.8.cloned.1.call-done = bf16[288,640]{1,0:T(8,128)(2,1)} async-done(((bf16[1152,640]{1,0:T(8,128)(2,1)}), bf16[288,640]{1,0:T(8,128)(2,1)}) %reduce-scatter.8.cloned.1.call-update) | async-done | bytes 368656 | tf_op jit(solution)/shard_map/reduce_scatter | solution.py:1042
  411.8 1.8 slice_convert_fusion.1
  (362 shorter events, 79.2 us)
Async XLA Ops:
  7.2 298.2 %reduce-scatter.4.cloned.1.call-start = ((), (), s32[]{:S(2)}) async-start(), calls=%async_computation.4 | async-start | bytes 1658880 | tf_op jit(solution)/shard_map/reduce_scatter | solution.py:1042
  9.1 11.3 %collective-permute-start.2 = (bf16[1,1152]{1,0:T(2,128)(2,1)S(1)}, bf16[1,1152]{1,0:T(2,128)(2,1)S(1)}, u32[]{:S(2)}, u32[]{:S(2)}) collective-permute-start(bf16[1,1152]{1,0:T(2,128)(2,1)S(1)} %get-tuple-element.231.cond_ref), channel_id=1, source_target_pairs={{0,3},{1,0},{2,1},{3,2},{4,7},{5,4},{6,5},{7,6},{8,11},{9,8},{10,9... | collective-permute-start | bytes 6920 | tf_op jit(solution)/shard_map/ppermute | solution.py:63
  9.4 11.1 %collective-permute-start.1 = (bf16[1,1152]{1,0:T(2,128)(2,1)S(1)}, bf16[1,1152]{1,0:T(2,128)(2,1)S(1)}, u32[]{:S(2)}, u32[]{:S(2)}) collective-permute-start(bf16[1,1152]{1,0:T(2,128)(2,1)S(1)} %get-tuple-element.231.cond_ref), channel_id=1, source_target_pairs={{0,2},{1,3},{2,0},{3,1},{4,6},{5,7},{6,4},{7,5},{8,10},{9,11},{10,... | collective-permute-start | bytes 6920 | tf_op jit(solution)/shard_map/ppermute | solution.py:63
  9.4 11.1 %collective-permute-start = (bf16[1,1152]{1,0:T(2,128)(2,1)S(1)}, bf16[1,1152]{1,0:T(2,128)(2,1)S(1)}, u32[]{:S(2)}, u32[]{:S(2)}) collective-permute-start(bf16[1,1152]{1,0:T(2,128)(2,1)S(1)} %get-tuple-element.231.cond_ref), channel_id=1, source_target_pairs={{0,1},{1,2},{2,3},{3,0},{4,5},{5,6},{6,7},{7,4},{8,9},{9,10},{10,1... | collective-permute-start | bytes 6920 | tf_op jit(solution)/shard_map/ppermute | solution.py:63
  12.5 11.7 %collective-permute-start.3 = (bf16[9,8,3456]{2,1,0:T(8,128)(2,1)S(1)}, bf16[9,8,3456]{2,1,0:T(8,128)(2,1)S(1)}, u32[]{:S(2)}, u32[]{:S(2)}) collective-permute-start(bf16[9,8,3456]{2,1,0:T(8,128)(2,1)S(1)} %dynamic-slice_bitcast_fusion.2), channel_id=1, source_target_pairs={{0,1},{1,2},{2,3},{3,0},{4,5},{5,6},{6,7},{7,4},{8,9},{9,10},{10,1... | collective-permute-start | bytes 1493000 | tf_op jit(solution)/shard_map/ppermute | solution.py:63
  24.8 31.5 %collective-permute-start.9 = (bf16[256,2304]{1,0:T(8,128)(2,1)}, bf16[256,2304]{1,0:T(8,128)(2,1)S(1)}, u32[]{:S(2)}, u32[]{:S(2)}) collective-permute-start(bf16[256,2304]{1,0:T(8,128)(2,1)} %pad_maximum_fusion.1.refs_0_), channel_id=1, source_target_pairs={{0,16},{4,20},{8,24},{12,28},{16,0},{20,4},{24,8},{28,12},{1,17},{... | collective-permute-start | bytes 3538952 | tf_op jit(solution)/shard_map/ppermute | solution.py:57
  26.1 30.3 %collective-permute-start.8 = (bf16[256,2304]{1,0:T(8,128)(2,1)}, bf16[256,2304]{1,0:T(8,128)(2,1)S(1)}, u32[]{:S(2)}, u32[]{:S(2)}) collective-permute-start(bf16[256,2304]{1,0:T(8,128)(2,1)} %pad_maximum_fusion.1.refs_0_), channel_id=1, source_target_pairs={{0,8},{4,12},{8,0},{12,4},{16,24},{20,28},{24,16},{28,20},{1,9},{5... | collective-permute-start | bytes 3538952 | tf_op jit(solution)/shard_map/ppermute | solution.py:57
  27.3 16.2 %collective-permute-start.7 = (bf16[9,8,3456]{2,1,0:T(8,128)(2,1)S(1)}, bf16[9,8,3456]{2,1,0:T(8,128)(2,1)S(1)}, u32[]{:S(2)}, u32[]{:S(2)}) collective-permute-start(bf16[9,8,3456]{2,1,0:T(8,128)(2,1)S(1)} %collective-permute-done.3), channel_id=1, source_target_pairs={{0,1},{1,2},{2,3},{3,0},{4,5},{5,6},{6,7},{7,4},{8,9},{9,10},{10,1... | collective-permute-start | bytes 1493000 | tf_op jit(solution)/shard_map/ppermute | solution.py:63
  32.8 9.3 %collective-permute-start.5 = (f32[8,1152]{1,0:T(8,128)}, f32[8,1152]{1,0:T(8,128)S(1)}, u32[]{:S(2)}, u32[]{:S(2)}) collective-permute-start(f32[8,1152]{1,0:T(8,128)} %get-tuple-element.239), channel_id=1, source_target_pairs={{0,2},{1,3},{2,0},{3,1},{4,6},{5,7},{6,4},{7,5},{8,10},{9,11},{10,... | collective-permute-start | bytes 110600 | tf_op jit(solution)/shard_map/ppermute | solution.py:63
  43.5 12.9 %collective-permute-start.10 = (bf16[9,8,3456]{2,1,0:T(8,128)(2,1)S(1)}, bf16[9,8,3456]{2,1,0:T(8,128)(2,1)}, u32[]{:S(2)}, u32[]{:S(2)}) collective-permute-start(bf16[9,8,3456]{2,1,0:T(8,128)(2,1)S(1)} %collective-permute-done.7), channel_id=1, source_target_pairs={{0,1},{1,2},{2,3},{3,0},{4,5},{5,6},{6,7},{7,4},{8,9},{9,10},{10,1... | collective-permute-start | bytes 1493000 | tf_op jit(solution)/shard_map/ppermute | solution.py:63
  58.8 22.5 %collective-permute-start.12 = (bf16[3,9,8,3456]{3,2,1,0:T(8,128)(2,1)S(1)}, bf16[3,9,8,3456]{3,2,1,0:T(8,128)(2,1)}, u32[]{:S(2)}, u32[]{:S(2)}) collective-permute-start(bf16[3,9,8,3456]{3,2,1,0:T(8,128)(2,1)S(1)} %pad_maximum_fusion.refs_0_), channel_id=1, source_target_pairs={{0,4},{4,0},{8,12},{12,8},{16,20},{20,16},{24,28},{28,24},{1,5},{5... | collective-permute-start | bytes 4478984 | tf_op jit(solution)/shard_map/ppermute | solution.py:57
  61.7 19.6 %collective-permute-start.11 = (bf16[3,9,8,3456]{3,2,1,0:T(8,128)(2,1)S(1)}, bf16[3,9,8,3456]{3,2,1,0:T(8,128)(2,1)}, u32[]{:S(2)}, u32[]{:S(2)}) collective-permute-start(bf16[3,9,8,3456]{3,2,1,0:T(8,128)(2,1)S(1)} %pad_maximum_fusion.refs_0_), channel_id=1, source_target_pairs={{0,8},{4,20},{8,0},{12,28},{16,24},{20,4},{24,16},{28,12},{1,9},{5... | collective-permute-start | bytes 4478984 | tf_op jit(solution)/shard_map/ppermute | solution.py:60
  62.8 18.6 %collective-permute-start.13 = (bf16[9,8,2944]{2,1,0:T(8,128)(2,1)}, bf16[9,8,2944]{2,1,0:T(8,128)(2,1)}, u32[]{:S(2)}, u32[]{:S(2)}) collective-permute-start(bf16[9,8,2944]{2,1,0:T(8,128)(2,1)} %fusion), channel_id=1, source_target_pairs={{0,1},{1,2},{2,3},{3,0},{4,5},{5,6},{6,7},{7,4},{8,9},{9,10},{10,1... | collective-permute-start | bytes 1271816 | tf_op jit(solution)/shard_map/ppermute | solution.py:63
  67.5 13.8 %collective-permute-start.15 = (f32[8,1152]{1,0:T(8,128)S(1)}, f32[8,1152]{1,0:T(8,128)S(1)}, u32[]{:S(2)}, u32[]{:S(2)}) collective-permute-start(f32[8,1152]{1,0:T(8,128)S(1)} %copy-done.67), channel_id=1, source_target_pairs={{0,16},{4,20},{8,24},{12,28},{16,0},{20,4},{24,8},{28,12},{1,17},{... | collective-permute-start | bytes 110600 | tf_op jit(solution)/shard_map/ppermute | solution.py:57
  68.8 12.5 %collective-permute-start.14 = (f32[8,1152]{1,0:T(8,128)S(1)}, f32[8,1152]{1,0:T(8,128)S(1)}, u32[]{:S(2)}, u32[]{:S(2)}) collective-permute-start(f32[8,1152]{1,0:T(8,128)S(1)} %copy-done.67), channel_id=1, source_target_pairs={{0,8},{4,12},{8,0},{12,4},{16,24},{20,28},{24,16},{28,20},{1,9},{5... | collective-permute-start | bytes 110600 | tf_op jit(solution)/shard_map/ppermute | solution.py:57
  81.4 10.4 %collective-permute-start.16 = (bf16[3,9,8,3456]{3,2,1,0:T(8,128)(2,1)}, bf16[3,9,8,3456]{3,2,1,0:T(8,128)(2,1)}, u32[]{:S(2)}, u32[]{:S(2)}) collective-permute-start(bf16[3,9,8,3456]{3,2,1,0:T(8,128)(2,1)} %collective-permute-done.11.refs_1_), channel_id=1, source_target_pairs={{0,4},{4,0},{8,12},{12,8},{16,20},{20,16},{24,28},{28,24},{1,5},{5... | collective-permute-start | bytes 4478984 | tf_op jit(solution)/shard_map/ppermute | solution.py:57
  84.2 17.0 %collective-permute-start.19 = (bf16[128,2304]{1,0:T(8,128)(2,1)}, bf16[128,2304]{1,0:T(8,128)(2,1)S(1)}, u32[]{:S(2)}, u32[]{:S(2)}) collective-permute-start(bf16[128,2304]{1,0:T(8,128)(2,1)} %slice.132), channel_id=1, source_target_pairs={{0,8},{4,12},{8,0},{12,4},{16,24},{20,28},{24,16},{28,20},{1,9},{5... | collective-permute-start | bytes 1769480 | tf_op jit(solution)/shard_map/ppermute | solution.py:57
  84.5 16.8 %collective-permute-start.18 = (bf16[128,2304]{1,0:T(8,128)(2,1)S(1)}, bf16[128,2304]{1,0:T(8,128)(2,1)S(1)}, u32[]{:S(2)}, u32[]{:S(2)}) collective-permute-start(bf16[128,2304]{1,0:T(8,128)(2,1)S(1)} %slice.131), channel_id=1, source_target_pairs={{0,16},{4,20},{8,24},{12,28},{16,0},{20,4},{24,8},{28,12},{1,17},{... | collective-permute-start | bytes 1769480 | tf_op jit(solution)/shard_map/ppermute | solution.py:57
  84.7 16.6 %collective-permute-start.17 = (bf16[9,8,2944]{2,1,0:T(8,128)(2,1)}, bf16[9,8,2944]{2,1,0:T(8,128)(2,1)}, u32[]{:S(2)}, u32[]{:S(2)}) collective-permute-start(bf16[9,8,2944]{2,1,0:T(8,128)(2,1)} %collective-permute-done.13), channel_id=1, source_target_pairs={{0,1},{1,2},{2,3},{3,0},{4,5},{5,6},{6,7},{7,4},{8,9},{9,10},{10,1... | collective-permute-start | bytes 1271816 | tf_op jit(solution)/shard_map/ppermute | solution.py:63
  89.6 11.6 %collective-permute-start.20 = (f32[8,1152]{1,0:T(8,128)S(1)}, f32[8,1152]{1,0:T(8,128)S(1)}, u32[]{:S(2)}, u32[]{:S(2)}) collective-permute-start(f32[8,1152]{1,0:T(8,128)S(1)} %copy-done.67), channel_id=1, source_target_pairs={{0,24},{4,28},{8,16},{12,20},{16,8},{20,12},{24,0},{28,4},{1,25},{... | collective-permute-start | bytes 110600 | tf_op jit(solution)/shard_map/ppermute | solution.py:57
  104.2 19.3 %collective-permute-start.22 = (bf16[18,8,2944]{2,1,0:T(8,128)(2,1)S(1)}, bf16[18,8,2944]{2,1,0:T(8,128)(2,1)S(1)}, u32[]{:S(2)}, u32[]{:S(2)}) collective-permute-start(bf16[18,8,2944]{2,1,0:T(8,128)(2,1)S(1)} %constant_dynamic-update-slice_fusion.refs_2_), channel_id=1, source_target_pairs={{0,16},{4,20},{8,24},{12,28},{16,0},{20,4},{24,8},{28,12},{1,17},{... | collective-permute-start | bytes 2543624 | tf_op jit(solution)/shard_map/ppermute | solution.py:57
  104.5 19.0 %collective-permute-start.21 = (bf16[18,8,2944]{2,1,0:T(8,128)(2,1)S(1)}, bf16[18,8,2944]{2,1,0:T(8,128)(2,1)S(1)}, u32[]{:S(2)}, u32[]{:S(2)}) collective-permute-start(bf16[18,8,2944]{2,1,0:T(8,128)(2,1)S(1)} %constant_dynamic-update-slice_fusion.refs_2_), channel_id=1, source_target_pairs={{0,8},{4,12},{8,0},{12,4},{16,24},{20,28},{24,16},{28,20},{1,9},{5... | collective-permute-start | bytes 2543624 | tf_op jit(solution)/shard_map/ppermute | solution.py:57
  104.8 11.9 %collective-permute-start.23 = (bf16[9,8,2944]{2,1,0:T(8,128)(2,1)}, bf16[9,8,2944]{2,1,0:T(8,128)(2,1)S(1)}, u32[]{:S(2)}, u32[]{:S(2)}) collective-permute-start(bf16[9,8,2944]{2,1,0:T(8,128)(2,1)} %collective-permute-done.17), channel_id=1, source_target_pairs={{0,1},{1,2},{2,3},{3,0},{4,5},{5,6},{6,7},{7,4},{8,9},{9,10},{10,1... | collective-permute-start | bytes 1271816 | tf_op jit(solution)/shard_map/ppermute | solution.py:63
  123.5 20.1 %collective-permute-start.26 = (bf16[18,8,2944]{2,1,0:T(8,128)(2,1)S(1)}, bf16[18,8,2944]{2,1,0:T(8,128)(2,1)}, u32[]{:S(2)}, u32[]{:S(2)}) collective-permute-start(bf16[18,8,2944]{2,1,0:T(8,128)(2,1)S(1)} %constant_dynamic-update-slice_fusion.refs_2_), channel_id=1, source_target_pairs={{0,4},{4,0},{8,12},{12,8},{16,20},{20,16},{24,28},{28,24},{1,5},{5... | collective-permute-start | bytes 2543624 | tf_op jit(solution)/shard_map/ppermute | solution.py:57
  125.8 17.8 %collective-permute-start.27 = (bf16[36,8,1152]{2,1,0:T(8,128)(2,1)}, bf16[36,8,1152]{2,1,0:T(8,128)(2,1)}, u32[]{:S(2)}, u32[]{:S(2)}) collective-permute-start(bf16[36,8,1152]{2,1,0:T(8,128)(2,1)} %dynamic-slice_bitcast_fusion), channel_id=1, source_target_pairs={{0,1},{1,2},{2,3},{3,0},{4,5},{5,6},{6,7},{7,4},{8,9},{9,10},{10,1... | collective-permute-start | bytes 1990664 | tf_op jit(solution)/shard_map/ppermute | solution.py:63
  129.0 14.6 %collective-permute-start.25 = (bf16[9,8,2944]{2,1,0:T(8,128)(2,1)S(1)}, bf16[9,8,2944]{2,1,0:T(8,128)(2,1)S(1)}, u32[]{:S(2)}, u32[]{:S(2)}) collective-permute-start(bf16[9,8,2944]{2,1,0:T(8,128)(2,1)S(1)} %collective-permute-done.23.refs_3_), channel_id=1, source_target_pairs={{0,16},{4,20},{8,24},{12,28},{16,0},{20,4},{24,8},{28,12},{1,17},{... | collective-permute-start | bytes 1271816 | tf_op jit(solution)/shard_map/ppermute | solution.py:57
  129.2 14.4 %collective-permute-start.24 = (bf16[9,8,2944]{2,1,0:T(8,128)(2,1)S(1)}, bf16[9,8,2944]{2,1,0:T(8,128)(2,1)S(1)}, u32[]{:S(2)}, u32[]{:S(2)}) collective-permute-start(bf16[9,8,2944]{2,1,0:T(8,128)(2,1)S(1)} %collective-permute-done.23.refs_3_), channel_id=1, source_target_pairs={{0,8},{4,12},{8,0},{12,4},{16,24},{20,28},{24,16},{28,20},{1,9},{5... | collective-permute-start | bytes 1271816 | tf_op jit(solution)/shard_map/ppermute | solution.py:57
  143.6 21.5 %collective-permute-start.32 = (bf16[36,8,1152]{2,1,0:T(8,128)(2,1)}, bf16[36,8,1152]{2,1,0:T(8,128)(2,1)}, u32[]{:S(2)}, u32[]{:S(2)}) collective-permute-start(bf16[36,8,1152]{2,1,0:T(8,128)(2,1)} %collective-permute-done.27.refs_0_), channel_id=1, source_target_pairs={{0,1},{1,2},{2,3},{3,0},{4,5},{5,6},{6,7},{7,4},{8,9},{9,10},{10,1... | collective-permute-start | bytes 1990664 | tf_op jit(solution)/shard_map/ppermute | solution.py:63
  147.8 16.8 %collective-permute-start.29 = (bf16[14,8,2944]{2,1,0:T(8,128)(2,1)S(1)}, bf16[14,8,2944]{2,1,0:T(8,128)(2,1)}, u32[]{:S(2)}, u32[]{:S(2)}) collective-permute-start(bf16[14,8,2944]{2,1,0:T(8,128)(2,1)S(1)} %pad_maximum_fusion.2), channel_id=1, source_target_pairs={{0,8},{4,12},{8,0},{12,4},{16,24},{20,28},{24,16},{28,20},{1,9},{5... | collective-permute-start | bytes 1978376 | tf_op jit(solution)/shard_map/ppermute | solution.py:57
  148.1 14.1 %collective-permute-start.28 = (bf16[13,8,2944]{2,1,0:T(8,128)(2,1)S(1)}, bf16[13,8,2944]{2,1,0:T(8,128)(2,1)}, u32[]{:S(2)}, u32[]{:S(2)}) collective-permute-start(bf16[13,8,2944]{2,1,0:T(8,128)(2,1)S(1)} %slice.133), channel_id=1, source_target_pairs={{0,16},{4,20},{8,24},{12,28},{16,0},{20,4},{24,8},{28,12},{1,17},{... | collective-permute-start | bytes 1837064 | tf_op jit(solution)/shard_map/ppermute | solution.py:57
  148.8 16.3 %collective-permute-start.30 = (bf16[18,8,2944]{2,1,0:T(8,128)(2,1)S(1)}, bf16[18,8,2944]{2,1,0:T(8,128)(2,1)S(1)}, u32[]{:S(2)}, u32[]{:S(2)}) collective-permute-start(bf16[18,8,2944]{2,1,0:T(8,128)(2,1)S(1)} %collective-permute-done.21.refs_4_), channel_id=1, source_target_pairs={{0,4},{4,0},{8,12},{12,8},{16,20},{20,16},{24,28},{28,24},{1,5},{5... | collective-permute-start | bytes 2543624 | tf_op jit(solution)/shard_map/ppermute | solution.py:57
  150.5 14.7 %collective-permute-start.31 = (bf16[18,8,2944]{2,1,0:T(8,128)(2,1)S(1)}, bf16[18,8,2944]{2,1,0:T(8,128)(2,1)S(1)}, u32[]{:S(2)}, u32[]{:S(2)}) collective-permute-start(bf16[18,8,2944]{2,1,0:T(8,128)(2,1)S(1)} %collective-permute-done.22.refs_6_), channel_id=1, source_target_pairs={{0,4},{4,0},{8,12},{12,8},{16,20},{20,16},{24,28},{28,24},{1,5},{5... | collective-permute-start | bytes 2543624 | tf_op jit(solution)/shard_map/ppermute | solution.py:57
  165.9 25.0 %collective-permute-start.39 = (bf16[36,8,1152]{2,1,0:T(8,128)(2,1)}, bf16[36,8,1152]{2,1,0:T(8,128)(2,1)S(1)}, u32[]{:S(2)}, u32[]{:S(2)}) collective-permute-start(bf16[36,8,1152]{2,1,0:T(8,128)(2,1)} %collective-permute-done.27.refs_0_), channel_id=1, source_target_pairs={{0,8},{4,20},{8,0},{12,28},{16,24},{20,4},{24,16},{28,12},{1,9},{5... | collective-permute-start | bytes 1990664 | tf_op jit(solution)/shard_map/ppermute | solution.py:60
  166.6 24.4 %collective-permute-start.40 = (bf16[36,8,1152]{2,1,0:T(8,128)(2,1)}, bf16[36,8,1152]{2,1,0:T(8,128)(2,1)S(1)}, u32[]{:S(2)}, u32[]{:S(2)}) collective-permute-start(bf16[36,8,1152]{2,1,0:T(8,128)(2,1)} %collective-permute-done.32.refs_1_), channel_id=1, source_target_pairs={{0,8},{4,20},{8,0},{12,28},{16,24},{20,4},{24,16},{28,12},{1,9},{5... | collective-permute-start | bytes 1990664 | tf_op jit(solution)/shard_map/ppermute | solution.py:60
  167.8 23.2 %collective-permute-start.38 = (bf16[36,8,1152]{2,1,0:T(8,128)(2,1)}, bf16[36,8,1152]{2,1,0:T(8,128)(2,1)S(1)}, u32[]{:S(2)}, u32[]{:S(2)}) collective-permute-start(bf16[36,8,1152]{2,1,0:T(8,128)(2,1)} %collective-permute-done.32.refs_1_), channel_id=1, source_target_pairs={{0,1},{1,2},{2,3},{3,0},{4,5},{5,6},{6,7},{7,4},{8,9},{9,10},{10,1... | collective-permute-start | bytes 1990664 | tf_op jit(solution)/shard_map/ppermute | solution.py:63
  192.0 9.8 %collective-permute-start.41 = (bf16[36,8,1152]{2,1,0:T(8,128)(2,1)S(1)}, bf16[36,8,1152]{2,1,0:T(8,128)(2,1)S(1)}, u32[]{:S(2)}, u32[]{:S(2)}) collective-permute-start(bf16[36,8,1152]{2,1,0:T(8,128)(2,1)S(1)} %collective-permute-done.38.refs_2_), channel_id=1, source_target_pairs={{0,8},{4,20},{8,0},{12,28},{16,24},{20,4},{24,16},{28,12},{1,9},{5... | collective-permute-start | bytes 1990664 | tf_op jit(solution)/shard_map/ppermute | solution.py:60
  192.3 10.6 %collective-permute-start.44 = (bf16[36,8,1152]{2,1,0:T(8,128)(2,1)S(1)}, bf16[36,8,1152]{2,1,0:T(8,128)(2,1)S(1)}, u32[]{:S(2)}, u32[]{:S(2)}) collective-permute-start(bf16[36,8,1152]{2,1,0:T(8,128)(2,1)S(1)} %collective-permute-done.38.refs_2_), channel_id=1, source_target_pairs={{0,4},{4,0},{8,12},{12,8},{16,20},{20,16},{24,28},{28,24},{1,5},{5... | collective-permute-start | bytes 1990664 | tf_op jit(solution)/shard_map/ppermute | solution.py:57
  192.6 10.1 %collective-permute-start.43 = (bf16[36,8,1152]{2,1,0:T(8,128)(2,1)}, bf16[36,8,1152]{2,1,0:T(8,128)(2,1)S(1)}, u32[]{:S(2)}, u32[]{:S(2)}) collective-permute-start(bf16[36,8,1152]{2,1,0:T(8,128)(2,1)} %collective-permute-done.32.refs_1_), channel_id=1, source_target_pairs={{0,4},{4,0},{8,12},{12,8},{16,20},{20,16},{24,28},{28,24},{1,5},{5... | collective-permute-start | bytes 1990664 | tf_op jit(solution)/shard_map/ppermute | solution.py:57
  192.8 10.0 %collective-permute-start.45 = (bf16[36,8,1152]{2,1,0:T(8,128)(2,1)S(1)}, bf16[36,8,1152]{2,1,0:T(8,128)(2,1)S(1)}, u32[]{:S(2)}, u32[]{:S(2)}) collective-permute-start(bf16[36,8,1152]{2,1,0:T(8,128)(2,1)S(1)} %collective-permute-done.39.refs_3_), channel_id=1, source_target_pairs={{0,4},{4,0},{8,12},{12,8},{16,20},{20,16},{24,28},{28,24},{1,5},{5... | collective-permute-start | bytes 1990664 | tf_op jit(solution)/shard_map/ppermute | solution.py:57
  194.0 8.8 %collective-permute-start.46 = (bf16[36,8,1152]{2,1,0:T(8,128)(2,1)S(1)}, bf16[36,8,1152]{2,1,0:T(8,128)(2,1)S(1)}, u32[]{:S(2)}, u32[]{:S(2)}) collective-permute-start(bf16[36,8,1152]{2,1,0:T(8,128)(2,1)S(1)} %collective-permute-done.40.refs_4_), channel_id=1, source_target_pairs={{0,4},{4,0},{8,12},{12,8},{16,20},{20,16},{24,28},{28,24},{1,5},{5... | collective-permute-start | bytes 1990664 | tf_op jit(solution)/shard_map/ppermute | solution.py:57
  204.5 30.6 %collective-permute-start.48 = (bf16[1152,256]{1,0:T(8,128)(2,1)}, bf16[1152,256]{1,0:T(8,128)(2,1)}, u32[]{:S(2)}, u32[]{:S(2)}) collective-permute-start(bf16[1152,256]{1,0:T(8,128)(2,1)} %get-tuple-element.351), channel_id=1, source_target_pairs={{0,8},{4,12},{8,0},{12,4},{16,24},{20,28},{24,16},{28,20},{1,9},{5... | collective-permute-start | bytes 1769480 | tf_op jit(solution)/shard_map/ppermute | solution.py:57
  204.8 30.3 %collective-permute-start.49 = (bf16[1152,256]{1,0:T(8,128)(2,1)}, bf16[1152,256]{1,0:T(8,128)(2,1)}, u32[]{:S(2)}, u32[]{:S(2)}) collective-permute-start(bf16[1152,256]{1,0:T(8,128)(2,1)} %get-tuple-element.352), channel_id=1, source_target_pairs={{0,16},{4,20},{8,24},{12,28},{16,0},{20,4},{24,8},{28,12},{1,17},{... | collective-permute-start | bytes 1769480 | tf_op jit(solution)/shard_map/ppermute | solution.py:57
  205.4 29.7 %collective-permute-start.50 = (bf16[1152,256]{1,0:T(8,128)(2,1)}, bf16[1152,256]{1,0:T(8,128)(2,1)}, u32[]{:S(2)}, u32[]{:S(2)}) collective-permute-start(bf16[1152,256]{1,0:T(8,128)(2,1)} %get-tuple-element.353), channel_id=1, source_target_pairs={{0,24},{4,28},{8,16},{12,20},{16,8},{20,12},{24,0},{28,4},{1,25},{... | collective-permute-start | bytes 1769480 | tf_op jit(solution)/shard_map/ppermute | solution.py:57
  235.1 25.0 %collective-permute-start.51 = (bf16[1152,256]{1,0:T(8,128)(2,1)S(1)}, bf16[1152,256]{1,0:T(8,128)(2,1)S(1)}, u32[]{:S(2)}, u32[]{:S(2)}) collective-permute-start(bf16[1152,256]{1,0:T(8,128)(2,1)S(1)} %copy-done.65), channel_id=1, source_target_pairs={{0,8},{4,12},{8,0},{12,4},{16,24},{20,28},{24,16},{28,20},{1,9},{5... | collective-permute-start | bytes 1769480 | tf_op jit(solution)/shard_map/ppermute | solution.py:57
  235.4 24.6 %collective-permute-start.52 = (bf16[1152,256]{1,0:T(8,128)(2,1)S(1)}, bf16[1152,256]{1,0:T(8,128)(2,1)S(1)}, u32[]{:S(2)}, u32[]{:S(2)}) collective-permute-start(bf16[1152,256]{1,0:T(8,128)(2,1)S(1)} %copy-done.64), channel_id=1, source_target_pairs={{0,16},{4,20},{8,24},{12,28},{16,0},{20,4},{24,8},{28,12},{1,17},{... | collective-permute-start | bytes 1769480 | tf_op jit(solution)/shard_map/ppermute | solution.py:57
  236.1 25.3 %collective-permute-start.53 = (bf16[1152,256]{1,0:T(8,128)(2,1)S(1)}, bf16[1152,256]{1,0:T(8,128)(2,1)S(1)}, u32[]{:S(2)}, u32[]{:S(2)}) collective-permute-start(bf16[1152,256]{1,0:T(8,128)(2,1)S(1)} %copy-done.63), channel_id=1, source_target_pairs={{0,24},{4,28},{8,16},{12,20},{16,8},{20,12},{24,0},{28,4},{1,25},{... | collective-permute-start | bytes 1769480 | tf_op jit(solution)/shard_map/ppermute | solution.py:57
  270.6 24.8 %collective-permute-start.59 = (f32[4,144,1152]{2,1,0:T(8,128)}, f32[4,144,1152]{2,1,0:T(8,128)}, u32[]{:S(2)}, u32[]{:S(2)}) collective-permute-start(f32[4,144,1152]{2,1,0:T(8,128)} %get-tuple-element.391), channel_id=1, source_target_pairs={{0,4},{4,0},{8,12},{12,8},{16,20},{20,16},{24,28},{28,24},{1,5},{5... | collective-permute-start | bytes 7962632 | tf_op jit(solution)/shard_map/ppermute | solution.py:57
  276.0 98.1 %reduce-scatter.6.cloned.1.call-start = ((), (), s32[]{:S(2)}) async-start(), calls=%async_computation.5 | async-start | bytes 1843200 | tf_op jit(solution)/shard_map/reduce_scatter | solution.py:1042
  276.3 17.5 %collective-permute-start.56 = (bf16[256,1152]{1,0:T(8,128)(2,1)S(1)}, bf16[256,1152]{1,0:T(8,128)(2,1)S(1)}, u32[]{:S(2)}, u32[]{:S(2)}) collective-permute-start(bf16[256,1152]{1,0:T(8,128)(2,1)S(1)} %copy-done.25), channel_id=1, source_target_pairs={{0,16},{4,20},{8,24},{12,28},{16,0},{20,4},{24,8},{28,12},{1,17},{... | collective-permute-start | bytes 1769480 | tf_op jit(solution)/shard_map/ppermute | solution.py:57
  277.1 16.7 %collective-permute-start.55 = (bf16[256,1152]{1,0:T(8,128)(2,1)S(1)}, bf16[256,1152]{1,0:T(8,128)(2,1)S(1)}, u32[]{:S(2)}, u32[]{:S(2)}) collective-permute-start(bf16[256,1152]{1,0:T(8,128)(2,1)S(1)} %copy-done.25), channel_id=1, source_target_pairs={{0,8},{4,12},{8,0},{12,4},{16,24},{20,28},{24,16},{28,20},{1,9},{5... | collective-permute-start | bytes 1769480 | tf_op jit(solution)/shard_map/ppermute | solution.py:57
  313.3 17.4 %collective-permute-start.63 = (f32[576,1152]{1,0:T(8,128)}, f32[576,1152]{1,0:T(8,128)S(1)}, u32[]{:S(2)}, u32[]{:S(2)}) collective-permute-start(f32[576,1152]{1,0:T(8,128)} %get-tuple-element.416), channel_id=1, source_target_pairs={{0,4},{4,0},{8,12},{12,8},{16,20},{20,16},{24,28},{28,24},{1,5},{5... | collective-permute-start | bytes 7962632 | tf_op jit(solution)/shard_map/ppermute | solution.py:57
  314.1 22.3 %collective-permute-start.60 = (bf16[864,256]{1,0:T(8,128)(2,1)}, bf16[864,256]{1,0:T(8,128)(2,1)S(1)}, u32[]{:S(2)}, u32[]{:S(2)}) collective-permute-start(bf16[864,256]{1,0:T(8,128)(2,1)} %get-tuple-element.402), channel_id=1, source_target_pairs={{0,8},{4,12},{8,0},{12,4},{16,24},{20,28},{24,16},{28,20},{1,9},{5... | collective-permute-start | bytes 1327112 | tf_op jit(solution)/shard_map/ppermute | solution.py:57
  315.2 21.2 %collective-permute-start.61 = (bf16[864,256]{1,0:T(8,128)(2,1)}, bf16[864,256]{1,0:T(8,128)(2,1)S(1)}, u32[]{:S(2)}, u32[]{:S(2)}) collective-permute-start(bf16[864,256]{1,0:T(8,128)(2,1)} %get-tuple-element.403), channel_id=1, source_target_pairs={{0,16},{4,20},{8,24},{12,28},{16,0},{20,4},{24,8},{28,12},{1,17},{... | collective-permute-start | bytes 1327112 | tf_op jit(solution)/shard_map/ppermute | solution.py:57
  316.4 20.0 %collective-permute-start.62 = (bf16[864,256]{1,0:T(8,128)(2,1)}, bf16[864,256]{1,0:T(8,128)(2,1)S(1)}, u32[]{:S(2)}, u32[]{:S(2)}) collective-permute-start(bf16[864,256]{1,0:T(8,128)(2,1)} %get-tuple-element.404), channel_id=1, source_target_pairs={{0,24},{4,28},{8,16},{12,20},{16,8},{20,12},{24,0},{28,4},{1,25},{... | collective-permute-start | bytes 1327112 | tf_op jit(solution)/shard_map/ppermute | solution.py:57
  344.4 18.8 %collective-permute-start.64 = (f32[432,1152]{1,0:T(8,128)}, f32[432,1152]{1,0:T(8,128)}, u32[]{:S(2)}, u32[]{:S(2)}) collective-permute-start(f32[432,1152]{1,0:T(8,128)} %get-tuple-element.428), channel_id=1, source_target_pairs={{0,4},{4,0},{8,12},{12,8},{16,20},{20,16},{24,28},{28,24},{1,5},{5... | collective-permute-start | bytes 5971976 | tf_op jit(solution)/shard_map/ppermute | solution.py:57
  345.4 11.5 %collective-permute-start.65 = (bf16[144,1152]{1,0:T(8,128)(2,1)}, bf16[144,1152]{1,0:T(8,128)(2,1)S(1)}, u32[]{:S(2)}, u32[]{:S(2)}) collective-permute-start(bf16[144,1152]{1,0:T(8,128)(2,1)} %get-tuple-element.430), channel_id=1, source_target_pairs={{0,8},{4,12},{8,0},{12,4},{16,24},{20,28},{24,16},{28,20},{1,9},{5... | collective-permute-start | bytes 995336 | tf_op jit(solution)/shard_map/ppermute | solution.py:57
  346.5 12.0 %collective-permute-start.66 = (bf16[144,1152]{1,0:T(8,128)(2,1)}, bf16[144,1152]{1,0:T(8,128)(2,1)S(1)}, u32[]{:S(2)}, u32[]{:S(2)}) collective-permute-start(bf16[144,1152]{1,0:T(8,128)(2,1)} %get-tuple-element.431), channel_id=1, source_target_pairs={{0,16},{4,20},{8,24},{12,28},{16,0},{20,4},{24,8},{28,12},{1,17},{... | collective-permute-start | bytes 995336 | tf_op jit(solution)/shard_map/ppermute | solution.py:57
  347.7 15.5 %collective-permute-start.67 = (bf16[144,1152]{1,0:T(8,128)(2,1)S(1)}, bf16[144,1152]{1,0:T(8,128)(2,1)S(1)}, u32[]{:S(2)}, u32[]{:S(2)}) collective-permute-start(bf16[144,1152]{1,0:T(8,128)(2,1)S(1)} %copy-done.66), channel_id=1, source_target_pairs={{0,24},{4,28},{8,16},{12,20},{16,8},{20,12},{24,0},{28,4},{1,25},{... | collective-permute-start | bytes 995336 | tf_op jit(solution)/shard_map/ppermute | solution.py:57
  349.2 19.9 %all-to-all-start = ((bf16[8,144,144]{1,2,0:T(8,128)(2,1)}), bf16[8,144,144]{1,2,0:T(8,128)(2,1)S(1)}, u32[]{:S(2)}, u32[]{:S(2)}) async-start(bf16[8,144,144]{1,2,0:T(8,128)(2,1)} %bitcast.35), calls=%async_computation.2 | async-start | bytes 1179648 | tf_op jit(solution)/shard_map/all_to_all | solution.py:1402
  353.6 56.3 %reduce-scatter.8.cloned.1.call-start = ((), (), s32[]{:S(2)}) async-start(), calls=%async_computation.6 | async-start | bytes 1843200 | tf_op jit(solution)/shard_map/reduce_scatter | solution.py:1042
  355.7 12.4 %collective-permute-start.70 = (f32[16,1152]{1,0:T(8,128)}, f32[16,1152]{1,0:T(8,128)S(1)}, u32[]{:S(2)}, u32[]{:S(2)}) collective-permute-start(f32[16,1152]{1,0:T(8,128)} %shard_map.257), channel_id=1, source_target_pairs={{0,3},{1,0},{2,1},{3,2},{4,7},{5,4},{6,5},{7,6},{8,11},{9,8},{10,9... | collective-permute-start | bytes 221192 | tf_op jit(solution)/shard_map/ppermute | solution.py:63
  356.9 12.1 %collective-permute-start.69 = (f32[16,1152]{1,0:T(8,128)}, f32[16,1152]{1,0:T(8,128)S(1)}, u32[]{:S(2)}, u32[]{:S(2)}) collective-permute-start(f32[16,1152]{1,0:T(8,128)} %shard_map.257), channel_id=1, source_target_pairs={{0,2},{1,3},{2,0},{3,1},{4,6},{5,7},{6,4},{7,5},{8,10},{9,11},{10,... | collective-permute-start | bytes 221192 | tf_op jit(solution)/shard_map/ppermute | solution.py:63
  358.5 10.6 %collective-permute-start.68 = (f32[16,1152]{1,0:T(8,128)}, f32[16,1152]{1,0:T(8,128)S(1)}, u32[]{:S(2)}, u32[]{:S(2)}) collective-permute-start(f32[16,1152]{1,0:T(8,128)} %shard_map.257), channel_id=1, source_target_pairs={{0,1},{1,2},{2,3},{3,0},{4,5},{5,6},{6,7},{7,4},{8,9},{9,10},{10,1... | collective-permute-start | bytes 221192 | tf_op jit(solution)/shard_map/ppermute | solution.py:63
  375.1 11.6 %collective-permute-start.77 = (f32[8,1152]{1,0:T(8,128)S(1)}, f32[8,1152]{1,0:T(8,128)S(1)}, u32[]{:S(2)}, u32[]{:S(2)}) collective-permute-start(f32[8,1152]{1,0:T(8,128)S(1)} %slice_add_fusion), channel_id=1, source_target_pairs={{0,4},{4,0},{8,12},{12,8},{16,20},{20,16},{24,28},{28,24},{1,5},{5... | collective-permute-start | bytes 110600 | tf_op jit(solution)/shard_map/ppermute | solution.py:57
  (88 other events, 779.8 us)
Sparse Core Ops, SparseCore 0:
  276.1 29.2 reduce-scatter.3
  336.6 37.4 reduce-scatter.5
  376.6 33.3 reduce-scatter.7

commit v7 on v6

--- a/solution.py
+++ b/solution.py
@@ -1001,9 +1001,11 @@
         width = items[0][0].shape[1]
         n = sum(item[0].shape[0] for item in items)
         padded = -(-n // 128) * 128
+        half = width // fs // 2
         arrays = [array for item in items for array in item]
 
         def kernel(*refs):
+            out_ref, turned = refs[-2:]
             for first in range(0, width, 128):
                 totals, used = [], 0
                 for item in items:
@@ -1013,16 +1015,26 @@
                 if padded > n:
                     totals.append(jnp.zeros((padded - n, 128), f32))
                 total = jnp.concatenate(totals, axis=0) if len(totals) > 1 else totals[0]
-                refs[-1][first : first + 128, :] = total.T.astype(bf16)
+                turned[first : first + 128, :] = total.T[:, :n]
+            for block in range(fs):
+                rows = slice(block * half, (block + 1) * half)
+                upper = 2 * block * half
+                out_ref[rows, :n] = turned[upper : upper + half, :].astype(bf16)
+                out_ref[rows, n:] = turned[upper + half : upper + 2 * half, :].astype(bf16)
 
         return pl.pallas_call(
             kernel,
-            out_shape=jax.ShapeDtypeStruct((width, padded), bf16),
+            out_shape=jax.ShapeDtypeStruct((fs * half, 2 * n), bf16),
             in_specs=[vmem] * len(arrays),
             out_specs=vmem,
+            scratch_shapes=[pltpu.VMEM((width, n), f32)],
             cost_estimate=cost(5),
             compiler_params=params(60),
         )(*arrays)
+
+    def unfolded(x, start, stop):
+        n = x.shape[1] // 2
+        return jnp.concatenate([x[:, start:stop], x[:, n + start : n + stop]]).astype(f32)
 
     def row_total(keep, got):
         def kernel(keep_ref, got_ref, out_ref):
@@ -1420,10 +1432,10 @@
             images = jnp.concatenate([images, group_send(images_box, k)])
             total = total + group_send(total_box, k)
         grad_w_down = parts.reshape(BOX * down_rows, width // dp).astype(f32)
-        grad_w_up = over_groups(grad_up[:, : keep_up.shape[0]].astype(f32))
+        grad_w_up = over_groups(unfolded(grad_up, 0, keep_up.shape[0]))
         cut_cols, last_cols = keep_qkv.shape[0], keep_qkv.shape[0] + keep_out.shape[1]
-        grad_w_qkv = over_groups(grad_last[:, :cut_cols].astype(f32))
-        grad_w_out = over_groups(grad_last[:, cut_cols:last_cols].astype(f32))
+        grad_w_qkv = over_groups(unfolded(grad_last, 0, cut_cols))
+        grad_w_out = over_groups(unfolded(grad_last, cut_cols, last_cols))
         conds_all = lax.dynamic_slice_in_dim(images[:, 6], z * rows_z, rows_z, 1)
         d_mod_all = images[:, :6]
         ada_cols = 6 * width // dp

time: 425 us -> 421 us (level)
  waiting for transfers between devices: 94.5 us -> 89.4 us
    reduce_scatter x3, waiting for transfers between devices: 18 us -> 13.1 us  [fsdp_sum(): return lax.psum_scatter(x, 'fsdp', scatter_dimension=0, tiled=True)]
  transfers between devices with their start and end apart: 84 -> 84, of which waited for: 24 -> 24; matrix products, arithmetic and copies ran while one was open for 7% -> 7% of each run, Pallas kernels for 38% -> 39%
where the time goes in v7:
time: 421 us; the launch traced here: 416 us
  Pallas kernels  169 us (40%)
  starting transfers between devices  93.5 us (22%)
  waiting for transfers between devices  89.4 us (21%)
  local copies, waits for them, and re-layouts  35.7 us (8%)
  between operations  16.1 us (4%)
  other arithmetic  8.11 us (2%)
  matrix products  4.61 us (1%)
    ppermute x55, waiting for transfers between devices, box_send(): return lax.ppermute(x, 'dp', [(i, i ^ bits) for i in range(dp)])  51.2 us
    ppermute x55, starting transfers between devices, box_send(): return lax.ppermute(x, 'dp', [(i, i ^ bits) for i in range(dp)])  45.7 us
    ppermute x21, starting transfers between devices, ring_send(): return lax.ppermute(x, 'fsdp', [(i, (i + hops) % fs) for i in range(fs)])  41.1 us
    pallas_call x1, Pallas kernels, middle_forward(): pl.pallas_call(kernel, out_shape=[jax.ShapeDtypeStruct((slots, width), f3...  19.6 us
    ppermute x21, waiting for transfers between devices, ring_send(): return lax.ppermute(x, 'fsdp', [(i, (i + hops) % fs) for i in range(fs)])  17.5 us
    pallas_call x1, Pallas kernels, hidden_back(): pl.pallas_call(kernel, out_shape=[jax.ShapeDtypeStruct((slots, hidden), b...  17.1 us
    pallas_call x1, Pallas kernels, attention_back(): pl.pallas_call(kernel, out_shape=[jax.ShapeDtypeStruct((3 * width, slots)...  15.4 us
    pallas_call x2, Pallas kernels, column_grad(): pl.pallas_call(kernel, out_shape=[jax.ShapeDtypeStruct((n_out, width), f3...  14.8 us
  transfers between devices with their start and end apart: 84, of which 24 were waited for; matrix products, arithmetic and copies ran while one was open for 7% of the time, Pallas kernels for 39%

profile of v7, /device:TPU:25, one launch (start us, length us, event | category | flops | bytes accessed | tf_op | source)
XLA Modules:
  0.0 416.4 jit_solution(15068027761946456221)
XLA Ops:
  9.4 3.1 collective-permute-start
  17.0 2.0 dynamic-slice_bitcast_fusion
  20.5 3.7 collective-permute-done.3
  27.3 2.0 collective-permute-start.7
  29.3 3.5 shard_map.237
  33.4 5.1 %collective-permute-done.4.refs_1_ = f32[8,1152]{1,0:T(8,128)S(1)} collective-permute-done((f32[8,1152]{1,0:T(8,128)}, f32[8,1152]{1,0:T(8,128)S(1)}, u32[]{:S(2)}, u32[]{:S(2)}) %collective-permute-start.4) | collective-permute-done | bytes 36896 | tf_op jit(solution)/shard_map/ppermute | solution.py:63
  38.4 3.7 collective-permute-start.6
  42.1 1.4 collective-permute-done.6.refs_3_
  43.5 3.7 collective-permute-start.10
  49.1 1.5 shard_map.238
  50.6 3.9 shard_map.239
  54.4 2.0 collective-permute-done.10
  58.8 2.9 collective-permute-start.12
  62.8 3.7 collective-permute-start.13
  69.4 11.9 %collective-permute-done.15.refs_5_ = f32[8,1152]{1,0:T(8,128)S(1)} collective-permute-done((f32[8,1152]{1,0:T(8,128)S(1)}, f32[8,1152]{1,0:T(8,128)S(1)}, u32[]{:S(2)}, u32[]{:S(2)}) %collective-permute-start.15) | collective-permute-done | bytes 36896 | tf_op jit(solution)/shard_map/ppermute | solution.py:57
  84.7 3.6 collective-permute-start.17
  89.6 2.2 collective-permute-start.20
  91.8 9.4 %shard_map.240 = (f32[3456,256]{1,0:T(8,128)}, bf16[4,4,9,8,3456]{4,3,2,1,0:T(8,128)(2,1)}) custom-call(s32[12]{0:T(128)} %stack.119.where_ref, bf16[256,1152]{1,0:T(8,128)(2,1)} %get-tuple-element.396.normed_ref.refs_0_, f32[2,1152]{1,0:T(2,128)} %reshape.132.bias_ref, bf16[4,9,8,3456]{3,2,1,0:T(8,128)(2,1)} %bitcast.102, ...), custom_call_target="tpu_custom_call" | custom-call | flops 1100000000 | bytes 3520000 | tf_op jit(solution)/shard_map/pallas_call | solution.py:300
  104.7 3.3 collective-permute-start.23
  108.0 8.7 %shard_map.241.attended_ref.x_ref = bf16[256,1152]{1,0:T(8,128)(2,1)} custom-call(s32[1]{0:T(128)} %bitcast.live_ref, f32[3456,256]{1,0:T(8,128)} %get-tuple-element.275.turned_ref), custom_call_target="tpu_custom_call" | custom-call | flops 1100000000 | bytes 3520000 | tf_op jit(solution)/shard_map/pallas_call | solution.py:357
  116.6 6.8 %collective-permute-done.22.refs_6_ = bf16[18,8,2944]{2,1,0:T(8,128)(2,1)S(1)} collective-permute-done((bf16[18,8,2944]{2,1,0:T(8,128)(2,1)S(1)}, bf16[18,8,2944]{2,1,0:T(8,128)(2,1)S(1)}, u32[]{:S(2)}, u32[]{:S(2)}) %collective-permute-start.22) | collective-permute-done | bytes 847904 | tf_op jit(solution)/shard_map/ppermute | solution.py:57
  123.5 2.3 collective-permute-start.26
  125.7 3.3 collective-permute-start.27
  129.9 8.8 %shard_map.242 = (bf16[256,1152]{1,0:T(8,128)(2,1)}, bf16[256,1152]{1,0:T(8,128)(2,1)}, bf16[128,1152]{1,0:T(8,128)(2,1)}, bf16[128,1152]{1,0:T(8,128)(2,1)}, bf...) custom-call(bf16[256,2304]{1,0:T(8,128)(2,1)} %copy-done.4, ...), custom_call_target="tpu_custom_call" | custom-call | flops 800000000 | bytes 2560000 | tf_op jit(solution)/shard_map/pallas_call | solution.py:192
  138.7 4.9 %collective-permute-done.27.refs_0_ = bf16[36,8,1152]{2,1,0:T(8,128)(2,1)} collective-permute-done((bf16[36,8,1152]{2,1,0:T(8,128)(2,1)}, bf16[36,8,1152]{2,1,0:T(8,128)(2,1)}, u32[]{:S(2)}, u32[]{:S(2)}) %collective-permute-start.27) | collective-permute-done | bytes 663584 | tf_op jit(solution)/shard_map/ppermute | solution.py:63
  143.6 4.1 collective-permute-start.32
  148.8 1.7 collective-permute-start.30
  150.6 11.6 %collective-permute-done.28.refs_8_ = bf16[13,8,2944]{2,1,0:T(8,128)(2,1)} collective-permute-done((bf16[13,8,2944]{2,1,0:T(8,128)(2,1)S(1)}, bf16[13,8,2944]{2,1,0:T(8,128)(2,1)}, u32[]{:S(2)}, u32[]{:S(2)}) %collective-permute-start.28) | collective-permute-done | bytes 612384 | tf_op jit(solution)/shard_map/ppermute | solution.py:57
  162.2 2.3 collective-permute-start.33
  167.8 1.7 collective-permute-start.38
  171.4 19.6 %shard_map.243 = (f32[256,1152]{1,0:T(8,128)}, bf16[256,1152]{1,0:T(8,128)(2,1)}, f32[256,4608]{1,0:T(8,128)}, bf16[256,4608]{1,0:T(8,128)(2,1)}, bf16[1152,256]...) custom-call(s32[9]{0:T(128)} %stack.114.where_ref, ...), custom_call_target="tpu_custom_call" | custom-call | flops 2000000000 | bytes 6400000 | tf_op jit(solution)/shard_map/pallas_call | solution.py:530
  194.4 7.5 %collective-permute-done.41.refs_5_ = bf16[36,8,1152]{2,1,0:T(8,128)(2,1)S(1)} collective-permute-done((bf16[36,8,1152]{2,1,0:T(8,128)(2,1)S(1)}, bf16[36,8,1152]{2,1,0:T(8,128)(2,1)S(1)}, u32[]{:S(2)}, u32[]{:S(2)}) %collective-permute-start.41) | collective-permute-done | bytes 663584 | tf_op jit(solution)/shard_map/ppermute | solution.py:60
  202.9 1.7 collective-permute-done.47.refs_11_
  205.5 1.8 collective-permute-start.50
  207.9 17.1 %shard_map.244 = (bf16[256,4608]{1,0:T(8,128)(2,1)}, bf16[1152,256]{1,0:T(8,128)(2,1)}, bf16[1152,256]{1,0:T(8,128)(2,1)}, bf16[1152,256]{1,0:T(8,128)(2,1)}, bf...) custom-call(s32[12]{0:T(128)} %stack.119.where_ref, ...), custom_call_target="tpu_custom_call" | custom-call | flops 1500000000 | bytes 4800000 | tf_op jit(solution)/shard_map/pallas_call | solution.py:650
  225.1 10.1 %shard_map.245 = (bf16[256,1152]{1,0:T(8,128)(2,1)}, f32[8,1152]{1,0:T(8,128)}) custom-call(s32[1]{0:T(128)} %bitcast.live_ref, bf16[256,4608]{1,0:T(8,128)(2,1)} %get-tuple-element.314.act_ref, bf16[4608,1152]{1,0:T(8,128)(2,1)} %bitcast.90, f32[1,1152]{1,0:T(1,128)} %reshape.137.bias_ref, bf16[256,1152]{1,0:T(8,128)(2,1)} %bitcast.86, ...), custom_call_target="tpu_custom_call" | custom-call | flops 600000000 | bytes 1920000 | tf_op jit(solution)/shard_map/pallas_call | solution.py:892
  236.1 1.8 collective-permute-start.53
  237.9 7.7 %shard_map.247 = (f32[4,144,1152]{2,1,0:T(8,128)}, f32[4,144,1152]{2,1,0:T(8,128)}) custom-call(s32[1]{0:T(128)} %bitcast.5.where_ref, bf16[1152,256]{1,0:T(8,128)(2,1)} %get-tuple-element.365.x0, bf16[1152,256]{1,0:T(8,128)(2,1)} %collective-permute-done.48.x1, bf16[1152,256]{1,0:T(8,128)(2,1)} %collective-permute-done.49.x2, ...), custom_call_target="tpu_custom_call" | custom-call | flops 600000000 | bytes 1920000 | tf_op jit(solution)/shard_map/pallas_call | solution.py:1130
  245.6 14.6 %shard_map.246 = (f32[256,1152]{1,0:T(8,128)}, bf16[1152,256]{1,0:T(8,128)(2,1)}, f32[1152,256]{1,0:T(8,128)}, f32[8,1152]{1,0:T(8,128)}) custom-call(s32[1]{0:T(128)} %bitcast.live_ref, bf16[256,4608]{1,0:T(8,128)(2,1)} %get-tuple-element.356.d_pre_ref, bf16[1152,4608]{1,0:T(8,128)(2,1)} %bitcast.91, bf16[1152,1152]{1,0:T(8,128)(2,1)} %bitcast.104, ...), custom_call_target="tpu_custom_call" | custom-call | flops 1200000000 | bytes 3840000 | tf_op jit(solution)/shard_map/pallas_call | solution.py:756
  262.3 2.6 collective-permute-start.54
  265.5 5.1 %shard_map.250 = (f32[4,144,1152]{2,1,0:T(8,128)}, f32[4,144,1152]{2,1,0:T(8,128)}) custom-call(s32[5]{0:T(128)} %concatenate.52.where_ref, bf16[1152,256]{1,0:T(8,128)(2,1)} %get-tuple-element.389.d_ref, bf16[256,1152]{1,0:T(8,128)(2,1)} %shard_map.241.attended_ref.x_ref), custom_call_target="tpu_custom_call" | custom-call | flops 500000000 | bytes 1600000 | tf_op jit(solution)/shard_map/pallas_call | solution.py:1069
  270.6 1.5 copy-done.6
  272.1 3.9 shard_map.248
  278.4 15.4 %shard_map.249 = (bf16[3456,256]{1,0:T(8,128)(2,1)}, bf16[864,256]{1,0:T(8,128)(2,1)}, bf16[864,256]{1,0:T(8,128)(2,1)}, bf16[864,256]{1,0:T(8,128)(2,1)}, bf16[864,256]{1,0:T(8,128)(2,1)}) custom-call(s32[1]{0:T(128)} %bitcast.live_ref, s32[4]{0:T(128)} %pad_add_fusion.chip_ref, f32[3456,256]{1,0:T(8,128)} %get-tuple-element.275.turned_ref, ...), custom_call_target="tpu_custom_call" | custom-call | flops 1200000000 | bytes 3840000 | tf_op jit(solution)/shard_map/pallas_call | solution.py:423
  295.4 6.1 %collective-permute-done.58.refs_4_ = bf16[128,1152]{1,0:T(8,128)(2,1)S(1)} collective-permute-done((bf16[128,1152]{1,0:T(8,128)(2,1)S(1)}, bf16[128,1152]{1,0:T(8,128)(2,1)S(1)}, u32[]{:S(2)}, u32[]{:S(2)}) %collective-permute-start.58) | collective-permute-done | bytes 294944 | tf_op jit(solution)/shard_map/ppermute | solution.py:57
  302.0 3.5 reduce-scatter.4.cloned.1.call-done
  305.5 7.8 %shard_map.252 = (f32[576,1152]{1,0:T(8,128)}, f32[576,1152]{1,0:T(8,128)}) custom-call(s32[1]{0:T(128)} %bitcast.5.where_ref, bf16[256,1152]{1,0:T(8,128)(2,1)} %get-tuple-element.406.refs_0_, bf16[256,1152]{1,0:T(8,128)(2,1)} %copy-done.12, bf16[256,1152]{1,0:T(8,128)(2,1)} %copy-done.11, bf16[128,1152]{1,0:T(8,128)(2,1)} %copy-done.46, ...), custom_call_target="tpu_custom_call" | custom-call | flops 800000000 | bytes 2560000 | tf_op jit(solution)/shard_map/pallas_call | solution.py:963
  316.7 3.8 shard_map.254
  320.5 10.1 %shard_map.251 = (bf16[256,1152]{1,0:T(8,128)(2,1)}, f32[8,1152]{1,0:T(8,128)}) custom-call(bf16[3456,256]{1,0:T(8,128)(2,1)} %get-tuple-element.392.d_ref, bf16[1152,3456]{1,0:T(8,128)(2,1)} %bitcast.92, bf16[256,1152]{1,0:T(8,128)(2,1)} %bitcast.88, f32[256,1152]{1,0:T(8,128)} %get-tuple-element.394.d_middle_ref, f32[8,1152]{1,0:T(8,128)} %get-tuple-element.307.mods_ref), custom_call_target="tpu_custom_call" | custom-call | flops 900000000 | bytes 2880000 | tf_op jit(solution)/shard_map/pallas_call | solution.py:825
  330.6 1.5 copy-done.5
  332.1 4.8 %shard_map.253 = bf16[576,1152]{1,0:T(8,128)(2,1)} custom-call(f32[576,1152]{1,0:T(8,128)} %get-tuple-element.415.refs_0_, f32[576,1152]{1,0:T(8,128)} %copy-done.5), custom_call_target="tpu_custom_call" | custom-call | flops 500000000 | bytes 1600000 | tf_op jit(solution)/shard_map/pallas_call | solution.py:1025
  338.0 6.9 %shard_map.255 = (f32[432,1152]{1,0:T(8,128)}, f32[432,1152]{1,0:T(8,128)}) custom-call(s32[1]{0:T(128)} %bitcast.5.where_ref, bf16[256,1152]{1,0:T(8,128)(2,1)} %get-tuple-element.396.normed_ref.refs_0_, bf16[256,1152]{1,0:T(8,128)(2,1)} %get-tuple-element.397.refs_1_, bf16[256,1152]{1,0:T(8,128)(2,1)} %get-tuple-element.398.refs_2_, ...), custom_call_target="tpu_custom_call" | custom-call | flops 800000000 | bytes 2560000 | tf_op jit(solution)/shard_map/pallas_call | solution.py:963
  349.7 4.5 %all-to-all-start = ((bf16[8,144,144]{1,2,0:T(8,128)(2,1)}), bf16[8,144,144]{1,2,0:T(8,128)(2,1)S(1)}, u32[]{:S(2)}, u32[]{:S(2)}) async-start(bf16[8,144,144]{1,2,0:T(8,128)(2,1)} %bitcast.35), calls=%async_computation.2 | async-start | bytes 1179648 | tf_op jit(solution)/shard_map/all_to_all | solution.py:1414
  354.8 1.5 shard_map.257
  357.5 1.5 collective-permute-start.69
  359.6 4.1 collective-permute-done.67.refs_5_
  364.4 4.8 %shard_map.256 = bf16[576,1152]{1,0:T(8,128)(2,1)} custom-call(f32[432,1152]{1,0:T(8,128)} %get-tuple-element.427.refs_0_, f32[432,1152]{1,0:T(8,128)} %collective-permute-done.64.refs_1_, f32[144,1152]{1,0:T(8,128)} %get-tuple-element.429.refs_2_, bf16[144,1152]{1,0:T(8,128)(2,1)} %copy-done.42, bf16[144,1152]{1,0:T(8,128)(2,1)} %copy-done.43, ...), custom_call_target="tpu_custom_call" | custom-call | flops 500000000 | bytes 1600000 | tf_op jit(solution)/shard_map/pallas_call | solution.py:1025
  369.8 2.7 reduce-scatter.6.cloned.1.call-done
  373.3 3.3 fusion.26
  376.7 2.6 collective-permute-start.73
  379.8 1.4 collective-permute-start.71
  385.6 2.8 collective-permute-done.78
  394.3 2.1 collective-permute-done.76
  399.0 7.0 %reduce-scatter.8.cloned.1.call-done = bf16[144,1152]{1,0:T(8,128)(2,1)} async-done(((bf16[576,1152]{1,0:T(8,128)(2,1)}), bf16[144,1152]{1,0:T(8,128)(2,1)}) %reduce-scatter.8.cloned.1.call-update) | async-done | bytes 331792 | tf_op jit(solution)/shard_map/reduce_scatter | solution.py:1054
  (365 shorter events, 78.9 us)
Async XLA Ops:
  7.2 298.3 %reduce-scatter.4.cloned.1.call-start = ((), (), s32[]{:S(2)}) async-start(), calls=%async_computation.4 | async-start | bytes 1658880 | tf_op jit(solution)/shard_map/reduce_scatter | solution.py:1054
  9.1 11.3 %collective-permute-start.2 = (bf16[1,1152]{1,0:T(2,128)(2,1)S(1)}, bf16[1,1152]{1,0:T(2,128)(2,1)S(1)}, u32[]{:S(2)}, u32[]{:S(2)}) collective-permute-start(bf16[1,1152]{1,0:T(2,128)(2,1)S(1)} %get-tuple-element.231.cond_ref), channel_id=1, source_target_pairs={{0,3},{1,0},{2,1},{3,2},{4,7},{5,4},{6,5},{7,6},{8,11},{9,8},{10,9... | collective-permute-start | bytes 6920 | tf_op jit(solution)/shard_map/ppermute | solution.py:63
  9.4 11.1 %collective-permute-start.1 = (bf16[1,1152]{1,0:T(2,128)(2,1)S(1)}, bf16[1,1152]{1,0:T(2,128)(2,1)S(1)}, u32[]{:S(2)}, u32[]{:S(2)}) collective-permute-start(bf16[1,1152]{1,0:T(2,128)(2,1)S(1)} %get-tuple-element.231.cond_ref), channel_id=1, source_target_pairs={{0,2},{1,3},{2,0},{3,1},{4,6},{5,7},{6,4},{7,5},{8,10},{9,11},{10,... | collective-permute-start | bytes 6920 | tf_op jit(solution)/shard_map/ppermute | solution.py:63
  9.4 11.1 %collective-permute-start = (bf16[1,1152]{1,0:T(2,128)(2,1)S(1)}, bf16[1,1152]{1,0:T(2,128)(2,1)S(1)}, u32[]{:S(2)}, u32[]{:S(2)}) collective-permute-start(bf16[1,1152]{1,0:T(2,128)(2,1)S(1)} %get-tuple-element.231.cond_ref), channel_id=1, source_target_pairs={{0,1},{1,2},{2,3},{3,0},{4,5},{5,6},{6,7},{7,4},{8,9},{9,10},{10,1... | collective-permute-start | bytes 6920 | tf_op jit(solution)/shard_map/ppermute | solution.py:63
  12.5 11.7 %collective-permute-start.3 = (bf16[9,8,3456]{2,1,0:T(8,128)(2,1)S(1)}, bf16[9,8,3456]{2,1,0:T(8,128)(2,1)S(1)}, u32[]{:S(2)}, u32[]{:S(2)}) collective-permute-start(bf16[9,8,3456]{2,1,0:T(8,128)(2,1)S(1)} %dynamic-slice_bitcast_fusion.2), channel_id=1, source_target_pairs={{0,1},{1,2},{2,3},{3,0},{4,5},{5,6},{6,7},{7,4},{8,9},{9,10},{10,1... | collective-permute-start | bytes 1493000 | tf_op jit(solution)/shard_map/ppermute | solution.py:63
  24.8 31.5 %collective-permute-start.9 = (bf16[256,2304]{1,0:T(8,128)(2,1)}, bf16[256,2304]{1,0:T(8,128)(2,1)S(1)}, u32[]{:S(2)}, u32[]{:S(2)}) collective-permute-start(bf16[256,2304]{1,0:T(8,128)(2,1)} %pad_maximum_fusion.1.refs_0_), channel_id=1, source_target_pairs={{0,16},{4,20},{8,24},{12,28},{16,0},{20,4},{24,8},{28,12},{1,17},{... | collective-permute-start | bytes 3538952 | tf_op jit(solution)/shard_map/ppermute | solution.py:57
  26.1 30.3 %collective-permute-start.8 = (bf16[256,2304]{1,0:T(8,128)(2,1)}, bf16[256,2304]{1,0:T(8,128)(2,1)S(1)}, u32[]{:S(2)}, u32[]{:S(2)}) collective-permute-start(bf16[256,2304]{1,0:T(8,128)(2,1)} %pad_maximum_fusion.1.refs_0_), channel_id=1, source_target_pairs={{0,8},{4,12},{8,0},{12,4},{16,24},{20,28},{24,16},{28,20},{1,9},{5... | collective-permute-start | bytes 3538952 | tf_op jit(solution)/shard_map/ppermute | solution.py:57
  27.3 16.2 %collective-permute-start.7 = (bf16[9,8,3456]{2,1,0:T(8,128)(2,1)S(1)}, bf16[9,8,3456]{2,1,0:T(8,128)(2,1)S(1)}, u32[]{:S(2)}, u32[]{:S(2)}) collective-permute-start(bf16[9,8,3456]{2,1,0:T(8,128)(2,1)S(1)} %collective-permute-done.3), channel_id=1, source_target_pairs={{0,1},{1,2},{2,3},{3,0},{4,5},{5,6},{6,7},{7,4},{8,9},{9,10},{10,1... | collective-permute-start | bytes 1493000 | tf_op jit(solution)/shard_map/ppermute | solution.py:63
  32.8 9.3 %collective-permute-start.5 = (f32[8,1152]{1,0:T(8,128)}, f32[8,1152]{1,0:T(8,128)S(1)}, u32[]{:S(2)}, u32[]{:S(2)}) collective-permute-start(f32[8,1152]{1,0:T(8,128)} %get-tuple-element.239), channel_id=1, source_target_pairs={{0,2},{1,3},{2,0},{3,1},{4,6},{5,7},{6,4},{7,5},{8,10},{9,11},{10,... | collective-permute-start | bytes 110600 | tf_op jit(solution)/shard_map/ppermute | solution.py:63
  43.5 12.9 %collective-permute-start.10 = (bf16[9,8,3456]{2,1,0:T(8,128)(2,1)S(1)}, bf16[9,8,3456]{2,1,0:T(8,128)(2,1)}, u32[]{:S(2)}, u32[]{:S(2)}) collective-permute-start(bf16[9,8,3456]{2,1,0:T(8,128)(2,1)S(1)} %collective-permute-done.7), channel_id=1, source_target_pairs={{0,1},{1,2},{2,3},{3,0},{4,5},{5,6},{6,7},{7,4},{8,9},{9,10},{10,1... | collective-permute-start | bytes 1493000 | tf_op jit(solution)/shard_map/ppermute | solution.py:63
  58.8 22.5 %collective-permute-start.12 = (bf16[3,9,8,3456]{3,2,1,0:T(8,128)(2,1)S(1)}, bf16[3,9,8,3456]{3,2,1,0:T(8,128)(2,1)}, u32[]{:S(2)}, u32[]{:S(2)}) collective-permute-start(bf16[3,9,8,3456]{3,2,1,0:T(8,128)(2,1)S(1)} %pad_maximum_fusion.refs_0_), channel_id=1, source_target_pairs={{0,4},{4,0},{8,12},{12,8},{16,20},{20,16},{24,28},{28,24},{1,5},{5... | collective-permute-start | bytes 4478984 | tf_op jit(solution)/shard_map/ppermute | solution.py:57
  61.7 19.6 %collective-permute-start.11 = (bf16[3,9,8,3456]{3,2,1,0:T(8,128)(2,1)S(1)}, bf16[3,9,8,3456]{3,2,1,0:T(8,128)(2,1)}, u32[]{:S(2)}, u32[]{:S(2)}) collective-permute-start(bf16[3,9,8,3456]{3,2,1,0:T(8,128)(2,1)S(1)} %pad_maximum_fusion.refs_0_), channel_id=1, source_target_pairs={{0,8},{4,20},{8,0},{12,28},{16,24},{20,4},{24,16},{28,12},{1,9},{5... | collective-permute-start | bytes 4478984 | tf_op jit(solution)/shard_map/ppermute | solution.py:60
  62.8 18.6 %collective-permute-start.13 = (bf16[9,8,2944]{2,1,0:T(8,128)(2,1)}, bf16[9,8,2944]{2,1,0:T(8,128)(2,1)}, u32[]{:S(2)}, u32[]{:S(2)}) collective-permute-start(bf16[9,8,2944]{2,1,0:T(8,128)(2,1)} %fusion), channel_id=1, source_target_pairs={{0,1},{1,2},{2,3},{3,0},{4,5},{5,6},{6,7},{7,4},{8,9},{9,10},{10,1... | collective-permute-start | bytes 1271816 | tf_op jit(solution)/shard_map/ppermute | solution.py:63
  67.5 13.8 %collective-permute-start.15 = (f32[8,1152]{1,0:T(8,128)S(1)}, f32[8,1152]{1,0:T(8,128)S(1)}, u32[]{:S(2)}, u32[]{:S(2)}) collective-permute-start(f32[8,1152]{1,0:T(8,128)S(1)} %copy-done.67), channel_id=1, source_target_pairs={{0,16},{4,20},{8,24},{12,28},{16,0},{20,4},{24,8},{28,12},{1,17},{... | collective-permute-start | bytes 110600 | tf_op jit(solution)/shard_map/ppermute | solution.py:57
  68.8 12.5 %collective-permute-start.14 = (f32[8,1152]{1,0:T(8,128)S(1)}, f32[8,1152]{1,0:T(8,128)S(1)}, u32[]{:S(2)}, u32[]{:S(2)}) collective-permute-start(f32[8,1152]{1,0:T(8,128)S(1)} %copy-done.67), channel_id=1, source_target_pairs={{0,8},{4,12},{8,0},{12,4},{16,24},{20,28},{24,16},{28,20},{1,9},{5... | collective-permute-start | bytes 110600 | tf_op jit(solution)/shard_map/ppermute | solution.py:57
  81.4 10.4 %collective-permute-start.16 = (bf16[3,9,8,3456]{3,2,1,0:T(8,128)(2,1)}, bf16[3,9,8,3456]{3,2,1,0:T(8,128)(2,1)}, u32[]{:S(2)}, u32[]{:S(2)}) collective-permute-start(bf16[3,9,8,3456]{3,2,1,0:T(8,128)(2,1)} %collective-permute-done.11.refs_1_), channel_id=1, source_target_pairs={{0,4},{4,0},{8,12},{12,8},{16,20},{20,16},{24,28},{28,24},{1,5},{5... | collective-permute-start | bytes 4478984 | tf_op jit(solution)/shard_map/ppermute | solution.py:57
  84.2 17.0 %collective-permute-start.19 = (bf16[128,2304]{1,0:T(8,128)(2,1)}, bf16[128,2304]{1,0:T(8,128)(2,1)S(1)}, u32[]{:S(2)}, u32[]{:S(2)}) collective-permute-start(bf16[128,2304]{1,0:T(8,128)(2,1)} %slice.141), channel_id=1, source_target_pairs={{0,8},{4,12},{8,0},{12,4},{16,24},{20,28},{24,16},{28,20},{1,9},{5... | collective-permute-start | bytes 1769480 | tf_op jit(solution)/shard_map/ppermute | solution.py:57
  84.5 16.8 %collective-permute-start.18 = (bf16[128,2304]{1,0:T(8,128)(2,1)S(1)}, bf16[128,2304]{1,0:T(8,128)(2,1)S(1)}, u32[]{:S(2)}, u32[]{:S(2)}) collective-permute-start(bf16[128,2304]{1,0:T(8,128)(2,1)S(1)} %slice.140), channel_id=1, source_target_pairs={{0,16},{4,20},{8,24},{12,28},{16,0},{20,4},{24,8},{28,12},{1,17},{... | collective-permute-start | bytes 1769480 | tf_op jit(solution)/shard_map/ppermute | solution.py:57
  84.7 16.5 %collective-permute-start.17 = (bf16[9,8,2944]{2,1,0:T(8,128)(2,1)}, bf16[9,8,2944]{2,1,0:T(8,128)(2,1)}, u32[]{:S(2)}, u32[]{:S(2)}) collective-permute-start(bf16[9,8,2944]{2,1,0:T(8,128)(2,1)} %collective-permute-done.13), channel_id=1, source_target_pairs={{0,1},{1,2},{2,3},{3,0},{4,5},{5,6},{6,7},{7,4},{8,9},{9,10},{10,1... | collective-permute-start | bytes 1271816 | tf_op jit(solution)/shard_map/ppermute | solution.py:63
  89.6 11.6 %collective-permute-start.20 = (f32[8,1152]{1,0:T(8,128)S(1)}, f32[8,1152]{1,0:T(8,128)S(1)}, u32[]{:S(2)}, u32[]{:S(2)}) collective-permute-start(f32[8,1152]{1,0:T(8,128)S(1)} %copy-done.67), channel_id=1, source_target_pairs={{0,24},{4,28},{8,16},{12,20},{16,8},{20,12},{24,0},{28,4},{1,25},{... | collective-permute-start | bytes 110600 | tf_op jit(solution)/shard_map/ppermute | solution.py:57
  104.2 19.3 %collective-permute-start.22 = (bf16[18,8,2944]{2,1,0:T(8,128)(2,1)S(1)}, bf16[18,8,2944]{2,1,0:T(8,128)(2,1)S(1)}, u32[]{:S(2)}, u32[]{:S(2)}) collective-permute-start(bf16[18,8,2944]{2,1,0:T(8,128)(2,1)S(1)} %constant_dynamic-update-slice_fusion.refs_2_), channel_id=1, source_target_pairs={{0,16},{4,20},{8,24},{12,28},{16,0},{20,4},{24,8},{28,12},{1,17},{... | collective-permute-start | bytes 2543624 | tf_op jit(solution)/shard_map/ppermute | solution.py:57
  104.5 19.0 %collective-permute-start.21 = (bf16[18,8,2944]{2,1,0:T(8,128)(2,1)S(1)}, bf16[18,8,2944]{2,1,0:T(8,128)(2,1)S(1)}, u32[]{:S(2)}, u32[]{:S(2)}) collective-permute-start(bf16[18,8,2944]{2,1,0:T(8,128)(2,1)S(1)} %constant_dynamic-update-slice_fusion.refs_2_), channel_id=1, source_target_pairs={{0,8},{4,12},{8,0},{12,4},{16,24},{20,28},{24,16},{28,20},{1,9},{5... | collective-permute-start | bytes 2543624 | tf_op jit(solution)/shard_map/ppermute | solution.py:57
  104.7 11.9 %collective-permute-start.23 = (bf16[9,8,2944]{2,1,0:T(8,128)(2,1)}, bf16[9,8,2944]{2,1,0:T(8,128)(2,1)S(1)}, u32[]{:S(2)}, u32[]{:S(2)}) collective-permute-start(bf16[9,8,2944]{2,1,0:T(8,128)(2,1)} %collective-permute-done.17), channel_id=1, source_target_pairs={{0,1},{1,2},{2,3},{3,0},{4,5},{5,6},{6,7},{7,4},{8,9},{9,10},{10,1... | collective-permute-start | bytes 1271816 | tf_op jit(solution)/shard_map/ppermute | solution.py:63
  123.5 20.1 %collective-permute-start.26 = (bf16[18,8,2944]{2,1,0:T(8,128)(2,1)S(1)}, bf16[18,8,2944]{2,1,0:T(8,128)(2,1)}, u32[]{:S(2)}, u32[]{:S(2)}) collective-permute-start(bf16[18,8,2944]{2,1,0:T(8,128)(2,1)S(1)} %constant_dynamic-update-slice_fusion.refs_2_), channel_id=1, source_target_pairs={{0,4},{4,0},{8,12},{12,8},{16,20},{20,16},{24,28},{28,24},{1,5},{5... | collective-permute-start | bytes 2543624 | tf_op jit(solution)/shard_map/ppermute | solution.py:57
  125.7 17.8 %collective-permute-start.27 = (bf16[36,8,1152]{2,1,0:T(8,128)(2,1)}, bf16[36,8,1152]{2,1,0:T(8,128)(2,1)}, u32[]{:S(2)}, u32[]{:S(2)}) collective-permute-start(bf16[36,8,1152]{2,1,0:T(8,128)(2,1)} %dynamic-slice_bitcast_fusion), channel_id=1, source_target_pairs={{0,1},{1,2},{2,3},{3,0},{4,5},{5,6},{6,7},{7,4},{8,9},{9,10},{10,1... | collective-permute-start | bytes 1990664 | tf_op jit(solution)/shard_map/ppermute | solution.py:63
  129.0 14.6 %collective-permute-start.25 = (bf16[9,8,2944]{2,1,0:T(8,128)(2,1)S(1)}, bf16[9,8,2944]{2,1,0:T(8,128)(2,1)S(1)}, u32[]{:S(2)}, u32[]{:S(2)}) collective-permute-start(bf16[9,8,2944]{2,1,0:T(8,128)(2,1)S(1)} %collective-permute-done.23.refs_3_), channel_id=1, source_target_pairs={{0,16},{4,20},{8,24},{12,28},{16,0},{20,4},{24,8},{28,12},{1,17},{... | collective-permute-start | bytes 1271816 | tf_op jit(solution)/shard_map/ppermute | solution.py:57
  129.2 14.4 %collective-permute-start.24 = (bf16[9,8,2944]{2,1,0:T(8,128)(2,1)S(1)}, bf16[9,8,2944]{2,1,0:T(8,128)(2,1)S(1)}, u32[]{:S(2)}, u32[]{:S(2)}) collective-permute-start(bf16[9,8,2944]{2,1,0:T(8,128)(2,1)S(1)} %collective-permute-done.23.refs_3_), channel_id=1, source_target_pairs={{0,8},{4,12},{8,0},{12,4},{16,24},{20,28},{24,16},{28,20},{1,9},{5... | collective-permute-start | bytes 1271816 | tf_op jit(solution)/shard_map/ppermute | solution.py:57
  143.6 21.5 %collective-permute-start.32 = (bf16[36,8,1152]{2,1,0:T(8,128)(2,1)}, bf16[36,8,1152]{2,1,0:T(8,128)(2,1)}, u32[]{:S(2)}, u32[]{:S(2)}) collective-permute-start(bf16[36,8,1152]{2,1,0:T(8,128)(2,1)} %collective-permute-done.27.refs_0_), channel_id=1, source_target_pairs={{0,1},{1,2},{2,3},{3,0},{4,5},{5,6},{6,7},{7,4},{8,9},{9,10},{10,1... | collective-permute-start | bytes 1990664 | tf_op jit(solution)/shard_map/ppermute | solution.py:63
  147.8 16.8 %collective-permute-start.29 = (bf16[14,8,2944]{2,1,0:T(8,128)(2,1)S(1)}, bf16[14,8,2944]{2,1,0:T(8,128)(2,1)}, u32[]{:S(2)}, u32[]{:S(2)}) collective-permute-start(bf16[14,8,2944]{2,1,0:T(8,128)(2,1)S(1)} %pad_maximum_fusion.2), channel_id=1, source_target_pairs={{0,8},{4,12},{8,0},{12,4},{16,24},{20,28},{24,16},{28,20},{1,9},{5... | collective-permute-start | bytes 1978376 | tf_op jit(solution)/shard_map/ppermute | solution.py:57
  148.1 14.1 %collective-permute-start.28 = (bf16[13,8,2944]{2,1,0:T(8,128)(2,1)S(1)}, bf16[13,8,2944]{2,1,0:T(8,128)(2,1)}, u32[]{:S(2)}, u32[]{:S(2)}) collective-permute-start(bf16[13,8,2944]{2,1,0:T(8,128)(2,1)S(1)} %slice.142), channel_id=1, source_target_pairs={{0,16},{4,20},{8,24},{12,28},{16,0},{20,4},{24,8},{28,12},{1,17},{... | collective-permute-start | bytes 1837064 | tf_op jit(solution)/shard_map/ppermute | solution.py:57
  148.8 16.3 %collective-permute-start.30 = (bf16[18,8,2944]{2,1,0:T(8,128)(2,1)S(1)}, bf16[18,8,2944]{2,1,0:T(8,128)(2,1)S(1)}, u32[]{:S(2)}, u32[]{:S(2)}) collective-permute-start(bf16[18,8,2944]{2,1,0:T(8,128)(2,1)S(1)} %collective-permute-done.21.refs_4_), channel_id=1, source_target_pairs={{0,4},{4,0},{8,12},{12,8},{16,20},{20,16},{24,28},{28,24},{1,5},{5... | collective-permute-start | bytes 2543624 | tf_op jit(solution)/shard_map/ppermute | solution.py:57
  150.5 14.7 %collective-permute-start.31 = (bf16[18,8,2944]{2,1,0:T(8,128)(2,1)S(1)}, bf16[18,8,2944]{2,1,0:T(8,128)(2,1)S(1)}, u32[]{:S(2)}, u32[]{:S(2)}) collective-permute-start(bf16[18,8,2944]{2,1,0:T(8,128)(2,1)S(1)} %collective-permute-done.22.refs_6_), channel_id=1, source_target_pairs={{0,4},{4,0},{8,12},{12,8},{16,20},{20,16},{24,28},{28,24},{1,5},{5... | collective-permute-start | bytes 2543624 | tf_op jit(solution)/shard_map/ppermute | solution.py:57
  165.9 25.1 %collective-permute-start.39 = (bf16[36,8,1152]{2,1,0:T(8,128)(2,1)}, bf16[36,8,1152]{2,1,0:T(8,128)(2,1)S(1)}, u32[]{:S(2)}, u32[]{:S(2)}) collective-permute-start(bf16[36,8,1152]{2,1,0:T(8,128)(2,1)} %collective-permute-done.27.refs_0_), channel_id=1, source_target_pairs={{0,8},{4,20},{8,0},{12,28},{16,24},{20,4},{24,16},{28,12},{1,9},{5... | collective-permute-start | bytes 1990664 | tf_op jit(solution)/shard_map/ppermute | solution.py:60
  166.6 24.4 %collective-permute-start.40 = (bf16[36,8,1152]{2,1,0:T(8,128)(2,1)}, bf16[36,8,1152]{2,1,0:T(8,128)(2,1)S(1)}, u32[]{:S(2)}, u32[]{:S(2)}) collective-permute-start(bf16[36,8,1152]{2,1,0:T(8,128)(2,1)} %collective-permute-done.32.refs_1_), channel_id=1, source_target_pairs={{0,8},{4,20},{8,0},{12,28},{16,24},{20,4},{24,16},{28,12},{1,9},{5... | collective-permute-start | bytes 1990664 | tf_op jit(solution)/shard_map/ppermute | solution.py:60
  167.8 23.3 %collective-permute-start.38 = (bf16[36,8,1152]{2,1,0:T(8,128)(2,1)}, bf16[36,8,1152]{2,1,0:T(8,128)(2,1)S(1)}, u32[]{:S(2)}, u32[]{:S(2)}) collective-permute-start(bf16[36,8,1152]{2,1,0:T(8,128)(2,1)} %collective-permute-done.32.refs_1_), channel_id=1, source_target_pairs={{0,1},{1,2},{2,3},{3,0},{4,5},{5,6},{6,7},{7,4},{8,9},{9,10},{10,1... | collective-permute-start | bytes 1990664 | tf_op jit(solution)/shard_map/ppermute | solution.py:63
  192.1 9.8 %collective-permute-start.41 = (bf16[36,8,1152]{2,1,0:T(8,128)(2,1)S(1)}, bf16[36,8,1152]{2,1,0:T(8,128)(2,1)S(1)}, u32[]{:S(2)}, u32[]{:S(2)}) collective-permute-start(bf16[36,8,1152]{2,1,0:T(8,128)(2,1)S(1)} %collective-permute-done.38.refs_2_), channel_id=1, source_target_pairs={{0,8},{4,20},{8,0},{12,28},{16,24},{20,4},{24,16},{28,12},{1,9},{5... | collective-permute-start | bytes 1990664 | tf_op jit(solution)/shard_map/ppermute | solution.py:60
  192.3 10.6 %collective-permute-start.44 = (bf16[36,8,1152]{2,1,0:T(8,128)(2,1)S(1)}, bf16[36,8,1152]{2,1,0:T(8,128)(2,1)S(1)}, u32[]{:S(2)}, u32[]{:S(2)}) collective-permute-start(bf16[36,8,1152]{2,1,0:T(8,128)(2,1)S(1)} %collective-permute-done.38.refs_2_), channel_id=1, source_target_pairs={{0,4},{4,0},{8,12},{12,8},{16,20},{20,16},{24,28},{28,24},{1,5},{5... | collective-permute-start | bytes 1990664 | tf_op jit(solution)/shard_map/ppermute | solution.py:57
  192.7 10.2 %collective-permute-start.43 = (bf16[36,8,1152]{2,1,0:T(8,128)(2,1)}, bf16[36,8,1152]{2,1,0:T(8,128)(2,1)S(1)}, u32[]{:S(2)}, u32[]{:S(2)}) collective-permute-start(bf16[36,8,1152]{2,1,0:T(8,128)(2,1)} %collective-permute-done.32.refs_1_), channel_id=1, source_target_pairs={{0,4},{4,0},{8,12},{12,8},{16,20},{20,16},{24,28},{28,24},{1,5},{5... | collective-permute-start | bytes 1990664 | tf_op jit(solution)/shard_map/ppermute | solution.py:57
  192.8 10.0 %collective-permute-start.45 = (bf16[36,8,1152]{2,1,0:T(8,128)(2,1)S(1)}, bf16[36,8,1152]{2,1,0:T(8,128)(2,1)S(1)}, u32[]{:S(2)}, u32[]{:S(2)}) collective-permute-start(bf16[36,8,1152]{2,1,0:T(8,128)(2,1)S(1)} %collective-permute-done.39.refs_3_), channel_id=1, source_target_pairs={{0,4},{4,0},{8,12},{12,8},{16,20},{20,16},{24,28},{28,24},{1,5},{5... | collective-permute-start | bytes 1990664 | tf_op jit(solution)/shard_map/ppermute | solution.py:57
  194.0 8.8 %collective-permute-start.46 = (bf16[36,8,1152]{2,1,0:T(8,128)(2,1)S(1)}, bf16[36,8,1152]{2,1,0:T(8,128)(2,1)S(1)}, u32[]{:S(2)}, u32[]{:S(2)}) collective-permute-start(bf16[36,8,1152]{2,1,0:T(8,128)(2,1)S(1)} %collective-permute-done.40.refs_4_), channel_id=1, source_target_pairs={{0,4},{4,0},{8,12},{12,8},{16,20},{20,16},{24,28},{28,24},{1,5},{5... | collective-permute-start | bytes 1990664 | tf_op jit(solution)/shard_map/ppermute | solution.py:57
  204.6 30.6 %collective-permute-start.48 = (bf16[1152,256]{1,0:T(8,128)(2,1)}, bf16[1152,256]{1,0:T(8,128)(2,1)}, u32[]{:S(2)}, u32[]{:S(2)}) collective-permute-start(bf16[1152,256]{1,0:T(8,128)(2,1)} %get-tuple-element.351), channel_id=1, source_target_pairs={{0,8},{4,12},{8,0},{12,4},{16,24},{20,28},{24,16},{28,20},{1,9},{5... | collective-permute-start | bytes 1769480 | tf_op jit(solution)/shard_map/ppermute | solution.py:57
  204.8 30.3 %collective-permute-start.49 = (bf16[1152,256]{1,0:T(8,128)(2,1)}, bf16[1152,256]{1,0:T(8,128)(2,1)}, u32[]{:S(2)}, u32[]{:S(2)}) collective-permute-start(bf16[1152,256]{1,0:T(8,128)(2,1)} %get-tuple-element.352), channel_id=1, source_target_pairs={{0,16},{4,20},{8,24},{12,28},{16,0},{20,4},{24,8},{28,12},{1,17},{... | collective-permute-start | bytes 1769480 | tf_op jit(solution)/shard_map/ppermute | solution.py:57
  205.5 29.7 %collective-permute-start.50 = (bf16[1152,256]{1,0:T(8,128)(2,1)}, bf16[1152,256]{1,0:T(8,128)(2,1)}, u32[]{:S(2)}, u32[]{:S(2)}) collective-permute-start(bf16[1152,256]{1,0:T(8,128)(2,1)} %get-tuple-element.353), channel_id=1, source_target_pairs={{0,24},{4,28},{8,16},{12,20},{16,8},{20,12},{24,0},{28,4},{1,25},{... | collective-permute-start | bytes 1769480 | tf_op jit(solution)/shard_map/ppermute | solution.py:57
  235.2 25.0 %collective-permute-start.51 = (bf16[1152,256]{1,0:T(8,128)(2,1)S(1)}, bf16[1152,256]{1,0:T(8,128)(2,1)S(1)}, u32[]{:S(2)}, u32[]{:S(2)}) collective-permute-start(bf16[1152,256]{1,0:T(8,128)(2,1)S(1)} %copy-done.65), channel_id=1, source_target_pairs={{0,8},{4,12},{8,0},{12,4},{16,24},{20,28},{24,16},{28,20},{1,9},{5... | collective-permute-start | bytes 1769480 | tf_op jit(solution)/shard_map/ppermute | solution.py:57
  235.5 24.7 %collective-permute-start.52 = (bf16[1152,256]{1,0:T(8,128)(2,1)S(1)}, bf16[1152,256]{1,0:T(8,128)(2,1)S(1)}, u32[]{:S(2)}, u32[]{:S(2)}) collective-permute-start(bf16[1152,256]{1,0:T(8,128)(2,1)S(1)} %copy-done.64), channel_id=1, source_target_pairs={{0,16},{4,20},{8,24},{12,28},{16,0},{20,4},{24,8},{28,12},{1,17},{... | collective-permute-start | bytes 1769480 | tf_op jit(solution)/shard_map/ppermute | solution.py:57
  236.1 25.3 %collective-permute-start.53 = (bf16[1152,256]{1,0:T(8,128)(2,1)S(1)}, bf16[1152,256]{1,0:T(8,128)(2,1)S(1)}, u32[]{:S(2)}, u32[]{:S(2)}) collective-permute-start(bf16[1152,256]{1,0:T(8,128)(2,1)S(1)} %copy-done.63), channel_id=1, source_target_pairs={{0,24},{4,28},{8,16},{12,20},{16,8},{20,12},{24,0},{28,4},{1,25},{... | collective-permute-start | bytes 1769480 | tf_op jit(solution)/shard_map/ppermute | solution.py:57
  270.6 24.8 %collective-permute-start.59 = (f32[4,144,1152]{2,1,0:T(8,128)}, f32[4,144,1152]{2,1,0:T(8,128)}, u32[]{:S(2)}, u32[]{:S(2)}) collective-permute-start(f32[4,144,1152]{2,1,0:T(8,128)} %get-tuple-element.391), channel_id=1, source_target_pairs={{0,4},{4,0},{8,12},{12,8},{16,20},{20,16},{24,28},{28,24},{1,5},{5... | collective-permute-start | bytes 7962632 | tf_op jit(solution)/shard_map/ppermute | solution.py:57
  276.0 96.5 %reduce-scatter.6.cloned.1.call-start = ((), (), s32[]{:S(2)}) async-start(), calls=%async_computation.5 | async-start | bytes 1658880 | tf_op jit(solution)/shard_map/reduce_scatter | solution.py:1054
  276.3 17.5 %collective-permute-start.56 = (bf16[256,1152]{1,0:T(8,128)(2,1)S(1)}, bf16[256,1152]{1,0:T(8,128)(2,1)S(1)}, u32[]{:S(2)}, u32[]{:S(2)}) collective-permute-start(bf16[256,1152]{1,0:T(8,128)(2,1)S(1)} %copy-done.25), channel_id=1, source_target_pairs={{0,16},{4,20},{8,24},{12,28},{16,0},{20,4},{24,8},{28,12},{1,17},{... | collective-permute-start | bytes 1769480 | tf_op jit(solution)/shard_map/ppermute | solution.py:57
  277.1 16.7 %collective-permute-start.55 = (bf16[256,1152]{1,0:T(8,128)(2,1)S(1)}, bf16[256,1152]{1,0:T(8,128)(2,1)S(1)}, u32[]{:S(2)}, u32[]{:S(2)}) collective-permute-start(bf16[256,1152]{1,0:T(8,128)(2,1)S(1)} %copy-done.25), channel_id=1, source_target_pairs={{0,8},{4,12},{8,0},{12,4},{16,24},{20,28},{24,16},{28,20},{1,9},{5... | collective-permute-start | bytes 1769480 | tf_op jit(solution)/shard_map/ppermute | solution.py:57
  313.3 17.3 %collective-permute-start.63 = (f32[576,1152]{1,0:T(8,128)}, f32[576,1152]{1,0:T(8,128)S(1)}, u32[]{:S(2)}, u32[]{:S(2)}) collective-permute-start(f32[576,1152]{1,0:T(8,128)} %get-tuple-element.416), channel_id=1, source_target_pairs={{0,4},{4,0},{8,12},{12,8},{16,20},{20,16},{24,28},{28,24},{1,5},{5... | collective-permute-start | bytes 7962632 | tf_op jit(solution)/shard_map/ppermute | solution.py:57
  314.1 22.8 %collective-permute-start.60 = (bf16[864,256]{1,0:T(8,128)(2,1)}, bf16[864,256]{1,0:T(8,128)(2,1)S(1)}, u32[]{:S(2)}, u32[]{:S(2)}) collective-permute-start(bf16[864,256]{1,0:T(8,128)(2,1)} %get-tuple-element.402), channel_id=1, source_target_pairs={{0,8},{4,12},{8,0},{12,4},{16,24},{20,28},{24,16},{28,20},{1,9},{5... | collective-permute-start | bytes 1327112 | tf_op jit(solution)/shard_map/ppermute | solution.py:57
  315.2 21.7 %collective-permute-start.61 = (bf16[864,256]{1,0:T(8,128)(2,1)}, bf16[864,256]{1,0:T(8,128)(2,1)S(1)}, u32[]{:S(2)}, u32[]{:S(2)}) collective-permute-start(bf16[864,256]{1,0:T(8,128)(2,1)} %get-tuple-element.403), channel_id=1, source_target_pairs={{0,16},{4,20},{8,24},{12,28},{16,0},{20,4},{24,8},{28,12},{1,17},{... | collective-permute-start | bytes 1327112 | tf_op jit(solution)/shard_map/ppermute | solution.py:57
  316.4 20.5 %collective-permute-start.62 = (bf16[864,256]{1,0:T(8,128)(2,1)}, bf16[864,256]{1,0:T(8,128)(2,1)S(1)}, u32[]{:S(2)}, u32[]{:S(2)}) collective-permute-start(bf16[864,256]{1,0:T(8,128)(2,1)} %get-tuple-element.404), channel_id=1, source_target_pairs={{0,24},{4,28},{8,16},{12,20},{16,8},{20,12},{24,0},{28,4},{1,25},{... | collective-permute-start | bytes 1327112 | tf_op jit(solution)/shard_map/ppermute | solution.py:57
  345.0 18.7 %collective-permute-start.64 = (f32[432,1152]{1,0:T(8,128)}, f32[432,1152]{1,0:T(8,128)}, u32[]{:S(2)}, u32[]{:S(2)}) collective-permute-start(f32[432,1152]{1,0:T(8,128)} %get-tuple-element.428), channel_id=1, source_target_pairs={{0,4},{4,0},{8,12},{12,8},{16,20},{20,16},{24,28},{28,24},{1,5},{5... | collective-permute-start | bytes 5971976 | tf_op jit(solution)/shard_map/ppermute | solution.py:57
  345.9 11.5 %collective-permute-start.65 = (bf16[144,1152]{1,0:T(8,128)(2,1)}, bf16[144,1152]{1,0:T(8,128)(2,1)S(1)}, u32[]{:S(2)}, u32[]{:S(2)}) collective-permute-start(bf16[144,1152]{1,0:T(8,128)(2,1)} %get-tuple-element.430), channel_id=1, source_target_pairs={{0,8},{4,12},{8,0},{12,4},{16,24},{20,28},{24,16},{28,20},{1,9},{5... | collective-permute-start | bytes 995336 | tf_op jit(solution)/shard_map/ppermute | solution.py:57
  347.1 11.9 %collective-permute-start.66 = (bf16[144,1152]{1,0:T(8,128)(2,1)S(1)}, bf16[144,1152]{1,0:T(8,128)(2,1)S(1)}, u32[]{:S(2)}, u32[]{:S(2)}) collective-permute-start(bf16[144,1152]{1,0:T(8,128)(2,1)S(1)} %copy-done.66), channel_id=1, source_target_pairs={{0,16},{4,20},{8,24},{12,28},{16,0},{20,4},{24,8},{28,12},{1,17},{... | collective-permute-start | bytes 995336 | tf_op jit(solution)/shard_map/ppermute | solution.py:57
  348.3 15.4 %collective-permute-start.67 = (bf16[144,1152]{1,0:T(8,128)(2,1)}, bf16[144,1152]{1,0:T(8,128)(2,1)S(1)}, u32[]{:S(2)}, u32[]{:S(2)}) collective-permute-start(bf16[144,1152]{1,0:T(8,128)(2,1)} %get-tuple-element.432), channel_id=1, source_target_pairs={{0,24},{4,28},{8,16},{12,20},{16,8},{20,12},{24,0},{28,4},{1,25},{... | collective-permute-start | bytes 995336 | tf_op jit(solution)/shard_map/ppermute | solution.py:57
  349.7 20.1 %all-to-all-start = ((bf16[8,144,144]{1,2,0:T(8,128)(2,1)}), bf16[8,144,144]{1,2,0:T(8,128)(2,1)S(1)}, u32[]{:S(2)}, u32[]{:S(2)}) async-start(bf16[8,144,144]{1,2,0:T(8,128)(2,1)} %bitcast.35), calls=%async_computation.2 | async-start | bytes 1179648 | tf_op jit(solution)/shard_map/all_to_all | solution.py:1414
  354.2 51.8 %reduce-scatter.8.cloned.1.call-start = ((), (), s32[]{:S(2)}) async-start(), calls=%async_computation.6 | async-start | bytes 1658880 | tf_op jit(solution)/shard_map/reduce_scatter | solution.py:1054
  356.3 13.0 %collective-permute-start.70 = (f32[16,1152]{1,0:T(8,128)}, f32[16,1152]{1,0:T(8,128)S(1)}, u32[]{:S(2)}, u32[]{:S(2)}) collective-permute-start(f32[16,1152]{1,0:T(8,128)} %shard_map.257), channel_id=1, source_target_pairs={{0,3},{1,0},{2,1},{3,2},{4,7},{5,4},{6,5},{7,6},{8,11},{9,8},{10,9... | collective-permute-start | bytes 221192 | tf_op jit(solution)/shard_map/ppermute | solution.py:63
  357.5 12.3 %collective-permute-start.69 = (f32[16,1152]{1,0:T(8,128)}, f32[16,1152]{1,0:T(8,128)S(1)}, u32[]{:S(2)}, u32[]{:S(2)}) collective-permute-start(f32[16,1152]{1,0:T(8,128)} %shard_map.257), channel_id=1, source_target_pairs={{0,2},{1,3},{2,0},{3,1},{4,6},{5,7},{6,4},{7,5},{8,10},{9,11},{10,... | collective-permute-start | bytes 221192 | tf_op jit(solution)/shard_map/ppermute | solution.py:63
  359.0 10.8 %collective-permute-start.68 = (f32[16,1152]{1,0:T(8,128)}, f32[16,1152]{1,0:T(8,128)S(1)}, u32[]{:S(2)}, u32[]{:S(2)}) collective-permute-start(f32[16,1152]{1,0:T(8,128)} %shard_map.257), channel_id=1, source_target_pairs={{0,1},{1,2},{2,3},{3,0},{4,5},{5,6},{6,7},{7,4},{8,9},{9,10},{10,1... | collective-permute-start | bytes 221192 | tf_op jit(solution)/shard_map/ppermute | solution.py:63
  373.2 11.8 %collective-permute-start.77 = (f32[8,1152]{1,0:T(8,128)S(1)}, f32[8,1152]{1,0:T(8,128)S(1)}, u32[]{:S(2)}, u32[]{:S(2)}) collective-permute-start(f32[8,1152]{1,0:T(8,128)S(1)} %slice_add_fusion), channel_id=1, source_target_pairs={{0,4},{4,0},{8,12},{12,8},{16,20},{20,16},{24,28},{28,24},{1,5},{5... | collective-permute-start | bytes 110600 | tf_op jit(solution)/shard_map/ppermute | solution.py:57
  (88 other events, 775.9 us)
Sparse Core Ops, SparseCore 0:
  276.1 29.3 reduce-scatter.3
  337.1 35.2 reduce-scatter.5
  374.8 31.1 reduce-scatter.7

commit v8 on v7

--- a/solution.py
+++ b/solution.py
@@ -319,7 +319,7 @@
         slots = turned.shape[1]
         width = turned.shape[0] // 3
         count = width // HEAD_DIM
-        heads_at_once = 2 if count % 2 == 0 else 1
+        heads_at_once = 1
         scale = HEAD_DIM ** (-0.5)
 
         def kernel(live_ref, turned_ref, attended_ref, out_turned):

time: 421 us -> 421 us (level)
  transfers between devices with their start and end apart: 84 -> 84, of which waited for: 24 -> 24; matrix products, arithmetic and copies ran while one was open for 7% -> 7% of each run, Pallas kernels for 39% -> 40%
where the time goes in v8:
time: 421 us; the launch traced here: 416 us
  Pallas kernels  173 us (41%)
  starting transfers between devices  93.5 us (22%)
  waiting for transfers between devices  85.7 us (20%)
  local copies, waits for them, and re-layouts  35.7 us (8%)
  between operations  16.1 us (4%)
  other arithmetic  8.11 us (2%)
  matrix products  4.61 us (1%)
    ppermute x55, waiting for transfers between devices, box_send(): return lax.ppermute(x, 'dp', [(i, i ^ bits) for i in range(dp)])  47.4 us
    ppermute x55, starting transfers between devices, box_send(): return lax.ppermute(x, 'dp', [(i, i ^ bits) for i in range(dp)])  45.7 us
    ppermute x21, starting transfers between devices, ring_send(): return lax.ppermute(x, 'fsdp', [(i, (i + hops) % fs) for i in range(fs)])  41.1 us
    pallas_call x1, Pallas kernels, middle_forward(): pl.pallas_call(kernel, out_shape=[jax.ShapeDtypeStruct((slots, width), f3...  19.6 us
    ppermute x21, waiting for transfers between devices, ring_send(): return lax.ppermute(x, 'fsdp', [(i, (i + hops) % fs) for i in range(fs)])  17.5 us
    pallas_call x1, Pallas kernels, hidden_back(): pl.pallas_call(kernel, out_shape=[jax.ShapeDtypeStruct((slots, hidden), b...  17.1 us
    pallas_call x1, Pallas kernels, attention_back(): pl.pallas_call(kernel, out_shape=[jax.ShapeDtypeStruct((3 * width, slots)...  15.4 us
    pallas_call x2, Pallas kernels, column_grad(): pl.pallas_call(kernel, out_shape=[jax.ShapeDtypeStruct((n_out, width), f3...  14.8 us
  transfers between devices with their start and end apart: 84, of which 24 were waited for; matrix products, arithmetic and copies ran while one was open for 7% of the time, Pallas kernels for 40%

profile of v8, /device:TPU:25, one launch (start us, length us, event | category | flops | bytes accessed | tf_op | source)
XLA Modules:
  0.0 416.4 jit_solution(3299169604330688052)
XLA Ops:
  9.4 3.1 collective-permute-start
  17.0 2.0 dynamic-slice_bitcast_fusion
  20.5 3.7 collective-permute-done.3
  27.3 2.0 collective-permute-start.7
  29.3 3.5 shard_map.237
  33.4 5.1 %collective-permute-done.4.refs_1_ = f32[8,1152]{1,0:T(8,128)S(1)} collective-permute-done((f32[8,1152]{1,0:T(8,128)}, f32[8,1152]{1,0:T(8,128)S(1)}, u32[]{:S(2)}, u32[]{:S(2)}) %collective-permute-start.4) | collective-permute-done | bytes 36896 | tf_op jit(solution)/shard_map/ppermute | solution.py:63
  38.4 3.7 collective-permute-start.6
  42.1 1.4 collective-permute-done.6.refs_3_
  43.5 3.7 collective-permute-start.10
  49.1 1.5 shard_map.238
  50.6 3.9 shard_map.239
  54.4 2.0 collective-permute-done.10
  58.8 2.9 collective-permute-start.12
  62.8 3.7 collective-permute-start.13
  69.4 11.9 %collective-permute-done.15.refs_5_ = f32[8,1152]{1,0:T(8,128)S(1)} collective-permute-done((f32[8,1152]{1,0:T(8,128)S(1)}, f32[8,1152]{1,0:T(8,128)S(1)}, u32[]{:S(2)}, u32[]{:S(2)}) %collective-permute-start.15) | collective-permute-done | bytes 36896 | tf_op jit(solution)/shard_map/ppermute | solution.py:57
  84.7 3.6 collective-permute-start.17
  89.6 2.2 collective-permute-start.20
  91.8 9.4 %shard_map.240 = (f32[3456,256]{1,0:T(8,128)}, bf16[4,4,9,8,3456]{4,3,2,1,0:T(8,128)(2,1)}) custom-call(s32[12]{0:T(128)} %stack.119.where_ref, bf16[256,1152]{1,0:T(8,128)(2,1)} %get-tuple-element.396.normed_ref.refs_0_, f32[2,1152]{1,0:T(2,128)} %reshape.132.bias_ref, bf16[4,9,8,3456]{3,2,1,0:T(8,128)(2,1)} %bitcast.102, ...), custom_call_target="tpu_custom_call" | custom-call | flops 1100000000 | bytes 3520000 | tf_op jit(solution)/shard_map/pallas_call | solution.py:300
  104.7 3.3 collective-permute-start.23
  108.0 12.4 %shard_map.241.attended_ref.x_ref = bf16[256,1152]{1,0:T(8,128)(2,1)} custom-call(s32[1]{0:T(128)} %bitcast.live_ref, f32[3456,256]{1,0:T(8,128)} %get-tuple-element.275.turned_ref), custom_call_target="tpu_custom_call" | custom-call | flops 1100000000 | bytes 3520000 | tf_op jit(solution)/shard_map/pallas_call | solution.py:357
  120.4 3.1 collective-permute-done.22.refs_6_
  123.5 2.3 collective-permute-start.26
  125.7 3.3 collective-permute-start.27
  129.9 8.8 %shard_map.242 = (bf16[256,1152]{1,0:T(8,128)(2,1)}, bf16[256,1152]{1,0:T(8,128)(2,1)}, bf16[128,1152]{1,0:T(8,128)(2,1)}, bf16[128,1152]{1,0:T(8,128)(2,1)}, bf...) custom-call(bf16[256,2304]{1,0:T(8,128)(2,1)} %copy-done.4, ...), custom_call_target="tpu_custom_call" | custom-call | flops 800000000 | bytes 2560000 | tf_op jit(solution)/shard_map/pallas_call | solution.py:192
  138.7 4.9 %collective-permute-done.27.refs_0_ = bf16[36,8,1152]{2,1,0:T(8,128)(2,1)} collective-permute-done((bf16[36,8,1152]{2,1,0:T(8,128)(2,1)}, bf16[36,8,1152]{2,1,0:T(8,128)(2,1)}, u32[]{:S(2)}, u32[]{:S(2)}) %collective-permute-start.27) | collective-permute-done | bytes 663584 | tf_op jit(solution)/shard_map/ppermute | solution.py:63
  143.6 4.1 collective-permute-start.32
  148.8 1.7 collective-permute-start.30
  150.6 11.6 %collective-permute-done.28.refs_8_ = bf16[13,8,2944]{2,1,0:T(8,128)(2,1)} collective-permute-done((bf16[13,8,2944]{2,1,0:T(8,128)(2,1)S(1)}, bf16[13,8,2944]{2,1,0:T(8,128)(2,1)}, u32[]{:S(2)}, u32[]{:S(2)}) %collective-permute-start.28) | collective-permute-done | bytes 612384 | tf_op jit(solution)/shard_map/ppermute | solution.py:57
  162.2 2.3 collective-permute-start.33
  167.8 1.7 collective-permute-start.38
  171.4 19.6 %shard_map.243 = (f32[256,1152]{1,0:T(8,128)}, bf16[256,1152]{1,0:T(8,128)(2,1)}, f32[256,4608]{1,0:T(8,128)}, bf16[256,4608]{1,0:T(8,128)(2,1)}, bf16[1152,256]...) custom-call(s32[9]{0:T(128)} %stack.114.where_ref, ...), custom_call_target="tpu_custom_call" | custom-call | flops 2000000000 | bytes 6400000 | tf_op jit(solution)/shard_map/pallas_call | solution.py:530
  194.4 7.5 %collective-permute-done.41.refs_5_ = bf16[36,8,1152]{2,1,0:T(8,128)(2,1)S(1)} collective-permute-done((bf16[36,8,1152]{2,1,0:T(8,128)(2,1)S(1)}, bf16[36,8,1152]{2,1,0:T(8,128)(2,1)S(1)}, u32[]{:S(2)}, u32[]{:S(2)}) %collective-permute-start.41) | collective-permute-done | bytes 663584 | tf_op jit(solution)/shard_map/ppermute | solution.py:60
  202.9 1.7 collective-permute-done.47.refs_11_
  205.5 1.8 collective-permute-start.50
  207.9 17.1 %shard_map.244 = (bf16[256,4608]{1,0:T(8,128)(2,1)}, bf16[1152,256]{1,0:T(8,128)(2,1)}, bf16[1152,256]{1,0:T(8,128)(2,1)}, bf16[1152,256]{1,0:T(8,128)(2,1)}, bf...) custom-call(s32[12]{0:T(128)} %stack.119.where_ref, ...), custom_call_target="tpu_custom_call" | custom-call | flops 1500000000 | bytes 4800000 | tf_op jit(solution)/shard_map/pallas_call | solution.py:650
  225.1 10.1 %shard_map.245 = (bf16[256,1152]{1,0:T(8,128)(2,1)}, f32[8,1152]{1,0:T(8,128)}) custom-call(s32[1]{0:T(128)} %bitcast.live_ref, bf16[256,4608]{1,0:T(8,128)(2,1)} %get-tuple-element.314.act_ref, bf16[4608,1152]{1,0:T(8,128)(2,1)} %bitcast.90, f32[1,1152]{1,0:T(1,128)} %reshape.137.bias_ref, bf16[256,1152]{1,0:T(8,128)(2,1)} %bitcast.86, ...), custom_call_target="tpu_custom_call" | custom-call | flops 600000000 | bytes 1920000 | tf_op jit(solution)/shard_map/pallas_call | solution.py:892
  236.1 1.8 collective-permute-start.53
  237.9 7.7 %shard_map.247 = (f32[4,144,1152]{2,1,0:T(8,128)}, f32[4,144,1152]{2,1,0:T(8,128)}) custom-call(s32[1]{0:T(128)} %bitcast.5.where_ref, bf16[1152,256]{1,0:T(8,128)(2,1)} %get-tuple-element.365.x0, bf16[1152,256]{1,0:T(8,128)(2,1)} %collective-permute-done.48.x1, bf16[1152,256]{1,0:T(8,128)(2,1)} %collective-permute-done.49.x2, ...), custom_call_target="tpu_custom_call" | custom-call | flops 600000000 | bytes 1920000 | tf_op jit(solution)/shard_map/pallas_call | solution.py:1130
  245.6 14.6 %shard_map.246 = (f32[256,1152]{1,0:T(8,128)}, bf16[1152,256]{1,0:T(8,128)(2,1)}, f32[1152,256]{1,0:T(8,128)}, f32[8,1152]{1,0:T(8,128)}) custom-call(s32[1]{0:T(128)} %bitcast.live_ref, bf16[256,4608]{1,0:T(8,128)(2,1)} %get-tuple-element.356.d_pre_ref, bf16[1152,4608]{1,0:T(8,128)(2,1)} %bitcast.91, bf16[1152,1152]{1,0:T(8,128)(2,1)} %bitcast.104, ...), custom_call_target="tpu_custom_call" | custom-call | flops 1200000000 | bytes 3840000 | tf_op jit(solution)/shard_map/pallas_call | solution.py:756
  262.3 2.6 collective-permute-start.54
  265.5 5.1 %shard_map.250 = (f32[4,144,1152]{2,1,0:T(8,128)}, f32[4,144,1152]{2,1,0:T(8,128)}) custom-call(s32[5]{0:T(128)} %concatenate.52.where_ref, bf16[1152,256]{1,0:T(8,128)(2,1)} %get-tuple-element.389.d_ref, bf16[256,1152]{1,0:T(8,128)(2,1)} %shard_map.241.attended_ref.x_ref), custom_call_target="tpu_custom_call" | custom-call | flops 500000000 | bytes 1600000 | tf_op jit(solution)/shard_map/pallas_call | solution.py:1069
  270.6 1.5 copy-done.6
  272.1 3.9 shard_map.248
  278.4 15.4 %shard_map.249 = (bf16[3456,256]{1,0:T(8,128)(2,1)}, bf16[864,256]{1,0:T(8,128)(2,1)}, bf16[864,256]{1,0:T(8,128)(2,1)}, bf16[864,256]{1,0:T(8,128)(2,1)}, bf16[864,256]{1,0:T(8,128)(2,1)}) custom-call(s32[1]{0:T(128)} %bitcast.live_ref, s32[4]{0:T(128)} %pad_add_fusion.chip_ref, f32[3456,256]{1,0:T(8,128)} %get-tuple-element.275.turned_ref, ...), custom_call_target="tpu_custom_call" | custom-call | flops 1200000000 | bytes 3840000 | tf_op jit(solution)/shard_map/pallas_call | solution.py:423
  295.4 6.1 %collective-permute-done.58.refs_4_ = bf16[128,1152]{1,0:T(8,128)(2,1)S(1)} collective-permute-done((bf16[128,1152]{1,0:T(8,128)(2,1)S(1)}, bf16[128,1152]{1,0:T(8,128)(2,1)S(1)}, u32[]{:S(2)}, u32[]{:S(2)}) %collective-permute-start.58) | collective-permute-done | bytes 294944 | tf_op jit(solution)/shard_map/ppermute | solution.py:57
  302.0 3.5 reduce-scatter.4.cloned.1.call-done
  305.5 7.8 %shard_map.252 = (f32[576,1152]{1,0:T(8,128)}, f32[576,1152]{1,0:T(8,128)}) custom-call(s32[1]{0:T(128)} %bitcast.5.where_ref, bf16[256,1152]{1,0:T(8,128)(2,1)} %get-tuple-element.406.refs_0_, bf16[256,1152]{1,0:T(8,128)(2,1)} %copy-done.12, bf16[256,1152]{1,0:T(8,128)(2,1)} %copy-done.11, bf16[128,1152]{1,0:T(8,128)(2,1)} %copy-done.46, ...), custom_call_target="tpu_custom_call" | custom-call | flops 800000000 | bytes 2560000 | tf_op jit(solution)/shard_map/pallas_call | solution.py:963
  316.7 3.8 shard_map.254
  320.5 10.1 %shard_map.251 = (bf16[256,1152]{1,0:T(8,128)(2,1)}, f32[8,1152]{1,0:T(8,128)}) custom-call(bf16[3456,256]{1,0:T(8,128)(2,1)} %get-tuple-element.392.d_ref, bf16[1152,3456]{1,0:T(8,128)(2,1)} %bitcast.92, bf16[256,1152]{1,0:T(8,128)(2,1)} %bitcast.88, f32[256,1152]{1,0:T(8,128)} %get-tuple-element.394.d_middle_ref, f32[8,1152]{1,0:T(8,128)} %get-tuple-element.307.mods_ref), custom_call_target="tpu_custom_call" | custom-call | flops 900000000 | bytes 2880000 | tf_op jit(solution)/shard_map/pallas_call | solution.py:825
  330.6 1.5 copy-done.5
  332.1 4.8 %shard_map.253 = bf16[576,1152]{1,0:T(8,128)(2,1)} custom-call(f32[576,1152]{1,0:T(8,128)} %get-tuple-element.415.refs_0_, f32[576,1152]{1,0:T(8,128)} %copy-done.5), custom_call_target="tpu_custom_call" | custom-call | flops 500000000 | bytes 1600000 | tf_op jit(solution)/shard_map/pallas_call | solution.py:1025
  338.0 6.9 %shard_map.255 = (f32[432,1152]{1,0:T(8,128)}, f32[432,1152]{1,0:T(8,128)}) custom-call(s32[1]{0:T(128)} %bitcast.5.where_ref, bf16[256,1152]{1,0:T(8,128)(2,1)} %get-tuple-element.396.normed_ref.refs_0_, bf16[256,1152]{1,0:T(8,128)(2,1)} %get-tuple-element.397.refs_1_, bf16[256,1152]{1,0:T(8,128)(2,1)} %get-tuple-element.398.refs_2_, ...), custom_call_target="tpu_custom_call" | custom-call | flops 800000000 | bytes 2560000 | tf_op jit(solution)/shard_map/pallas_call | solution.py:963
  349.7 4.5 %all-to-all-start = ((bf16[8,144,144]{1,2,0:T(8,128)(2,1)}), bf16[8,144,144]{1,2,0:T(8,128)(2,1)S(1)}, u32[]{:S(2)}, u32[]{:S(2)}) async-start(bf16[8,144,144]{1,2,0:T(8,128)(2,1)} %bitcast.35), calls=%async_computation.2 | async-start | bytes 1179648 | tf_op jit(solution)/shard_map/all_to_all | solution.py:1414
  354.8 1.5 shard_map.257
  357.5 1.5 collective-permute-start.69
  359.6 4.1 collective-permute-done.67.refs_5_
  364.4 4.8 %shard_map.256 = bf16[576,1152]{1,0:T(8,128)(2,1)} custom-call(f32[432,1152]{1,0:T(8,128)} %get-tuple-element.427.refs_0_, f32[432,1152]{1,0:T(8,128)} %collective-permute-done.64.refs_1_, f32[144,1152]{1,0:T(8,128)} %get-tuple-element.429.refs_2_, bf16[144,1152]{1,0:T(8,128)(2,1)} %copy-done.42, bf16[144,1152]{1,0:T(8,128)(2,1)} %copy-done.43, ...), custom_call_target="tpu_custom_call" | custom-call | flops 500000000 | bytes 1600000 | tf_op jit(solution)/shard_map/pallas_call | solution.py:1025
  369.8 2.7 reduce-scatter.6.cloned.1.call-done
  373.3 3.3 fusion.26
  376.7 2.6 collective-permute-start.73
  379.8 1.4 collective-permute-start.71
  385.6 2.8 collective-permute-done.78
  394.3 2.1 collective-permute-done.76
  399.0 7.0 %reduce-scatter.8.cloned.1.call-done = bf16[144,1152]{1,0:T(8,128)(2,1)} async-done(((bf16[576,1152]{1,0:T(8,128)(2,1)}), bf16[144,1152]{1,0:T(8,128)(2,1)}) %reduce-scatter.8.cloned.1.call-update) | async-done | bytes 331792 | tf_op jit(solution)/shard_map/reduce_scatter | solution.py:1054
  (365 shorter events, 78.9 us)
Async XLA Ops:
  7.2 298.3 %reduce-scatter.4.cloned.1.call-start = ((), (), s32[]{:S(2)}) async-start(), calls=%async_computation.4 | async-start | bytes 1658880 | tf_op jit(solution)/shard_map/reduce_scatter | solution.py:1054
  9.1 11.3 %collective-permute-start.2 = (bf16[1,1152]{1,0:T(2,128)(2,1)S(1)}, bf16[1,1152]{1,0:T(2,128)(2,1)S(1)}, u32[]{:S(2)}, u32[]{:S(2)}) collective-permute-start(bf16[1,1152]{1,0:T(2,128)(2,1)S(1)} %get-tuple-element.231.cond_ref), channel_id=1, source_target_pairs={{0,3},{1,0},{2,1},{3,2},{4,7},{5,4},{6,5},{7,6},{8,11},{9,8},{10,9... | collective-permute-start | bytes 6920 | tf_op jit(solution)/shard_map/ppermute | solution.py:63
  9.4 11.1 %collective-permute-start.1 = (bf16[1,1152]{1,0:T(2,128)(2,1)S(1)}, bf16[1,1152]{1,0:T(2,128)(2,1)S(1)}, u32[]{:S(2)}, u32[]{:S(2)}) collective-permute-start(bf16[1,1152]{1,0:T(2,128)(2,1)S(1)} %get-tuple-element.231.cond_ref), channel_id=1, source_target_pairs={{0,2},{1,3},{2,0},{3,1},{4,6},{5,7},{6,4},{7,5},{8,10},{9,11},{10,... | collective-permute-start | bytes 6920 | tf_op jit(solution)/shard_map/ppermute | solution.py:63
  9.4 11.1 %collective-permute-start = (bf16[1,1152]{1,0:T(2,128)(2,1)S(1)}, bf16[1,1152]{1,0:T(2,128)(2,1)S(1)}, u32[]{:S(2)}, u32[]{:S(2)}) collective-permute-start(bf16[1,1152]{1,0:T(2,128)(2,1)S(1)} %get-tuple-element.231.cond_ref), channel_id=1, source_target_pairs={{0,1},{1,2},{2,3},{3,0},{4,5},{5,6},{6,7},{7,4},{8,9},{9,10},{10,1... | collective-permute-start | bytes 6920 | tf_op jit(solution)/shard_map/ppermute | solution.py:63
  12.5 11.7 %collective-permute-start.3 = (bf16[9,8,3456]{2,1,0:T(8,128)(2,1)S(1)}, bf16[9,8,3456]{2,1,0:T(8,128)(2,1)S(1)}, u32[]{:S(2)}, u32[]{:S(2)}) collective-permute-start(bf16[9,8,3456]{2,1,0:T(8,128)(2,1)S(1)} %dynamic-slice_bitcast_fusion.2), channel_id=1, source_target_pairs={{0,1},{1,2},{2,3},{3,0},{4,5},{5,6},{6,7},{7,4},{8,9},{9,10},{10,1... | collective-permute-start | bytes 1493000 | tf_op jit(solution)/shard_map/ppermute | solution.py:63
  24.8 31.5 %collective-permute-start.9 = (bf16[256,2304]{1,0:T(8,128)(2,1)}, bf16[256,2304]{1,0:T(8,128)(2,1)S(1)}, u32[]{:S(2)}, u32[]{:S(2)}) collective-permute-start(bf16[256,2304]{1,0:T(8,128)(2,1)} %pad_maximum_fusion.1.refs_0_), channel_id=1, source_target_pairs={{0,16},{4,20},{8,24},{12,28},{16,0},{20,4},{24,8},{28,12},{1,17},{... | collective-permute-start | bytes 3538952 | tf_op jit(solution)/shard_map/ppermute | solution.py:57
  26.1 30.3 %collective-permute-start.8 = (bf16[256,2304]{1,0:T(8,128)(2,1)}, bf16[256,2304]{1,0:T(8,128)(2,1)S(1)}, u32[]{:S(2)}, u32[]{:S(2)}) collective-permute-start(bf16[256,2304]{1,0:T(8,128)(2,1)} %pad_maximum_fusion.1.refs_0_), channel_id=1, source_target_pairs={{0,8},{4,12},{8,0},{12,4},{16,24},{20,28},{24,16},{28,20},{1,9},{5... | collective-permute-start | bytes 3538952 | tf_op jit(solution)/shard_map/ppermute | solution.py:57
  27.3 16.2 %collective-permute-start.7 = (bf16[9,8,3456]{2,1,0:T(8,128)(2,1)S(1)}, bf16[9,8,3456]{2,1,0:T(8,128)(2,1)S(1)}, u32[]{:S(2)}, u32[]{:S(2)}) collective-permute-start(bf16[9,8,3456]{2,1,0:T(8,128)(2,1)S(1)} %collective-permute-done.3), channel_id=1, source_target_pairs={{0,1},{1,2},{2,3},{3,0},{4,5},{5,6},{6,7},{7,4},{8,9},{9,10},{10,1... | collective-permute-start | bytes 1493000 | tf_op jit(solution)/shard_map/ppermute | solution.py:63
  32.8 9.3 %collective-permute-start.5 = (f32[8,1152]{1,0:T(8,128)}, f32[8,1152]{1,0:T(8,128)S(1)}, u32[]{:S(2)}, u32[]{:S(2)}) collective-permute-start(f32[8,1152]{1,0:T(8,128)} %get-tuple-element.239), channel_id=1, source_target_pairs={{0,2},{1,3},{2,0},{3,1},{4,6},{5,7},{6,4},{7,5},{8,10},{9,11},{10,... | collective-permute-start | bytes 110600 | tf_op jit(solution)/shard_map/ppermute | solution.py:63
  43.5 12.9 %collective-permute-start.10 = (bf16[9,8,3456]{2,1,0:T(8,128)(2,1)S(1)}, bf16[9,8,3456]{2,1,0:T(8,128)(2,1)}, u32[]{:S(2)}, u32[]{:S(2)}) collective-permute-start(bf16[9,8,3456]{2,1,0:T(8,128)(2,1)S(1)} %collective-permute-done.7), channel_id=1, source_target_pairs={{0,1},{1,2},{2,3},{3,0},{4,5},{5,6},{6,7},{7,4},{8,9},{9,10},{10,1... | collective-permute-start | bytes 1493000 | tf_op jit(solution)/shard_map/ppermute | solution.py:63
  58.8 22.5 %collective-permute-start.12 = (bf16[3,9,8,3456]{3,2,1,0:T(8,128)(2,1)S(1)}, bf16[3,9,8,3456]{3,2,1,0:T(8,128)(2,1)}, u32[]{:S(2)}, u32[]{:S(2)}) collective-permute-start(bf16[3,9,8,3456]{3,2,1,0:T(8,128)(2,1)S(1)} %pad_maximum_fusion.refs_0_), channel_id=1, source_target_pairs={{0,4},{4,0},{8,12},{12,8},{16,20},{20,16},{24,28},{28,24},{1,5},{5... | collective-permute-start | bytes 4478984 | tf_op jit(solution)/shard_map/ppermute | solution.py:57
  61.7 19.6 %collective-permute-start.11 = (bf16[3,9,8,3456]{3,2,1,0:T(8,128)(2,1)S(1)}, bf16[3,9,8,3456]{3,2,1,0:T(8,128)(2,1)}, u32[]{:S(2)}, u32[]{:S(2)}) collective-permute-start(bf16[3,9,8,3456]{3,2,1,0:T(8,128)(2,1)S(1)} %pad_maximum_fusion.refs_0_), channel_id=1, source_target_pairs={{0,8},{4,20},{8,0},{12,28},{16,24},{20,4},{24,16},{28,12},{1,9},{5... | collective-permute-start | bytes 4478984 | tf_op jit(solution)/shard_map/ppermute | solution.py:60
  62.8 18.6 %collective-permute-start.13 = (bf16[9,8,2944]{2,1,0:T(8,128)(2,1)}, bf16[9,8,2944]{2,1,0:T(8,128)(2,1)}, u32[]{:S(2)}, u32[]{:S(2)}) collective-permute-start(bf16[9,8,2944]{2,1,0:T(8,128)(2,1)} %fusion), channel_id=1, source_target_pairs={{0,1},{1,2},{2,3},{3,0},{4,5},{5,6},{6,7},{7,4},{8,9},{9,10},{10,1... | collective-permute-start | bytes 1271816 | tf_op jit(solution)/shard_map/ppermute | solution.py:63
  67.5 13.8 %collective-permute-start.15 = (f32[8,1152]{1,0:T(8,128)S(1)}, f32[8,1152]{1,0:T(8,128)S(1)}, u32[]{:S(2)}, u32[]{:S(2)}) collective-permute-start(f32[8,1152]{1,0:T(8,128)S(1)} %copy-done.67), channel_id=1, source_target_pairs={{0,16},{4,20},{8,24},{12,28},{16,0},{20,4},{24,8},{28,12},{1,17},{... | collective-permute-start | bytes 110600 | tf_op jit(solution)/shard_map/ppermute | solution.py:57
  68.8 12.5 %collective-permute-start.14 = (f32[8,1152]{1,0:T(8,128)S(1)}, f32[8,1152]{1,0:T(8,128)S(1)}, u32[]{:S(2)}, u32[]{:S(2)}) collective-permute-start(f32[8,1152]{1,0:T(8,128)S(1)} %copy-done.67), channel_id=1, source_target_pairs={{0,8},{4,12},{8,0},{12,4},{16,24},{20,28},{24,16},{28,20},{1,9},{5... | collective-permute-start | bytes 110600 | tf_op jit(solution)/shard_map/ppermute | solution.py:57
  81.4 10.4 %collective-permute-start.16 = (bf16[3,9,8,3456]{3,2,1,0:T(8,128)(2,1)}, bf16[3,9,8,3456]{3,2,1,0:T(8,128)(2,1)}, u32[]{:S(2)}, u32[]{:S(2)}) collective-permute-start(bf16[3,9,8,3456]{3,2,1,0:T(8,128)(2,1)} %collective-permute-done.11.refs_1_), channel_id=1, source_target_pairs={{0,4},{4,0},{8,12},{12,8},{16,20},{20,16},{24,28},{28,24},{1,5},{5... | collective-permute-start | bytes 4478984 | tf_op jit(solution)/shard_map/ppermute | solution.py:57
  84.2 17.0 %collective-permute-start.19 = (bf16[128,2304]{1,0:T(8,128)(2,1)}, bf16[128,2304]{1,0:T(8,128)(2,1)S(1)}, u32[]{:S(2)}, u32[]{:S(2)}) collective-permute-start(bf16[128,2304]{1,0:T(8,128)(2,1)} %slice.141), channel_id=1, source_target_pairs={{0,8},{4,12},{8,0},{12,4},{16,24},{20,28},{24,16},{28,20},{1,9},{5... | collective-permute-start | bytes 1769480 | tf_op jit(solution)/shard_map/ppermute | solution.py:57
  84.5 16.8 %collective-permute-start.18 = (bf16[128,2304]{1,0:T(8,128)(2,1)S(1)}, bf16[128,2304]{1,0:T(8,128)(2,1)S(1)}, u32[]{:S(2)}, u32[]{:S(2)}) collective-permute-start(bf16[128,2304]{1,0:T(8,128)(2,1)S(1)} %slice.140), channel_id=1, source_target_pairs={{0,16},{4,20},{8,24},{12,28},{16,0},{20,4},{24,8},{28,12},{1,17},{... | collective-permute-start | bytes 1769480 | tf_op jit(solution)/shard_map/ppermute | solution.py:57
  84.7 16.5 %collective-permute-start.17 = (bf16[9,8,2944]{2,1,0:T(8,128)(2,1)}, bf16[9,8,2944]{2,1,0:T(8,128)(2,1)}, u32[]{:S(2)}, u32[]{:S(2)}) collective-permute-start(bf16[9,8,2944]{2,1,0:T(8,128)(2,1)} %collective-permute-done.13), channel_id=1, source_target_pairs={{0,1},{1,2},{2,3},{3,0},{4,5},{5,6},{6,7},{7,4},{8,9},{9,10},{10,1... | collective-permute-start | bytes 1271816 | tf_op jit(solution)/shard_map/ppermute | solution.py:63
  89.6 11.6 %collective-permute-start.20 = (f32[8,1152]{1,0:T(8,128)S(1)}, f32[8,1152]{1,0:T(8,128)S(1)}, u32[]{:S(2)}, u32[]{:S(2)}) collective-permute-start(f32[8,1152]{1,0:T(8,128)S(1)} %copy-done.67), channel_id=1, source_target_pairs={{0,24},{4,28},{8,16},{12,20},{16,8},{20,12},{24,0},{28,4},{1,25},{... | collective-permute-start | bytes 110600 | tf_op jit(solution)/shard_map/ppermute | solution.py:57
  104.2 19.3 %collective-permute-start.22 = (bf16[18,8,2944]{2,1,0:T(8,128)(2,1)S(1)}, bf16[18,8,2944]{2,1,0:T(8,128)(2,1)S(1)}, u32[]{:S(2)}, u32[]{:S(2)}) collective-permute-start(bf16[18,8,2944]{2,1,0:T(8,128)(2,1)S(1)} %constant_dynamic-update-slice_fusion.refs_2_), channel_id=1, source_target_pairs={{0,16},{4,20},{8,24},{12,28},{16,0},{20,4},{24,8},{28,12},{1,17},{... | collective-permute-start | bytes 2543624 | tf_op jit(solution)/shard_map/ppermute | solution.py:57
  104.5 19.0 %collective-permute-start.21 = (bf16[18,8,2944]{2,1,0:T(8,128)(2,1)S(1)}, bf16[18,8,2944]{2,1,0:T(8,128)(2,1)S(1)}, u32[]{:S(2)}, u32[]{:S(2)}) collective-permute-start(bf16[18,8,2944]{2,1,0:T(8,128)(2,1)S(1)} %constant_dynamic-update-slice_fusion.refs_2_), channel_id=1, source_target_pairs={{0,8},{4,12},{8,0},{12,4},{16,24},{20,28},{24,16},{28,20},{1,9},{5... | collective-permute-start | bytes 2543624 | tf_op jit(solution)/shard_map/ppermute | solution.py:57
  104.7 15.7 %collective-permute-start.23 = (bf16[9,8,2944]{2,1,0:T(8,128)(2,1)}, bf16[9,8,2944]{2,1,0:T(8,128)(2,1)S(1)}, u32[]{:S(2)}, u32[]{:S(2)}) collective-permute-start(bf16[9,8,2944]{2,1,0:T(8,128)(2,1)} %collective-permute-done.17), channel_id=1, source_target_pairs={{0,1},{1,2},{2,3},{3,0},{4,5},{5,6},{6,7},{7,4},{8,9},{9,10},{10,1... | collective-permute-start | bytes 1271816 | tf_op jit(solution)/shard_map/ppermute | solution.py:63
  123.5 20.1 %collective-permute-start.26 = (bf16[18,8,2944]{2,1,0:T(8,128)(2,1)S(1)}, bf16[18,8,2944]{2,1,0:T(8,128)(2,1)}, u32[]{:S(2)}, u32[]{:S(2)}) collective-permute-start(bf16[18,8,2944]{2,1,0:T(8,128)(2,1)S(1)} %constant_dynamic-update-slice_fusion.refs_2_), channel_id=1, source_target_pairs={{0,4},{4,0},{8,12},{12,8},{16,20},{20,16},{24,28},{28,24},{1,5},{5... | collective-permute-start | bytes 2543624 | tf_op jit(solution)/shard_map/ppermute | solution.py:57
  125.7 17.8 %collective-permute-start.27 = (bf16[36,8,1152]{2,1,0:T(8,128)(2,1)}, bf16[36,8,1152]{2,1,0:T(8,128)(2,1)}, u32[]{:S(2)}, u32[]{:S(2)}) collective-permute-start(bf16[36,8,1152]{2,1,0:T(8,128)(2,1)} %dynamic-slice_bitcast_fusion), channel_id=1, source_target_pairs={{0,1},{1,2},{2,3},{3,0},{4,5},{5,6},{6,7},{7,4},{8,9},{9,10},{10,1... | collective-permute-start | bytes 1990664 | tf_op jit(solution)/shard_map/ppermute | solution.py:63
  129.0 14.6 %collective-permute-start.25 = (bf16[9,8,2944]{2,1,0:T(8,128)(2,1)S(1)}, bf16[9,8,2944]{2,1,0:T(8,128)(2,1)S(1)}, u32[]{:S(2)}, u32[]{:S(2)}) collective-permute-start(bf16[9,8,2944]{2,1,0:T(8,128)(2,1)S(1)} %collective-permute-done.23.refs_3_), channel_id=1, source_target_pairs={{0,16},{4,20},{8,24},{12,28},{16,0},{20,4},{24,8},{28,12},{1,17},{... | collective-permute-start | bytes 1271816 | tf_op jit(solution)/shard_map/ppermute | solution.py:57
  129.2 14.4 %collective-permute-start.24 = (bf16[9,8,2944]{2,1,0:T(8,128)(2,1)S(1)}, bf16[9,8,2944]{2,1,0:T(8,128)(2,1)S(1)}, u32[]{:S(2)}, u32[]{:S(2)}) collective-permute-start(bf16[9,8,2944]{2,1,0:T(8,128)(2,1)S(1)} %collective-permute-done.23.refs_3_), channel_id=1, source_target_pairs={{0,8},{4,12},{8,0},{12,4},{16,24},{20,28},{24,16},{28,20},{1,9},{5... | collective-permute-start | bytes 1271816 | tf_op jit(solution)/shard_map/ppermute | solution.py:57
  143.6 21.5 %collective-permute-start.32 = (bf16[36,8,1152]{2,1,0:T(8,128)(2,1)}, bf16[36,8,1152]{2,1,0:T(8,128)(2,1)}, u32[]{:S(2)}, u32[]{:S(2)}) collective-permute-start(bf16[36,8,1152]{2,1,0:T(8,128)(2,1)} %collective-permute-done.27.refs_0_), channel_id=1, source_target_pairs={{0,1},{1,2},{2,3},{3,0},{4,5},{5,6},{6,7},{7,4},{8,9},{9,10},{10,1... | collective-permute-start | bytes 1990664 | tf_op jit(solution)/shard_map/ppermute | solution.py:63
  147.8 16.8 %collective-permute-start.29 = (bf16[14,8,2944]{2,1,0:T(8,128)(2,1)S(1)}, bf16[14,8,2944]{2,1,0:T(8,128)(2,1)}, u32[]{:S(2)}, u32[]{:S(2)}) collective-permute-start(bf16[14,8,2944]{2,1,0:T(8,128)(2,1)S(1)} %pad_maximum_fusion.2), channel_id=1, source_target_pairs={{0,8},{4,12},{8,0},{12,4},{16,24},{20,28},{24,16},{28,20},{1,9},{5... | collective-permute-start | bytes 1978376 | tf_op jit(solution)/shard_map/ppermute | solution.py:57
  148.1 14.1 %collective-permute-start.28 = (bf16[13,8,2944]{2,1,0:T(8,128)(2,1)S(1)}, bf16[13,8,2944]{2,1,0:T(8,128)(2,1)}, u32[]{:S(2)}, u32[]{:S(2)}) collective-permute-start(bf16[13,8,2944]{2,1,0:T(8,128)(2,1)S(1)} %slice.142), channel_id=1, source_target_pairs={{0,16},{4,20},{8,24},{12,28},{16,0},{20,4},{24,8},{28,12},{1,17},{... | collective-permute-start | bytes 1837064 | tf_op jit(solution)/shard_map/ppermute | solution.py:57
  148.8 16.3 %collective-permute-start.30 = (bf16[18,8,2944]{2,1,0:T(8,128)(2,1)S(1)}, bf16[18,8,2944]{2,1,0:T(8,128)(2,1)S(1)}, u32[]{:S(2)}, u32[]{:S(2)}) collective-permute-start(bf16[18,8,2944]{2,1,0:T(8,128)(2,1)S(1)} %collective-permute-done.21.refs_4_), channel_id=1, source_target_pairs={{0,4},{4,0},{8,12},{12,8},{16,20},{20,16},{24,28},{28,24},{1,5},{5... | collective-permute-start | bytes 2543624 | tf_op jit(solution)/shard_map/ppermute | solution.py:57
  150.5 14.7 %collective-permute-start.31 = (bf16[18,8,2944]{2,1,0:T(8,128)(2,1)S(1)}, bf16[18,8,2944]{2,1,0:T(8,128)(2,1)S(1)}, u32[]{:S(2)}, u32[]{:S(2)}) collective-permute-start(bf16[18,8,2944]{2,1,0:T(8,128)(2,1)S(1)} %collective-permute-done.22.refs_6_), channel_id=1, source_target_pairs={{0,4},{4,0},{8,12},{12,8},{16,20},{20,16},{24,28},{28,24},{1,5},{5... | collective-permute-start | bytes 2543624 | tf_op jit(solution)/shard_map/ppermute | solution.py:57
  165.9 25.1 %collective-permute-start.39 = (bf16[36,8,1152]{2,1,0:T(8,128)(2,1)}, bf16[36,8,1152]{2,1,0:T(8,128)(2,1)S(1)}, u32[]{:S(2)}, u32[]{:S(2)}) collective-permute-start(bf16[36,8,1152]{2,1,0:T(8,128)(2,1)} %collective-permute-done.27.refs_0_), channel_id=1, source_target_pairs={{0,8},{4,20},{8,0},{12,28},{16,24},{20,4},{24,16},{28,12},{1,9},{5... | collective-permute-start | bytes 1990664 | tf_op jit(solution)/shard_map/ppermute | solution.py:60
  166.6 24.4 %collective-permute-start.40 = (bf16[36,8,1152]{2,1,0:T(8,128)(2,1)}, bf16[36,8,1152]{2,1,0:T(8,128)(2,1)S(1)}, u32[]{:S(2)}, u32[]{:S(2)}) collective-permute-start(bf16[36,8,1152]{2,1,0:T(8,128)(2,1)} %collective-permute-done.32.refs_1_), channel_id=1, source_target_pairs={{0,8},{4,20},{8,0},{12,28},{16,24},{20,4},{24,16},{28,12},{1,9},{5... | collective-permute-start | bytes 1990664 | tf_op jit(solution)/shard_map/ppermute | solution.py:60
  167.8 23.3 %collective-permute-start.38 = (bf16[36,8,1152]{2,1,0:T(8,128)(2,1)}, bf16[36,8,1152]{2,1,0:T(8,128)(2,1)S(1)}, u32[]{:S(2)}, u32[]{:S(2)}) collective-permute-start(bf16[36,8,1152]{2,1,0:T(8,128)(2,1)} %collective-permute-done.32.refs_1_), channel_id=1, source_target_pairs={{0,1},{1,2},{2,3},{3,0},{4,5},{5,6},{6,7},{7,4},{8,9},{9,10},{10,1... | collective-permute-start | bytes 1990664 | tf_op jit(solution)/shard_map/ppermute | solution.py:63
  192.1 9.8 %collective-permute-start.41 = (bf16[36,8,1152]{2,1,0:T(8,128)(2,1)S(1)}, bf16[36,8,1152]{2,1,0:T(8,128)(2,1)S(1)}, u32[]{:S(2)}, u32[]{:S(2)}) collective-permute-start(bf16[36,8,1152]{2,1,0:T(8,128)(2,1)S(1)} %collective-permute-done.38.refs_2_), channel_id=1, source_target_pairs={{0,8},{4,20},{8,0},{12,28},{16,24},{20,4},{24,16},{28,12},{1,9},{5... | collective-permute-start | bytes 1990664 | tf_op jit(solution)/shard_map/ppermute | solution.py:60
  192.3 10.6 %collective-permute-start.44 = (bf16[36,8,1152]{2,1,0:T(8,128)(2,1)S(1)}, bf16[36,8,1152]{2,1,0:T(8,128)(2,1)S(1)}, u32[]{:S(2)}, u32[]{:S(2)}) collective-permute-start(bf16[36,8,1152]{2,1,0:T(8,128)(2,1)S(1)} %collective-permute-done.38.refs_2_), channel_id=1, source_target_pairs={{0,4},{4,0},{8,12},{12,8},{16,20},{20,16},{24,28},{28,24},{1,5},{5... | collective-permute-start | bytes 1990664 | tf_op jit(solution)/shard_map/ppermute | solution.py:57
  192.7 10.2 %collective-permute-start.43 = (bf16[36,8,1152]{2,1,0:T(8,128)(2,1)}, bf16[36,8,1152]{2,1,0:T(8,128)(2,1)S(1)}, u32[]{:S(2)}, u32[]{:S(2)}) collective-permute-start(bf16[36,8,1152]{2,1,0:T(8,128)(2,1)} %collective-permute-done.32.refs_1_), channel_id=1, source_target_pairs={{0,4},{4,0},{8,12},{12,8},{16,20},{20,16},{24,28},{28,24},{1,5},{5... | collective-permute-start | bytes 1990664 | tf_op jit(solution)/shard_map/ppermute | solution.py:57
  192.8 10.0 %collective-permute-start.45 = (bf16[36,8,1152]{2,1,0:T(8,128)(2,1)S(1)}, bf16[36,8,1152]{2,1,0:T(8,128)(2,1)S(1)}, u32[]{:S(2)}, u32[]{:S(2)}) collective-permute-start(bf16[36,8,1152]{2,1,0:T(8,128)(2,1)S(1)} %collective-permute-done.39.refs_3_), channel_id=1, source_target_pairs={{0,4},{4,0},{8,12},{12,8},{16,20},{20,16},{24,28},{28,24},{1,5},{5... | collective-permute-start | bytes 1990664 | tf_op jit(solution)/shard_map/ppermute | solution.py:57
  194.0 8.8 %collective-permute-start.46 = (bf16[36,8,1152]{2,1,0:T(8,128)(2,1)S(1)}, bf16[36,8,1152]{2,1,0:T(8,128)(2,1)S(1)}, u32[]{:S(2)}, u32[]{:S(2)}) collective-permute-start(bf16[36,8,1152]{2,1,0:T(8,128)(2,1)S(1)} %collective-permute-done.40.refs_4_), channel_id=1, source_target_pairs={{0,4},{4,0},{8,12},{12,8},{16,20},{20,16},{24,28},{28,24},{1,5},{5... | collective-permute-start | bytes 1990664 | tf_op jit(solution)/shard_map/ppermute | solution.py:57
  204.6 30.6 %collective-permute-start.48 = (bf16[1152,256]{1,0:T(8,128)(2,1)}, bf16[1152,256]{1,0:T(8,128)(2,1)}, u32[]{:S(2)}, u32[]{:S(2)}) collective-permute-start(bf16[1152,256]{1,0:T(8,128)(2,1)} %get-tuple-element.351), channel_id=1, source_target_pairs={{0,8},{4,12},{8,0},{12,4},{16,24},{20,28},{24,16},{28,20},{1,9},{5... | collective-permute-start | bytes 1769480 | tf_op jit(solution)/shard_map/ppermute | solution.py:57
  204.8 30.3 %collective-permute-start.49 = (bf16[1152,256]{1,0:T(8,128)(2,1)}, bf16[1152,256]{1,0:T(8,128)(2,1)}, u32[]{:S(2)}, u32[]{:S(2)}) collective-permute-start(bf16[1152,256]{1,0:T(8,128)(2,1)} %get-tuple-element.352), channel_id=1, source_target_pairs={{0,16},{4,20},{8,24},{12,28},{16,0},{20,4},{24,8},{28,12},{1,17},{... | collective-permute-start | bytes 1769480 | tf_op jit(solution)/shard_map/ppermute | solution.py:57
  205.5 29.7 %collective-permute-start.50 = (bf16[1152,256]{1,0:T(8,128)(2,1)}, bf16[1152,256]{1,0:T(8,128)(2,1)}, u32[]{:S(2)}, u32[]{:S(2)}) collective-permute-start(bf16[1152,256]{1,0:T(8,128)(2,1)} %get-tuple-element.353), channel_id=1, source_target_pairs={{0,24},{4,28},{8,16},{12,20},{16,8},{20,12},{24,0},{28,4},{1,25},{... | collective-permute-start | bytes 1769480 | tf_op jit(solution)/shard_map/ppermute | solution.py:57
  235.2 25.0 %collective-permute-start.51 = (bf16[1152,256]{1,0:T(8,128)(2,1)S(1)}, bf16[1152,256]{1,0:T(8,128)(2,1)S(1)}, u32[]{:S(2)}, u32[]{:S(2)}) collective-permute-start(bf16[1152,256]{1,0:T(8,128)(2,1)S(1)} %copy-done.65), channel_id=1, source_target_pairs={{0,8},{4,12},{8,0},{12,4},{16,24},{20,28},{24,16},{28,20},{1,9},{5... | collective-permute-start | bytes 1769480 | tf_op jit(solution)/shard_map/ppermute | solution.py:57
  235.5 24.7 %collective-permute-start.52 = (bf16[1152,256]{1,0:T(8,128)(2,1)S(1)}, bf16[1152,256]{1,0:T(8,128)(2,1)S(1)}, u32[]{:S(2)}, u32[]{:S(2)}) collective-permute-start(bf16[1152,256]{1,0:T(8,128)(2,1)S(1)} %copy-done.64), channel_id=1, source_target_pairs={{0,16},{4,20},{8,24},{12,28},{16,0},{20,4},{24,8},{28,12},{1,17},{... | collective-permute-start | bytes 1769480 | tf_op jit(solution)/shard_map/ppermute | solution.py:57
  236.1 25.3 %collective-permute-start.53 = (bf16[1152,256]{1,0:T(8,128)(2,1)S(1)}, bf16[1152,256]{1,0:T(8,128)(2,1)S(1)}, u32[]{:S(2)}, u32[]{:S(2)}) collective-permute-start(bf16[1152,256]{1,0:T(8,128)(2,1)S(1)} %copy-done.63), channel_id=1, source_target_pairs={{0,24},{4,28},{8,16},{12,20},{16,8},{20,12},{24,0},{28,4},{1,25},{... | collective-permute-start | bytes 1769480 | tf_op jit(solution)/shard_map/ppermute | solution.py:57
  270.6 24.8 %collective-permute-start.59 = (f32[4,144,1152]{2,1,0:T(8,128)}, f32[4,144,1152]{2,1,0:T(8,128)}, u32[]{:S(2)}, u32[]{:S(2)}) collective-permute-start(f32[4,144,1152]{2,1,0:T(8,128)} %get-tuple-element.391), channel_id=1, source_target_pairs={{0,4},{4,0},{8,12},{12,8},{16,20},{20,16},{24,28},{28,24},{1,5},{5... | collective-permute-start | bytes 7962632 | tf_op jit(solution)/shard_map/ppermute | solution.py:57
  276.0 96.5 %reduce-scatter.6.cloned.1.call-start = ((), (), s32[]{:S(2)}) async-start(), calls=%async_computation.5 | async-start | bytes 1658880 | tf_op jit(solution)/shard_map/reduce_scatter | solution.py:1054
  276.3 17.5 %collective-permute-start.56 = (bf16[256,1152]{1,0:T(8,128)(2,1)S(1)}, bf16[256,1152]{1,0:T(8,128)(2,1)S(1)}, u32[]{:S(2)}, u32[]{:S(2)}) collective-permute-start(bf16[256,1152]{1,0:T(8,128)(2,1)S(1)} %copy-done.25), channel_id=1, source_target_pairs={{0,16},{4,20},{8,24},{12,28},{16,0},{20,4},{24,8},{28,12},{1,17},{... | collective-permute-start | bytes 1769480 | tf_op jit(solution)/shard_map/ppermute | solution.py:57
  277.1 16.7 %collective-permute-start.55 = (bf16[256,1152]{1,0:T(8,128)(2,1)S(1)}, bf16[256,1152]{1,0:T(8,128)(2,1)S(1)}, u32[]{:S(2)}, u32[]{:S(2)}) collective-permute-start(bf16[256,1152]{1,0:T(8,128)(2,1)S(1)} %copy-done.25), channel_id=1, source_target_pairs={{0,8},{4,12},{8,0},{12,4},{16,24},{20,28},{24,16},{28,20},{1,9},{5... | collective-permute-start | bytes 1769480 | tf_op jit(solution)/shard_map/ppermute | solution.py:57
  313.3 17.3 %collective-permute-start.63 = (f32[576,1152]{1,0:T(8,128)}, f32[576,1152]{1,0:T(8,128)S(1)}, u32[]{:S(2)}, u32[]{:S(2)}) collective-permute-start(f32[576,1152]{1,0:T(8,128)} %get-tuple-element.416), channel_id=1, source_target_pairs={{0,4},{4,0},{8,12},{12,8},{16,20},{20,16},{24,28},{28,24},{1,5},{5... | collective-permute-start | bytes 7962632 | tf_op jit(solution)/shard_map/ppermute | solution.py:57
  314.1 22.8 %collective-permute-start.60 = (bf16[864,256]{1,0:T(8,128)(2,1)}, bf16[864,256]{1,0:T(8,128)(2,1)S(1)}, u32[]{:S(2)}, u32[]{:S(2)}) collective-permute-start(bf16[864,256]{1,0:T(8,128)(2,1)} %get-tuple-element.402), channel_id=1, source_target_pairs={{0,8},{4,12},{8,0},{12,4},{16,24},{20,28},{24,16},{28,20},{1,9},{5... | collective-permute-start | bytes 1327112 | tf_op jit(solution)/shard_map/ppermute | solution.py:57
  315.2 21.7 %collective-permute-start.61 = (bf16[864,256]{1,0:T(8,128)(2,1)}, bf16[864,256]{1,0:T(8,128)(2,1)S(1)}, u32[]{:S(2)}, u32[]{:S(2)}) collective-permute-start(bf16[864,256]{1,0:T(8,128)(2,1)} %get-tuple-element.403), channel_id=1, source_target_pairs={{0,16},{4,20},{8,24},{12,28},{16,0},{20,4},{24,8},{28,12},{1,17},{... | collective-permute-start | bytes 1327112 | tf_op jit(solution)/shard_map/ppermute | solution.py:57
  316.4 20.5 %collective-permute-start.62 = (bf16[864,256]{1,0:T(8,128)(2,1)}, bf16[864,256]{1,0:T(8,128)(2,1)S(1)}, u32[]{:S(2)}, u32[]{:S(2)}) collective-permute-start(bf16[864,256]{1,0:T(8,128)(2,1)} %get-tuple-element.404), channel_id=1, source_target_pairs={{0,24},{4,28},{8,16},{12,20},{16,8},{20,12},{24,0},{28,4},{1,25},{... | collective-permute-start | bytes 1327112 | tf_op jit(solution)/shard_map/ppermute | solution.py:57
  345.0 18.7 %collective-permute-start.64 = (f32[432,1152]{1,0:T(8,128)}, f32[432,1152]{1,0:T(8,128)}, u32[]{:S(2)}, u32[]{:S(2)}) collective-permute-start(f32[432,1152]{1,0:T(8,128)} %get-tuple-element.428), channel_id=1, source_target_pairs={{0,4},{4,0},{8,12},{12,8},{16,20},{20,16},{24,28},{28,24},{1,5},{5... | collective-permute-start | bytes 5971976 | tf_op jit(solution)/shard_map/ppermute | solution.py:57
  345.9 11.5 %collective-permute-start.65 = (bf16[144,1152]{1,0:T(8,128)(2,1)}, bf16[144,1152]{1,0:T(8,128)(2,1)S(1)}, u32[]{:S(2)}, u32[]{:S(2)}) collective-permute-start(bf16[144,1152]{1,0:T(8,128)(2,1)} %get-tuple-element.430), channel_id=1, source_target_pairs={{0,8},{4,12},{8,0},{12,4},{16,24},{20,28},{24,16},{28,20},{1,9},{5... | collective-permute-start | bytes 995336 | tf_op jit(solution)/shard_map/ppermute | solution.py:57
  347.1 11.9 %collective-permute-start.66 = (bf16[144,1152]{1,0:T(8,128)(2,1)S(1)}, bf16[144,1152]{1,0:T(8,128)(2,1)S(1)}, u32[]{:S(2)}, u32[]{:S(2)}) collective-permute-start(bf16[144,1152]{1,0:T(8,128)(2,1)S(1)} %copy-done.66), channel_id=1, source_target_pairs={{0,16},{4,20},{8,24},{12,28},{16,0},{20,4},{24,8},{28,12},{1,17},{... | collective-permute-start | bytes 995336 | tf_op jit(solution)/shard_map/ppermute | solution.py:57
  348.3 15.4 %collective-permute-start.67 = (bf16[144,1152]{1,0:T(8,128)(2,1)}, bf16[144,1152]{1,0:T(8,128)(2,1)S(1)}, u32[]{:S(2)}, u32[]{:S(2)}) collective-permute-start(bf16[144,1152]{1,0:T(8,128)(2,1)} %get-tuple-element.432), channel_id=1, source_target_pairs={{0,24},{4,28},{8,16},{12,20},{16,8},{20,12},{24,0},{28,4},{1,25},{... | collective-permute-start | bytes 995336 | tf_op jit(solution)/shard_map/ppermute | solution.py:57
  349.7 20.1 %all-to-all-start = ((bf16[8,144,144]{1,2,0:T(8,128)(2,1)}), bf16[8,144,144]{1,2,0:T(8,128)(2,1)S(1)}, u32[]{:S(2)}, u32[]{:S(2)}) async-start(bf16[8,144,144]{1,2,0:T(8,128)(2,1)} %bitcast.35), calls=%async_computation.2 | async-start | bytes 1179648 | tf_op jit(solution)/shard_map/all_to_all | solution.py:1414
  354.2 51.8 %reduce-scatter.8.cloned.1.call-start = ((), (), s32[]{:S(2)}) async-start(), calls=%async_computation.6 | async-start | bytes 1658880 | tf_op jit(solution)/shard_map/reduce_scatter | solution.py:1054
  356.3 13.0 %collective-permute-start.70 = (f32[16,1152]{1,0:T(8,128)}, f32[16,1152]{1,0:T(8,128)S(1)}, u32[]{:S(2)}, u32[]{:S(2)}) collective-permute-start(f32[16,1152]{1,0:T(8,128)} %shard_map.257), channel_id=1, source_target_pairs={{0,3},{1,0},{2,1},{3,2},{4,7},{5,4},{6,5},{7,6},{8,11},{9,8},{10,9... | collective-permute-start | bytes 221192 | tf_op jit(solution)/shard_map/ppermute | solution.py:63
  357.5 12.3 %collective-permute-start.69 = (f32[16,1152]{1,0:T(8,128)}, f32[16,1152]{1,0:T(8,128)S(1)}, u32[]{:S(2)}, u32[]{:S(2)}) collective-permute-start(f32[16,1152]{1,0:T(8,128)} %shard_map.257), channel_id=1, source_target_pairs={{0,2},{1,3},{2,0},{3,1},{4,6},{5,7},{6,4},{7,5},{8,10},{9,11},{10,... | collective-permute-start | bytes 221192 | tf_op jit(solution)/shard_map/ppermute | solution.py:63
  359.0 10.8 %collective-permute-start.68 = (f32[16,1152]{1,0:T(8,128)}, f32[16,1152]{1,0:T(8,128)S(1)}, u32[]{:S(2)}, u32[]{:S(2)}) collective-permute-start(f32[16,1152]{1,0:T(8,128)} %shard_map.257), channel_id=1, source_target_pairs={{0,1},{1,2},{2,3},{3,0},{4,5},{5,6},{6,7},{7,4},{8,9},{9,10},{10,1... | collective-permute-start | bytes 221192 | tf_op jit(solution)/shard_map/ppermute | solution.py:63
  373.2 11.8 %collective-permute-start.77 = (f32[8,1152]{1,0:T(8,128)S(1)}, f32[8,1152]{1,0:T(8,128)S(1)}, u32[]{:S(2)}, u32[]{:S(2)}) collective-permute-start(f32[8,1152]{1,0:T(8,128)S(1)} %slice_add_fusion), channel_id=1, source_target_pairs={{0,4},{4,0},{8,12},{12,8},{16,20},{20,16},{24,28},{28,24},{1,5},{5... | collective-permute-start | bytes 110600 | tf_op jit(solution)/shard_map/ppermute | solution.py:57
  (88 other events, 772.2 us)
Sparse Core Ops, SparseCore 0:
  276.1 29.3 reduce-scatter.3
  337.1 35.2 reduce-scatter.5
  374.8 31.1 reduce-scatter.7
